TPU v7x, 256 devices: a whole 4x4x8 slice. The times are simulated.
256 devices in a mesh: group: 8 (over x, core), dev: 32 (over y, z).
Axes of the slice: x: 4, y: 4, z: 8, core: 2. Of those that a mesh axis runs over, the one named last changes fastest.
Arguments:
- queries: bfloat16 [2048, 32, 128], P(('group', 'dev')), may hold values from -0.5390625 to 0.5390625
- passages: bfloat16 [4096, 256, 128], P(('group', 'dev')), may hold values from -6 to 6
- candidates: int32 [2048, 16], P(('group', 'dev')), may hold values from 0 to 4095, as said below
- location: int32 [4096], replicated, may hold values from 0 to 4095, as said below
Outputs:
- loss: float32 [2048], P(('group', 'dev'))
- query_grad: float32 [2048, 32, 128], P(('group', 'dev'))
Inputs may be any that keep to these rules, and one draw needn't show every extreme that they name: `candidates`: for each device holding queries and each device holding passage rows (rows of passages split evenly over group+dev in order), at most 2 of the sending device's pairs (query, listed document) have their document's row on that device. In every draw one device receives exactly 2 such pairs from every device. `location`: A permutation of the documents.
All inputs are finite; a program needn't handle non-finite values.
Results may differ from a plain program's by a relative error of at most 0.011.
Values may be sent and summed in bfloat16 or wider, within the bound.
A program may use at most 64 MiB of HBM per device.

v0:
```python
import jax
import jax.numpy as jnp
from jax import lax
from jax.sharding import PartitionSpec as P

SOFTNESS = 0.02
EPSILON = 1e-06


def normalize(values):
    floats = values.astype(jnp.float32)
    scale = lax.rsqrt(jnp.sum(floats * floats, axis=-1, keepdims=True) + EPSILON)
    return (floats * scale, scale)


def local(queries, passages, candidates, location):
    group_count = lax.axis_size("group")
    dev_count = lax.axis_size("dev")
    device_total = group_count * dev_count
    query_count, query_len, feat_width = queries.shape
    pass_count = passages.shape[0]
    list_len = candidates.shape[1]
    pair_count = query_count * list_len
    slot_cap = max(2, (3 * pair_count + device_total - 1) // device_total)
    slot_total = device_total * slot_cap
    query_unit, query_scale = normalize(queries)
    query_send = query_unit.astype(jnp.bfloat16)
    passage_unit = normalize(passages)[0].astype(jnp.bfloat16)
    rows = jnp.take(location, candidates.reshape(-1), axis=0)
    target = rows // pass_count
    local_row = rows % pass_count
    same_target = target[:, None] == target[None, :]
    positions = jnp.arange(pair_count, dtype=jnp.int32)
    earlier = positions[None, :] < positions[:, None]
    before = jnp.sum(same_target & earlier, axis=1)
    slot_index = target * slot_cap + before
    query_owner = positions // list_len
    outgoing = jnp.zeros((slot_total, query_len, feat_width), jnp.bfloat16)
    outgoing = outgoing.at[slot_index].set(query_send[query_owner])
    labels = (
        jnp.zeros((slot_total,), jnp.bfloat16).at[slot_index].set(local_row.astype(jnp.bfloat16))
    )
    outgoing = outgoing.reshape(group_count, dev_count, slot_cap, query_len, feat_width)
    labels = labels.reshape(group_count, dev_count, slot_cap)
    mid_queries, mid_labels = (
        lax.all_to_all(outgoing, "dev", split_axis=1, concat_axis=1, tiled=True),
        lax.all_to_all(labels, "dev", split_axis=1, concat_axis=1, tiled=True),
    )
    arrived, tags = (
        lax.all_to_all(mid_queries, "group", split_axis=0, concat_axis=0, tiled=True),
        lax.all_to_all(mid_labels, "group", split_axis=0, concat_axis=0, tiled=True),
    )
    block_rows = dev_count * slot_cap
    arrived = arrived.reshape(group_count, block_rows, query_len, feat_width)
    tags = tags.reshape(group_count, block_rows).astype(jnp.int32)

    def score_block(inputs):
        query_block, tag_block = inputs
        passage_block = jnp.take(passage_unit, tag_block, axis=0)
        logits = (
            jnp.einsum(
                "bqe,bpe->bqp", query_block, passage_block, preferred_element_type=jnp.float32
            )
            / SOFTNESS
        )
        exp_terms = jnp.exp(logits)
        token_mass = jnp.sum(exp_terms, axis=-1, keepdims=True)
        pair_score = jnp.sum(SOFTNESS * jnp.log(token_mass[..., 0]), axis=-1)
        attention = (exp_terms / token_mass).astype(jnp.bfloat16)
        pulled = jnp.einsum(
            "bqp,bpe->bqe", attention, passage_block, preferred_element_type=jnp.float32
        )
        return (pulled.astype(jnp.bfloat16), pair_score)

    pulled, scores = lax.map(score_block, (arrived, tags))
    pulled = pulled.reshape(group_count, dev_count, slot_cap, query_len, feat_width)
    scores = scores.reshape(group_count, dev_count, slot_cap)
    mid_pulled = lax.all_to_all(pulled, "dev", split_axis=1, concat_axis=1, tiled=True)
    pulled_back = lax.all_to_all(mid_pulled, "group", split_axis=0, concat_axis=0, tiled=True)
    mid_scores = lax.all_to_all(scores, "dev", split_axis=1, concat_axis=1, tiled=True)
    scores_back = lax.all_to_all(mid_scores, "group", split_axis=0, concat_axis=0, tiled=True)
    pulled_flat = pulled_back.reshape(slot_total, query_len, feat_width)
    scores_flat = scores_back.reshape(slot_total)
    pair_pulled = jnp.take(pulled_flat, slot_index, axis=0).reshape(
        query_count, list_len, query_len, feat_width
    )
    pair_score = jnp.take(scores_flat, slot_index, axis=0).reshape(query_count, list_len)
    exp_scores = jnp.exp(pair_score)
    total = jnp.sum(exp_scores, axis=-1, keepdims=True)
    loss = jnp.log(total[:, 0]) - pair_score[:, 0]
    first = (jnp.arange(list_len) == 0).astype(jnp.float32)
    coeff = exp_scores / total - first[None, :]
    unit_grad = jnp.einsum("bk,bkqe->bqe", coeff, pair_pulled.astype(jnp.float32))
    along = jnp.sum(query_unit * unit_grad, axis=-1, keepdims=True)
    query_grad = (unit_grad - query_unit * along) * query_scale
    return (loss, query_grad)


def solution(mesh):
    placed = (
        P(("group", "dev"), None, None),
        P(("group", "dev"), None, None),
        P(("group", "dev"), None),
        P(),
    )
    return jax.shard_map(
        local,
        mesh=mesh,
        in_specs=placed,
        out_specs=(P(("group", "dev")), P(("group", "dev"), None, None)),
        check_vma=False,
    )
```

profile of v0, /device:TPU:8, one launch (start us, length us, event | category | flops | bytes accessed | tf_op | source)
XLA Modules:
  0.0 471.2 jit_solution(18040989166478552376)
XLA Ops:
  6.0 11.7 %all-to-all-start.2 = ((bf16[8,32,2]{0,2,1:T(2,128)(2,1)}), bf16[8,32,2]{0,2,1:T(2,128)(2,1)S(1)}, u32[]{:S(2)}, u32[]{:S(2)}) async-start(bf16[8,32,2]{0,2,1:T(2,128)(2,1)} %copy.41), calls=%async_computation.2 | async-start | bytes 32768 | tf_op jit(solution)/shard_map/all_to_all | solution.py:47
  22.9 13.7 %scatter_fusion = bf16[512,32,128]{2,1,0:T(8,128)(2,1)} fusion(bf16[512,32,128]{2,1,0:T(8,128)(2,1)} %broadcast_in_dim.73, s32[128]{0:T(128)S(1)} %fusion.36, bf16[128,32,128]{2,1,0:T(8,128)(2,1)S(1)} %gather_fusion.2), kind=kCustom, calls=%fused_computation.5 | custom fusion | bytes 3146240 | tf_op jit(solution)/shard_map/scatter | solution.py:39
  36.5 5.6 %copy.39 = bf16[8,32,2,32,128]{4,3,2,0,1:T(8,128)(2,1)} copy(bf16[8,32,2,32,128]{4,3,2,1,0:T(8,128)(2,1)} %bitcast.55) | data formatting | bytes 8388608 | tf_op jit(solution)/shard_map/reshape | solution.py:43
  42.1 9.9 %all-to-all-start = ((bf16[8,32,2,32,128]{4,3,2,0,1:T(8,128)(2,1)}), bf16[8,32,2,32,128]{4,3,2,0,1:T(8,128)(2,1)}, u32[]{:S(2)}, u32[]{:S(2)}) async-start(bf16[8,32,2,32,128]{4,3,2,0,1:T(8,128)(2,1)} %copy.39), calls=%async_computation | async-start | bytes 8388608 | tf_op jit(solution)/shard_map/all_to_all | solution.py:46
  52.7 92.5 %all-to-all-done = bf16[8,32,2,32,128]{4,3,2,0,1:T(8,128)(2,1)} async-done(((bf16[8,32,2,32,128]{4,3,2,0,1:T(8,128)(2,1)}), bf16[8,32,2,32,128]{4,3,2,0,1:T(8,128)(2,1)}, u32[]{:S(2)}, u32[]{:S(2)}) %all-to-all-start) | async-done | bytes 4194336 | tf_op jit(solution)/shard_map/all_to_all | solution.py:46
  145.1 4.3 all-to-all-start.3
  149.4 5.5 %copy.40 = bf16[8,32,2,32,128]{4,3,2,1,0:T(8,128)(2,1)} copy(bf16[8,32,2,32,128]{4,3,2,0,1:T(8,128)(2,1)} %all-to-all-done) | data formatting | bytes 8388608 | tf_op jit(solution)/shard_map/all_to_all | solution.py:46
  155.0 4.9 %all-to-all-start.1 = ((bf16[8,32,2,32,128]{4,3,2,1,0:T(8,128)(2,1)}), bf16[8,32,2,32,128]{4,3,2,1,0:T(8,128)(2,1)}, u32[]{:S(2)}, u32[]{:S(2)}) async-start(bf16[8,32,2,32,128]{4,3,2,1,0:T(8,128)(2,1)} %copy.40), calls=%async_computation.1 | async-start | bytes 8388608 | tf_op jit(solution)/shard_map/all_to_all | solution.py:50
  161.4 48.2 %all-to-all-done.1 = bf16[8,32,2,32,128]{4,3,2,1,0:T(8,128)(2,1)} async-done(((bf16[8,32,2,32,128]{4,3,2,1,0:T(8,128)(2,1)}), bf16[8,32,2,32,128]{4,3,2,1,0:T(8,128)(2,1)}, u32[]{:S(2)}, u32[]{:S(2)}) %all-to-all-start.1) | async-done | bytes 4194336 | tf_op jit(solution)/shard_map/all_to_all | solution.py:50
  209.7 74.8 %while.12 = (s32[]{:T(128)}, bf16[8,64,32,128]{3,2,1,0:T(8,128)(2,1)}, f32[8,64]{1,0:T(8,128)S(1)}, bf16[8,64,32,128]{3,2,1,0:T(8,128)(2,1)}, s32[8,64]{1,0:T(8,...) while((s32[]{:T(128)}, bf16[8,64,32,128]{3,2,1,0:T(8,128)(2,1)}, ...), condition=%wide.region_8.9_spmd, body=%wide.region_5.8_spmd.sunk | while | flops 275516928 | bytes 38829372 | solution.py:75
  212.8 4.2 fusion.45
  219.0 3.1 gather_fusion
  222.1 4.2 fusion.45
  228.4 3.1 gather_fusion
  231.5 4.2 fusion.45
  237.8 3.1 gather_fusion
  240.8 4.2 fusion.45
  247.1 3.1 gather_fusion
  250.2 4.2 fusion.45
  256.5 3.1 gather_fusion
  259.6 4.2 fusion.45
  268.9 4.2 fusion.45
  278.2 4.2 fusion.45
  285.2 8.4 %all-to-all-start.4 = ((f32[8,32,2]{0,2,1:T(2,128)}), f32[8,32,2]{0,2,1:T(2,128)S(1)}, u32[]{:S(2)}, u32[]{:S(2)}) async-start(f32[8,32,2]{0,2,1:T(2,128)} %bitcast.14), calls=%async_computation.4 | async-start | bytes 65536 | tf_op jit(solution)/shard_map/all_to_all | solution.py:80
  293.5 5.6 %copy.49 = bf16[8,32,2,32,128]{4,3,2,0,1:T(8,128)(2,1)} copy(bf16[8,32,2,32,128]{4,3,2,1,0:T(8,128)(2,1)} %bitcast.56) | data formatting | bytes 8388608 | tf_op jit(solution)/shard_map/reshape | solution.py:76
  299.1 3.1 all-to-all-done.4
  302.2 6.7 %all-to-all-start.6 = ((bf16[8,32,2,32,128]{4,3,2,0,1:T(8,128)(2,1)}), bf16[8,32,2,32,128]{4,3,2,0,1:T(8,128)(2,1)}, u32[]{:S(2)}, u32[]{:S(2)}) async-start(bf16[8,32,2,32,128]{4,3,2,0,1:T(8,128)(2,1)} %copy.49), calls=%async_computation.6 | async-start | bytes 8388608 | tf_op jit(solution)/shard_map/all_to_all | solution.py:78
  309.6 92.5 %all-to-all-done.6 = bf16[8,32,2,32,128]{4,3,2,0,1:T(8,128)(2,1)} async-done(((bf16[8,32,2,32,128]{4,3,2,0,1:T(8,128)(2,1)}), bf16[8,32,2,32,128]{4,3,2,0,1:T(8,128)(2,1)}, u32[]{:S(2)}, u32[]{:S(2)}) %all-to-all-start.6) | async-done | bytes 4194336 | tf_op jit(solution)/shard_map/all_to_all | solution.py:78
  402.1 3.5 all-to-all-start.5
  405.6 5.5 %copy.50 = bf16[8,32,2,32,128]{4,3,2,1,0:T(8,128)(2,1)} copy(bf16[8,32,2,32,128]{4,3,2,0,1:T(8,128)(2,1)} %all-to-all-done.6) | data formatting | bytes 8388608 | tf_op jit(solution)/shard_map/all_to_all | solution.py:78
  411.1 4.9 %all-to-all-start.7 = ((bf16[8,32,2,32,128]{4,3,2,1,0:T(8,128)(2,1)}), bf16[8,32,2,32,128]{4,3,2,1,0:T(8,128)(2,1)}, u32[]{:S(2)}, u32[]{:S(2)}) async-start(bf16[8,32,2,32,128]{4,3,2,1,0:T(8,128)(2,1)} %copy.50), calls=%async_computation.7 | async-start | bytes 8388608 | tf_op jit(solution)/shard_map/all_to_all | solution.py:79
  418.7 47.1 %all-to-all-done.7 = bf16[8,32,2,32,128]{4,3,2,1,0:T(8,128)(2,1)} async-done(((bf16[8,32,2,32,128]{4,3,2,1,0:T(8,128)(2,1)}), bf16[8,32,2,32,128]{4,3,2,1,0:T(8,128)(2,1)}, u32[]{:S(2)}, u32[]{:S(2)}) %all-to-all-start.7) | async-done | bytes 4194336 | tf_op jit(solution)/shard_map/all_to_all | solution.py:79
  (124 shorter events, 48.0 us)
Async XLA Ops:
  0.6 1.6 copy-start
  6.0 36.1 %all-to-all-start.2 = ((bf16[8,32,2]{0,2,1:T(2,128)(2,1)}), bf16[8,32,2]{0,2,1:T(2,128)(2,1)S(1)}, u32[]{:S(2)}, u32[]{:S(2)}) async-start(bf16[8,32,2]{0,2,1:T(2,128)(2,1)} %copy.41), calls=%async_computation.2 | async-start | bytes 32768 | tf_op jit(solution)/shard_map/all_to_all | solution.py:47
  42.1 103.0 %all-to-all-start = ((bf16[8,32,2,32,128]{4,3,2,0,1:T(8,128)(2,1)}), bf16[8,32,2,32,128]{4,3,2,0,1:T(8,128)(2,1)}, u32[]{:S(2)}, u32[]{:S(2)}) async-start(bf16[8,32,2,32,128]{4,3,2,0,1:T(8,128)(2,1)} %copy.39), calls=%async_computation | async-start | bytes 8388608 | tf_op jit(solution)/shard_map/all_to_all | solution.py:46
  145.1 9.8 %all-to-all-start.3 = ((bf16[8,32,2]{1,2,0:T(2,128)(2,1)}), bf16[8,32,2]{1,2,0:T(2,128)(2,1)S(1)}, u32[]{:S(2)}, u32[]{:S(2)}) async-start(bf16[8,32,2]{1,2,0:T(2,128)(2,1)} %copy.42), calls=%async_computation.3 | async-start | bytes 8192 | tf_op jit(solution)/shard_map/all_to_all | solution.py:51
  155.0 4.9 %copy-start.2 = (bf16[16,256,128]{2,1,0:T(8,128)(2,1)S(1)}, bf16[16,256,128]{2,1,0:T(8,128)(2,1)}, u32[]{:S(2)}) copy-start(bf16[16,256,128]{2,1,0:T(8,128)(2,1)} %param.7) | copy-start | bytes 3145732
  155.0 54.7 %all-to-all-start.1 = ((bf16[8,32,2,32,128]{4,3,2,1,0:T(8,128)(2,1)}), bf16[8,32,2,32,128]{4,3,2,1,0:T(8,128)(2,1)}, u32[]{:S(2)}, u32[]{:S(2)}) async-start(bf16[8,32,2,32,128]{4,3,2,1,0:T(8,128)(2,1)} %copy.40), calls=%async_computation.1 | async-start | bytes 8388608 | tf_op jit(solution)/shard_map/all_to_all | solution.py:50
  212.7 4.2 copy-start.1
  222.1 4.2 copy-start.1
  231.5 4.2 copy-start.1
  240.8 4.2 copy-start.1
  250.2 4.2 copy-start.1
  259.5 4.2 copy-start.1
  268.9 4.2 copy-start.1
  278.2 4.2 copy-start.1
  285.2 17.0 %all-to-all-start.4 = ((f32[8,32,2]{0,2,1:T(2,128)}), f32[8,32,2]{0,2,1:T(2,128)S(1)}, u32[]{:S(2)}, u32[]{:S(2)}) async-start(f32[8,32,2]{0,2,1:T(2,128)} %bitcast.14), calls=%async_computation.4 | async-start | bytes 65536 | tf_op jit(solution)/shard_map/all_to_all | solution.py:80
  302.2 99.9 %all-to-all-start.6 = ((bf16[8,32,2,32,128]{4,3,2,0,1:T(8,128)(2,1)}), bf16[8,32,2,32,128]{4,3,2,0,1:T(8,128)(2,1)}, u32[]{:S(2)}, u32[]{:S(2)}) async-start(bf16[8,32,2,32,128]{4,3,2,0,1:T(8,128)(2,1)} %copy.49), calls=%async_computation.6 | async-start | bytes 8388608 | tf_op jit(solution)/shard_map/all_to_all | solution.py:78
  402.1 9.0 %all-to-all-start.5 = ((f32[8,32,2]{1,2,0:T(2,128)}), f32[8,32,2]{1,2,0:T(2,128)S(1)}, u32[]{:S(2)}, u32[]{:S(2)}) async-start(f32[8,32,2]{1,2,0:T(2,128)} %copy.47), calls=%async_computation.5 | async-start | bytes 16384 | tf_op jit(solution)/shard_map/all_to_all | solution.py:81
  411.1 6.7 %copy-start.4 = (s32[8,16]{1,0:T(8,128)S(1)}, s32[8,16]{1,0:T(8,128)}, u32[]{:S(2)}) copy-start(s32[8,16]{1,0:T(8,128)} %param.8) | copy-start | bytes 1540
  411.1 54.6 %all-to-all-start.7 = ((bf16[8,32,2,32,128]{4,3,2,1,0:T(8,128)(2,1)}), bf16[8,32,2,32,128]{4,3,2,1,0:T(8,128)(2,1)}, u32[]{:S(2)}, u32[]{:S(2)}) async-start(bf16[8,32,2,32,128]{4,3,2,1,0:T(8,128)(2,1)} %copy.50), calls=%async_computation.7 | async-start | bytes 8388608 | tf_op jit(solution)/shard_map/all_to_all | solution.py:79
  416.0 53.3 %copy-start.3 = (bf16[8,32,128]{2,1,0:T(8,128)(2,1)S(1)}, bf16[8,32,128]{2,1,0:T(8,128)(2,1)}, u32[]{:S(2)}) copy-start(bf16[8,32,128]{2,1,0:T(8,128)(2,1)} %param.6) | copy-start | bytes 196612
where the time goes:
time: 476 us; the launch traced here: 471 us
  waiting for transfers between devices  283 us (59%)
  local copies, waits for them, and re-layouts  75.9 us (16%)
  starting transfers between devices  54.3 us (11%)
  matrix products  49 us (10%)
  other arithmetic  7.34 us (2%)
    all_to_all x1, waiting for transfers between devices, local(): lax.all_to_all(pulled, 'dev', split_axis=1, concat_axis=1, tiled=True)  92.5 us
    all_to_all x1, waiting for transfers between devices, local(): lax.all_to_all(outgoing, 'dev', split_axis=1, concat_axis=1, tiled=True)  92.5 us
    all_to_all x1, waiting for transfers between devices, local(): lax.all_to_all(mid_queries, 'group', split_axis=0, concat_axis=0, tiled=T...  48.2 us
    all_to_all x1, waiting for transfers between devices, local(): lax.all_to_all(mid_pulled, 'group', split_axis=0, concat_axis=0, tiled=True)  47.1 us
    dot_general x8, matrix products, score_block(): jnp.einsum('bqe,bpe->bqp', query_block, passage_block, preferred_element_...  33.3 us
    gather x8, local copies, waits for them, and re-layouts, score_block(): passage_block = jnp.take(passage_unit, tag_block, axis=0)  24.4 us
    dot_general x8, matrix products, score_block(): jnp.einsum('bqp,bpe->bqe', attention, passage_block, preferred_element_ty...  15.4 us
    scatter x1, local copies, waits for them, and re-layouts, local(): outgoing = outgoing.at[slot_index].set(query_send[query_owner])  13.7 us
  transfers between devices with their start and end apart: 8, of which 5 were waited for; matrix products, arithmetic and copies ran while one was open for 10% of the time, Pallas kernels for 0%

commit v1 on v0

--- a/solution.py
+++ b/solution.py
@@ -40,16 +40,9 @@
     labels = (
         jnp.zeros((slot_total,), jnp.bfloat16).at[slot_index].set(local_row.astype(jnp.bfloat16))
     )
-    outgoing = outgoing.reshape(group_count, dev_count, slot_cap, query_len, feat_width)
-    labels = labels.reshape(group_count, dev_count, slot_cap)
-    mid_queries, mid_labels = (
-        lax.all_to_all(outgoing, "dev", split_axis=1, concat_axis=1, tiled=True),
-        lax.all_to_all(labels, "dev", split_axis=1, concat_axis=1, tiled=True),
-    )
-    arrived, tags = (
-        lax.all_to_all(mid_queries, "group", split_axis=0, concat_axis=0, tiled=True),
-        lax.all_to_all(mid_labels, "group", split_axis=0, concat_axis=0, tiled=True),
-    )
+    both_axes = ("group", "dev")
+    arrived = lax.all_to_all(outgoing, both_axes, split_axis=0, concat_axis=0, tiled=True)
+    tags = lax.all_to_all(labels, both_axes, split_axis=0, concat_axis=0, tiled=True)
     block_rows = dev_count * slot_cap
     arrived = arrived.reshape(group_count, block_rows, query_len, feat_width)
     tags = tags.reshape(group_count, block_rows).astype(jnp.int32)
@@ -73,14 +66,10 @@
         return (pulled.astype(jnp.bfloat16), pair_score)
 
     pulled, scores = lax.map(score_block, (arrived, tags))
-    pulled = pulled.reshape(group_count, dev_count, slot_cap, query_len, feat_width)
-    scores = scores.reshape(group_count, dev_count, slot_cap)
-    mid_pulled = lax.all_to_all(pulled, "dev", split_axis=1, concat_axis=1, tiled=True)
-    pulled_back = lax.all_to_all(mid_pulled, "group", split_axis=0, concat_axis=0, tiled=True)
-    mid_scores = lax.all_to_all(scores, "dev", split_axis=1, concat_axis=1, tiled=True)
-    scores_back = lax.all_to_all(mid_scores, "group", split_axis=0, concat_axis=0, tiled=True)
-    pulled_flat = pulled_back.reshape(slot_total, query_len, feat_width)
-    scores_flat = scores_back.reshape(slot_total)
+    pulled = pulled.reshape(slot_total, query_len, feat_width)
+    scores = scores.reshape(slot_total)
+    pulled_flat = lax.all_to_all(pulled, both_axes, split_axis=0, concat_axis=0, tiled=True)
+    scores_flat = lax.all_to_all(scores, both_axes, split_axis=0, concat_axis=0, tiled=True)
     pair_pulled = jnp.take(pulled_flat, slot_index, axis=0).reshape(
         query_count, list_len, query_len, feat_width
     )

time: 476 us -> 358 us (0.75)
  waiting for transfers between devices: 283 us -> 189 us
  local copies, waits for them, and re-layouts: 75.9 us -> 52.1 us
  blocking collectives: 0 us -> 18 us
  starting transfers between devices: 54.3 us -> 37.7 us
    all_to_all x8 -> x3, waiting for transfers between devices: 283 us -> 189 us  [the longest x1 95.8 us: local(): lax.all_to_all(outgoing, both_axes, split_axis=0, concat_axis=0, tiled=True)]
    all_to_all x0 -> x1, blocking collectives: none -> 18 us  [local(): lax.all_to_all(scores, both_axes, split_axis=0, concat_axis=0, tiled=True)]
    all_to_all x8 -> x3, starting transfers between devices: 54.3 us -> 37.7 us  [the longest x1 14.7 us: local(): lax.all_to_all(outgoing, both_axes, split_axis=0, concat_axis=0, tiled=True)]
    reshape x5 -> x0, local copies, waits for them, and re-layouts: 12.3 us -> none  [the longest x1 5.56 us: local(): pulled.reshape(group_count, dev_count, slot_cap, query_len, feat_width)]
    all_to_all x5 -> x4, local copies, waits for them, and re-layouts: 12.5 us -> 1.63 us  [the longest x1 0.85 us: local(): lax.all_to_all(labels, both_axes, split_axis=0, concat_axis=0, tiled=True)]
  transfers between devices with their start and end apart: 8 -> 3, of which waited for: 5 -> 2; matrix products, arithmetic and copies ran while one was open for 10% -> 7% of each run, Pallas kernels for 0% -> 0%
where the time goes in v1:
time: 358 us; the launch traced here: 356 us
  waiting for transfers between devices  189 us (53%)
  local copies, waits for them, and re-layouts  52.1 us (15%)
  matrix products  49 us (14%)
  starting transfers between devices  37.7 us (11%)
  blocking collectives  18 us (5%)
  other arithmetic  8.71 us (2%)
    all_to_all x1, waiting for transfers between devices, local(): lax.all_to_all(outgoing, both_axes, split_axis=0, concat_axis=0, tiled=True)  95.8 us
    all_to_all x1, waiting for transfers between devices, local(): lax.all_to_all(pulled, both_axes, split_axis=0, concat_axis=0, tiled=True)  93.7 us
    dot_general x8, matrix products, score_block(): jnp.einsum('bqe,bpe->bqp', query_block, passage_block, preferred_element_...  33.3 us
    gather x8, local copies, waits for them, and re-layouts, score_block(): passage_block = jnp.take(passage_unit, tag_block, axis=0)  24.5 us
    all_to_all x1, blocking collectives, local(): lax.all_to_all(scores, both_axes, split_axis=0, concat_axis=0, tiled=True)  18 us
    dot_general x8, matrix products, score_block(): jnp.einsum('bqp,bpe->bqe', attention, passage_block, preferred_element_ty...  15.4 us
    all_to_all x1, starting transfers between devices, local(): lax.all_to_all(outgoing, both_axes, split_axis=0, concat_axis=0, tiled=True)  14.7 us
    all_to_all x1, starting transfers between devices, local(): lax.all_to_all(labels, both_axes, split_axis=0, concat_axis=0, tiled=True)  14.6 us
  transfers between devices with their start and end apart: 3, of which 2 were waited for; matrix products, arithmetic and copies ran while one was open for 7% of the time, Pallas kernels for 0%

profile of v1, /device:TPU:8, one launch (start us, length us, event | category | flops | bytes accessed | tf_op | source)
XLA Modules:
  0.0 356.3 jit_solution(4543191595386989078)
XLA Ops:
  5.8 14.6 %all-to-all-start.1 = ((bf16[256,2,1]{1,2,0:T(2,128)(2,1)}), bf16[256,2,1]{1,2,0:T(2,128)(2,1)S(1)}, u32[]{:S(2)}, u32[]{:S(2)}) async-start(bf16[256,2,1]{1,2,0:T(2,128)(2,1)} %all_to_all.27), calls=%async_computation.1 | async-start | bytes 262144 | tf_op jit(solution)/shard_map/all_to_all | solution.py:45
  23.1 2.5 broadcast_in_dim.73
  25.6 13.7 %scatter_fusion = bf16[512,32,128]{2,1,0:T(8,128)(2,1)} fusion(bf16[512,32,128]{2,1,0:T(8,128)(2,1)} %broadcast_in_dim.73, s32[128]{0:T(128)S(1)} %fusion.36, bf16[128,32,128]{2,1,0:T(8,128)(2,1)S(1)} %gather_fusion.2), kind=kCustom, calls=%fused_computation.5 | custom fusion | bytes 3146240 | tf_op jit(solution)/shard_map/scatter | solution.py:39
  39.3 14.7 %all-to-all-start = ((bf16[512,32,128]{2,1,0:T(8,128)(2,1)}), bf16[512,32,128]{2,1,0:T(8,128)(2,1)}, u32[]{:S(2)}, u32[]{:S(2)}) async-start(bf16[512,32,128]{2,1,0:T(8,128)(2,1)} %scatter_fusion), calls=%async_computation | async-start | bytes 8388608 | tf_op jit(solution)/shard_map/all_to_all | solution.py:44
  56.0 95.8 %all-to-all-done = bf16[512,32,128]{2,1,0:T(8,128)(2,1)} async-done(((bf16[512,32,128]{2,1,0:T(8,128)(2,1)}), bf16[512,32,128]{2,1,0:T(8,128)(2,1)}, u32[]{:S(2)}, u32[]{:S(2)}) %all-to-all-start) | async-done | bytes 4194336 | tf_op jit(solution)/shard_map/all_to_all | solution.py:44
  151.7 74.8 %while.12 = (s32[]{:T(128)}, bf16[8,64,32,128]{3,2,1,0:T(8,128)(2,1)}, f32[8,64]{1,0:T(8,128)S(1)}, bf16[8,64,32,128]{3,2,1,0:T(8,128)(2,1)}, s32[8,64]{1,0:T(8,...) while((s32[]{:T(128)}, bf16[8,64,32,128]{3,2,1,0:T(8,128)(2,1)}, ...), condition=%wide.region_8.9_spmd, body=%wide.region_5.8_spmd.sunk | while | flops 275516928 | bytes 38829372 | solution.py:68
  151.8 3.1 gather_fusion
  154.8 4.2 %fusion.45 = (f32[64,32]{1,0:T(8,128)S(1)}, f32[64,32,256]{2,1,0:T(8,128)S(1)}) fusion(bf16[64,256,128]{2,1,0:T(8,128)(2,1)} %gather_fusion, pred[64]{0:T(512)(128)(4,1)S(1)} %compare_and_fusion.4, bf16[8,64,32,128]{3,2,1,0:T(8,128)(2,1)} %get-tuple-element.116, s32[]{:T(128)} %get-tuple-element.105), kind=kOutput, calls=%fused_computation.10.clone.1 | convolution fusion | flops 137361408 | bytes 6824512 | tf_op jit(solution)/shard_map/while/body/eval_jaxpr/bqe,bpe->bqp/dot_general | solution.py:54
  161.1 3.1 gather_fusion
  164.2 4.2 %fusion.45 = (f32[64,32]{1,0:T(8,128)S(1)}, f32[64,32,256]{2,1,0:T(8,128)S(1)}) fusion(bf16[64,256,128]{2,1,0:T(8,128)(2,1)} %gather_fusion, pred[64]{0:T(512)(128)(4,1)S(1)} %compare_and_fusion.4, bf16[8,64,32,128]{3,2,1,0:T(8,128)(2,1)} %get-tuple-element.116, s32[]{:T(128)} %get-tuple-element.105), kind=kOutput, calls=%fused_computation.10.clone.1 | convolution fusion | flops 137361408 | bytes 6824512 | tf_op jit(solution)/shard_map/while/body/eval_jaxpr/bqe,bpe->bqp/dot_general | solution.py:54
  168.3 1.9 fusion.46
  170.5 3.1 gather_fusion
  173.5 4.2 %fusion.45 = (f32[64,32]{1,0:T(8,128)S(1)}, f32[64,32,256]{2,1,0:T(8,128)S(1)}) fusion(bf16[64,256,128]{2,1,0:T(8,128)(2,1)} %gather_fusion, pred[64]{0:T(512)(128)(4,1)S(1)} %compare_and_fusion.4, bf16[8,64,32,128]{3,2,1,0:T(8,128)(2,1)} %get-tuple-element.116, s32[]{:T(128)} %get-tuple-element.105), kind=kOutput, calls=%fused_computation.10.clone.1 | convolution fusion | flops 137361408 | bytes 6824512 | tf_op jit(solution)/shard_map/while/body/eval_jaxpr/bqe,bpe->bqp/dot_general | solution.py:54
  177.7 1.9 fusion.46
  179.8 3.1 gather_fusion
  182.9 4.2 %fusion.45 = (f32[64,32]{1,0:T(8,128)S(1)}, f32[64,32,256]{2,1,0:T(8,128)S(1)}) fusion(bf16[64,256,128]{2,1,0:T(8,128)(2,1)} %gather_fusion, pred[64]{0:T(512)(128)(4,1)S(1)} %compare_and_fusion.4, bf16[8,64,32,128]{3,2,1,0:T(8,128)(2,1)} %get-tuple-element.116, s32[]{:T(128)} %get-tuple-element.105), kind=kOutput, calls=%fused_computation.10.clone.1 | convolution fusion | flops 137361408 | bytes 6824512 | tf_op jit(solution)/shard_map/while/body/eval_jaxpr/bqe,bpe->bqp/dot_general | solution.py:54
  187.1 1.9 fusion.46
  189.2 3.1 gather_fusion
  192.3 4.2 %fusion.45 = (f32[64,32]{1,0:T(8,128)S(1)}, f32[64,32,256]{2,1,0:T(8,128)S(1)}) fusion(bf16[64,256,128]{2,1,0:T(8,128)(2,1)} %gather_fusion, pred[64]{0:T(512)(128)(4,1)S(1)} %compare_and_fusion.4, bf16[8,64,32,128]{3,2,1,0:T(8,128)(2,1)} %get-tuple-element.116, s32[]{:T(128)} %get-tuple-element.105), kind=kOutput, calls=%fused_computation.10.clone.1 | convolution fusion | flops 137361408 | bytes 6824512 | tf_op jit(solution)/shard_map/while/body/eval_jaxpr/bqe,bpe->bqp/dot_general | solution.py:54
  196.4 1.9 fusion.46
  198.5 3.1 gather_fusion
  201.6 4.2 %fusion.45 = (f32[64,32]{1,0:T(8,128)S(1)}, f32[64,32,256]{2,1,0:T(8,128)S(1)}) fusion(bf16[64,256,128]{2,1,0:T(8,128)(2,1)} %gather_fusion, pred[64]{0:T(512)(128)(4,1)S(1)} %compare_and_fusion.4, bf16[8,64,32,128]{3,2,1,0:T(8,128)(2,1)} %get-tuple-element.116, s32[]{:T(128)} %get-tuple-element.105), kind=kOutput, calls=%fused_computation.10.clone.1 | convolution fusion | flops 137361408 | bytes 6824512 | tf_op jit(solution)/shard_map/while/body/eval_jaxpr/bqe,bpe->bqp/dot_general | solution.py:54
  205.8 1.9 fusion.46
  207.9 3.1 gather_fusion
  211.0 4.2 %fusion.45 = (f32[64,32]{1,0:T(8,128)S(1)}, f32[64,32,256]{2,1,0:T(8,128)S(1)}) fusion(bf16[64,256,128]{2,1,0:T(8,128)(2,1)} %gather_fusion, pred[64]{0:T(512)(128)(4,1)S(1)} %compare_and_fusion.4, bf16[8,64,32,128]{3,2,1,0:T(8,128)(2,1)} %get-tuple-element.116, s32[]{:T(128)} %get-tuple-element.105), kind=kOutput, calls=%fused_computation.10.clone.1 | convolution fusion | flops 137361408 | bytes 6824512 | tf_op jit(solution)/shard_map/while/body/eval_jaxpr/bqe,bpe->bqp/dot_general | solution.py:54
  217.2 3.1 gather_fusion
  220.3 4.2 %fusion.45 = (f32[64,32]{1,0:T(8,128)S(1)}, f32[64,32,256]{2,1,0:T(8,128)S(1)}) fusion(bf16[64,256,128]{2,1,0:T(8,128)(2,1)} %gather_fusion, pred[64]{0:T(512)(128)(4,1)S(1)} %compare_and_fusion.4, bf16[8,64,32,128]{3,2,1,0:T(8,128)(2,1)} %get-tuple-element.116, s32[]{:T(128)} %get-tuple-element.105), kind=kOutput, calls=%fused_computation.10.clone.1 | convolution fusion | flops 137361408 | bytes 6824512 | tf_op jit(solution)/shard_map/while/body/eval_jaxpr/bqe,bpe->bqp/dot_general | solution.py:54
  224.5 1.9 fusion.46
  226.7 18.0 %all_to_all.32 = f32[256,2,1]{1,2,0:T(1,128)S(1)} all-to-all(f32[256,2,1]{1,2,0:T(1,128)S(1)} %bitcast.56), channel_id=1, replica_groups=mesh['group'=8,'dev'=32] {'group','dev'}, dimensions={0} | all-to-all | bytes 4096 | tf_op jit(solution)/shard_map/all_to_all | solution.py:72
  244.7 8.4 %all-to-all-start.3 = ((bf16[512,32,128]{2,1,0:T(8,128)(2,1)}), bf16[512,32,128]{2,1,0:T(8,128)(2,1)}, u32[]{:S(2)}, u32[]{:S(2)}) async-start(bf16[512,32,128]{2,1,0:T(8,128)(2,1)} %bitcast.53), calls=%async_computation.3 | async-start | bytes 8388608 | tf_op jit(solution)/shard_map/all_to_all | solution.py:71
  257.2 93.7 %all-to-all-done.3 = bf16[512,32,128]{2,1,0:T(8,128)(2,1)} async-done(((bf16[512,32,128]{2,1,0:T(8,128)(2,1)}), bf16[512,32,128]{2,1,0:T(8,128)(2,1)}, u32[]{:S(2)}, u32[]{:S(2)}) %all-to-all-start.3) | async-done | bytes 4194336 | tf_op jit(solution)/shard_map/all_to_all | solution.py:71
  350.9 2.9 gather_fusion.4
  (108 shorter events, 21.4 us)
Async XLA Ops:
  0.6 1.6 copy-start
  5.8 33.5 %all-to-all-start.1 = ((bf16[256,2,1]{1,2,0:T(2,128)(2,1)}), bf16[256,2,1]{1,2,0:T(2,128)(2,1)S(1)}, u32[]{:S(2)}, u32[]{:S(2)}) async-start(bf16[256,2,1]{1,2,0:T(2,128)(2,1)} %all_to_all.27), calls=%async_computation.1 | async-start | bytes 262144 | tf_op jit(solution)/shard_map/all_to_all | solution.py:45
  39.3 14.7 %copy-start.2 = (bf16[16,256,128]{2,1,0:T(8,128)(2,1)S(1)}, bf16[16,256,128]{2,1,0:T(8,128)(2,1)}, u32[]{:S(2)}) copy-start(bf16[16,256,128]{2,1,0:T(8,128)(2,1)} %param.7) | copy-start | bytes 3145732
  39.3 112.4 %all-to-all-start = ((bf16[512,32,128]{2,1,0:T(8,128)(2,1)}), bf16[512,32,128]{2,1,0:T(8,128)(2,1)}, u32[]{:S(2)}, u32[]{:S(2)}) async-start(bf16[512,32,128]{2,1,0:T(8,128)(2,1)} %scatter_fusion), calls=%async_computation | async-start | bytes 8388608 | tf_op jit(solution)/shard_map/all_to_all | solution.py:44
  154.8 4.2 %copy-start.1 = (bf16[64,256,128]{2,1,0:T(8,128)(2,1)S(1)}, bf16[64,256,128]{2,1,0:T(8,128)(2,1)}, u32[]{:S(2)}) copy-start(bf16[64,256,128]{2,1,0:T(8,128)(2,1)} %gather_fusion) | copy-start | bytes 12582916 | tf_op jit(solution)/shard_map/while
  164.2 4.2 %copy-start.1 = (bf16[64,256,128]{2,1,0:T(8,128)(2,1)S(1)}, bf16[64,256,128]{2,1,0:T(8,128)(2,1)}, u32[]{:S(2)}) copy-start(bf16[64,256,128]{2,1,0:T(8,128)(2,1)} %gather_fusion) | copy-start | bytes 12582916 | tf_op jit(solution)/shard_map/while
  173.5 4.2 %copy-start.1 = (bf16[64,256,128]{2,1,0:T(8,128)(2,1)S(1)}, bf16[64,256,128]{2,1,0:T(8,128)(2,1)}, u32[]{:S(2)}) copy-start(bf16[64,256,128]{2,1,0:T(8,128)(2,1)} %gather_fusion) | copy-start | bytes 12582916 | tf_op jit(solution)/shard_map/while
  182.9 4.2 %copy-start.1 = (bf16[64,256,128]{2,1,0:T(8,128)(2,1)S(1)}, bf16[64,256,128]{2,1,0:T(8,128)(2,1)}, u32[]{:S(2)}) copy-start(bf16[64,256,128]{2,1,0:T(8,128)(2,1)} %gather_fusion) | copy-start | bytes 12582916 | tf_op jit(solution)/shard_map/while
  192.3 4.2 %copy-start.1 = (bf16[64,256,128]{2,1,0:T(8,128)(2,1)S(1)}, bf16[64,256,128]{2,1,0:T(8,128)(2,1)}, u32[]{:S(2)}) copy-start(bf16[64,256,128]{2,1,0:T(8,128)(2,1)} %gather_fusion) | copy-start | bytes 12582916 | tf_op jit(solution)/shard_map/while
  201.6 4.2 %copy-start.1 = (bf16[64,256,128]{2,1,0:T(8,128)(2,1)S(1)}, bf16[64,256,128]{2,1,0:T(8,128)(2,1)}, u32[]{:S(2)}) copy-start(bf16[64,256,128]{2,1,0:T(8,128)(2,1)} %gather_fusion) | copy-start | bytes 12582916 | tf_op jit(solution)/shard_map/while
  211.0 4.2 %copy-start.1 = (bf16[64,256,128]{2,1,0:T(8,128)(2,1)S(1)}, bf16[64,256,128]{2,1,0:T(8,128)(2,1)}, u32[]{:S(2)}) copy-start(bf16[64,256,128]{2,1,0:T(8,128)(2,1)} %gather_fusion) | copy-start | bytes 12582916 | tf_op jit(solution)/shard_map/while
  220.3 4.2 %copy-start.1 = (bf16[64,256,128]{2,1,0:T(8,128)(2,1)S(1)}, bf16[64,256,128]{2,1,0:T(8,128)(2,1)}, u32[]{:S(2)}) copy-start(bf16[64,256,128]{2,1,0:T(8,128)(2,1)} %gather_fusion) | copy-start | bytes 12582916 | tf_op jit(solution)/shard_map/while
  244.7 11.6 %copy-start.4 = (s32[8,16]{1,0:T(8,128)S(1)}, s32[8,16]{1,0:T(8,128)}, u32[]{:S(2)}) copy-start(s32[8,16]{1,0:T(8,128)} %param.8) | copy-start | bytes 1540
  244.7 106.2 %all-to-all-start.3 = ((bf16[512,32,128]{2,1,0:T(8,128)(2,1)}), bf16[512,32,128]{2,1,0:T(8,128)(2,1)}, u32[]{:S(2)}, u32[]{:S(2)}) async-start(bf16[512,32,128]{2,1,0:T(8,128)(2,1)} %bitcast.53), calls=%async_computation.3 | async-start | bytes 8388608 | tf_op jit(solution)/shard_map/all_to_all | solution.py:71
  253.1 101.3 %copy-start.3 = (bf16[8,32,128]{2,1,0:T(8,128)(2,1)S(1)}, bf16[8,32,128]{2,1,0:T(8,128)(2,1)}, u32[]{:S(2)}) copy-start(bf16[8,32,128]{2,1,0:T(8,128)(2,1)} %param.6) | copy-start | bytes 196612

commit v2 on v1

--- a/solution.py
+++ b/solution.py
@@ -34,18 +34,20 @@
     earlier = positions[None, :] < positions[:, None]
     before = jnp.sum(same_target & earlier, axis=1)
     slot_index = target * slot_cap + before
-    query_owner = positions // list_len
-    outgoing = jnp.zeros((slot_total, query_len, feat_width), jnp.bfloat16)
-    outgoing = outgoing.at[slot_index].set(query_send[query_owner])
-    labels = (
-        jnp.zeros((slot_total,), jnp.bfloat16).at[slot_index].set(local_row.astype(jnp.bfloat16))
+    token_width = query_len * feat_width
+    pair_of_slot = jnp.zeros((slot_total,), jnp.int32).at[slot_index].set(positions)
+    slot_owner = pair_of_slot // list_len
+    slot_label = jnp.take(local_row, pair_of_slot, axis=0).astype(jnp.bfloat16)
+    label_block = jnp.zeros((slot_total, feat_width), jnp.bfloat16).at[:, 0].set(slot_label)
+    outgoing = jnp.concatenate(
+        [jnp.take(query_send.reshape(query_count, token_width), slot_owner, axis=0), label_block],
+        axis=1,
     )
     both_axes = ("group", "dev")
     arrived = lax.all_to_all(outgoing, both_axes, split_axis=0, concat_axis=0, tiled=True)
-    tags = lax.all_to_all(labels, both_axes, split_axis=0, concat_axis=0, tiled=True)
     block_rows = dev_count * slot_cap
-    arrived = arrived.reshape(group_count, block_rows, query_len, feat_width)
-    tags = tags.reshape(group_count, block_rows).astype(jnp.int32)
+    tags = arrived[:, token_width].astype(jnp.int32).reshape(group_count, block_rows)
+    arrived = arrived[:, :token_width].reshape(group_count, block_rows, query_len, feat_width)
 
     def score_block(inputs):
         query_block, tag_block = inputs
@@ -63,13 +65,19 @@
         pulled = jnp.einsum(
             "bqp,bpe->bqe", attention, passage_block, preferred_element_type=jnp.float32
         )
-        return (pulled.astype(jnp.bfloat16), pair_score)
+        score_high = pair_score.astype(jnp.bfloat16)
+        score_low = (pair_score - score_high.astype(jnp.float32)).astype(jnp.bfloat16)
+        score_cols = jnp.zeros((pulled.shape[0], feat_width), jnp.bfloat16)
+        score_cols = score_cols.at[:, 0].set(score_high).at[:, 1].set(score_low)
+        pulled_rows = pulled.astype(jnp.bfloat16).reshape(pulled.shape[0], token_width)
+        return jnp.concatenate([pulled_rows, score_cols], axis=1)
 
-    pulled, scores = lax.map(score_block, (arrived, tags))
-    pulled = pulled.reshape(slot_total, query_len, feat_width)
-    scores = scores.reshape(slot_total)
-    pulled_flat = lax.all_to_all(pulled, both_axes, split_axis=0, concat_axis=0, tiled=True)
-    scores_flat = lax.all_to_all(scores, both_axes, split_axis=0, concat_axis=0, tiled=True)
+    returning = lax.map(score_block, (arrived, tags)).reshape(slot_total, token_width + feat_width)
+    returned = lax.all_to_all(returning, both_axes, split_axis=0, concat_axis=0, tiled=True)
+    pulled_flat = returned[:, :token_width].reshape(slot_total, query_len, feat_width)
+    scores_flat = returned[:, token_width].astype(jnp.float32) + returned[
+        :, token_width + 1
+    ].astype(jnp.float32)
     pair_pulled = jnp.take(pulled_flat, slot_index, axis=0).reshape(
         query_count, list_len, query_len, feat_width
     )

time: 358 us -> 390 us (1.089)
  local copies, waits for them, and re-layouts: 52.1 us -> 84.1 us
  other arithmetic: 8.71 us -> 38.4 us
  blocking collectives: 18 us -> 0 us
  starting transfers between devices: 37.7 us -> 22.6 us
  waiting for transfers between devices: 189 us -> 199 us
  matrix products: 49 us -> 43.3 us
    all_to_all x4, local copies, waits for them, and re-layouts: 1.63 us -> 29.3 us  [the longest x2 14.7 us: local(): lax.all_to_all(returning, both_axes, split_axis=0, concat_axis=0, tiled=T...]
    another operation x0 -> x19, other arithmetic: none -> 18.2 us
    all_to_all x1 -> x0, blocking collectives: 18 us -> none  [local(): lax.all_to_all(scores, both_axes, split_axis=0, concat_axis=0, tiled=True)]
    all_to_all x2 -> x1, starting transfers between devices: 23 us -> 7.11 us  [local(): lax.all_to_all(returning, both_axes, split_axis=0, concat_axis=0, tiled=T...]
    scatter x2 -> x25, local copies, waits for them, and re-layouts: 15 us -> 2.02 us  [the longest x24 1.05 us: score_block(): score_cols = score_cols.at[:, 0].set(score_high).at[:, 1].set(score_low)]
    unnamed x8 -> x16, local copies, waits for them, and re-layouts: 0.02 us -> 11.5 us
    gather x1 -> x2, local copies, waits for them, and re-layouts: 0.76 us -> 7.7 us  [the longest x1 4.35 us: local(): jnp.take(query_send.reshape(query_count, token_width), slot_owner, axis=0)]
    dynamic_update_slice x0 -> x8, other arithmetic: none -> 6.8 us  [local(): lax.map(score_block, (arrived, tags))]
  transfers between devices with their start and end apart: 3 -> 2, of which waited for: 2 -> 2; matrix products, arithmetic and copies ran while one was open for 7% -> 1% of each run, Pallas kernels for 0% -> 0%
where the time goes in v2:
time: 390 us; the launch traced here: 389 us
  waiting for transfers between devices  199 us (51%)
  local copies, waits for them, and re-layouts  84.1 us (22%)
  matrix products  43.3 us (11%)
  other arithmetic  38.4 us (10%)
  starting transfers between devices  22.6 us (6%)
    all_to_all x1, waiting for transfers between devices, local(): lax.all_to_all(returning, both_axes, split_axis=0, concat_axis=0, tiled=T...  100 us
    all_to_all x1, waiting for transfers between devices, local(): lax.all_to_all(outgoing, both_axes, split_axis=0, concat_axis=0, tiled=True)  98.6 us
    dot_general x8, matrix products, score_block(): jnp.einsum('bqe,bpe->bqp', query_block, passage_block, preferred_element_...  33.3 us
    gather x8, local copies, waits for them, and re-layouts, score_block(): passage_block = jnp.take(passage_unit, tag_block, axis=0)  24.4 us
    another operation x19, other arithmetic  18.2 us
    all_to_all x1, starting transfers between devices, local(): lax.all_to_all(outgoing, both_axes, split_axis=0, concat_axis=0, tiled=True)  15.5 us
    all_to_all x2, local copies, waits for them, and re-layouts, local(): lax.all_to_all(returning, both_axes, split_axis=0, concat_axis=0, tiled=T...  14.7 us
    all_to_all x2, local copies, waits for them, and re-layouts, local(): lax.all_to_all(outgoing, both_axes, split_axis=0, concat_axis=0, tiled=True)  14.6 us
  transfers between devices with their start and end apart: 2, of which 2 were waited for; matrix products, arithmetic and copies ran while one was open for 1% of the time, Pallas kernels for 0%

profile of v2, /device:TPU:8, one launch (start us, length us, event | category | flops | bytes accessed | tf_op | source)
XLA Modules:
  0.0 388.9 jit_solution(4888917533858376525)
XLA Ops:
  5.3 3.3 gather_fusion.3
  11.4 4.4 %gather_fusion.2 = bf16[512,4096]{1,0:T(8,128)(2,1)} fusion(bf16[8,4096]{1,0:T(8,128)(2,1)S(1)} %bitcast.77, s32[1024]{0:T(1024)S(1)} %pad_clamp_fusion.3), kind=kCustom, calls=%fused_computation.2 | custom fusion | bytes 8390656 | tf_op jit(solution)/shard_map/jit(_take)/gather | solution.py:43
  15.7 2.6 broadcast_select_fusion.7
  20.6 7.3 %all_to_all.16 = bf16[256,2,4224]{2,1,0:T(2,128)(2,1)} reshape(bf16[512,4224]{1,0:T(8,128)(2,1)} %fusion.17) | data formatting | bytes 8650752 | tf_op jit(solution)/shard_map/all_to_all | solution.py:47
  27.9 15.5 %all-to-all-start = ((bf16[256,2,4224]{2,1,0:T(2,128)(2,1)}), bf16[256,2,4224]{2,1,0:T(2,128)(2,1)}, u32[]{:S(2)}, u32[]{:S(2)}) async-start(bf16[256,2,4224]{2,1,0:T(2,128)(2,1)} %all_to_all.16), calls=%async_computation | async-start | bytes 8650752 | tf_op jit(solution)/shard_map/all_to_all | solution.py:47
  45.3 98.6 %all-to-all-done = bf16[256,2,4224]{2,1,0:T(2,128)(2,1)} async-done(((bf16[256,2,4224]{2,1,0:T(2,128)(2,1)}), bf16[256,2,4224]{2,1,0:T(2,128)(2,1)}, u32[]{:S(2)}, u32[]{:S(2)}) %all-to-all-start) | async-done | bytes 4325408 | tf_op jit(solution)/shard_map/all_to_all | solution.py:47
  143.9 7.3 %all_to_all.18 = bf16[512,4224]{1,0:T(8,128)(2,1)} reshape(bf16[256,2,4224]{2,1,0:T(2,128)(2,1)} %all-to-all-done) | data formatting | bytes 8650752 | tf_op jit(solution)/shard_map/all_to_all | solution.py:47
  151.2 2.5 slice_bitcast_fusion.1
  153.7 3.3 copy.24
  157.2 94.7 %while.17 = (s32[]{:T(128)}, bf16[8,64,4224]{2,1,0:T(8,128)(2,1)}, bf16[8,64,32,128]{3,2,1,0:T(8,128)(2,1)}, s32[8,64]{1,0:T(8,128)S(1)}, bf16[16,256,128]{2,1,0...) while((s32[]{:T(128)}, bf16[8,64,4224]{2,1,0:T(8,128)(2,1)}, ...), condition=%wide.region_10.11_spmd, body=%wide.region_6.10_spmd.sunk | while | flops 276598656 | bytes 41008840 | solution.py:75
  157.2 3.0 gather_fusion
  160.3 4.2 %fusion.50 = (f32[64,32]{1,0:T(8,128)S(1)}, f32[64,32,256]{2,1,0:T(8,128)S(1)}) fusion(bf16[64,256,128]{2,1,0:T(8,128)(2,1)} %gather_fusion, pred[64]{0:T(512)(128)(4,1)S(1)} %compare_and_fusion.5, bf16[8,64,32,128]{3,2,1,0:T(8,128)(2,1)} %get-tuple-element.237, s32[]{:T(128)} %get-tuple-element.226), kind=kOutput, calls=%fused_computation.10.clone.1 | convolution fusion | flops 137361408 | bytes 6824512 | tf_op jit(solution)/shard_map/while/body/eval_jaxpr/bqe,bpe->bqp/dot_general | solution.py:56
  169.0 3.0 gather_fusion
  172.1 4.2 %fusion.50 = (f32[64,32]{1,0:T(8,128)S(1)}, f32[64,32,256]{2,1,0:T(8,128)S(1)}) fusion(bf16[64,256,128]{2,1,0:T(8,128)(2,1)} %gather_fusion, pred[64]{0:T(512)(128)(4,1)S(1)} %compare_and_fusion.5, bf16[8,64,32,128]{3,2,1,0:T(8,128)(2,1)} %get-tuple-element.237, s32[]{:T(128)} %get-tuple-element.226), kind=kOutput, calls=%fused_computation.10.clone.1 | convolution fusion | flops 137361408 | bytes 6824512 | tf_op jit(solution)/shard_map/while/body/eval_jaxpr/bqe,bpe->bqp/dot_general | solution.py:56
  180.9 3.0 gather_fusion
  183.9 4.2 %fusion.50 = (f32[64,32]{1,0:T(8,128)S(1)}, f32[64,32,256]{2,1,0:T(8,128)S(1)}) fusion(bf16[64,256,128]{2,1,0:T(8,128)(2,1)} %gather_fusion, pred[64]{0:T(512)(128)(4,1)S(1)} %compare_and_fusion.5, bf16[8,64,32,128]{3,2,1,0:T(8,128)(2,1)} %get-tuple-element.237, s32[]{:T(128)} %get-tuple-element.226), kind=kOutput, calls=%fused_computation.10.clone.1 | convolution fusion | flops 137361408 | bytes 6824512 | tf_op jit(solution)/shard_map/while/body/eval_jaxpr/bqe,bpe->bqp/dot_general | solution.py:56
  192.7 3.0 gather_fusion
  195.8 4.2 %fusion.50 = (f32[64,32]{1,0:T(8,128)S(1)}, f32[64,32,256]{2,1,0:T(8,128)S(1)}) fusion(bf16[64,256,128]{2,1,0:T(8,128)(2,1)} %gather_fusion, pred[64]{0:T(512)(128)(4,1)S(1)} %compare_and_fusion.5, bf16[8,64,32,128]{3,2,1,0:T(8,128)(2,1)} %get-tuple-element.237, s32[]{:T(128)} %get-tuple-element.226), kind=kOutput, calls=%fused_computation.10.clone.1 | convolution fusion | flops 137361408 | bytes 6824512 | tf_op jit(solution)/shard_map/while/body/eval_jaxpr/bqe,bpe->bqp/dot_general | solution.py:56
  204.6 3.0 gather_fusion
  207.6 4.2 %fusion.50 = (f32[64,32]{1,0:T(8,128)S(1)}, f32[64,32,256]{2,1,0:T(8,128)S(1)}) fusion(bf16[64,256,128]{2,1,0:T(8,128)(2,1)} %gather_fusion, pred[64]{0:T(512)(128)(4,1)S(1)} %compare_and_fusion.5, bf16[8,64,32,128]{3,2,1,0:T(8,128)(2,1)} %get-tuple-element.237, s32[]{:T(128)} %get-tuple-element.226), kind=kOutput, calls=%fused_computation.10.clone.1 | convolution fusion | flops 137361408 | bytes 6824512 | tf_op jit(solution)/shard_map/while/body/eval_jaxpr/bqe,bpe->bqp/dot_general | solution.py:56
  216.4 3.0 gather_fusion
  219.4 4.2 %fusion.50 = (f32[64,32]{1,0:T(8,128)S(1)}, f32[64,32,256]{2,1,0:T(8,128)S(1)}) fusion(bf16[64,256,128]{2,1,0:T(8,128)(2,1)} %gather_fusion, pred[64]{0:T(512)(128)(4,1)S(1)} %compare_and_fusion.5, bf16[8,64,32,128]{3,2,1,0:T(8,128)(2,1)} %get-tuple-element.237, s32[]{:T(128)} %get-tuple-element.226), kind=kOutput, calls=%fused_computation.10.clone.1 | convolution fusion | flops 137361408 | bytes 6824512 | tf_op jit(solution)/shard_map/while/body/eval_jaxpr/bqe,bpe->bqp/dot_general | solution.py:56
  228.2 3.0 gather_fusion
  231.3 4.2 %fusion.50 = (f32[64,32]{1,0:T(8,128)S(1)}, f32[64,32,256]{2,1,0:T(8,128)S(1)}) fusion(bf16[64,256,128]{2,1,0:T(8,128)(2,1)} %gather_fusion, pred[64]{0:T(512)(128)(4,1)S(1)} %compare_and_fusion.5, bf16[8,64,32,128]{3,2,1,0:T(8,128)(2,1)} %get-tuple-element.237, s32[]{:T(128)} %get-tuple-element.226), kind=kOutput, calls=%fused_computation.10.clone.1 | convolution fusion | flops 137361408 | bytes 6824512 | tf_op jit(solution)/shard_map/while/body/eval_jaxpr/bqe,bpe->bqp/dot_general | solution.py:56
  240.0 3.0 gather_fusion
  243.1 4.2 %fusion.50 = (f32[64,32]{1,0:T(8,128)S(1)}, f32[64,32,256]{2,1,0:T(8,128)S(1)}) fusion(bf16[64,256,128]{2,1,0:T(8,128)(2,1)} %gather_fusion, pred[64]{0:T(512)(128)(4,1)S(1)} %compare_and_fusion.5, bf16[8,64,32,128]{3,2,1,0:T(8,128)(2,1)} %get-tuple-element.237, s32[]{:T(128)} %get-tuple-element.226), kind=kOutput, calls=%fused_computation.10.clone.1 | convolution fusion | flops 137361408 | bytes 6824512 | tf_op jit(solution)/shard_map/while/body/eval_jaxpr/bqe,bpe->bqp/dot_general | solution.py:56
  251.9 7.3 %all_to_all.19 = bf16[256,2,4224]{2,1,0:T(2,128)(2,1)} reshape(bf16[8,64,4224]{2,1,0:T(8,128)(2,1)} %get-tuple-element.148) | data formatting | bytes 8650752 | tf_op jit(solution)/shard_map/all_to_all | solution.py:76
  259.2 7.1 %all-to-all-start.1 = ((bf16[256,2,4224]{2,1,0:T(2,128)(2,1)}), bf16[256,2,4224]{2,1,0:T(2,128)(2,1)}, u32[]{:S(2)}, u32[]{:S(2)}) async-start(bf16[256,2,4224]{2,1,0:T(2,128)(2,1)} %all_to_all.19), calls=%async_computation.1 | async-start | bytes 8650752 | tf_op jit(solution)/shard_map/all_to_all | solution.py:76
  266.5 100.5 %all-to-all-done.1 = bf16[256,2,4224]{2,1,0:T(2,128)(2,1)} async-done(((bf16[256,2,4224]{2,1,0:T(2,128)(2,1)}), bf16[256,2,4224]{2,1,0:T(2,128)(2,1)}, u32[]{:S(2)}, u32[]{:S(2)}) %all-to-all-start.1) | async-done | bytes 4325408 | tf_op jit(solution)/shard_map/all_to_all | solution.py:76
  367.0 7.3 %all_to_all.21 = bf16[512,4224]{1,0:T(8,128)(2,1)} reshape(bf16[256,2,4224]{2,1,0:T(2,128)(2,1)} %all-to-all-done.1) | data formatting | bytes 8650752 | tf_op jit(solution)/shard_map/all_to_all | solution.py:76
  378.0 3.2 copy.25
  381.2 3.0 gather_fusion.5
  (170 shorter events, 56.7 us)
Async XLA Ops:
  0.6 2.2 copy-start
  27.9 16.1 %copy-start.3 = (bf16[16,256,128]{2,1,0:T(8,128)(2,1)S(1)}, bf16[16,256,128]{2,1,0:T(8,128)(2,1)}, u32[]{:S(2)}) copy-start(bf16[16,256,128]{2,1,0:T(8,128)(2,1)} %param.13) | copy-start | bytes 3145732
  27.9 116.1 %all-to-all-start = ((bf16[256,2,4224]{2,1,0:T(2,128)(2,1)}), bf16[256,2,4224]{2,1,0:T(2,128)(2,1)}, u32[]{:S(2)}, u32[]{:S(2)}) async-start(bf16[256,2,4224]{2,1,0:T(2,128)(2,1)} %all_to_all.16), calls=%async_computation | async-start | bytes 8650752 | tf_op jit(solution)/shard_map/all_to_all | solution.py:47
  153.7 3.3 slice-start
  160.3 4.2 %copy-start.2 = (bf16[64,256,128]{2,1,0:T(8,128)(2,1)S(1)}, bf16[64,256,128]{2,1,0:T(8,128)(2,1)}, u32[]{:S(2)}) copy-start(bf16[64,256,128]{2,1,0:T(8,128)(2,1)} %gather_fusion) | copy-start | bytes 12582916 | tf_op jit(solution)/shard_map/while
  172.1 4.2 %copy-start.2 = (bf16[64,256,128]{2,1,0:T(8,128)(2,1)S(1)}, bf16[64,256,128]{2,1,0:T(8,128)(2,1)}, u32[]{:S(2)}) copy-start(bf16[64,256,128]{2,1,0:T(8,128)(2,1)} %gather_fusion) | copy-start | bytes 12582916 | tf_op jit(solution)/shard_map/while
  183.9 4.2 %copy-start.2 = (bf16[64,256,128]{2,1,0:T(8,128)(2,1)S(1)}, bf16[64,256,128]{2,1,0:T(8,128)(2,1)}, u32[]{:S(2)}) copy-start(bf16[64,256,128]{2,1,0:T(8,128)(2,1)} %gather_fusion) | copy-start | bytes 12582916 | tf_op jit(solution)/shard_map/while
  195.8 4.2 %copy-start.2 = (bf16[64,256,128]{2,1,0:T(8,128)(2,1)S(1)}, bf16[64,256,128]{2,1,0:T(8,128)(2,1)}, u32[]{:S(2)}) copy-start(bf16[64,256,128]{2,1,0:T(8,128)(2,1)} %gather_fusion) | copy-start | bytes 12582916 | tf_op jit(solution)/shard_map/while
  207.6 4.2 %copy-start.2 = (bf16[64,256,128]{2,1,0:T(8,128)(2,1)S(1)}, bf16[64,256,128]{2,1,0:T(8,128)(2,1)}, u32[]{:S(2)}) copy-start(bf16[64,256,128]{2,1,0:T(8,128)(2,1)} %gather_fusion) | copy-start | bytes 12582916 | tf_op jit(solution)/shard_map/while
  219.4 4.2 %copy-start.2 = (bf16[64,256,128]{2,1,0:T(8,128)(2,1)S(1)}, bf16[64,256,128]{2,1,0:T(8,128)(2,1)}, u32[]{:S(2)}) copy-start(bf16[64,256,128]{2,1,0:T(8,128)(2,1)} %gather_fusion) | copy-start | bytes 12582916 | tf_op jit(solution)/shard_map/while
  231.3 4.2 %copy-start.2 = (bf16[64,256,128]{2,1,0:T(8,128)(2,1)S(1)}, bf16[64,256,128]{2,1,0:T(8,128)(2,1)}, u32[]{:S(2)}) copy-start(bf16[64,256,128]{2,1,0:T(8,128)(2,1)} %gather_fusion) | copy-start | bytes 12582916 | tf_op jit(solution)/shard_map/while
  243.1 4.2 %copy-start.2 = (bf16[64,256,128]{2,1,0:T(8,128)(2,1)S(1)}, bf16[64,256,128]{2,1,0:T(8,128)(2,1)}, u32[]{:S(2)}) copy-start(bf16[64,256,128]{2,1,0:T(8,128)(2,1)} %gather_fusion) | copy-start | bytes 12582916 | tf_op jit(solution)/shard_map/while
  259.2 107.8 %all-to-all-start.1 = ((bf16[256,2,4224]{2,1,0:T(2,128)(2,1)}), bf16[256,2,4224]{2,1,0:T(2,128)(2,1)}, u32[]{:S(2)}, u32[]{:S(2)}) async-start(bf16[256,2,4224]{2,1,0:T(2,128)(2,1)} %all_to_all.19), calls=%async_computation.1 | async-start | bytes 8650752 | tf_op jit(solution)/shard_map/all_to_all | solution.py:76
  378.0 7.6 %copy-start.5 = (s32[8,16]{1,0:T(8,128)S(1)}, s32[8,16]{1,0:T(8,128)}, u32[]{:S(2)}) copy-start(s32[8,16]{1,0:T(8,128)} %param.14) | copy-start | bytes 1540
  378.0 10.9 %copy-start.1 = (s32[4096]{0:T(1024)S(1)}, s32[4096]{0:T(1024)}, u32[]{:S(2)}) copy-start(s32[4096]{0:T(1024)} %param.15) | copy-start | bytes 49156
  381.2 5.3 %copy-start.4 = (bf16[8,32,128]{2,1,0:T(8,128)(2,1)S(1)}, bf16[8,32,128]{2,1,0:T(8,128)(2,1)}, u32[]{:S(2)}) copy-start(bf16[8,32,128]{2,1,0:T(8,128)(2,1)} %param.12) | copy-start | bytes 196612

commit v3 on v1

--- a/solution.py
+++ b/solution.py
@@ -34,18 +34,15 @@
     earlier = positions[None, :] < positions[:, None]
     before = jnp.sum(same_target & earlier, axis=1)
     slot_index = target * slot_cap + before
-    query_owner = positions // list_len
-    outgoing = jnp.zeros((slot_total, query_len, feat_width), jnp.bfloat16)
-    outgoing = outgoing.at[slot_index].set(query_send[query_owner])
-    labels = (
-        jnp.zeros((slot_total,), jnp.bfloat16).at[slot_index].set(local_row.astype(jnp.bfloat16))
-    )
+    pair_of_slot = jnp.zeros((slot_total,), jnp.int32).at[slot_index].set(positions)
+    outgoing = jnp.take(query_send, pair_of_slot // list_len, axis=0)
+    labels = jnp.take(local_row, pair_of_slot, axis=0).astype(jnp.bfloat16)
     both_axes = ("group", "dev")
-    arrived = lax.all_to_all(outgoing, both_axes, split_axis=0, concat_axis=0, tiled=True)
+    outgoing = outgoing.reshape(device_total, slot_cap, query_len, feat_width)
+    labels = labels.reshape(device_total, slot_cap)
     tags = lax.all_to_all(labels, both_axes, split_axis=0, concat_axis=0, tiled=True)
-    block_rows = dev_count * slot_cap
-    arrived = arrived.reshape(group_count, block_rows, query_len, feat_width)
-    tags = tags.reshape(group_count, block_rows).astype(jnp.int32)
+    tags = tags.astype(jnp.int32)
+    block_rows = 64
 
     def score_block(inputs):
         query_block, tag_block = inputs
@@ -65,15 +62,34 @@
         )
         return (pulled.astype(jnp.bfloat16), pair_score)
 
-    pulled, scores = lax.map(score_block, (arrived, tags))
-    pulled = pulled.reshape(slot_total, query_len, feat_width)
-    scores = scores.reshape(slot_total)
-    pulled_flat = lax.all_to_all(pulled, both_axes, split_axis=0, concat_axis=0, tiled=True)
+    returned = []
+    scores = []
+    for slot in range(slot_cap):
+        arrived = lax.all_to_all(
+            outgoing[:, slot], both_axes, split_axis=0, concat_axis=0, tiled=True
+        )
+        blocks = device_total // block_rows
+        pulled, score = lax.map(
+            score_block,
+            (
+                arrived.reshape(blocks, block_rows, query_len, feat_width),
+                tags[:, slot].reshape(blocks, block_rows),
+            ),
+        )
+        pulled = pulled.reshape(device_total, query_len, feat_width)
+        returned.append(lax.all_to_all(pulled, both_axes, split_axis=0, concat_axis=0, tiled=True))
+        scores.append(score.reshape(device_total))
+    scores = jnp.stack(scores, axis=1)
     scores_flat = lax.all_to_all(scores, both_axes, split_axis=0, concat_axis=0, tiled=True)
-    pair_pulled = jnp.take(pulled_flat, slot_index, axis=0).reshape(
-        query_count, list_len, query_len, feat_width
+    pair_score = jnp.take(scores_flat.reshape(slot_total), slot_index, axis=0).reshape(
+        query_count, list_len
     )
-    pair_score = jnp.take(scores_flat, slot_index, axis=0).reshape(query_count, list_len)
+    pair_pulled = jnp.take(returned[0], target, axis=0)
+    for slot in range(1, slot_cap):
+        pair_pulled = jnp.where(
+            (before == slot)[:, None, None], jnp.take(returned[slot], target, axis=0), pair_pulled
+        )
+    pair_pulled = pair_pulled.reshape(query_count, list_len, query_len, feat_width)
     exp_scores = jnp.exp(pair_score)
     total = jnp.sum(exp_scores, axis=-1, keepdims=True)
     loss = jnp.log(total[:, 0]) - pair_score[:, 0]

time: 358 us -> 346 us (0.966)
  waiting for transfers between devices: 189 us -> 119 us
  blocking collectives: 18 us -> 78.9 us
  local copies, waits for them, and re-layouts: 52.1 us -> 47.6 us
    all_to_all x0 -> x1, blocking collectives: none -> 60.6 us  [local(): lax.all_to_all(pulled, both_axes, split_axis=0, concat_axis=0, tiled=True)]
    all_to_all x1, waiting for transfers between devices: 93.7 us -> 47.3 us  [local(): lax.all_to_all(pulled, both_axes, split_axis=0, concat_axis=0, tiled=True)]
    all_to_all x1 -> x2, waiting for transfers between devices: 95.8 us -> 68.7 us  [local(): lax.all_to_all(outgoing[:, slot], both_axes, split_axis=0, concat_axis=0,...]
    scatter x2 -> x1, local copies, waits for them, and re-layouts: 15 us -> 0.98 us  [local(): jnp.zeros((slot_total,), jnp.int32).at[slot_index].set(positions)]
    gather x4 -> x6, local copies, waits for them, and re-layouts: 5.05 us -> 12.2 us  [the longest x1 3.43 us: local(): outgoing = jnp.take(query_send, pair_of_slot // list_len, axis=0)]
    all_to_all x1 -> x2, starting transfers between devices: 14.7 us -> 19.1 us  [local(): lax.all_to_all(outgoing[:, slot], both_axes, split_axis=0, concat_axis=0,...]
    select_n x12 -> x6, other arithmetic: 0.31 us -> 4.38 us  [the longest x1 2.58 us: local(): outgoing = jnp.take(query_send, pair_of_slot // list_len, axis=0)]
  transfers between devices with their start and end apart: 3 -> 4, of which waited for: 2 -> 4; matrix products, arithmetic and copies ran while one was open for 7% -> 15% of each run, Pallas kernels for 0% -> 0%
where the time goes in v3:
time: 346 us; the launch traced here: 344 us
  waiting for transfers between devices  119 us (34%)
  blocking collectives  78.9 us (23%)
  local copies, waits for them, and re-layouts  47.6 us (14%)
  matrix products  46.6 us (13%)
  starting transfers between devices  40 us (12%)
  other arithmetic  10.9 us (3%)
    all_to_all x2, waiting for transfers between devices, local(): lax.all_to_all(outgoing[:, slot], both_axes, split_axis=0, concat_axis=0,...  68.7 us
    all_to_all x1, blocking collectives, local(): lax.all_to_all(pulled, both_axes, split_axis=0, concat_axis=0, tiled=True)  60.6 us
    all_to_all x1, waiting for transfers between devices, local(): lax.all_to_all(pulled, both_axes, split_axis=0, concat_axis=0, tiled=True)  47.3 us
    dot_general x8, matrix products, score_block(): jnp.einsum('bqe,bpe->bqp', query_block, passage_block, preferred_element_...  33.2 us
    gather x8, local copies, waits for them, and re-layouts, score_block(): passage_block = jnp.take(passage_unit, tag_block, axis=0)  24.1 us
    all_to_all x2, starting transfers between devices, local(): lax.all_to_all(outgoing[:, slot], both_axes, split_axis=0, concat_axis=0,...  19.1 us
    all_to_all x1, blocking collectives, local(): lax.all_to_all(scores, both_axes, split_axis=0, concat_axis=0, tiled=True)  18.3 us
    all_to_all x1, starting transfers between devices, local(): lax.all_to_all(labels, both_axes, split_axis=0, concat_axis=0, tiled=True)  14.6 us
  transfers between devices with their start and end apart: 4, of which 4 were waited for; matrix products, arithmetic and copies ran while one was open for 15% of the time, Pallas kernels for 0%

profile of v3, /device:TPU:8, one launch (start us, length us, event | category | flops | bytes accessed | tf_op | source)
XLA Modules:
  0.0 344.1 jit_solution(5664793583999640141)
XLA Ops:
  4.7 3.3 gather_fusion.4
  8.9 14.6 %all-to-all-start.1 = ((bf16[256,1,2]{2,1,0:T(2,128)(2,1)}), bf16[256,1,2]{2,1,0:T(2,128)(2,1)S(1)}, u32[]{:S(2)}, u32[]{:S(2)}) async-start(bf16[256,1,2]{2,1,0:T(2,128)(2,1)} %convert_element_type.66), calls=%async_computation.1 | async-start | bytes 262144 | tf_op jit(solution)/shard_map/all_to_all | solution.py:43
  24.0 3.4 gather_fusion.3
  27.4 2.6 broadcast_select_fusion.18
  30.0 2.7 slice_bitcast_fusion.1
  32.7 2.9 all-to-all-done.1
  35.6 11.8 %all-to-all-start = ((bf16[256,32,128]{2,1,0:T(8,128)(2,1)}), bf16[256,32,128]{2,1,0:T(8,128)(2,1)}, u32[]{:S(2)}, u32[]{:S(2)}) async-start(bf16[256,32,128]{2,1,0:T(8,128)(2,1)} %get-tuple-element.115), calls=%async_computation | async-start | bytes 4194304 | tf_op jit(solution)/shard_map/all_to_all | solution.py:68
  49.3 50.9 %all-to-all-done = bf16[256,32,128]{2,1,0:T(8,128)(2,1)} async-done(((bf16[256,32,128]{2,1,0:T(8,128)(2,1)}), bf16[256,32,128]{2,1,0:T(8,128)(2,1)}, u32[]{:S(2)}, u32[]{:S(2)}) %all-to-all-start) | async-done | bytes 2097184 | tf_op jit(solution)/shard_map/all_to_all | solution.py:68
  100.2 7.3 %all-to-all-start.2 = ((bf16[256,32,128]{2,1,0:T(8,128)(2,1)}), bf16[256,32,128]{2,1,0:T(8,128)(2,1)}, u32[]{:S(2)}, u32[]{:S(2)}) async-start(bf16[256,32,128]{2,1,0:T(8,128)(2,1)} %get-tuple-element.116), calls=%async_computation.2 | async-start | bytes 4194304 | tf_op jit(solution)/shard_map/all_to_all | solution.py:68
  107.9 34.7 %while.24 = (s32[]{:T(128)}, bf16[4,64,32,128]{3,2,1,0:T(8,128)(2,1)S(1)}, f32[4,64]{1,0:T(4,128)S(1)}, bf16[4,64,32,128]{3,2,1,0:T(8,128)(2,1)}, s32[4,64]{1,0:...) while((s32[]{:T(128)}, bf16[4,64,32,128]{3,2,1,0:T(8,128)(2,1)S(1)}, ...), condition=%wide.region_7.9_spmd, body=%wide.region_4.8_spmd.sunk | while | flops 275516736 | bytes 38853628 | solution.py:72
  107.9 3.0 gather_fusion
  110.9 4.2 %fusion.60 = (f32[64,32]{1,0:T(8,128)S(1)}, f32[64,32,256]{2,1,0:T(8,128)S(1)}) fusion(bf16[64,256,128]{2,1,0:T(8,128)(2,1)} %gather_fusion, pred[64]{0:T(512)(128)(4,1)S(1)} %get-tuple-element.194, bf16[4,64,32,128]{3,2,1,0:T(8,128)(2,1)} %get-tuple-element.250, s32[]{:T(128)} %get-tuple-element.239), kind=kOutput, calls=%fused_computation.12.clone.1 | convolution fusion | flops 137361408 | bytes 6824512 | tf_op jit(solution)/shard_map/while/body/eval_jaxpr/bqe,bpe->bqp/dot_general | solution.py:51
  116.6 3.0 gather_fusion
  119.6 4.2 %fusion.60 = (f32[64,32]{1,0:T(8,128)S(1)}, f32[64,32,256]{2,1,0:T(8,128)S(1)}) fusion(bf16[64,256,128]{2,1,0:T(8,128)(2,1)} %gather_fusion, pred[64]{0:T(512)(128)(4,1)S(1)} %get-tuple-element.194, bf16[4,64,32,128]{3,2,1,0:T(8,128)(2,1)} %get-tuple-element.250, s32[]{:T(128)} %get-tuple-element.239), kind=kOutput, calls=%fused_computation.12.clone.1 | convolution fusion | flops 137361408 | bytes 6824512 | tf_op jit(solution)/shard_map/while/body/eval_jaxpr/bqe,bpe->bqp/dot_general | solution.py:51
  125.3 3.0 gather_fusion
  128.3 4.2 %fusion.60 = (f32[64,32]{1,0:T(8,128)S(1)}, f32[64,32,256]{2,1,0:T(8,128)S(1)}) fusion(bf16[64,256,128]{2,1,0:T(8,128)(2,1)} %gather_fusion, pred[64]{0:T(512)(128)(4,1)S(1)} %get-tuple-element.194, bf16[4,64,32,128]{3,2,1,0:T(8,128)(2,1)} %get-tuple-element.250, s32[]{:T(128)} %get-tuple-element.239), kind=kOutput, calls=%fused_computation.12.clone.1 | convolution fusion | flops 137361408 | bytes 6824512 | tf_op jit(solution)/shard_map/while/body/eval_jaxpr/bqe,bpe->bqp/dot_general | solution.py:51
  134.0 3.0 gather_fusion
  137.0 4.2 %fusion.60 = (f32[64,32]{1,0:T(8,128)S(1)}, f32[64,32,256]{2,1,0:T(8,128)S(1)}) fusion(bf16[64,256,128]{2,1,0:T(8,128)(2,1)} %gather_fusion, pred[64]{0:T(512)(128)(4,1)S(1)} %get-tuple-element.194, bf16[4,64,32,128]{3,2,1,0:T(8,128)(2,1)} %get-tuple-element.250, s32[]{:T(128)} %get-tuple-element.239), kind=kOutput, calls=%fused_computation.12.clone.1 | convolution fusion | flops 137361408 | bytes 6824512 | tf_op jit(solution)/shard_map/while/body/eval_jaxpr/bqe,bpe->bqp/dot_general | solution.py:51
  142.6 17.7 %all-to-all-done.2 = bf16[256,32,128]{2,1,0:T(8,128)(2,1)} async-done(((bf16[256,32,128]{2,1,0:T(8,128)(2,1)}), bf16[256,32,128]{2,1,0:T(8,128)(2,1)}, u32[]{:S(2)}, u32[]{:S(2)}) %all-to-all-start.2) | async-done | bytes 2097184 | tf_op jit(solution)/shard_map/all_to_all | solution.py:68
  162.0 37.2 %while.25 = (s32[]{:T(128)}, bf16[4,64,32,128]{3,2,1,0:T(8,128)(2,1)}, f32[4,64]{1,0:T(4,128)S(1)}, bf16[4,64,32,128]{3,2,1,0:T(8,128)(2,1)}, s32[4,64]{1,0:T(4,...) while((s32[]{:T(128)}, bf16[4,64,32,128]{3,2,1,0:T(8,128)(2,1)}, ...), condition=%wide.region_11.13_spmd, body=%wide.region_8.12_spmd.sunk | while | flops 275516736 | bytes 38829112 | solution.py:72
  162.0 3.0 gather_fusion.1
  165.1 4.2 %fusion.62 = (f32[64,32]{1,0:T(8,128)S(1)}, f32[64,32,256]{2,1,0:T(8,128)S(1)}) fusion(bf16[64,256,128]{2,1,0:T(8,128)(2,1)} %gather_fusion.1, pred[64]{0:T(512)(128)(4,1)S(1)} %get-tuple-element.204, bf16[4,64,32,128]{3,2,1,0:T(8,128)(2,1)} %get-tuple-element.226, s32[]{:T(128)} %get-tuple-element.215), kind=kOutput, calls=%fused_computation.35.clone.1 | convolution fusion | flops 137361408 | bytes 6824512 | tf_op jit(solution)/shard_map/while/body/eval_jaxpr/bqe,bpe->bqp/dot_general | solution.py:51
  171.3 3.0 gather_fusion.1
  174.4 4.2 %fusion.62 = (f32[64,32]{1,0:T(8,128)S(1)}, f32[64,32,256]{2,1,0:T(8,128)S(1)}) fusion(bf16[64,256,128]{2,1,0:T(8,128)(2,1)} %gather_fusion.1, pred[64]{0:T(512)(128)(4,1)S(1)} %get-tuple-element.204, bf16[4,64,32,128]{3,2,1,0:T(8,128)(2,1)} %get-tuple-element.226, s32[]{:T(128)} %get-tuple-element.215), kind=kOutput, calls=%fused_computation.35.clone.1 | convolution fusion | flops 137361408 | bytes 6824512 | tf_op jit(solution)/shard_map/while/body/eval_jaxpr/bqe,bpe->bqp/dot_general | solution.py:51
  180.6 3.0 gather_fusion.1
  183.7 4.2 %fusion.62 = (f32[64,32]{1,0:T(8,128)S(1)}, f32[64,32,256]{2,1,0:T(8,128)S(1)}) fusion(bf16[64,256,128]{2,1,0:T(8,128)(2,1)} %gather_fusion.1, pred[64]{0:T(512)(128)(4,1)S(1)} %get-tuple-element.204, bf16[4,64,32,128]{3,2,1,0:T(8,128)(2,1)} %get-tuple-element.226, s32[]{:T(128)} %get-tuple-element.215), kind=kOutput, calls=%fused_computation.35.clone.1 | convolution fusion | flops 137361408 | bytes 6824512 | tf_op jit(solution)/shard_map/while/body/eval_jaxpr/bqe,bpe->bqp/dot_general | solution.py:51
  189.9 3.0 gather_fusion.1
  192.9 4.2 %fusion.62 = (f32[64,32]{1,0:T(8,128)S(1)}, f32[64,32,256]{2,1,0:T(8,128)S(1)}) fusion(bf16[64,256,128]{2,1,0:T(8,128)(2,1)} %gather_fusion.1, pred[64]{0:T(512)(128)(4,1)S(1)} %get-tuple-element.204, bf16[4,64,32,128]{3,2,1,0:T(8,128)(2,1)} %get-tuple-element.226, s32[]{:T(128)} %get-tuple-element.215), kind=kOutput, calls=%fused_computation.35.clone.1 | convolution fusion | flops 137361408 | bytes 6824512 | tf_op jit(solution)/shard_map/while/body/eval_jaxpr/bqe,bpe->bqp/dot_general | solution.py:51
  199.5 18.3 %all_to_all.35 = f32[256,1,2]{2,1,0:T(1,128)S(1)} all-to-all(f32[256,1,2]{2,1,0:T(1,128)S(1)} %bitcast.77), channel_id=1, replica_groups=mesh['group'=8,'dev'=32] {'group','dev'}, dimensions={0} | all-to-all | bytes 4096 | tf_op jit(solution)/shard_map/all_to_all | solution.py:83
  217.8 60.6 %all_to_all.36 = bf16[256,32,128]{2,1,0:T(8,128)(2,1)} all-to-all(bf16[256,32,128]{2,1,0:T(8,128)(2,1)S(1)} %bitcast.73), channel_id=1, replica_groups=mesh['group'=8,'dev'=32] {'group','dev'}, dimensions={0} | all-to-all | bytes 4194304 | tf_op jit(solution)/shard_map/all_to_all | solution.py:80
  278.4 6.3 %all-to-all-start.4 = ((bf16[256,32,128]{2,1,0:T(8,128)(2,1)}), bf16[256,32,128]{2,1,0:T(8,128)(2,1)S(1)}, u32[]{:S(2)}, u32[]{:S(2)}) async-start(bf16[256,32,128]{2,1,0:T(8,128)(2,1)} %bitcast.21), calls=%async_computation.4 | async-start | bytes 4194304 | tf_op jit(solution)/shard_map/all_to_all | solution.py:80
  291.1 47.3 %all-to-all-done.4 = bf16[256,32,128]{2,1,0:T(8,128)(2,1)S(1)} async-done(((bf16[256,32,128]{2,1,0:T(8,128)(2,1)}), bf16[256,32,128]{2,1,0:T(8,128)(2,1)S(1)}, u32[]{:S(2)}, u32[]{:S(2)}) %all-to-all-start.4) | async-done | bytes 2097184 | tf_op jit(solution)/shard_map/all_to_all | solution.py:80
  (121 shorter events, 35.7 us)
Async XLA Ops:
  0.6 1.6 copy-start
  0.6 22.9 %copy-start.4 = (bf16[8,32,128]{2,1,0:T(8,128)(2,1)S(1)}, bf16[8,32,128]{2,1,0:T(8,128)(2,1)}, u32[]{:S(2)}) copy-start(bf16[8,32,128]{2,1,0:T(8,128)(2,1)} %param.12) | copy-start | bytes 196612
  8.9 26.7 %all-to-all-start.1 = ((bf16[256,1,2]{2,1,0:T(2,128)(2,1)}), bf16[256,1,2]{2,1,0:T(2,128)(2,1)S(1)}, u32[]{:S(2)}, u32[]{:S(2)}) async-start(bf16[256,1,2]{2,1,0:T(2,128)(2,1)} %convert_element_type.66), calls=%async_computation.1 | async-start | bytes 262144 | tf_op jit(solution)/shard_map/all_to_all | solution.py:43
  35.6 11.8 %copy-start.3 = (bf16[16,256,128]{2,1,0:T(8,128)(2,1)S(1)}, bf16[16,256,128]{2,1,0:T(8,128)(2,1)}, u32[]{:S(2)}) copy-start(bf16[16,256,128]{2,1,0:T(8,128)(2,1)} %param.13) | copy-start | bytes 3145732
  35.6 64.6 %all-to-all-start = ((bf16[256,32,128]{2,1,0:T(8,128)(2,1)}), bf16[256,32,128]{2,1,0:T(8,128)(2,1)}, u32[]{:S(2)}, u32[]{:S(2)}) async-start(bf16[256,32,128]{2,1,0:T(8,128)(2,1)} %get-tuple-element.115), calls=%async_computation | async-start | bytes 4194304 | tf_op jit(solution)/shard_map/all_to_all | solution.py:68
  100.2 60.1 %all-to-all-start.2 = ((bf16[256,32,128]{2,1,0:T(8,128)(2,1)}), bf16[256,32,128]{2,1,0:T(8,128)(2,1)}, u32[]{:S(2)}, u32[]{:S(2)}) async-start(bf16[256,32,128]{2,1,0:T(8,128)(2,1)} %get-tuple-element.116), calls=%async_computation.2 | async-start | bytes 4194304 | tf_op jit(solution)/shard_map/all_to_all | solution.py:68
  110.9 4.2 %copy-start.1 = (bf16[64,256,128]{2,1,0:T(8,128)(2,1)S(1)}, bf16[64,256,128]{2,1,0:T(8,128)(2,1)}, u32[]{:S(2)}) copy-start(bf16[64,256,128]{2,1,0:T(8,128)(2,1)} %gather_fusion) | copy-start | bytes 12582916 | tf_op jit(solution)/shard_map/while
  119.6 4.2 %copy-start.1 = (bf16[64,256,128]{2,1,0:T(8,128)(2,1)S(1)}, bf16[64,256,128]{2,1,0:T(8,128)(2,1)}, u32[]{:S(2)}) copy-start(bf16[64,256,128]{2,1,0:T(8,128)(2,1)} %gather_fusion) | copy-start | bytes 12582916 | tf_op jit(solution)/shard_map/while
  128.3 4.2 %copy-start.1 = (bf16[64,256,128]{2,1,0:T(8,128)(2,1)S(1)}, bf16[64,256,128]{2,1,0:T(8,128)(2,1)}, u32[]{:S(2)}) copy-start(bf16[64,256,128]{2,1,0:T(8,128)(2,1)} %gather_fusion) | copy-start | bytes 12582916 | tf_op jit(solution)/shard_map/while
  137.0 4.2 %copy-start.1 = (bf16[64,256,128]{2,1,0:T(8,128)(2,1)S(1)}, bf16[64,256,128]{2,1,0:T(8,128)(2,1)}, u32[]{:S(2)}) copy-start(bf16[64,256,128]{2,1,0:T(8,128)(2,1)} %gather_fusion) | copy-start | bytes 12582916 | tf_op jit(solution)/shard_map/while
  165.1 4.2 %copy-start.2 = (bf16[64,256,128]{2,1,0:T(8,128)(2,1)S(1)}, bf16[64,256,128]{2,1,0:T(8,128)(2,1)}, u32[]{:S(2)}) copy-start(bf16[64,256,128]{2,1,0:T(8,128)(2,1)} %gather_fusion.1) | copy-start | bytes 12582916 | tf_op jit(solution)/shard_map/while
  174.3 4.2 %copy-start.2 = (bf16[64,256,128]{2,1,0:T(8,128)(2,1)S(1)}, bf16[64,256,128]{2,1,0:T(8,128)(2,1)}, u32[]{:S(2)}) copy-start(bf16[64,256,128]{2,1,0:T(8,128)(2,1)} %gather_fusion.1) | copy-start | bytes 12582916 | tf_op jit(solution)/shard_map/while
  183.7 4.2 %copy-start.2 = (bf16[64,256,128]{2,1,0:T(8,128)(2,1)S(1)}, bf16[64,256,128]{2,1,0:T(8,128)(2,1)}, u32[]{:S(2)}) copy-start(bf16[64,256,128]{2,1,0:T(8,128)(2,1)} %gather_fusion.1) | copy-start | bytes 12582916 | tf_op jit(solution)/shard_map/while
  192.9 4.2 %copy-start.2 = (bf16[64,256,128]{2,1,0:T(8,128)(2,1)S(1)}, bf16[64,256,128]{2,1,0:T(8,128)(2,1)}, u32[]{:S(2)}) copy-start(bf16[64,256,128]{2,1,0:T(8,128)(2,1)} %gather_fusion.1) | copy-start | bytes 12582916 | tf_op jit(solution)/shard_map/while
  278.4 9.5 %copy-start.5 = (s32[8,16]{1,0:T(8,128)S(1)}, s32[8,16]{1,0:T(8,128)}, u32[]{:S(2)}) copy-start(s32[8,16]{1,0:T(8,128)} %param.14) | copy-start | bytes 1540
  278.4 60.0 %all-to-all-start.4 = ((bf16[256,32,128]{2,1,0:T(8,128)(2,1)}), bf16[256,32,128]{2,1,0:T(8,128)(2,1)S(1)}, u32[]{:S(2)}, u32[]{:S(2)}) async-start(bf16[256,32,128]{2,1,0:T(8,128)(2,1)} %bitcast.21), calls=%async_computation.4 | async-start | bytes 4194304 | tf_op jit(solution)/shard_map/all_to_all | solution.py:80

commit v4 on v3

--- a/solution.py
+++ b/solution.py
@@ -40,8 +40,9 @@
     both_axes = ("group", "dev")
     outgoing = outgoing.reshape(device_total, slot_cap, query_len, feat_width)
     labels = labels.reshape(device_total, slot_cap)
-    tags = lax.all_to_all(labels, both_axes, split_axis=0, concat_axis=0, tiled=True)
-    tags = tags.astype(jnp.int32)
+    me = lax.axis_index("group") * dev_count + lax.axis_index("dev")
+    all_labels = lax.all_gather(labels, both_axes, axis=0, tiled=False)
+    tags = lax.dynamic_index_in_dim(all_labels, me, axis=1, keepdims=False).astype(jnp.int32)
     block_rows = 64
 
     def score_block(inputs):
@@ -80,7 +81,8 @@
         returned.append(lax.all_to_all(pulled, both_axes, split_axis=0, concat_axis=0, tiled=True))
         scores.append(score.reshape(device_total))
     scores = jnp.stack(scores, axis=1)
-    scores_flat = lax.all_to_all(scores, both_axes, split_axis=0, concat_axis=0, tiled=True)
+    all_scores = lax.all_gather(scores, both_axes, axis=0, tiled=False)
+    scores_flat = lax.dynamic_index_in_dim(all_scores, me, axis=1, keepdims=False)
     pair_score = jnp.take(scores_flat.reshape(slot_total), slot_index, axis=0).reshape(
         query_count, list_len
     )

time: 346 us -> 384 us (1.11)
  blocking collectives: 78.9 us -> 206 us
  waiting for transfers between devices: 119 us -> 29.7 us
    all_gather x0 -> x2, blocking collectives: none -> 206 us  [the longest x1 108 us: local(): all_scores = lax.all_gather(scores, both_axes, axis=0, tiled=False)]
    all_to_all x2 -> x0, blocking collectives: 78.9 us -> none  [the longest x1 60.6 us: local(): lax.all_to_all(pulled, both_axes, split_axis=0, concat_axis=0, tiled=True)]
    all_to_all x2, waiting for transfers between devices: 68.7 us -> 14.8 us  [local(): lax.all_to_all(outgoing[:, slot], both_axes, split_axis=0, concat_axis=0,...]
    all_to_all x1 -> x2, waiting for transfers between devices: 47.3 us -> 14.9 us  [local(): lax.all_to_all(pulled, both_axes, split_axis=0, concat_axis=0, tiled=True)]
    all_to_all x1 -> x0, starting transfers between devices: 14.6 us -> none  [local(): lax.all_to_all(labels, both_axes, split_axis=0, concat_axis=0, tiled=True)]
    all_to_all x1 -> x2, starting transfers between devices: 6.29 us -> 13.6 us  [local(): lax.all_to_all(pulled, both_axes, split_axis=0, concat_axis=0, tiled=True)]
    all_to_all x2, starting transfers between devices: 19.1 us -> 23.8 us  [local(): lax.all_to_all(outgoing[:, slot], both_axes, split_axis=0, concat_axis=0,...]
  transfers between devices with their start and end apart: 4 -> 4, of which waited for: 4 -> 2; matrix products, arithmetic and copies ran while one was open for 15% -> 23% of each run, Pallas kernels for 0% -> 0%
where the time goes in v4:
time: 384 us
  blocking collectives  206 us (54%)
  local copies, waits for them, and re-layouts  50 us (13%)
  matrix products  49 us (13%)
  starting transfers between devices  37.4 us (10%)
  waiting for transfers between devices  29.7 us (8%)
  other arithmetic  10.4 us (3%)
    all_gather x1, blocking collectives, local(): all_scores = lax.all_gather(scores, both_axes, axis=0, tiled=False)  108 us
    all_gather x1, blocking collectives, local(): all_labels = lax.all_gather(labels, both_axes, axis=0, tiled=False)  97.6 us
    dot_general x8, matrix products, score_block(): jnp.einsum('bqe,bpe->bqp', query_block, passage_block, preferred_element_...  33.2 us
    gather x8, local copies, waits for them, and re-layouts, score_block(): passage_block = jnp.take(passage_unit, tag_block, axis=0)  24.1 us
    all_to_all x2, starting transfers between devices, local(): lax.all_to_all(outgoing[:, slot], both_axes, split_axis=0, concat_axis=0,...  23.8 us
    dot_general x8, matrix products, score_block(): jnp.einsum('bqp,bpe->bqe', attention, passage_block, preferred_element_ty...  15.4 us
    all_to_all x2, waiting for transfers between devices, local(): lax.all_to_all(pulled, both_axes, split_axis=0, concat_axis=0, tiled=True)  14.9 us
    all_to_all x2, waiting for transfers between devices, local(): lax.all_to_all(outgoing[:, slot], both_axes, split_axis=0, concat_axis=0,...  14.8 us
  transfers between devices with their start and end apart: 4, of which 2 were waited for; matrix products, arithmetic and copies ran while one was open for 23% of the time, Pallas kernels for 0%

profile of v4, /device:TPU:8, one launch (start us, length us, event | category | flops | bytes accessed | tf_op | source)
XLA Modules:
  0.0 383.7 jit_solution(7705438052744642677)
XLA Ops:
  6.7 3.4 gather_fusion.3
  10.1 2.6 broadcast_select_fusion.18
  12.7 2.7 slice_bitcast_fusion.1
  15.4 15.6 %all-to-all-start = ((bf16[256,32,128]{2,1,0:T(8,128)(2,1)}), bf16[256,32,128]{2,1,0:T(8,128)(2,1)}, u32[]{:S(2)}, u32[]{:S(2)}) async-start(bf16[256,32,128]{2,1,0:T(8,128)(2,1)} %get-tuple-element.115), calls=%async_computation | async-start | bytes 4194304 | tf_op jit(solution)/shard_map/all_to_all | solution.py:69
  31.1 3.3 gather_fusion.4
  34.7 97.6 %all_gather.9 = bf16[256,256,2]{1,2,0:T(2,128)(2,1)S(1)} all-gather(bf16[1,256,2]{1,2,0:T(2,128)(2,1)S(1)} %copy.15), channel_id=1, replica_groups=mesh['group'=8,'dev'=32] {'group','dev'}, dimensions={0}, use_global_device_ids=true | all-gather | bytes 263168 | tf_op jit(solution)/shard_map/all_gather | solution.py:44
  134.2 8.2 %all-to-all-start.1 = ((bf16[256,32,128]{2,1,0:T(8,128)(2,1)}), bf16[256,32,128]{2,1,0:T(8,128)(2,1)S(1)}, u32[]{:S(2)}, u32[]{:S(2)}) async-start(bf16[256,32,128]{2,1,0:T(8,128)(2,1)} %get-tuple-element.116), calls=%async_computation.1 | async-start | bytes 4194304 | tf_op jit(solution)/shard_map/all_to_all | solution.py:69
  144.1 37.2 %while.24 = (s32[]{:T(128)}, bf16[4,64,32,128]{3,2,1,0:T(8,128)(2,1)}, f32[4,64]{1,0:T(4,128)S(1)}, bf16[4,64,32,128]{3,2,1,0:T(8,128)(2,1)}, s32[4,64]{1,0:T(4,...) while((s32[]{:T(128)}, bf16[4,64,32,128]{3,2,1,0:T(8,128)(2,1)}, ...), condition=%wide.region_7.9_spmd, body=%wide.region_4.8_spmd.sunk | while | flops 275516736 | bytes 38829112 | solution.py:73
  144.1 3.0 gather_fusion
  147.2 4.2 %fusion.60 = (f32[64,32]{1,0:T(8,128)S(1)}, f32[64,32,256]{2,1,0:T(8,128)S(1)}) fusion(bf16[64,256,128]{2,1,0:T(8,128)(2,1)} %gather_fusion, pred[64]{0:T(512)(128)(4,1)S(1)} %get-tuple-element.194, bf16[4,64,32,128]{3,2,1,0:T(8,128)(2,1)} %get-tuple-element.250, s32[]{:T(128)} %get-tuple-element.239), kind=kOutput, calls=%fused_computation.12.clone.1 | convolution fusion | flops 137361408 | bytes 6824512 | tf_op jit(solution)/shard_map/while/body/eval_jaxpr/bqe,bpe->bqp/dot_general | solution.py:52
  153.4 3.0 gather_fusion
  156.4 4.2 %fusion.60 = (f32[64,32]{1,0:T(8,128)S(1)}, f32[64,32,256]{2,1,0:T(8,128)S(1)}) fusion(bf16[64,256,128]{2,1,0:T(8,128)(2,1)} %gather_fusion, pred[64]{0:T(512)(128)(4,1)S(1)} %get-tuple-element.194, bf16[4,64,32,128]{3,2,1,0:T(8,128)(2,1)} %get-tuple-element.250, s32[]{:T(128)} %get-tuple-element.239), kind=kOutput, calls=%fused_computation.12.clone.1 | convolution fusion | flops 137361408 | bytes 6824512 | tf_op jit(solution)/shard_map/while/body/eval_jaxpr/bqe,bpe->bqp/dot_general | solution.py:52
  160.6 1.9 fusion.61
  162.7 3.0 gather_fusion
  165.7 4.2 %fusion.60 = (f32[64,32]{1,0:T(8,128)S(1)}, f32[64,32,256]{2,1,0:T(8,128)S(1)}) fusion(bf16[64,256,128]{2,1,0:T(8,128)(2,1)} %gather_fusion, pred[64]{0:T(512)(128)(4,1)S(1)} %get-tuple-element.194, bf16[4,64,32,128]{3,2,1,0:T(8,128)(2,1)} %get-tuple-element.250, s32[]{:T(128)} %get-tuple-element.239), kind=kOutput, calls=%fused_computation.12.clone.1 | convolution fusion | flops 137361408 | bytes 6824512 | tf_op jit(solution)/shard_map/while/body/eval_jaxpr/bqe,bpe->bqp/dot_general | solution.py:52
  172.0 3.0 gather_fusion
  175.0 4.2 %fusion.60 = (f32[64,32]{1,0:T(8,128)S(1)}, f32[64,32,256]{2,1,0:T(8,128)S(1)}) fusion(bf16[64,256,128]{2,1,0:T(8,128)(2,1)} %gather_fusion, pred[64]{0:T(512)(128)(4,1)S(1)} %get-tuple-element.194, bf16[4,64,32,128]{3,2,1,0:T(8,128)(2,1)} %get-tuple-element.250, s32[]{:T(128)} %get-tuple-element.239), kind=kOutput, calls=%fused_computation.12.clone.1 | convolution fusion | flops 137361408 | bytes 6824512 | tf_op jit(solution)/shard_map/while/body/eval_jaxpr/bqe,bpe->bqp/dot_general | solution.py:52
  181.3 14.8 %all-to-all-done.1 = bf16[256,32,128]{2,1,0:T(8,128)(2,1)S(1)} async-done(((bf16[256,32,128]{2,1,0:T(8,128)(2,1)}), bf16[256,32,128]{2,1,0:T(8,128)(2,1)S(1)}, u32[]{:S(2)}, u32[]{:S(2)}) %all-to-all-start.1) | async-done | bytes 2097184 | tf_op jit(solution)/shard_map/all_to_all | solution.py:69
  197.4 6.3 %all-to-all-start.3 = ((bf16[256,32,128]{2,1,0:T(8,128)(2,1)}), bf16[256,32,128]{2,1,0:T(8,128)(2,1)S(1)}, u32[]{:S(2)}, u32[]{:S(2)}) async-start(bf16[256,32,128]{2,1,0:T(8,128)(2,1)} %bitcast.22), calls=%async_computation.3 | async-start | bytes 4194304 | tf_op jit(solution)/shard_map/all_to_all | solution.py:81
  205.4 37.1 %while.25 = (s32[]{:T(128)}, bf16[4,64,32,128]{3,2,1,0:T(8,128)(2,1)}, f32[4,64]{1,0:T(4,128)S(1)}, bf16[4,64,32,128]{3,2,1,0:T(8,128)(2,1)}, s32[4,64]{1,0:T(4,...) while((s32[]{:T(128)}, bf16[4,64,32,128]{3,2,1,0:T(8,128)(2,1)}, ...), condition=%wide.region_11.13_spmd, body=%wide.region_8.12_spmd.sunk | while | flops 275516736 | bytes 38829112 | solution.py:73
  205.4 3.0 gather_fusion.1
  208.4 4.2 %fusion.62 = (f32[64,32]{1,0:T(8,128)S(1)}, f32[64,32,256]{2,1,0:T(8,128)S(1)}) fusion(bf16[64,256,128]{2,1,0:T(8,128)(2,1)} %gather_fusion.1, pred[64]{0:T(512)(128)(4,1)S(1)} %get-tuple-element.204, bf16[4,64,32,128]{3,2,1,0:T(8,128)(2,1)} %get-tuple-element.226, s32[]{:T(128)} %get-tuple-element.215), kind=kOutput, calls=%fused_computation.35.clone.1 | convolution fusion | flops 137361408 | bytes 6824512 | tf_op jit(solution)/shard_map/while/body/eval_jaxpr/bqe,bpe->bqp/dot_general | solution.py:52
  214.7 3.0 gather_fusion.1
  217.7 4.2 %fusion.62 = (f32[64,32]{1,0:T(8,128)S(1)}, f32[64,32,256]{2,1,0:T(8,128)S(1)}) fusion(bf16[64,256,128]{2,1,0:T(8,128)(2,1)} %gather_fusion.1, pred[64]{0:T(512)(128)(4,1)S(1)} %get-tuple-element.204, bf16[4,64,32,128]{3,2,1,0:T(8,128)(2,1)} %get-tuple-element.226, s32[]{:T(128)} %get-tuple-element.215), kind=kOutput, calls=%fused_computation.35.clone.1 | convolution fusion | flops 137361408 | bytes 6824512 | tf_op jit(solution)/shard_map/while/body/eval_jaxpr/bqe,bpe->bqp/dot_general | solution.py:52
  224.0 3.0 gather_fusion.1
  227.0 4.2 %fusion.62 = (f32[64,32]{1,0:T(8,128)S(1)}, f32[64,32,256]{2,1,0:T(8,128)S(1)}) fusion(bf16[64,256,128]{2,1,0:T(8,128)(2,1)} %gather_fusion.1, pred[64]{0:T(512)(128)(4,1)S(1)} %get-tuple-element.204, bf16[4,64,32,128]{3,2,1,0:T(8,128)(2,1)} %get-tuple-element.226, s32[]{:T(128)} %get-tuple-element.215), kind=kOutput, calls=%fused_computation.35.clone.1 | convolution fusion | flops 137361408 | bytes 6824512 | tf_op jit(solution)/shard_map/while/body/eval_jaxpr/bqe,bpe->bqp/dot_general | solution.py:52
  233.3 3.0 gather_fusion.1
  236.3 4.2 %fusion.62 = (f32[64,32]{1,0:T(8,128)S(1)}, f32[64,32,256]{2,1,0:T(8,128)S(1)}) fusion(bf16[64,256,128]{2,1,0:T(8,128)(2,1)} %gather_fusion.1, pred[64]{0:T(512)(128)(4,1)S(1)} %get-tuple-element.204, bf16[4,64,32,128]{3,2,1,0:T(8,128)(2,1)} %get-tuple-element.226, s32[]{:T(128)} %get-tuple-element.215), kind=kOutput, calls=%fused_computation.35.clone.1 | convolution fusion | flops 137361408 | bytes 6824512 | tf_op jit(solution)/shard_map/while/body/eval_jaxpr/bqe,bpe->bqp/dot_general | solution.py:52
  242.5 14.9 %all-to-all-done.3 = bf16[256,32,128]{2,1,0:T(8,128)(2,1)S(1)} async-done(((bf16[256,32,128]{2,1,0:T(8,128)(2,1)}), bf16[256,32,128]{2,1,0:T(8,128)(2,1)S(1)}, u32[]{:S(2)}, u32[]{:S(2)}) %all-to-all-start.3) | async-done | bytes 2097184 | tf_op jit(solution)/shard_map/all_to_all | solution.py:81
  257.4 7.3 %all-to-all-start.2 = ((bf16[256,32,128]{2,1,0:T(8,128)(2,1)}), bf16[256,32,128]{2,1,0:T(8,128)(2,1)}, u32[]{:S(2)}, u32[]{:S(2)}) async-start(bf16[256,32,128]{2,1,0:T(8,128)(2,1)} %bitcast.21), calls=%async_computation.2 | async-start | bytes 4194304 | tf_op jit(solution)/shard_map/all_to_all | solution.py:81
  265.1 108.4 %all-gather = f32[65536,2]{0,1:T(2,128)S(1)} all-gather(f32[256,2]{0,1:T(2,128)S(1)} %pad_maximum_fusion), channel_id=2, replica_groups=mesh['group'=8,'dev'=32] {'group','dev'}, dimensions={0}, use_global_device_ids=true | all-gather | bytes 526336 | tf_op jit(solution)/shard_map/all_gather | solution.py:84
  378.4 2.4 gather_fusion.6
  (126 shorter events, 35.8 us)
Async XLA Ops:
  0.6 1.6 copy-start
  15.4 118.7 %all-to-all-start = ((bf16[256,32,128]{2,1,0:T(8,128)(2,1)}), bf16[256,32,128]{2,1,0:T(8,128)(2,1)}, u32[]{:S(2)}, u32[]{:S(2)}) async-start(bf16[256,32,128]{2,1,0:T(8,128)(2,1)} %get-tuple-element.115), calls=%async_computation | async-start | bytes 4194304 | tf_op jit(solution)/shard_map/all_to_all | solution.py:69
  31.0 101.8 %copy-start.3 = (bf16[16,256,128]{2,1,0:T(8,128)(2,1)S(1)}, bf16[16,256,128]{2,1,0:T(8,128)(2,1)}, u32[]{:S(2)}) copy-start(bf16[16,256,128]{2,1,0:T(8,128)(2,1)} %param.13) | copy-start | bytes 3145732
  134.2 61.9 %all-to-all-start.1 = ((bf16[256,32,128]{2,1,0:T(8,128)(2,1)}), bf16[256,32,128]{2,1,0:T(8,128)(2,1)S(1)}, u32[]{:S(2)}, u32[]{:S(2)}) async-start(bf16[256,32,128]{2,1,0:T(8,128)(2,1)} %get-tuple-element.116), calls=%async_computation.1 | async-start | bytes 4194304 | tf_op jit(solution)/shard_map/all_to_all | solution.py:69
  147.2 4.2 %copy-start.1 = (bf16[64,256,128]{2,1,0:T(8,128)(2,1)S(1)}, bf16[64,256,128]{2,1,0:T(8,128)(2,1)}, u32[]{:S(2)}) copy-start(bf16[64,256,128]{2,1,0:T(8,128)(2,1)} %gather_fusion) | copy-start | bytes 12582916 | tf_op jit(solution)/shard_map/while
  156.4 4.2 %copy-start.1 = (bf16[64,256,128]{2,1,0:T(8,128)(2,1)S(1)}, bf16[64,256,128]{2,1,0:T(8,128)(2,1)}, u32[]{:S(2)}) copy-start(bf16[64,256,128]{2,1,0:T(8,128)(2,1)} %gather_fusion) | copy-start | bytes 12582916 | tf_op jit(solution)/shard_map/while
  165.7 4.2 %copy-start.1 = (bf16[64,256,128]{2,1,0:T(8,128)(2,1)S(1)}, bf16[64,256,128]{2,1,0:T(8,128)(2,1)}, u32[]{:S(2)}) copy-start(bf16[64,256,128]{2,1,0:T(8,128)(2,1)} %gather_fusion) | copy-start | bytes 12582916 | tf_op jit(solution)/shard_map/while
  175.0 4.2 %copy-start.1 = (bf16[64,256,128]{2,1,0:T(8,128)(2,1)S(1)}, bf16[64,256,128]{2,1,0:T(8,128)(2,1)}, u32[]{:S(2)}) copy-start(bf16[64,256,128]{2,1,0:T(8,128)(2,1)} %gather_fusion) | copy-start | bytes 12582916 | tf_op jit(solution)/shard_map/while
  196.1 1.3 copy-start.4
  197.4 60.0 %all-to-all-start.3 = ((bf16[256,32,128]{2,1,0:T(8,128)(2,1)}), bf16[256,32,128]{2,1,0:T(8,128)(2,1)S(1)}, u32[]{:S(2)}, u32[]{:S(2)}) async-start(bf16[256,32,128]{2,1,0:T(8,128)(2,1)} %bitcast.22), calls=%async_computation.3 | async-start | bytes 4194304 | tf_op jit(solution)/shard_map/all_to_all | solution.py:81
  208.4 4.2 %copy-start.2 = (bf16[64,256,128]{2,1,0:T(8,128)(2,1)S(1)}, bf16[64,256,128]{2,1,0:T(8,128)(2,1)}, u32[]{:S(2)}) copy-start(bf16[64,256,128]{2,1,0:T(8,128)(2,1)} %gather_fusion.1) | copy-start | bytes 12582916 | tf_op jit(solution)/shard_map/while
  217.7 4.2 %copy-start.2 = (bf16[64,256,128]{2,1,0:T(8,128)(2,1)S(1)}, bf16[64,256,128]{2,1,0:T(8,128)(2,1)}, u32[]{:S(2)}) copy-start(bf16[64,256,128]{2,1,0:T(8,128)(2,1)} %gather_fusion.1) | copy-start | bytes 12582916 | tf_op jit(solution)/shard_map/while
  227.0 4.2 %copy-start.2 = (bf16[64,256,128]{2,1,0:T(8,128)(2,1)S(1)}, bf16[64,256,128]{2,1,0:T(8,128)(2,1)}, u32[]{:S(2)}) copy-start(bf16[64,256,128]{2,1,0:T(8,128)(2,1)} %gather_fusion.1) | copy-start | bytes 12582916 | tf_op jit(solution)/shard_map/while
  236.3 4.2 %copy-start.2 = (bf16[64,256,128]{2,1,0:T(8,128)(2,1)S(1)}, bf16[64,256,128]{2,1,0:T(8,128)(2,1)}, u32[]{:S(2)}) copy-start(bf16[64,256,128]{2,1,0:T(8,128)(2,1)} %gather_fusion.1) | copy-start | bytes 12582916 | tf_op jit(solution)/shard_map/while
  257.4 121.0 %all-to-all-start.2 = ((bf16[256,32,128]{2,1,0:T(8,128)(2,1)}), bf16[256,32,128]{2,1,0:T(8,128)(2,1)}, u32[]{:S(2)}, u32[]{:S(2)}) async-start(bf16[256,32,128]{2,1,0:T(8,128)(2,1)} %bitcast.21), calls=%async_computation.2 | async-start | bytes 4194304 | tf_op jit(solution)/shard_map/all_to_all | solution.py:81
  264.7 112.1 %copy-start.6 = (s32[8,16]{1,0:T(8,128)S(1)}, s32[8,16]{1,0:T(8,128)}, u32[]{:S(2)}) copy-start(s32[8,16]{1,0:T(8,128)} %param.14) | copy-start | bytes 1540
  380.8 1.1 copy-start.5

commit v5 on v3

--- a/solution.py
+++ b/solution.py
@@ -80,6 +80,7 @@
         returned.append(lax.all_to_all(pulled, both_axes, split_axis=0, concat_axis=0, tiled=True))
         scores.append(score.reshape(device_total))
     scores = jnp.stack(scores, axis=1)
+    scores, returned[-1] = lax.optimization_barrier((scores, returned[-1]))
     scores_flat = lax.all_to_all(scores, both_axes, split_axis=0, concat_axis=0, tiled=True)
     pair_score = jnp.take(scores_flat.reshape(slot_total), slot_index, axis=0).reshape(
         query_count, list_len

time: 346 us -> 308 us (0.89)
  blocking collectives: 78.9 us -> 0 us
  waiting for transfers between devices: 119 us -> 143 us
  starting transfers between devices: 40 us -> 53.6 us
    all_to_all x2 -> x0, blocking collectives: 78.9 us -> none  [the longest x1 60.6 us: local(): lax.all_to_all(pulled, both_axes, split_axis=0, concat_axis=0, tiled=True)]
    all_to_all x1 -> x2, waiting for transfers between devices: 47.3 us -> 65.7 us  [local(): lax.all_to_all(pulled, both_axes, split_axis=0, concat_axis=0, tiled=True)]
    all_to_all x0 -> x1, waiting for transfers between devices: none -> 9.07 us  [local(): lax.all_to_all(scores, both_axes, split_axis=0, concat_axis=0, tiled=True)]
    all_to_all x1 -> x2, starting transfers between devices: 6.29 us -> 13.6 us  [local(): lax.all_to_all(pulled, both_axes, split_axis=0, concat_axis=0, tiled=True)]
    all_to_all x0 -> x1, starting transfers between devices: none -> 6.29 us  [local(): lax.all_to_all(scores, both_axes, split_axis=0, concat_axis=0, tiled=True)]
    all_to_all x2, waiting for transfers between devices: 68.7 us -> 65 us  [local(): lax.all_to_all(outgoing[:, slot], both_axes, split_axis=0, concat_axis=0,...]
  transfers between devices with their start and end apart: 4 -> 6, of which waited for: 4 -> 6; matrix products, arithmetic and copies ran while one was open for 15% -> 31% of each run, Pallas kernels for 0% -> 0%
where the time goes in v5:
time: 308 us; the launch traced here: 305 us
  waiting for transfers between devices  143 us (46%)
  starting transfers between devices  53.6 us (17%)
  matrix products  49 us (16%)
  local copies, waits for them, and re-layouts  48.7 us (16%)
  other arithmetic  9.81 us (3%)
    all_to_all x2, waiting for transfers between devices, local(): lax.all_to_all(pulled, both_axes, split_axis=0, concat_axis=0, tiled=True)  65.7 us
    all_to_all x2, waiting for transfers between devices, local(): lax.all_to_all(outgoing[:, slot], both_axes, split_axis=0, concat_axis=0,...  65 us
    dot_general x8, matrix products, score_block(): jnp.einsum('bqe,bpe->bqp', query_block, passage_block, preferred_element_...  33.2 us
    gather x8, local copies, waits for them, and re-layouts, score_block(): passage_block = jnp.take(passage_unit, tag_block, axis=0)  24.1 us
    all_to_all x2, starting transfers between devices, local(): lax.all_to_all(outgoing[:, slot], both_axes, split_axis=0, concat_axis=0,...  19.1 us
    dot_general x8, matrix products, score_block(): jnp.einsum('bqp,bpe->bqe', attention, passage_block, preferred_element_ty...  15.4 us
    all_to_all x1, starting transfers between devices, local(): lax.all_to_all(labels, both_axes, split_axis=0, concat_axis=0, tiled=True)  14.6 us
    all_to_all x2, starting transfers between devices, local(): lax.all_to_all(pulled, both_axes, split_axis=0, concat_axis=0, tiled=True)  13.6 us
  transfers between devices with their start and end apart: 6, of which 6 were waited for; matrix products, arithmetic and copies ran while one was open for 31% of the time, Pallas kernels for 0%

profile of v5, /device:TPU:8, one launch (start us, length us, event | category | flops | bytes accessed | tf_op | source)
XLA Modules:
  0.0 305.0 jit_solution(11694325702183027337)
XLA Ops:
  4.7 3.3 %gather_fusion.4 = s32[512]{0:T(512)S(1)} fusion(s32[128]{0:T(128)S(1)} %and_select_fusion.1, s32[1024]{0:T(1024)S(1)} %pad_clamp_fusion.4), kind=kCustom, calls=%fused_computation.6 | custom fusion | bytes 6144 | tf_op jit(solution)/shard_map/jit(_take)/gather | solution.py:39
  8.9 14.6 %all-to-all-start.1 = ((bf16[256,1,2]{2,1,0:T(2,128)(2,1)}), bf16[256,1,2]{2,1,0:T(2,128)(2,1)S(1)}, u32[]{:S(2)}, u32[]{:S(2)}) async-start(bf16[256,1,2]{2,1,0:T(2,128)(2,1)} %convert_element_type.66), calls=%async_computation.1 | async-start | bytes 262144 | tf_op jit(solution)/shard_map/all_to_all | solution.py:43
  24.0 3.4 %gather_fusion.3 = bf16[512,32,128]{2,1,0:T(8,128)(2,1)} fusion(bf16[8,32,128]{2,1,0:T(8,128)(2,1)S(1)} %fusion.39, s32[1024]{0:T(1024)S(1)} %pad_clamp_fusion.5), kind=kCustom, calls=%fused_computation.5 | custom fusion | bytes 8390656 | tf_op jit(solution)/shard_map/jit(_take)/gather | solution.py:38
  32.8 2.9 all-to-all-done.1
  35.6 11.9 %all-to-all-start.2 = ((bf16[256,32,128]{2,1,0:T(8,128)(2,1)}), bf16[256,32,128]{2,1,0:T(8,128)(2,1)}, u32[]{:S(2)}, u32[]{:S(2)}) async-start(bf16[256,32,128]{2,1,0:T(8,128)(2,1)} %get-tuple-element.120), calls=%async_computation.2 | async-start | bytes 4194304 | tf_op jit(solution)/shard_map/all_to_all | solution.py:68
  49.4 50.9 %all-to-all-done.2 = bf16[256,32,128]{2,1,0:T(8,128)(2,1)} async-done(((bf16[256,32,128]{2,1,0:T(8,128)(2,1)}), bf16[256,32,128]{2,1,0:T(8,128)(2,1)}, u32[]{:S(2)}, u32[]{:S(2)}) %all-to-all-start.2) | async-done | bytes 2097184 | tf_op jit(solution)/shard_map/all_to_all | solution.py:68
  100.3 7.3 %all-to-all-start = ((bf16[256,32,128]{2,1,0:T(8,128)(2,1)}), bf16[256,32,128]{2,1,0:T(8,128)(2,1)}, u32[]{:S(2)}, u32[]{:S(2)}) async-start(bf16[256,32,128]{2,1,0:T(8,128)(2,1)} %get-tuple-element.119), calls=%async_computation | async-start | bytes 4194304 | tf_op jit(solution)/shard_map/all_to_all | solution.py:68
  109.2 37.1 %while.25 = (s32[]{:T(128)}, bf16[4,64,32,128]{3,2,1,0:T(8,128)(2,1)}, f32[4,64]{1,0:T(4,128)S(1)}, bf16[4,64,32,128]{3,2,1,0:T(8,128)(2,1)}, s32[4,64]{1,0:T(4,...) while((s32[]{:T(128)}, bf16[4,64,32,128]{3,2,1,0:T(8,128)(2,1)}, ...), condition=%wide.region_11.13_spmd, body=%wide.region_8.12_spmd.sunk | while | flops 275516736 | bytes 38829112 | solution.py:72
  109.2 3.0 gather_fusion.1
  112.2 4.2 %fusion.62 = (f32[64,32]{1,0:T(8,128)S(1)}, f32[64,32,256]{2,1,0:T(8,128)S(1)}) fusion(bf16[64,256,128]{2,1,0:T(8,128)(2,1)} %gather_fusion.1, pred[64]{0:T(512)(128)(4,1)S(1)} %get-tuple-element.208, bf16[4,64,32,128]{3,2,1,0:T(8,128)(2,1)} %get-tuple-element.230, s32[]{:T(128)} %get-tuple-element.219), kind=kOutput, calls=%fused_computation.35.clone.1 | convolution fusion | flops 137361408 | bytes 6824512 | tf_op jit(solution)/shard_map/while/body/eval_jaxpr/bqe,bpe->bqp/dot_general | solution.py:51
  118.5 3.0 gather_fusion.1
  121.5 4.2 %fusion.62 = (f32[64,32]{1,0:T(8,128)S(1)}, f32[64,32,256]{2,1,0:T(8,128)S(1)}) fusion(bf16[64,256,128]{2,1,0:T(8,128)(2,1)} %gather_fusion.1, pred[64]{0:T(512)(128)(4,1)S(1)} %get-tuple-element.208, bf16[4,64,32,128]{3,2,1,0:T(8,128)(2,1)} %get-tuple-element.230, s32[]{:T(128)} %get-tuple-element.219), kind=kOutput, calls=%fused_computation.35.clone.1 | convolution fusion | flops 137361408 | bytes 6824512 | tf_op jit(solution)/shard_map/while/body/eval_jaxpr/bqe,bpe->bqp/dot_general | solution.py:51
  127.8 3.0 gather_fusion.1
  130.8 4.2 %fusion.62 = (f32[64,32]{1,0:T(8,128)S(1)}, f32[64,32,256]{2,1,0:T(8,128)S(1)}) fusion(bf16[64,256,128]{2,1,0:T(8,128)(2,1)} %gather_fusion.1, pred[64]{0:T(512)(128)(4,1)S(1)} %get-tuple-element.208, bf16[4,64,32,128]{3,2,1,0:T(8,128)(2,1)} %get-tuple-element.230, s32[]{:T(128)} %get-tuple-element.219), kind=kOutput, calls=%fused_computation.35.clone.1 | convolution fusion | flops 137361408 | bytes 6824512 | tf_op jit(solution)/shard_map/while/body/eval_jaxpr/bqe,bpe->bqp/dot_general | solution.py:51
  137.1 3.0 gather_fusion.1
  140.1 4.2 %fusion.62 = (f32[64,32]{1,0:T(8,128)S(1)}, f32[64,32,256]{2,1,0:T(8,128)S(1)}) fusion(bf16[64,256,128]{2,1,0:T(8,128)(2,1)} %gather_fusion.1, pred[64]{0:T(512)(128)(4,1)S(1)} %get-tuple-element.208, bf16[4,64,32,128]{3,2,1,0:T(8,128)(2,1)} %get-tuple-element.230, s32[]{:T(128)} %get-tuple-element.219), kind=kOutput, calls=%fused_computation.35.clone.1 | convolution fusion | flops 137361408 | bytes 6824512 | tf_op jit(solution)/shard_map/while/body/eval_jaxpr/bqe,bpe->bqp/dot_general | solution.py:51
  146.3 14.1 %all-to-all-done = bf16[256,32,128]{2,1,0:T(8,128)(2,1)} async-done(((bf16[256,32,128]{2,1,0:T(8,128)(2,1)}), bf16[256,32,128]{2,1,0:T(8,128)(2,1)}, u32[]{:S(2)}, u32[]{:S(2)}) %all-to-all-start) | async-done | bytes 2097184 | tf_op jit(solution)/shard_map/all_to_all | solution.py:68
  160.4 6.3 %all-to-all-start.3 = ((bf16[256,32,128]{2,1,0:T(8,128)(2,1)}), bf16[256,32,128]{2,1,0:T(8,128)(2,1)S(1)}, u32[]{:S(2)}, u32[]{:S(2)}) async-start(bf16[256,32,128]{2,1,0:T(8,128)(2,1)} %bitcast.18), calls=%async_computation.3 | async-start | bytes 4194304 | tf_op jit(solution)/shard_map/all_to_all | solution.py:80
  168.4 37.2 %while.24 = (s32[]{:T(128)}, bf16[4,64,32,128]{3,2,1,0:T(8,128)(2,1)}, f32[4,64]{1,0:T(4,128)S(1)}, bf16[4,64,32,128]{3,2,1,0:T(8,128)(2,1)}, s32[4,64]{1,0:T(4,...) while((s32[]{:T(128)}, bf16[4,64,32,128]{3,2,1,0:T(8,128)(2,1)}, ...), condition=%wide.region_7.9_spmd, body=%wide.region_4.8_spmd.sunk | while | flops 275516736 | bytes 38829112 | solution.py:72
  168.4 3.0 gather_fusion
  171.4 4.2 %fusion.60 = (f32[64,32]{1,0:T(8,128)S(1)}, f32[64,32,256]{2,1,0:T(8,128)S(1)}) fusion(bf16[64,256,128]{2,1,0:T(8,128)(2,1)} %gather_fusion, pred[64]{0:T(512)(128)(4,1)S(1)} %get-tuple-element.198, bf16[4,64,32,128]{3,2,1,0:T(8,128)(2,1)} %get-tuple-element.254, s32[]{:T(128)} %get-tuple-element.243), kind=kOutput, calls=%fused_computation.12.clone.1 | convolution fusion | flops 137361408 | bytes 6824512 | tf_op jit(solution)/shard_map/while/body/eval_jaxpr/bqe,bpe->bqp/dot_general | solution.py:51
  177.7 3.0 gather_fusion
  180.7 4.2 %fusion.60 = (f32[64,32]{1,0:T(8,128)S(1)}, f32[64,32,256]{2,1,0:T(8,128)S(1)}) fusion(bf16[64,256,128]{2,1,0:T(8,128)(2,1)} %gather_fusion, pred[64]{0:T(512)(128)(4,1)S(1)} %get-tuple-element.198, bf16[4,64,32,128]{3,2,1,0:T(8,128)(2,1)} %get-tuple-element.254, s32[]{:T(128)} %get-tuple-element.243), kind=kOutput, calls=%fused_computation.12.clone.1 | convolution fusion | flops 137361408 | bytes 6824512 | tf_op jit(solution)/shard_map/while/body/eval_jaxpr/bqe,bpe->bqp/dot_general | solution.py:51
  187.0 3.0 gather_fusion
  190.0 4.2 %fusion.60 = (f32[64,32]{1,0:T(8,128)S(1)}, f32[64,32,256]{2,1,0:T(8,128)S(1)}) fusion(bf16[64,256,128]{2,1,0:T(8,128)(2,1)} %gather_fusion, pred[64]{0:T(512)(128)(4,1)S(1)} %get-tuple-element.198, bf16[4,64,32,128]{3,2,1,0:T(8,128)(2,1)} %get-tuple-element.254, s32[]{:T(128)} %get-tuple-element.243), kind=kOutput, calls=%fused_computation.12.clone.1 | convolution fusion | flops 137361408 | bytes 6824512 | tf_op jit(solution)/shard_map/while/body/eval_jaxpr/bqe,bpe->bqp/dot_general | solution.py:51
  196.3 3.0 gather_fusion
  199.3 4.2 %fusion.60 = (f32[64,32]{1,0:T(8,128)S(1)}, f32[64,32,256]{2,1,0:T(8,128)S(1)}) fusion(bf16[64,256,128]{2,1,0:T(8,128)(2,1)} %gather_fusion, pred[64]{0:T(512)(128)(4,1)S(1)} %get-tuple-element.198, bf16[4,64,32,128]{3,2,1,0:T(8,128)(2,1)} %get-tuple-element.254, s32[]{:T(128)} %get-tuple-element.243), kind=kOutput, calls=%fused_computation.12.clone.1 | convolution fusion | flops 137361408 | bytes 6824512 | tf_op jit(solution)/shard_map/while/body/eval_jaxpr/bqe,bpe->bqp/dot_general | solution.py:51
  205.5 14.9 %all-to-all-done.3 = bf16[256,32,128]{2,1,0:T(8,128)(2,1)S(1)} async-done(((bf16[256,32,128]{2,1,0:T(8,128)(2,1)}), bf16[256,32,128]{2,1,0:T(8,128)(2,1)S(1)}, u32[]{:S(2)}, u32[]{:S(2)}) %all-to-all-start.3) | async-done | bytes 2097184 | tf_op jit(solution)/shard_map/all_to_all | solution.py:80
  220.4 7.3 %all-to-all-start.5 = ((bf16[256,32,128]{2,1,0:T(8,128)(2,1)}), bf16[256,32,128]{2,1,0:T(8,128)(2,1)}, u32[]{:S(2)}, u32[]{:S(2)}) async-start(bf16[256,32,128]{2,1,0:T(8,128)(2,1)} %bitcast.22), calls=%async_computation.5 | async-start | bytes 4194304 | tf_op jit(solution)/shard_map/all_to_all | solution.py:80
  229.7 50.9 %all-to-all-done.5 = bf16[256,32,128]{2,1,0:T(8,128)(2,1)} async-done(((bf16[256,32,128]{2,1,0:T(8,128)(2,1)}), bf16[256,32,128]{2,1,0:T(8,128)(2,1)}, u32[]{:S(2)}, u32[]{:S(2)}) %all-to-all-start.5) | async-done | bytes 2097184 | tf_op jit(solution)/shard_map/all_to_all | solution.py:80
  280.5 6.3 %all-to-all-start.4 = ((f32[256,1,2]{2,1,0:T(1,128)}), f32[256,1,2]{2,1,0:T(1,128)S(1)}, u32[]{:S(2)}, u32[]{:S(2)}) async-start(f32[256,1,2]{2,1,0:T(1,128)} %bitcast.19), calls=%async_computation.4 | async-start | bytes 262144 | tf_op jit(solution)/shard_map/all_to_all | solution.py:84
  289.9 9.1 %all-to-all-done.4 = f32[256,1,2]{2,1,0:T(1,128)S(1)} async-done(((f32[256,1,2]{2,1,0:T(1,128)}), f32[256,1,2]{2,1,0:T(1,128)S(1)}, u32[]{:S(2)}, u32[]{:S(2)}) %all-to-all-start.4) | async-done | bytes 2080 | tf_op jit(solution)/shard_map/all_to_all | solution.py:84
  (123 shorter events, 43.5 us)
Async XLA Ops:
  0.6 1.6 copy-start
  0.6 22.9 %copy-start.4 = (bf16[8,32,128]{2,1,0:T(8,128)(2,1)S(1)}, bf16[8,32,128]{2,1,0:T(8,128)(2,1)}, u32[]{:S(2)}) copy-start(bf16[8,32,128]{2,1,0:T(8,128)(2,1)} %param.12) | copy-start | bytes 196612
  8.9 26.7 %all-to-all-start.1 = ((bf16[256,1,2]{2,1,0:T(2,128)(2,1)}), bf16[256,1,2]{2,1,0:T(2,128)(2,1)S(1)}, u32[]{:S(2)}, u32[]{:S(2)}) async-start(bf16[256,1,2]{2,1,0:T(2,128)(2,1)} %convert_element_type.66), calls=%async_computation.1 | async-start | bytes 262144 | tf_op jit(solution)/shard_map/all_to_all | solution.py:43
  35.6 11.9 %copy-start.3 = (bf16[16,256,128]{2,1,0:T(8,128)(2,1)S(1)}, bf16[16,256,128]{2,1,0:T(8,128)(2,1)}, u32[]{:S(2)}) copy-start(bf16[16,256,128]{2,1,0:T(8,128)(2,1)} %param.13) | copy-start | bytes 3145732
  35.6 64.7 %all-to-all-start.2 = ((bf16[256,32,128]{2,1,0:T(8,128)(2,1)}), bf16[256,32,128]{2,1,0:T(8,128)(2,1)}, u32[]{:S(2)}, u32[]{:S(2)}) async-start(bf16[256,32,128]{2,1,0:T(8,128)(2,1)} %get-tuple-element.120), calls=%async_computation.2 | async-start | bytes 4194304 | tf_op jit(solution)/shard_map/all_to_all | solution.py:68
  100.3 60.1 %all-to-all-start = ((bf16[256,32,128]{2,1,0:T(8,128)(2,1)}), bf16[256,32,128]{2,1,0:T(8,128)(2,1)}, u32[]{:S(2)}, u32[]{:S(2)}) async-start(bf16[256,32,128]{2,1,0:T(8,128)(2,1)} %get-tuple-element.119), calls=%async_computation | async-start | bytes 4194304 | tf_op jit(solution)/shard_map/all_to_all | solution.py:68
  112.2 4.2 %copy-start.1 = (bf16[64,256,128]{2,1,0:T(8,128)(2,1)S(1)}, bf16[64,256,128]{2,1,0:T(8,128)(2,1)}, u32[]{:S(2)}) copy-start(bf16[64,256,128]{2,1,0:T(8,128)(2,1)} %gather_fusion.1) | copy-start | bytes 12582916 | tf_op jit(solution)/shard_map/while
  121.5 4.2 %copy-start.1 = (bf16[64,256,128]{2,1,0:T(8,128)(2,1)S(1)}, bf16[64,256,128]{2,1,0:T(8,128)(2,1)}, u32[]{:S(2)}) copy-start(bf16[64,256,128]{2,1,0:T(8,128)(2,1)} %gather_fusion.1) | copy-start | bytes 12582916 | tf_op jit(solution)/shard_map/while
  130.8 4.2 %copy-start.1 = (bf16[64,256,128]{2,1,0:T(8,128)(2,1)S(1)}, bf16[64,256,128]{2,1,0:T(8,128)(2,1)}, u32[]{:S(2)}) copy-start(bf16[64,256,128]{2,1,0:T(8,128)(2,1)} %gather_fusion.1) | copy-start | bytes 12582916 | tf_op jit(solution)/shard_map/while
  140.1 4.2 %copy-start.1 = (bf16[64,256,128]{2,1,0:T(8,128)(2,1)S(1)}, bf16[64,256,128]{2,1,0:T(8,128)(2,1)}, u32[]{:S(2)}) copy-start(bf16[64,256,128]{2,1,0:T(8,128)(2,1)} %gather_fusion.1) | copy-start | bytes 12582916 | tf_op jit(solution)/shard_map/while
  160.4 60.0 %all-to-all-start.3 = ((bf16[256,32,128]{2,1,0:T(8,128)(2,1)}), bf16[256,32,128]{2,1,0:T(8,128)(2,1)S(1)}, u32[]{:S(2)}, u32[]{:S(2)}) async-start(bf16[256,32,128]{2,1,0:T(8,128)(2,1)} %bitcast.18), calls=%async_computation.3 | async-start | bytes 4194304 | tf_op jit(solution)/shard_map/all_to_all | solution.py:80
  171.4 4.2 %copy-start.2 = (bf16[64,256,128]{2,1,0:T(8,128)(2,1)S(1)}, bf16[64,256,128]{2,1,0:T(8,128)(2,1)}, u32[]{:S(2)}) copy-start(bf16[64,256,128]{2,1,0:T(8,128)(2,1)} %gather_fusion) | copy-start | bytes 12582916 | tf_op jit(solution)/shard_map/while
  180.7 4.2 %copy-start.2 = (bf16[64,256,128]{2,1,0:T(8,128)(2,1)S(1)}, bf16[64,256,128]{2,1,0:T(8,128)(2,1)}, u32[]{:S(2)}) copy-start(bf16[64,256,128]{2,1,0:T(8,128)(2,1)} %gather_fusion) | copy-start | bytes 12582916 | tf_op jit(solution)/shard_map/while
  190.0 4.2 %copy-start.2 = (bf16[64,256,128]{2,1,0:T(8,128)(2,1)S(1)}, bf16[64,256,128]{2,1,0:T(8,128)(2,1)}, u32[]{:S(2)}) copy-start(bf16[64,256,128]{2,1,0:T(8,128)(2,1)} %gather_fusion) | copy-start | bytes 12582916 | tf_op jit(solution)/shard_map/while
  199.3 4.2 %copy-start.2 = (bf16[64,256,128]{2,1,0:T(8,128)(2,1)S(1)}, bf16[64,256,128]{2,1,0:T(8,128)(2,1)}, u32[]{:S(2)}) copy-start(bf16[64,256,128]{2,1,0:T(8,128)(2,1)} %gather_fusion) | copy-start | bytes 12582916 | tf_op jit(solution)/shard_map/while
  220.4 60.1 %all-to-all-start.5 = ((bf16[256,32,128]{2,1,0:T(8,128)(2,1)}), bf16[256,32,128]{2,1,0:T(8,128)(2,1)}, u32[]{:S(2)}, u32[]{:S(2)}) async-start(bf16[256,32,128]{2,1,0:T(8,128)(2,1)} %bitcast.22), calls=%async_computation.5 | async-start | bytes 4194304 | tf_op jit(solution)/shard_map/all_to_all | solution.py:80
  280.5 18.4 %all-to-all-start.4 = ((f32[256,1,2]{2,1,0:T(1,128)}), f32[256,1,2]{2,1,0:T(1,128)S(1)}, u32[]{:S(2)}, u32[]{:S(2)}) async-start(f32[256,1,2]{2,1,0:T(1,128)} %bitcast.19), calls=%async_computation.4 | async-start | bytes 262144 | tf_op jit(solution)/shard_map/all_to_all | solution.py:84
  289.2 12.8 %copy-start.5 = (s32[8,16]{1,0:T(8,128)S(1)}, s32[8,16]{1,0:T(8,128)}, u32[]{:S(2)}) copy-start(s32[8,16]{1,0:T(8,128)} %param.14) | copy-start | bytes 1540

commit v6 on v5

--- a/solution.py
+++ b/solution.py
@@ -40,8 +40,15 @@
     both_axes = ("group", "dev")
     outgoing = outgoing.reshape(device_total, slot_cap, query_len, feat_width)
     labels = labels.reshape(device_total, slot_cap)
-    tags = lax.all_to_all(labels, both_axes, split_axis=0, concat_axis=0, tiled=True)
-    tags = tags.astype(jnp.int32)
+    me = lax.axis_index("group") * dev_count + lax.axis_index("dev")
+    mine = (jnp.arange(device_total) == me)[None, :, None]
+    tags = lax.psum_scatter(
+        jnp.where(mine, labels[:, None, :], 0).astype(jnp.bfloat16),
+        both_axes,
+        scatter_dimension=0,
+        tiled=True,
+    )
+    tags = tags.reshape(device_total, slot_cap).astype(jnp.int32)
     block_rows = 64
 
     def score_block(inputs):
@@ -81,7 +88,9 @@
         scores.append(score.reshape(device_total))
     scores = jnp.stack(scores, axis=1)
     scores, returned[-1] = lax.optimization_barrier((scores, returned[-1]))
-    scores_flat = lax.all_to_all(scores, both_axes, split_axis=0, concat_axis=0, tiled=True)
+    scores_flat = lax.psum_scatter(
+        jnp.where(mine, scores[:, None, :], 0.0), both_axes, scatter_dimension=0, tiled=True
+    )
     pair_score = jnp.take(scores_flat.reshape(slot_total), slot_index, axis=0).reshape(
         query_count, list_len
     )

time: 308 us -> 2850 us (9.25)
  waiting for transfers between devices: 143 us -> 2640 us
    reduce_scatter x0 -> x2, waiting for transfers between devices: none -> 2570 us  [the longest x1 1290 us: local(): lax.psum_scatter(jnp.where(mine, labels[:, None, :], 0).astype(jnp.bfloat...]
    all_to_all x2, waiting for transfers between devices: 65 us -> 13.9 us  [local(): lax.all_to_all(outgoing[:, slot], both_axes, split_axis=0, concat_axis=0,...]
  transfers between devices with their start and end apart: 6 -> 6, of which waited for: 6 -> 5; matrix products, arithmetic and copies ran while one was open for 31% -> 4% of each run, Pallas kernels for 0% -> 0%
where the time goes in v6:
time: 2850 us; the launch traced here: 2840 us
  waiting for transfers between devices  2640 us (93%)
  starting transfers between devices  53.6 us (2%)
  matrix products  49.2 us (2%)
  local copies, waits for them, and re-layouts  48.9 us (2%)
  other arithmetic  28.7 us (1%)
    reduce_scatter x1, waiting for transfers between devices, local(): lax.psum_scatter(jnp.where(mine, labels[:, None, :], 0).astype(jnp.bfloat...  1290 us
    reduce_scatter x1, waiting for transfers between devices, local(): lax.psum_scatter(jnp.where(mine, scores[:, None, :], 0.0), both_axes, sca...  1280 us
    all_to_all x2, waiting for transfers between devices, local(): lax.all_to_all(pulled, both_axes, split_axis=0, concat_axis=0, tiled=True)  62.5 us
  transfers between devices with their start and end apart: 6, of which 5 were waited for; matrix products, arithmetic and copies ran while one was open for 4% of the time, Pallas kernels for 0%

profile of v6, /device:TPU:8, one launch (start us, length us, event | category | flops | bytes accessed | tf_op | source)
XLA Modules:
  0.0 2837.8 jit_solution(3681526595202745279)
XLA Ops:
  13.2 3.4 gather_fusion.3
  19.3 2.7 slice_bitcast_fusion.1
  21.9 15.6 all-to-all-start.1
  37.6 3.3 gather_fusion.4
  41.2 6.0 broadcast_select_fusion.19
  49.8 1286.0 %reduce-scatter.3.cloned.1.call-done = bf16[1,256,2]{2,1,0:T(8,128)(2,1)} async-done(((bf16[256,256,2]{2,1,0:T(8,128)(2,1)}), bf16[1,256,2]{2,1,0:T(8,128)(2,1)}) %reduce-scatter.3.cloned.1.call-update) | async-done | bytes 1040 | tf_op jit(solution)/shard_map/reduce_scatter | solution.py:45
  1337.0 24.3 all-to-all-start
  1363.0 37.3 %while.25 = (s32[]{:T(128)}, bf16[4,64,32,128]{3,2,1,0:T(8,128)(2,1)}, f32[4,64]{1,0:T(4,128)S(1)}, bf16[4,64,32,128]{3,2,1,0:T(8,128)(2,1)}, s32[4,64]{1,0:T(4,...) while((s32[]{:T(128)}, bf16[4,64,32,128]{3,2,1,0:T(8,128)(2,1)}, ...), condition=%wide.region_12.14_spmd, body=%wide.region_9.13_spmd.sunk | while | flops 275516736 | bytes 38829112 | solution.py:79
  1363.0 3.0 gather_fusion.1
  1366.1 4.2 fusion.62
  1372.4 3.0 gather_fusion.1
  1375.4 4.2 fusion.62
  1381.7 3.0 gather_fusion.1
  1384.7 4.2 fusion.62
  1391.0 3.0 gather_fusion.1
  1394.0 4.2 fusion.62
  1400.3 13.9 all-to-all-done
  1414.2 6.3 all-to-all-start.2
  1422.2 37.1 %while.24 = (s32[]{:T(128)}, bf16[4,64,32,128]{3,2,1,0:T(8,128)(2,1)}, f32[4,64]{1,0:T(4,128)S(1)}, bf16[4,64,32,128]{3,2,1,0:T(8,128)(2,1)}, s32[4,64]{1,0:T(4,...) while((s32[]{:T(128)}, bf16[4,64,32,128]{3,2,1,0:T(8,128)(2,1)}, ...), condition=%wide.region_8.10_spmd, body=%wide.region_5.9_spmd.sunk | while | flops 275516736 | bytes 38829112 | solution.py:79
  1422.3 3.0 gather_fusion
  1425.3 4.2 fusion.60
  1431.6 3.0 gather_fusion
  1434.6 4.2 fusion.60
  1440.8 3.0 gather_fusion
  1443.8 4.2 fusion.60
  1450.1 3.0 gather_fusion
  1453.1 4.2 fusion.60
  1459.4 14.9 all-to-all-done.2
  1474.2 7.3 all-to-all-start.3
  1482.1 11.4 broadcast_select_fusion.18
  1494.3 47.7 %all-to-all-done.3 = bf16[256,32,128]{2,1,0:T(8,128)(2,1)} async-done(((bf16[256,32,128]{2,1,0:T(8,128)(2,1)}), bf16[256,32,128]{2,1,0:T(8,128)(2,1)}, u32[]{:S(2)}, u32[]{:S(2)}) %all-to-all-start.3) | async-done | bytes 2097184 | tf_op jit(solution)/shard_map/all_to_all | solution.py:87
  1545.1 1280.4 %reduce-scatter.5.cloned.1.call-done = f32[1,256,2]{2,1,0:T(8,128)} async-done(((f32[256,256,2]{2,1,0:T(8,128)}), f32[1,256,2]{2,1,0:T(8,128)}) %reduce-scatter.5.cloned.1.call-update) | async-done | bytes 2064 | tf_op jit(solution)/shard_map/reduce_scatter | solution.py:91
  (128 shorter events, 42.7 us)
Async XLA Ops:
  7.2 1.6 copy-start
  21.9 1315.1 %all-to-all-start.1 = ((bf16[256,32,128]{2,1,0:T(8,128)(2,1)}), bf16[256,32,128]{2,1,0:T(8,128)(2,1)}, u32[]{:S(2)}, u32[]{:S(2)}) async-start(bf16[256,32,128]{2,1,0:T(8,128)(2,1)} %get-tuple-element.120), calls=%async_computation.2 | async-start | bytes 4194304 | tf_op jit(solution)/shard_map/all_to_all | solution.py:75
  37.6 1298.3 %reduce-scatter.3.cloned.1.call-start = ((), (), s32[]{:S(2)}) async-start(), calls=%async_computation.6 | async-start | bytes 16842752 | tf_op jit(solution)/shard_map/reduce_scatter | solution.py:45
  47.2 1.2 copy-start.4
  1337.0 77.2 %all-to-all-start = ((bf16[256,32,128]{2,1,0:T(8,128)(2,1)}), bf16[256,32,128]{2,1,0:T(8,128)(2,1)}, u32[]{:S(2)}, u32[]{:S(2)}) async-start(bf16[256,32,128]{2,1,0:T(8,128)(2,1)} %get-tuple-element.119), calls=%async_computation | async-start | bytes 4194304 | tf_op jit(solution)/shard_map/all_to_all | solution.py:75
  1366.0 4.2 copy-start.2
  1375.4 4.2 copy-start.2
  1384.7 4.2 copy-start.2
  1394.0 4.2 copy-start.2
  1414.2 60.0 %all-to-all-start.2 = ((bf16[256,32,128]{2,1,0:T(8,128)(2,1)}), bf16[256,32,128]{2,1,0:T(8,128)(2,1)S(1)}, u32[]{:S(2)}, u32[]{:S(2)}) async-start(bf16[256,32,128]{2,1,0:T(8,128)(2,1)} %bitcast.19), calls=%async_computation.3 | async-start | bytes 4194304 | tf_op jit(solution)/shard_map/all_to_all | solution.py:87
  1425.3 4.2 copy-start.3
  1434.6 4.2 copy-start.3
  1443.8 4.2 copy-start.3
  1453.1 4.2 copy-start.3
  1474.2 67.8 %all-to-all-start.3 = ((bf16[256,32,128]{2,1,0:T(8,128)(2,1)}), bf16[256,32,128]{2,1,0:T(8,128)(2,1)}, u32[]{:S(2)}, u32[]{:S(2)}) async-start(bf16[256,32,128]{2,1,0:T(8,128)(2,1)} %bitcast.22), calls=%async_computation.5 | async-start | bytes 4194304 | tf_op jit(solution)/shard_map/all_to_all | solution.py:87
  1481.5 1344.0 %reduce-scatter.5.cloned.1.call-start = ((), (), s32[]{:S(2)}) async-start(), calls=%async_computation.7 | async-start | bytes 33685504 | tf_op jit(solution)/shard_map/reduce_scatter | solution.py:91
  1544.3 1283.5 %copy-start.6 = (s32[8,16]{1,0:T(8,128)S(1)}, s32[8,16]{1,0:T(8,128)}, u32[]{:S(2)}) copy-start(s32[8,16]{1,0:T(8,128)} %param.14) | copy-start | bytes 1540
  1544.4 1286.6 %copy-start.1 = (s32[4096]{0:T(1024)S(1)}, s32[4096]{0:T(1024)}, u32[]{:S(2)}) copy-start(s32[4096]{0:T(1024)} %param.15) | copy-start | bytes 49156
  1544.4 1284.3 %copy-start.5 = (bf16[8,32,128]{2,1,0:T(8,128)(2,1)S(1)}, bf16[8,32,128]{2,1,0:T(8,128)(2,1)}, u32[]{:S(2)}) copy-start(bf16[8,32,128]{2,1,0:T(8,128)(2,1)} %param.12) | copy-start | bytes 196612
Sparse Core Ops, SparseCore 0:
  47.4 1288.4 reduce-scatter.2
  1493.6 1331.8 reduce-scatter.4

commit v7 on v5

--- a/solution.py
+++ b/solution.py
@@ -1,7 +1,13 @@
+import functools
+
 import jax
 import jax.numpy as jnp
 from jax import lax
+from jax.experimental import pallas as pl
+from jax.experimental.pallas import tpu as pltpu
 from jax.sharding import PartitionSpec as P
+
+MESH = pl.DeviceIdType.MESH
 
 SOFTNESS = 0.02
 EPSILON = 1e-06
@@ -11,6 +17,69 @@
     floats = values.astype(jnp.float32)
     scale = lax.rsqrt(jnp.sum(floats * floats, axis=-1, keepdims=True) + EPSILON)
     return (floats * scale, scale)
+
+
+def exchange_kernel(dev_count, rows_ref, out_ref, landing, send_sem, recv_sem):
+    total = rows_ref.shape[0]
+    me = lax.axis_index("group") * dev_count + lax.axis_index("dev")
+
+    def peer_id(step):
+        peer = lax.rem(me + step, total)
+        return peer, (lax.div(peer, dev_count), lax.rem(peer, dev_count))
+
+    barrier = pltpu.get_barrier_semaphore()
+
+    def greet(step, carry):
+        pl.semaphore_signal(barrier, inc=1, device_id=peer_id(step)[1], device_id_type=MESH)
+        return carry
+
+    lax.fori_loop(1, total, greet, 0)
+    pl.semaphore_wait(barrier, total - 1)
+
+    def send(step, carry):
+        peer, device = peer_id(step)
+        pltpu.make_async_remote_copy(
+            src_ref=rows_ref.at[pl.ds(peer, 1)],
+            dst_ref=landing.at[pl.ds(me, 1)],
+            send_sem=send_sem,
+            recv_sem=recv_sem,
+            device_id=device,
+            device_id_type=MESH,
+        ).start()
+        return carry
+
+    lax.fori_loop(1, total, send, 0)
+    landing[pl.ds(me, 1), :] = rows_ref[pl.ds(me, 1), :]
+    every = pltpu.make_async_remote_copy(
+        src_ref=rows_ref.at[pl.ds(0, total - 1)],
+        dst_ref=landing.at[pl.ds(0, total - 1)],
+        send_sem=send_sem,
+        recv_sem=recv_sem,
+        device_id=peer_id(1)[1],
+        device_id_type=MESH,
+    )
+    every.wait_send()
+    every.wait_recv()
+    out_ref[...] = landing[...]
+
+
+def exchange(rows, dev_count, tag):
+    return pl.pallas_call(
+        functools.partial(exchange_kernel, dev_count),
+        out_shape=jax.ShapeDtypeStruct(rows.shape, rows.dtype),
+        in_specs=[pl.BlockSpec(memory_space=pltpu.VMEM)],
+        out_specs=pl.BlockSpec(memory_space=pltpu.VMEM),
+        scratch_shapes=[
+            pltpu.VMEM(rows.shape, rows.dtype),
+            pltpu.SemaphoreType.DMA(()),
+            pltpu.SemaphoreType.DMA(()),
+        ],
+        compiler_params=pltpu.CompilerParams(collective_id=tag, has_side_effects=True),
+    )(rows)
+
+
+def widen(small, feat_width):
+    return jnp.pad(small.astype(jnp.float32), ((0, 0), (0, feat_width - small.shape[1])))
 
 
 def local(queries, passages, candidates, location):
@@ -40,8 +109,7 @@
     both_axes = ("group", "dev")
     outgoing = outgoing.reshape(device_total, slot_cap, query_len, feat_width)
     labels = labels.reshape(device_total, slot_cap)
-    tags = lax.all_to_all(labels, both_axes, split_axis=0, concat_axis=0, tiled=True)
-    tags = tags.astype(jnp.int32)
+    tags = exchange(widen(labels, feat_width), dev_count, 0)[:, :slot_cap].astype(jnp.int32)
     block_rows = 64
 
     def score_block(inputs):
@@ -81,7 +149,7 @@
         scores.append(score.reshape(device_total))
     scores = jnp.stack(scores, axis=1)
     scores, returned[-1] = lax.optimization_barrier((scores, returned[-1]))
-    scores_flat = lax.all_to_all(scores, both_axes, split_axis=0, concat_axis=0, tiled=True)
+    scores_flat = exchange(widen(scores, feat_width), dev_count, 1)[:, :slot_cap]
     pair_score = jnp.take(scores_flat.reshape(slot_total), slot_index, axis=0).reshape(
         query_count, list_len
     )

time: 308 us -> 288 us (0.935)
  waiting for transfers between devices: 143 us -> 29.8 us
  Pallas kernels: 0 us -> 108 us
  starting transfers between devices: 53.6 us -> 35.7 us
    pallas_call x0 -> x2, Pallas kernels: none -> 108 us  [exchange(): pl.pallas_call(functools.partial(exchange_kernel, dev_count), out_shape=j...]
    all_to_all x2, waiting for transfers between devices: 65.7 us -> 14.9 us  [local(): lax.all_to_all(pulled, both_axes, split_axis=0, concat_axis=0, tiled=True)]
    all_to_all x2, waiting for transfers between devices: 65 us -> 14.9 us  [local(): lax.all_to_all(outgoing[:, slot], both_axes, split_axis=0, concat_axis=0,...]
    all_to_all x2 -> x0, starting transfers between devices: 20.9 us -> none  [the longest x1 14.6 us: local(): lax.all_to_all(labels, both_axes, split_axis=0, concat_axis=0, tiled=True)]
    all_to_all x2 -> x0, waiting for transfers between devices: 11.9 us -> none  [the longest x1 9.07 us: local(): lax.all_to_all(scores, both_axes, split_axis=0, concat_axis=0, tiled=True)]
  transfers between devices with their start and end apart: 6 -> 4, of which waited for: 6 -> 2; matrix products, arithmetic and copies ran while one was open for 31% -> 31% of each run, Pallas kernels for 0% -> 38%
where the time goes in v7:
time: 288 us; the launch traced here: 285 us
  Pallas kernels  108 us (38%)
  local copies, waits for them, and re-layouts  49.8 us (17%)
  matrix products  49 us (17%)
  starting transfers between devices  35.7 us (12%)
  waiting for transfers between devices  29.8 us (10%)
  other arithmetic  12 us (4%)
    pallas_call x2, Pallas kernels, exchange(): pl.pallas_call(functools.partial(exchange_kernel, dev_count), out_shape=j...  108 us
    dot_general x8, matrix products, score_block(): jnp.einsum('bqe,bpe->bqp', query_block, passage_block, preferred_element_...  33.2 us
    gather x8, local copies, waits for them, and re-layouts, score_block(): passage_block = jnp.take(passage_unit, tag_block, axis=0)  24.1 us
    all_to_all x2, starting transfers between devices, local(): lax.all_to_all(outgoing[:, slot], both_axes, split_axis=0, concat_axis=0,...  22.1 us
    dot_general x8, matrix products, score_block(): jnp.einsum('bqp,bpe->bqe', attention, passage_block, preferred_element_ty...  15.4 us
    all_to_all x2, waiting for transfers between devices, local(): lax.all_to_all(outgoing[:, slot], both_axes, split_axis=0, concat_axis=0,...  14.9 us
    all_to_all x2, waiting for transfers between devices, local(): lax.all_to_all(pulled, both_axes, split_axis=0, concat_axis=0, tiled=True)  14.9 us
    all_to_all x2, starting transfers between devices, local(): lax.all_to_all(pulled, both_axes, split_axis=0, concat_axis=0, tiled=True)  13.6 us
  transfers between devices with their start and end apart: 4, of which 2 were waited for; matrix products, arithmetic and copies ran while one was open for 31% of the time, Pallas kernels for 38%

profile of v7, /device:TPU:8, one launch (start us, length us, event | category | flops | bytes accessed | tf_op | source)
XLA Modules:
  0.0 285.0 jit_solution(6187917636156239933)
XLA Ops:
  6.7 3.4 %gather_fusion.3 = bf16[512,32,128]{2,1,0:T(8,128)(2,1)} fusion(bf16[8,32,128]{2,1,0:T(8,128)(2,1)S(1)} %fusion.39, s32[1024]{0:T(1024)S(1)} %pad_clamp_fusion.5), kind=kCustom, calls=%fused_computation.5 | custom fusion | bytes 8390656 | tf_op jit(solution)/shard_map/jit(_take)/gather | solution.py:107
  10.1 2.6 broadcast_select_fusion.18
  12.7 2.7 slice_bitcast_fusion.1
  15.4 15.6 %all-to-all-start.1 = ((bf16[256,32,128]{2,1,0:T(8,128)(2,1)}), bf16[256,32,128]{2,1,0:T(8,128)(2,1)}, u32[]{:S(2)}, u32[]{:S(2)}) async-start(bf16[256,32,128]{2,1,0:T(8,128)(2,1)} %get-tuple-element.120), calls=%async_computation.1 | async-start | bytes 4194304 | tf_op jit(solution)/shard_map/all_to_all | solution.py:136
  31.1 3.3 %gather_fusion.4 = s32[512]{0:T(512)S(1)} fusion(s32[128]{0:T(128)S(1)} %and_select_fusion.1, s32[1024]{0:T(1024)S(1)} %pad_clamp_fusion.4), kind=kCustom, calls=%fused_computation.6 | custom fusion | bytes 6144 | tf_op jit(solution)/shard_map/jit(_take)/gather | solution.py:108
  35.3 52.3 %shard_map.59 = f32[256,128]{1,0:T(8,128)} custom-call(f32[256,128]{1,0:T(8,128)} %pad_convert_fusion.rows_ref), custom_call_target="tpu_custom_call" | custom-call | tf_op jit(solution)/shard_map/pallas_call | solution.py:67
  90.2 6.5 %all-to-all-start = ((bf16[256,32,128]{2,1,0:T(8,128)(2,1)}), bf16[256,32,128]{2,1,0:T(8,128)(2,1)S(1)}, u32[]{:S(2)}, u32[]{:S(2)}) async-start(bf16[256,32,128]{2,1,0:T(8,128)(2,1)} %get-tuple-element.119), calls=%async_computation | async-start | bytes 4194304 | tf_op jit(solution)/shard_map/all_to_all | solution.py:136
  98.5 37.2 %while.25 = (s32[]{:T(128)}, bf16[4,64,32,128]{3,2,1,0:T(8,128)(2,1)}, f32[4,64]{1,0:T(4,128)S(1)}, bf16[4,64,32,128]{3,2,1,0:T(8,128)(2,1)}, s32[4,64]{1,0:T(4,...) while((s32[]{:T(128)}, bf16[4,64,32,128]{3,2,1,0:T(8,128)(2,1)}, ...), condition=%wide.region_11.13_spmd, body=%wide.region_8.12_spmd.sunk | while | flops 275516736 | bytes 38829112 | solution.py:140
  98.5 3.0 %gather_fusion.1 = bf16[64,256,128]{2,1,0:T(8,128)(2,1)} fusion(bf16[16,256,128]{2,1,0:T(8,128)(2,1)S(1)} %get-tuple-element.232, s32[1024]{0:T(1024)S(1)} %pad_clamp_fusion.10), kind=kCustom, calls=%fused_computation.2.clone.clone.1 | custom fusion | bytes 8388864 | tf_op jit(solution)/shard_map/while/body/eval_jaxpr/jit(_take)/gather | solution.py:117
  101.5 4.2 %fusion.62 = (f32[64,32]{1,0:T(8,128)S(1)}, f32[64,32,256]{2,1,0:T(8,128)S(1)}) fusion(bf16[64,256,128]{2,1,0:T(8,128)(2,1)} %gather_fusion.1, pred[64]{0:T(512)(128)(4,1)S(1)} %get-tuple-element.208, bf16[4,64,32,128]{3,2,1,0:T(8,128)(2,1)} %get-tuple-element.230, s32[]{:T(128)} %get-tuple-element.219), kind=kOutput, calls=%fused_computation.35.clone.1 | convolution fusion | flops 137361408 | bytes 6824512 | tf_op jit(solution)/shard_map/while/body/eval_jaxpr/bqe,bpe->bqp/dot_general | solution.py:119
  107.8 3.0 %gather_fusion.1 = bf16[64,256,128]{2,1,0:T(8,128)(2,1)} fusion(bf16[16,256,128]{2,1,0:T(8,128)(2,1)S(1)} %get-tuple-element.232, s32[1024]{0:T(1024)S(1)} %pad_clamp_fusion.10), kind=kCustom, calls=%fused_computation.2.clone.clone.1 | custom fusion | bytes 8388864 | tf_op jit(solution)/shard_map/while/body/eval_jaxpr/jit(_take)/gather | solution.py:117
  110.8 4.2 %fusion.62 = (f32[64,32]{1,0:T(8,128)S(1)}, f32[64,32,256]{2,1,0:T(8,128)S(1)}) fusion(bf16[64,256,128]{2,1,0:T(8,128)(2,1)} %gather_fusion.1, pred[64]{0:T(512)(128)(4,1)S(1)} %get-tuple-element.208, bf16[4,64,32,128]{3,2,1,0:T(8,128)(2,1)} %get-tuple-element.230, s32[]{:T(128)} %get-tuple-element.219), kind=kOutput, calls=%fused_computation.35.clone.1 | convolution fusion | flops 137361408 | bytes 6824512 | tf_op jit(solution)/shard_map/while/body/eval_jaxpr/bqe,bpe->bqp/dot_general | solution.py:119
  115.0 1.9 fusion.63
  117.1 3.0 %gather_fusion.1 = bf16[64,256,128]{2,1,0:T(8,128)(2,1)} fusion(bf16[16,256,128]{2,1,0:T(8,128)(2,1)S(1)} %get-tuple-element.232, s32[1024]{0:T(1024)S(1)} %pad_clamp_fusion.10), kind=kCustom, calls=%fused_computation.2.clone.clone.1 | custom fusion | bytes 8388864 | tf_op jit(solution)/shard_map/while/body/eval_jaxpr/jit(_take)/gather | solution.py:117
  120.1 4.2 %fusion.62 = (f32[64,32]{1,0:T(8,128)S(1)}, f32[64,32,256]{2,1,0:T(8,128)S(1)}) fusion(bf16[64,256,128]{2,1,0:T(8,128)(2,1)} %gather_fusion.1, pred[64]{0:T(512)(128)(4,1)S(1)} %get-tuple-element.208, bf16[4,64,32,128]{3,2,1,0:T(8,128)(2,1)} %get-tuple-element.230, s32[]{:T(128)} %get-tuple-element.219), kind=kOutput, calls=%fused_computation.35.clone.1 | convolution fusion | flops 137361408 | bytes 6824512 | tf_op jit(solution)/shard_map/while/body/eval_jaxpr/bqe,bpe->bqp/dot_general | solution.py:119
  126.4 3.0 %gather_fusion.1 = bf16[64,256,128]{2,1,0:T(8,128)(2,1)} fusion(bf16[16,256,128]{2,1,0:T(8,128)(2,1)S(1)} %get-tuple-element.232, s32[1024]{0:T(1024)S(1)} %pad_clamp_fusion.10), kind=kCustom, calls=%fused_computation.2.clone.clone.1 | custom fusion | bytes 8388864 | tf_op jit(solution)/shard_map/while/body/eval_jaxpr/jit(_take)/gather | solution.py:117
  129.4 4.2 %fusion.62 = (f32[64,32]{1,0:T(8,128)S(1)}, f32[64,32,256]{2,1,0:T(8,128)S(1)}) fusion(bf16[64,256,128]{2,1,0:T(8,128)(2,1)} %gather_fusion.1, pred[64]{0:T(512)(128)(4,1)S(1)} %get-tuple-element.208, bf16[4,64,32,128]{3,2,1,0:T(8,128)(2,1)} %get-tuple-element.230, s32[]{:T(128)} %get-tuple-element.219), kind=kOutput, calls=%fused_computation.35.clone.1 | convolution fusion | flops 137361408 | bytes 6824512 | tf_op jit(solution)/shard_map/while/body/eval_jaxpr/bqe,bpe->bqp/dot_general | solution.py:119
  135.6 14.9 %all-to-all-done = bf16[256,32,128]{2,1,0:T(8,128)(2,1)S(1)} async-done(((bf16[256,32,128]{2,1,0:T(8,128)(2,1)}), bf16[256,32,128]{2,1,0:T(8,128)(2,1)S(1)}, u32[]{:S(2)}, u32[]{:S(2)}) %all-to-all-start) | async-done | bytes 2097184 | tf_op jit(solution)/shard_map/all_to_all | solution.py:136
  151.9 6.3 %all-to-all-start.2 = ((bf16[256,32,128]{2,1,0:T(8,128)(2,1)}), bf16[256,32,128]{2,1,0:T(8,128)(2,1)S(1)}, u32[]{:S(2)}, u32[]{:S(2)}) async-start(bf16[256,32,128]{2,1,0:T(8,128)(2,1)} %bitcast.17), calls=%async_computation.2 | async-start | bytes 4194304 | tf_op jit(solution)/shard_map/all_to_all | solution.py:148
  159.8 37.1 %while.24 = (s32[]{:T(128)}, bf16[4,64,32,128]{3,2,1,0:T(8,128)(2,1)}, f32[4,64]{1,0:T(4,128)S(1)}, bf16[4,64,32,128]{3,2,1,0:T(8,128)(2,1)}, s32[4,64]{1,0:T(4,...) while((s32[]{:T(128)}, bf16[4,64,32,128]{3,2,1,0:T(8,128)(2,1)}, ...), condition=%wide.region_7.9_spmd, body=%wide.region_4.8_spmd.sunk | while | flops 275516736 | bytes 38829112 | solution.py:140
  159.9 3.0 %gather_fusion = bf16[64,256,128]{2,1,0:T(8,128)(2,1)} fusion(bf16[16,256,128]{2,1,0:T(8,128)(2,1)S(1)} %get-tuple-element.256, s32[1024]{0:T(1024)S(1)} %pad_clamp_fusion.9), kind=kCustom, calls=%fused_computation.clone.clone.1 | custom fusion | bytes 8388864 | tf_op jit(solution)/shard_map/while/body/eval_jaxpr/jit(_take)/gather | solution.py:117
  162.9 4.2 %fusion.60 = (f32[64,32]{1,0:T(8,128)S(1)}, f32[64,32,256]{2,1,0:T(8,128)S(1)}) fusion(bf16[64,256,128]{2,1,0:T(8,128)(2,1)} %gather_fusion, pred[64]{0:T(512)(128)(4,1)S(1)} %get-tuple-element.198, bf16[4,64,32,128]{3,2,1,0:T(8,128)(2,1)} %get-tuple-element.254, s32[]{:T(128)} %get-tuple-element.243), kind=kOutput, calls=%fused_computation.12.clone.1 | convolution fusion | flops 137361408 | bytes 6824512 | tf_op jit(solution)/shard_map/while/body/eval_jaxpr/bqe,bpe->bqp/dot_general | solution.py:119
  169.1 3.0 %gather_fusion = bf16[64,256,128]{2,1,0:T(8,128)(2,1)} fusion(bf16[16,256,128]{2,1,0:T(8,128)(2,1)S(1)} %get-tuple-element.256, s32[1024]{0:T(1024)S(1)} %pad_clamp_fusion.9), kind=kCustom, calls=%fused_computation.clone.clone.1 | custom fusion | bytes 8388864 | tf_op jit(solution)/shard_map/while/body/eval_jaxpr/jit(_take)/gather | solution.py:117
  172.2 4.2 %fusion.60 = (f32[64,32]{1,0:T(8,128)S(1)}, f32[64,32,256]{2,1,0:T(8,128)S(1)}) fusion(bf16[64,256,128]{2,1,0:T(8,128)(2,1)} %gather_fusion, pred[64]{0:T(512)(128)(4,1)S(1)} %get-tuple-element.198, bf16[4,64,32,128]{3,2,1,0:T(8,128)(2,1)} %get-tuple-element.254, s32[]{:T(128)} %get-tuple-element.243), kind=kOutput, calls=%fused_computation.12.clone.1 | convolution fusion | flops 137361408 | bytes 6824512 | tf_op jit(solution)/shard_map/while/body/eval_jaxpr/bqe,bpe->bqp/dot_general | solution.py:119
  178.4 3.0 %gather_fusion = bf16[64,256,128]{2,1,0:T(8,128)(2,1)} fusion(bf16[16,256,128]{2,1,0:T(8,128)(2,1)S(1)} %get-tuple-element.256, s32[1024]{0:T(1024)S(1)} %pad_clamp_fusion.9), kind=kCustom, calls=%fused_computation.clone.clone.1 | custom fusion | bytes 8388864 | tf_op jit(solution)/shard_map/while/body/eval_jaxpr/jit(_take)/gather | solution.py:117
  181.5 4.2 %fusion.60 = (f32[64,32]{1,0:T(8,128)S(1)}, f32[64,32,256]{2,1,0:T(8,128)S(1)}) fusion(bf16[64,256,128]{2,1,0:T(8,128)(2,1)} %gather_fusion, pred[64]{0:T(512)(128)(4,1)S(1)} %get-tuple-element.198, bf16[4,64,32,128]{3,2,1,0:T(8,128)(2,1)} %get-tuple-element.254, s32[]{:T(128)} %get-tuple-element.243), kind=kOutput, calls=%fused_computation.12.clone.1 | convolution fusion | flops 137361408 | bytes 6824512 | tf_op jit(solution)/shard_map/while/body/eval_jaxpr/bqe,bpe->bqp/dot_general | solution.py:119
  187.7 3.0 %gather_fusion = bf16[64,256,128]{2,1,0:T(8,128)(2,1)} fusion(bf16[16,256,128]{2,1,0:T(8,128)(2,1)S(1)} %get-tuple-element.256, s32[1024]{0:T(1024)S(1)} %pad_clamp_fusion.9), kind=kCustom, calls=%fused_computation.clone.clone.1 | custom fusion | bytes 8388864 | tf_op jit(solution)/shard_map/while/body/eval_jaxpr/jit(_take)/gather | solution.py:117
  190.7 4.2 %fusion.60 = (f32[64,32]{1,0:T(8,128)S(1)}, f32[64,32,256]{2,1,0:T(8,128)S(1)}) fusion(bf16[64,256,128]{2,1,0:T(8,128)(2,1)} %gather_fusion, pred[64]{0:T(512)(128)(4,1)S(1)} %get-tuple-element.198, bf16[4,64,32,128]{3,2,1,0:T(8,128)(2,1)} %get-tuple-element.254, s32[]{:T(128)} %get-tuple-element.243), kind=kOutput, calls=%fused_computation.12.clone.1 | convolution fusion | flops 137361408 | bytes 6824512 | tf_op jit(solution)/shard_map/while/body/eval_jaxpr/bqe,bpe->bqp/dot_general | solution.py:119
  197.0 14.9 %all-to-all-done.2 = bf16[256,32,128]{2,1,0:T(8,128)(2,1)S(1)} async-done(((bf16[256,32,128]{2,1,0:T(8,128)(2,1)}), bf16[256,32,128]{2,1,0:T(8,128)(2,1)S(1)}, u32[]{:S(2)}, u32[]{:S(2)}) %all-to-all-start.2) | async-done | bytes 2097184 | tf_op jit(solution)/shard_map/all_to_all | solution.py:148
  211.9 7.3 %all-to-all-start.3 = ((bf16[256,32,128]{2,1,0:T(8,128)(2,1)}), bf16[256,32,128]{2,1,0:T(8,128)(2,1)}, u32[]{:S(2)}, u32[]{:S(2)}) async-start(bf16[256,32,128]{2,1,0:T(8,128)(2,1)} %bitcast.20), calls=%async_computation.3 | async-start | bytes 4194304 | tf_op jit(solution)/shard_map/all_to_all | solution.py:148
  220.4 55.3 %shard_map.60 = f32[256,128]{1,0:T(8,128)} custom-call(f32[256,128]{1,0:T(8,128)} %pad.11.rows_ref), custom_call_target="tpu_custom_call" | custom-call | tf_op jit(solution)/shard_map/pallas_call | solution.py:67
  279.2 2.4 gather_fusion.7
  (123 shorter events, 37.1 us)
Async XLA Ops:
  0.6 1.6 copy-start
  15.4 74.8 %all-to-all-start.1 = ((bf16[256,32,128]{2,1,0:T(8,128)(2,1)}), bf16[256,32,128]{2,1,0:T(8,128)(2,1)}, u32[]{:S(2)}, u32[]{:S(2)}) async-start(bf16[256,32,128]{2,1,0:T(8,128)(2,1)} %get-tuple-element.120), calls=%async_computation.1 | async-start | bytes 4194304 | tf_op jit(solution)/shard_map/all_to_all | solution.py:136
  31.0 57.8 %copy-start.3 = (bf16[16,256,128]{2,1,0:T(8,128)(2,1)S(1)}, bf16[16,256,128]{2,1,0:T(8,128)(2,1)}, u32[]{:S(2)}) copy-start(bf16[16,256,128]{2,1,0:T(8,128)(2,1)} %param.13) | copy-start | bytes 3145732
  90.2 60.3 %all-to-all-start = ((bf16[256,32,128]{2,1,0:T(8,128)(2,1)}), bf16[256,32,128]{2,1,0:T(8,128)(2,1)S(1)}, u32[]{:S(2)}, u32[]{:S(2)}) async-start(bf16[256,32,128]{2,1,0:T(8,128)(2,1)} %get-tuple-element.119), calls=%async_computation | async-start | bytes 4194304 | tf_op jit(solution)/shard_map/all_to_all | solution.py:136
  101.5 4.2 %copy-start.1 = (bf16[64,256,128]{2,1,0:T(8,128)(2,1)S(1)}, bf16[64,256,128]{2,1,0:T(8,128)(2,1)}, u32[]{:S(2)}) copy-start(bf16[64,256,128]{2,1,0:T(8,128)(2,1)} %gather_fusion.1) | copy-start | bytes 12582916 | tf_op jit(solution)/shard_map/while
  110.8 4.2 %copy-start.1 = (bf16[64,256,128]{2,1,0:T(8,128)(2,1)S(1)}, bf16[64,256,128]{2,1,0:T(8,128)(2,1)}, u32[]{:S(2)}) copy-start(bf16[64,256,128]{2,1,0:T(8,128)(2,1)} %gather_fusion.1) | copy-start | bytes 12582916 | tf_op jit(solution)/shard_map/while
  120.1 4.2 %copy-start.1 = (bf16[64,256,128]{2,1,0:T(8,128)(2,1)S(1)}, bf16[64,256,128]{2,1,0:T(8,128)(2,1)}, u32[]{:S(2)}) copy-start(bf16[64,256,128]{2,1,0:T(8,128)(2,1)} %gather_fusion.1) | copy-start | bytes 12582916 | tf_op jit(solution)/shard_map/while
  129.4 4.2 %copy-start.1 = (bf16[64,256,128]{2,1,0:T(8,128)(2,1)S(1)}, bf16[64,256,128]{2,1,0:T(8,128)(2,1)}, u32[]{:S(2)}) copy-start(bf16[64,256,128]{2,1,0:T(8,128)(2,1)} %gather_fusion.1) | copy-start | bytes 12582916 | tf_op jit(solution)/shard_map/while
  150.5 1.3 copy-start.4
  151.9 60.0 %all-to-all-start.2 = ((bf16[256,32,128]{2,1,0:T(8,128)(2,1)}), bf16[256,32,128]{2,1,0:T(8,128)(2,1)S(1)}, u32[]{:S(2)}, u32[]{:S(2)}) async-start(bf16[256,32,128]{2,1,0:T(8,128)(2,1)} %bitcast.17), calls=%async_computation.2 | async-start | bytes 4194304 | tf_op jit(solution)/shard_map/all_to_all | solution.py:148
  162.9 4.2 %copy-start.2 = (bf16[64,256,128]{2,1,0:T(8,128)(2,1)S(1)}, bf16[64,256,128]{2,1,0:T(8,128)(2,1)}, u32[]{:S(2)}) copy-start(bf16[64,256,128]{2,1,0:T(8,128)(2,1)} %gather_fusion) | copy-start | bytes 12582916 | tf_op jit(solution)/shard_map/while
  172.2 4.2 %copy-start.2 = (bf16[64,256,128]{2,1,0:T(8,128)(2,1)S(1)}, bf16[64,256,128]{2,1,0:T(8,128)(2,1)}, u32[]{:S(2)}) copy-start(bf16[64,256,128]{2,1,0:T(8,128)(2,1)} %gather_fusion) | copy-start | bytes 12582916 | tf_op jit(solution)/shard_map/while
  181.5 4.2 %copy-start.2 = (bf16[64,256,128]{2,1,0:T(8,128)(2,1)S(1)}, bf16[64,256,128]{2,1,0:T(8,128)(2,1)}, u32[]{:S(2)}) copy-start(bf16[64,256,128]{2,1,0:T(8,128)(2,1)} %gather_fusion) | copy-start | bytes 12582916 | tf_op jit(solution)/shard_map/while
  190.7 4.2 %copy-start.2 = (bf16[64,256,128]{2,1,0:T(8,128)(2,1)S(1)}, bf16[64,256,128]{2,1,0:T(8,128)(2,1)}, u32[]{:S(2)}) copy-start(bf16[64,256,128]{2,1,0:T(8,128)(2,1)} %gather_fusion) | copy-start | bytes 12582916 | tf_op jit(solution)/shard_map/while
  211.9 67.3 %all-to-all-start.3 = ((bf16[256,32,128]{2,1,0:T(8,128)(2,1)}), bf16[256,32,128]{2,1,0:T(8,128)(2,1)}, u32[]{:S(2)}, u32[]{:S(2)}) async-start(bf16[256,32,128]{2,1,0:T(8,128)(2,1)} %bitcast.20), calls=%async_computation.3 | async-start | bytes 4194304 | tf_op jit(solution)/shard_map/all_to_all | solution.py:148
  219.2 59.7 %copy-start.6 = (s32[8,16]{1,0:T(8,128)S(1)}, s32[8,16]{1,0:T(8,128)}, u32[]{:S(2)}) copy-start(s32[8,16]{1,0:T(8,128)} %param.14) | copy-start | bytes 1540
  281.6 1.1 copy-start.5

commit v8 on v3

--- a/solution.py
+++ b/solution.py
@@ -1,7 +1,13 @@
+import functools
+
 import jax
 import jax.numpy as jnp
 from jax import lax
+from jax.experimental import pallas as pl
+from jax.experimental.pallas import tpu as pltpu
 from jax.sharding import PartitionSpec as P
+
+MESH = pl.DeviceIdType.MESH
 
 SOFTNESS = 0.02
 EPSILON = 1e-06
@@ -11,6 +17,74 @@
     floats = values.astype(jnp.float32)
     scale = lax.rsqrt(jnp.sum(floats * floats, axis=-1, keepdims=True) + EPSILON)
     return (floats * scale, scale)
+
+
+def exchange_kernel(dev_count, count, *refs):
+    sources, targets = refs[:count], refs[count : 2 * count]
+    landings = refs[2 * count : 3 * count]
+    send_sems, recv_sems = refs[3 * count], refs[3 * count + 1]
+    total = sources[0].shape[0]
+    me = lax.axis_index("group") * dev_count + lax.axis_index("dev")
+
+    def peer_id(step):
+        peer = lax.rem(me + step, total)
+        return peer, (lax.div(peer, dev_count), lax.rem(peer, dev_count))
+
+    barrier = pltpu.get_barrier_semaphore()
+
+    def greet(step, carry):
+        pl.semaphore_signal(barrier, inc=1, device_id=peer_id(step)[1], device_id_type=MESH)
+        return carry
+
+    lax.fori_loop(1, total, greet, 0)
+    pl.semaphore_wait(barrier, total - 1)
+
+    def send(step, carry):
+        peer, device = peer_id(step)
+        for index in range(count):
+            pltpu.make_async_remote_copy(
+                src_ref=sources[index].at[pl.ds(peer, 1)],
+                dst_ref=landings[index].at[pl.ds(me, 1)],
+                send_sem=send_sems.at[index],
+                recv_sem=recv_sems.at[index],
+                device_id=device,
+                device_id_type=MESH,
+            ).start()
+        return carry
+
+    lax.fori_loop(1, total, send, 0)
+    for index in range(count):
+        landings[index][pl.ds(me, 1)] = sources[index][pl.ds(me, 1)]
+    for index in range(count):
+        every = pltpu.make_async_remote_copy(
+            src_ref=sources[index].at[pl.ds(0, total - 1)],
+            dst_ref=landings[index].at[pl.ds(0, total - 1)],
+            send_sem=send_sems.at[index],
+            recv_sem=recv_sems.at[index],
+            device_id=peer_id(1)[1],
+            device_id_type=MESH,
+        )
+        every.wait_send()
+        every.wait_recv()
+    for index in range(count):
+        targets[index][...] = landings[index][...]
+
+
+def exchange(arrays, dev_count, tag):
+    count = len(arrays)
+    return pl.pallas_call(
+        functools.partial(exchange_kernel, dev_count, count),
+        out_shape=[jax.ShapeDtypeStruct(array.shape, array.dtype) for array in arrays],
+        in_specs=[pl.BlockSpec(memory_space=pltpu.VMEM)] * count,
+        out_specs=[pl.BlockSpec(memory_space=pltpu.VMEM)] * count,
+        scratch_shapes=[pltpu.VMEM(array.shape, array.dtype) for array in arrays]
+        + [pltpu.SemaphoreType.DMA((count,)), pltpu.SemaphoreType.DMA((count,))],
+        compiler_params=pltpu.CompilerParams(collective_id=tag, has_side_effects=True),
+    )(*arrays)
+
+
+def widen(small, feat_width):
+    return jnp.pad(small.astype(jnp.float32), ((0, 0), (0, feat_width - small.shape[1])))
 
 
 def local(queries, passages, candidates, location):
@@ -40,8 +114,8 @@
     both_axes = ("group", "dev")
     outgoing = outgoing.reshape(device_total, slot_cap, query_len, feat_width)
     labels = labels.reshape(device_total, slot_cap)
-    tags = lax.all_to_all(labels, both_axes, split_axis=0, concat_axis=0, tiled=True)
-    tags = tags.astype(jnp.int32)
+    first_arrived, tags = exchange([outgoing[:, 0], widen(labels, feat_width)], dev_count, 0)
+    tags = tags[:, :slot_cap].astype(jnp.int32)
     block_rows = 64
 
     def score_block(inputs):
@@ -65,9 +139,12 @@
     returned = []
     scores = []
     for slot in range(slot_cap):
-        arrived = lax.all_to_all(
-            outgoing[:, slot], both_axes, split_axis=0, concat_axis=0, tiled=True
-        )
+        if slot == 0:
+            arrived = first_arrived
+        else:
+            arrived = lax.all_to_all(
+                outgoing[:, slot], both_axes, split_axis=0, concat_axis=0, tiled=True
+            )
         blocks = device_total // block_rows
         pulled, score = lax.map(
             score_block,
@@ -77,10 +154,15 @@
             ),
         )
         pulled = pulled.reshape(device_total, query_len, feat_width)
-        returned.append(lax.all_to_all(pulled, both_axes, split_axis=0, concat_axis=0, tiled=True))
         scores.append(score.reshape(device_total))
+        if slot < slot_cap - 1:
+            returned.append(
+                lax.all_to_all(pulled, both_axes, split_axis=0, concat_axis=0, tiled=True)
+            )
     scores = jnp.stack(scores, axis=1)
-    scores_flat = lax.all_to_all(scores, both_axes, split_axis=0, concat_axis=0, tiled=True)
+    last_returned, scores_flat = exchange([pulled, widen(scores, feat_width)], dev_count, 1)
+    returned.append(last_returned)
+    scores_flat = scores_flat[:, :slot_cap]
     pair_score = jnp.take(scores_flat.reshape(slot_total), slot_index, axis=0).reshape(
         query_count, list_len
     )

time: 346 us -> 295 us (0.85)
  Pallas kernels: 0 us -> 160 us
  waiting for transfers between devices: 119 us -> 0.01 us
  blocking collectives: 78.9 us -> 0 us
  starting transfers between devices: 40 us -> 24.6 us
    pallas_call x0 -> x2, Pallas kernels: none -> 160 us  [exchange(): pl.pallas_call(functools.partial(exchange_kernel, dev_count, count), out_...]
    all_to_all x2 -> x0, blocking collectives: 78.9 us -> none  [the longest x1 60.6 us: local(): lax.all_to_all(pulled, both_axes, split_axis=0, concat_axis=0, tiled=True)]
    all_to_all x2 -> x1, waiting for transfers between devices: 68.7 us -> 0.01 us  [local(): lax.all_to_all(outgoing[:, slot], both_axes, split_axis=0, concat_axis=0,...]
    all_to_all x1, waiting for transfers between devices: 47.3 us -> 0.01 us  [local(): lax.all_to_all(pulled, both_axes, split_axis=0, concat_axis=0, tiled=True)]
    all_to_all x1 -> x0, starting transfers between devices: 14.6 us -> none  [local(): lax.all_to_all(labels, both_axes, split_axis=0, concat_axis=0, tiled=True)]
    all_to_all x2 -> x1, starting transfers between devices: 19.1 us -> 15.6 us  [local(): lax.all_to_all(outgoing[:, slot], both_axes, split_axis=0, concat_axis=0,...]
  transfers between devices with their start and end apart: 4 -> 2, of which waited for: 4 -> 0; matrix products, arithmetic and copies ran while one was open for 15% -> 30% of each run, Pallas kernels for 0% -> 55%
where the time goes in v8:
time: 295 us; the launch traced here: 293 us
  Pallas kernels  160 us (54%)
  local copies, waits for them, and re-layouts  48.7 us (17%)
  matrix products  46.5 us (16%)
  starting transfers between devices  24.6 us (8%)
  other arithmetic  12 us (4%)
    pallas_call x2, Pallas kernels, exchange(): pl.pallas_call(functools.partial(exchange_kernel, dev_count, count), out_...  160 us
    dot_general x8, matrix products, score_block(): jnp.einsum('bqe,bpe->bqp', query_block, passage_block, preferred_element_...  33.2 us
    gather x8, local copies, waits for them, and re-layouts, score_block(): passage_block = jnp.take(passage_unit, tag_block, axis=0)  24.1 us
    all_to_all x1, starting transfers between devices, local(): lax.all_to_all(outgoing[:, slot], both_axes, split_axis=0, concat_axis=0,...  15.6 us
    dot_general x8, matrix products, score_block(): jnp.einsum('bqp,bpe->bqe', attention, passage_block, preferred_element_ty...  12.9 us
    all_to_all x1, starting transfers between devices, local(): lax.all_to_all(pulled, both_axes, split_axis=0, concat_axis=0, tiled=True)  8.95 us
  transfers between devices with their start and end apart: 2, of which 0 were waited for; matrix products, arithmetic and copies ran while one was open for 30% of the time, Pallas kernels for 55%

profile of v8, /device:TPU:8, one launch (start us, length us, event | category | flops | bytes accessed | tf_op | source)
XLA Modules:
  0.0 292.5 jit_solution(8279915690305851788)
XLA Ops:
  6.8 3.4 %gather_fusion.3 = bf16[512,32,128]{2,1,0:T(8,128)(2,1)} fusion(bf16[8,32,128]{2,1,0:T(8,128)(2,1)S(1)} %fusion.39, s32[1024]{0:T(1024)S(1)} %pad_clamp_fusion.5), kind=kCustom, calls=%fused_computation.5 | custom fusion | bytes 8390656 | tf_op jit(solution)/shard_map/jit(_take)/gather | solution.py:112
  10.2 2.6 copy_select_fusion
  12.8 2.7 slice_bitcast_fusion
  15.6 15.6 %all-to-all-start = ((bf16[256,32,128]{2,1,0:T(8,128)(2,1)}), bf16[256,32,128]{2,1,0:T(8,128)(2,1)}, u32[]{:S(2)}, u32[]{:S(2)}) async-start(bf16[256,32,128]{2,1,0:T(8,128)(2,1)} %get-tuple-element.124), calls=%async_computation | async-start | bytes 4194304 | tf_op jit(solution)/shard_map/all_to_all | solution.py:145
  31.4 3.3 %gather_fusion.4 = s32[512]{0:T(512)S(1)} fusion(s32[128]{0:T(128)S(1)} %and_select_fusion.1, s32[1024]{0:T(1024)S(1)} %pad_clamp_fusion.4), kind=kCustom, calls=%fused_computation.6 | custom fusion | bytes 6144 | tf_op jit(solution)/shard_map/jit(_take)/gather | solution.py:113
  35.6 95.0 %shard_map.59 = (bf16[256,32,128]{2,1,0:T(8,128)(2,1)}, f32[256,128]{1,0:T(8,128)}) custom-call(bf16[256,32,128]{2,1,0:T(8,128)(2,1)} %get-tuple-element.123.refs_0_, f32[256,128]{1,0:T(8,128)} %pad_convert_fusion.refs_1_), custom_call_target="tpu_custom_call" | custom-call | tf_op jit(solution)/shard_map/pallas_call | solution.py:75
  134.8 37.2 %while.25 = (s32[]{:T(128)}, bf16[4,64,32,128]{3,2,1,0:T(8,128)(2,1)}, f32[4,64]{1,0:T(4,128)S(1)}, bf16[4,64,32,128]{3,2,1,0:T(8,128)(2,1)}, s32[4,64]{1,0:T(4,...) while((s32[]{:T(128)}, bf16[4,64,32,128]{3,2,1,0:T(8,128)(2,1)}, ...), condition=%wide.region_11.13_spmd, body=%wide.region_8.12_spmd.sunk | while | flops 275516736 | bytes 38829112 | solution.py:149
  134.8 3.0 %gather_fusion.1 = bf16[64,256,128]{2,1,0:T(8,128)(2,1)} fusion(bf16[16,256,128]{2,1,0:T(8,128)(2,1)S(1)} %get-tuple-element.260, s32[1024]{0:T(1024)S(1)} %pad_clamp_fusion.10), kind=kCustom, calls=%fused_computation.2.clone.clone.1 | custom fusion | bytes 8388864 | tf_op jit(solution)/shard_map/while/body/eval_jaxpr/jit(_take)/gather | solution.py:123
  137.9 4.2 %fusion.62 = (f32[64,32]{1,0:T(8,128)S(1)}, f32[64,32,256]{2,1,0:T(8,128)S(1)}) fusion(bf16[64,256,128]{2,1,0:T(8,128)(2,1)} %gather_fusion.1, pred[64]{0:T(512)(128)(4,1)S(1)} %get-tuple-element.212, bf16[4,64,32,128]{3,2,1,0:T(8,128)(2,1)} %get-tuple-element.258, s32[]{:T(128)} %get-tuple-element.247), kind=kOutput, calls=%fused_computation.35.clone.1 | convolution fusion | flops 137361408 | bytes 6824512 | tf_op jit(solution)/shard_map/while/body/eval_jaxpr/bqe,bpe->bqp/dot_general | solution.py:125
  142.0 1.9 fusion.63
  144.1 3.0 %gather_fusion.1 = bf16[64,256,128]{2,1,0:T(8,128)(2,1)} fusion(bf16[16,256,128]{2,1,0:T(8,128)(2,1)S(1)} %get-tuple-element.260, s32[1024]{0:T(1024)S(1)} %pad_clamp_fusion.10), kind=kCustom, calls=%fused_computation.2.clone.clone.1 | custom fusion | bytes 8388864 | tf_op jit(solution)/shard_map/while/body/eval_jaxpr/jit(_take)/gather | solution.py:123
  147.2 4.2 %fusion.62 = (f32[64,32]{1,0:T(8,128)S(1)}, f32[64,32,256]{2,1,0:T(8,128)S(1)}) fusion(bf16[64,256,128]{2,1,0:T(8,128)(2,1)} %gather_fusion.1, pred[64]{0:T(512)(128)(4,1)S(1)} %get-tuple-element.212, bf16[4,64,32,128]{3,2,1,0:T(8,128)(2,1)} %get-tuple-element.258, s32[]{:T(128)} %get-tuple-element.247), kind=kOutput, calls=%fused_computation.35.clone.1 | convolution fusion | flops 137361408 | bytes 6824512 | tf_op jit(solution)/shard_map/while/body/eval_jaxpr/bqe,bpe->bqp/dot_general | solution.py:125
  151.3 1.9 fusion.63
  153.4 3.0 %gather_fusion.1 = bf16[64,256,128]{2,1,0:T(8,128)(2,1)} fusion(bf16[16,256,128]{2,1,0:T(8,128)(2,1)S(1)} %get-tuple-element.260, s32[1024]{0:T(1024)S(1)} %pad_clamp_fusion.10), kind=kCustom, calls=%fused_computation.2.clone.clone.1 | custom fusion | bytes 8388864 | tf_op jit(solution)/shard_map/while/body/eval_jaxpr/jit(_take)/gather | solution.py:123
  156.4 4.2 %fusion.62 = (f32[64,32]{1,0:T(8,128)S(1)}, f32[64,32,256]{2,1,0:T(8,128)S(1)}) fusion(bf16[64,256,128]{2,1,0:T(8,128)(2,1)} %gather_fusion.1, pred[64]{0:T(512)(128)(4,1)S(1)} %get-tuple-element.212, bf16[4,64,32,128]{3,2,1,0:T(8,128)(2,1)} %get-tuple-element.258, s32[]{:T(128)} %get-tuple-element.247), kind=kOutput, calls=%fused_computation.35.clone.1 | convolution fusion | flops 137361408 | bytes 6824512 | tf_op jit(solution)/shard_map/while/body/eval_jaxpr/bqe,bpe->bqp/dot_general | solution.py:125
  160.6 1.9 fusion.63
  162.7 3.0 %gather_fusion.1 = bf16[64,256,128]{2,1,0:T(8,128)(2,1)} fusion(bf16[16,256,128]{2,1,0:T(8,128)(2,1)S(1)} %get-tuple-element.260, s32[1024]{0:T(1024)S(1)} %pad_clamp_fusion.10), kind=kCustom, calls=%fused_computation.2.clone.clone.1 | custom fusion | bytes 8388864 | tf_op jit(solution)/shard_map/while/body/eval_jaxpr/jit(_take)/gather | solution.py:123
  165.7 4.2 %fusion.62 = (f32[64,32]{1,0:T(8,128)S(1)}, f32[64,32,256]{2,1,0:T(8,128)S(1)}) fusion(bf16[64,256,128]{2,1,0:T(8,128)(2,1)} %gather_fusion.1, pred[64]{0:T(512)(128)(4,1)S(1)} %get-tuple-element.212, bf16[4,64,32,128]{3,2,1,0:T(8,128)(2,1)} %get-tuple-element.258, s32[]{:T(128)} %get-tuple-element.247), kind=kOutput, calls=%fused_computation.35.clone.1 | convolution fusion | flops 137361408 | bytes 6824512 | tf_op jit(solution)/shard_map/while/body/eval_jaxpr/bqe,bpe->bqp/dot_general | solution.py:125
  169.9 1.9 fusion.63
  172.2 8.9 %all-to-all-start.1 = ((bf16[256,32,128]{2,1,0:T(8,128)(2,1)}), bf16[256,32,128]{2,1,0:T(8,128)(2,1)}, u32[]{:S(2)}, u32[]{:S(2)}) async-start(bf16[256,32,128]{2,1,0:T(8,128)(2,1)} %bitcast.20), calls=%async_computation.1 | async-start | bytes 4194304 | tf_op jit(solution)/shard_map/all_to_all | solution.py:160
  181.5 34.7 %while.24 = (s32[]{:T(128)}, bf16[4,64,32,128]{3,2,1,0:T(8,128)(2,1)S(1)}, f32[4,64]{1,0:T(4,128)S(1)}, bf16[4,64,32,128]{3,2,1,0:T(8,128)(2,1)}, s32[4,64]{1,0:...) while((s32[]{:T(128)}, bf16[4,64,32,128]{3,2,1,0:T(8,128)(2,1)S(1)}, ...), condition=%wide.region_7.9_spmd, body=%wide.region_4.8_spmd.sunk | while | flops 275516736 | bytes 38853628 | solution.py:149
  181.5 3.0 %gather_fusion = bf16[64,256,128]{2,1,0:T(8,128)(2,1)} fusion(bf16[16,256,128]{2,1,0:T(8,128)(2,1)S(1)} %get-tuple-element.236, s32[1024]{0:T(1024)S(1)} %pad_clamp_fusion.9), kind=kCustom, calls=%fused_computation.clone.clone.1 | custom fusion | bytes 8388864 | tf_op jit(solution)/shard_map/while/body/eval_jaxpr/jit(_take)/gather | solution.py:123
  184.5 4.2 %fusion.60 = (f32[64,32]{1,0:T(8,128)S(1)}, f32[64,32,256]{2,1,0:T(8,128)S(1)}) fusion(bf16[64,256,128]{2,1,0:T(8,128)(2,1)} %gather_fusion, pred[64]{0:T(512)(128)(4,1)S(1)} %get-tuple-element.202, bf16[4,64,32,128]{3,2,1,0:T(8,128)(2,1)} %get-tuple-element.234, s32[]{:T(128)} %get-tuple-element.223), kind=kOutput, calls=%fused_computation.12.clone.1 | convolution fusion | flops 137361408 | bytes 6824512 | tf_op jit(solution)/shard_map/while/body/eval_jaxpr/bqe,bpe->bqp/dot_general | solution.py:125
  190.2 3.0 %gather_fusion = bf16[64,256,128]{2,1,0:T(8,128)(2,1)} fusion(bf16[16,256,128]{2,1,0:T(8,128)(2,1)S(1)} %get-tuple-element.236, s32[1024]{0:T(1024)S(1)} %pad_clamp_fusion.9), kind=kCustom, calls=%fused_computation.clone.clone.1 | custom fusion | bytes 8388864 | tf_op jit(solution)/shard_map/while/body/eval_jaxpr/jit(_take)/gather | solution.py:123
  193.2 4.2 %fusion.60 = (f32[64,32]{1,0:T(8,128)S(1)}, f32[64,32,256]{2,1,0:T(8,128)S(1)}) fusion(bf16[64,256,128]{2,1,0:T(8,128)(2,1)} %gather_fusion, pred[64]{0:T(512)(128)(4,1)S(1)} %get-tuple-element.202, bf16[4,64,32,128]{3,2,1,0:T(8,128)(2,1)} %get-tuple-element.234, s32[]{:T(128)} %get-tuple-element.223), kind=kOutput, calls=%fused_computation.12.clone.1 | convolution fusion | flops 137361408 | bytes 6824512 | tf_op jit(solution)/shard_map/while/body/eval_jaxpr/bqe,bpe->bqp/dot_general | solution.py:125
  198.9 3.0 %gather_fusion = bf16[64,256,128]{2,1,0:T(8,128)(2,1)} fusion(bf16[16,256,128]{2,1,0:T(8,128)(2,1)S(1)} %get-tuple-element.236, s32[1024]{0:T(1024)S(1)} %pad_clamp_fusion.9), kind=kCustom, calls=%fused_computation.clone.clone.1 | custom fusion | bytes 8388864 | tf_op jit(solution)/shard_map/while/body/eval_jaxpr/jit(_take)/gather | solution.py:123
  201.9 4.2 %fusion.60 = (f32[64,32]{1,0:T(8,128)S(1)}, f32[64,32,256]{2,1,0:T(8,128)S(1)}) fusion(bf16[64,256,128]{2,1,0:T(8,128)(2,1)} %gather_fusion, pred[64]{0:T(512)(128)(4,1)S(1)} %get-tuple-element.202, bf16[4,64,32,128]{3,2,1,0:T(8,128)(2,1)} %get-tuple-element.234, s32[]{:T(128)} %get-tuple-element.223), kind=kOutput, calls=%fused_computation.12.clone.1 | convolution fusion | flops 137361408 | bytes 6824512 | tf_op jit(solution)/shard_map/while/body/eval_jaxpr/bqe,bpe->bqp/dot_general | solution.py:125
  207.6 3.0 %gather_fusion = bf16[64,256,128]{2,1,0:T(8,128)(2,1)} fusion(bf16[16,256,128]{2,1,0:T(8,128)(2,1)S(1)} %get-tuple-element.236, s32[1024]{0:T(1024)S(1)} %pad_clamp_fusion.9), kind=kCustom, calls=%fused_computation.clone.clone.1 | custom fusion | bytes 8388864 | tf_op jit(solution)/shard_map/while/body/eval_jaxpr/jit(_take)/gather | solution.py:123
  210.6 4.2 %fusion.60 = (f32[64,32]{1,0:T(8,128)S(1)}, f32[64,32,256]{2,1,0:T(8,128)S(1)}) fusion(bf16[64,256,128]{2,1,0:T(8,128)(2,1)} %gather_fusion, pred[64]{0:T(512)(128)(4,1)S(1)} %get-tuple-element.202, bf16[4,64,32,128]{3,2,1,0:T(8,128)(2,1)} %get-tuple-element.234, s32[]{:T(128)} %get-tuple-element.223), kind=kOutput, calls=%fused_computation.12.clone.1 | convolution fusion | flops 137361408 | bytes 6824512 | tf_op jit(solution)/shard_map/while/body/eval_jaxpr/bqe,bpe->bqp/dot_general | solution.py:125
  217.1 64.5 %shard_map.60 = (bf16[256,32,128]{2,1,0:T(8,128)(2,1)}, f32[256,128]{1,0:T(8,128)}) custom-call(bf16[256,32,128]{2,1,0:T(8,128)(2,1)S(1)} %bitcast.72, f32[256,128]{1,0:T(8,128)} %pad.11.refs_1_), custom_call_target="tpu_custom_call" | custom-call | tf_op jit(solution)/shard_map/pallas_call | solution.py:75
  284.0 2.4 gather_fusion.6
  286.7 2.4 gather_fusion.7
  (118 shorter events, 25.4 us)
Async XLA Ops:
  0.6 1.6 copy-start
  15.6 156.6 %all-to-all-start = ((bf16[256,32,128]{2,1,0:T(8,128)(2,1)}), bf16[256,32,128]{2,1,0:T(8,128)(2,1)}, u32[]{:S(2)}, u32[]{:S(2)}) async-start(bf16[256,32,128]{2,1,0:T(8,128)(2,1)} %get-tuple-element.124), calls=%async_computation | async-start | bytes 4194304 | tf_op jit(solution)/shard_map/all_to_all | solution.py:145
  31.4 100.5 %copy-start.3 = (bf16[16,256,128]{2,1,0:T(8,128)(2,1)S(1)}, bf16[16,256,128]{2,1,0:T(8,128)(2,1)}, u32[]{:S(2)}) copy-start(bf16[16,256,128]{2,1,0:T(8,128)(2,1)} %param.13) | copy-start | bytes 3145732
  137.9 4.2 %copy-start.1 = (bf16[64,256,128]{2,1,0:T(8,128)(2,1)S(1)}, bf16[64,256,128]{2,1,0:T(8,128)(2,1)}, u32[]{:S(2)}) copy-start(bf16[64,256,128]{2,1,0:T(8,128)(2,1)} %gather_fusion.1) | copy-start | bytes 12582916 | tf_op jit(solution)/shard_map/while
  147.2 4.2 %copy-start.1 = (bf16[64,256,128]{2,1,0:T(8,128)(2,1)S(1)}, bf16[64,256,128]{2,1,0:T(8,128)(2,1)}, u32[]{:S(2)}) copy-start(bf16[64,256,128]{2,1,0:T(8,128)(2,1)} %gather_fusion.1) | copy-start | bytes 12582916 | tf_op jit(solution)/shard_map/while
  156.4 4.2 %copy-start.1 = (bf16[64,256,128]{2,1,0:T(8,128)(2,1)S(1)}, bf16[64,256,128]{2,1,0:T(8,128)(2,1)}, u32[]{:S(2)}) copy-start(bf16[64,256,128]{2,1,0:T(8,128)(2,1)} %gather_fusion.1) | copy-start | bytes 12582916 | tf_op jit(solution)/shard_map/while
  165.7 4.2 %copy-start.1 = (bf16[64,256,128]{2,1,0:T(8,128)(2,1)S(1)}, bf16[64,256,128]{2,1,0:T(8,128)(2,1)}, u32[]{:S(2)}) copy-start(bf16[64,256,128]{2,1,0:T(8,128)(2,1)} %gather_fusion.1) | copy-start | bytes 12582916 | tf_op jit(solution)/shard_map/while
  172.2 114.5 %all-to-all-start.1 = ((bf16[256,32,128]{2,1,0:T(8,128)(2,1)}), bf16[256,32,128]{2,1,0:T(8,128)(2,1)}, u32[]{:S(2)}, u32[]{:S(2)}) async-start(bf16[256,32,128]{2,1,0:T(8,128)(2,1)} %bitcast.20), calls=%async_computation.1 | async-start | bytes 4194304 | tf_op jit(solution)/shard_map/all_to_all | solution.py:160
  184.5 4.2 %copy-start.2 = (bf16[64,256,128]{2,1,0:T(8,128)(2,1)S(1)}, bf16[64,256,128]{2,1,0:T(8,128)(2,1)}, u32[]{:S(2)}) copy-start(bf16[64,256,128]{2,1,0:T(8,128)(2,1)} %gather_fusion) | copy-start | bytes 12582916 | tf_op jit(solution)/shard_map/while
  193.2 4.2 %copy-start.2 = (bf16[64,256,128]{2,1,0:T(8,128)(2,1)S(1)}, bf16[64,256,128]{2,1,0:T(8,128)(2,1)}, u32[]{:S(2)}) copy-start(bf16[64,256,128]{2,1,0:T(8,128)(2,1)} %gather_fusion) | copy-start | bytes 12582916 | tf_op jit(solution)/shard_map/while
  201.9 4.2 %copy-start.2 = (bf16[64,256,128]{2,1,0:T(8,128)(2,1)S(1)}, bf16[64,256,128]{2,1,0:T(8,128)(2,1)}, u32[]{:S(2)}) copy-start(bf16[64,256,128]{2,1,0:T(8,128)(2,1)} %gather_fusion) | copy-start | bytes 12582916 | tf_op jit(solution)/shard_map/while
  210.6 4.2 %copy-start.2 = (bf16[64,256,128]{2,1,0:T(8,128)(2,1)S(1)}, bf16[64,256,128]{2,1,0:T(8,128)(2,1)}, u32[]{:S(2)}) copy-start(bf16[64,256,128]{2,1,0:T(8,128)(2,1)} %gather_fusion) | copy-start | bytes 12582916 | tf_op jit(solution)/shard_map/while
  217.1 69.3 %copy-start.5 = (s32[8,16]{1,0:T(8,128)S(1)}, s32[8,16]{1,0:T(8,128)}, u32[]{:S(2)}) copy-start(s32[8,16]{1,0:T(8,128)} %param.14) | copy-start | bytes 1540
  289.1 1.1 copy-start.4

commit v9 on v8

--- a/solution.py
+++ b/solution.py
@@ -115,6 +115,7 @@
     outgoing = outgoing.reshape(device_total, slot_cap, query_len, feat_width)
     labels = labels.reshape(device_total, slot_cap)
     first_arrived, tags = exchange([outgoing[:, 0], widen(labels, feat_width)], dev_count, 0)
+    first_arrived, tags, outgoing = lax.optimization_barrier((first_arrived, tags, outgoing))
     tags = tags[:, :slot_cap].astype(jnp.int32)
     block_rows = 64
 
@@ -160,6 +161,7 @@
                 lax.all_to_all(pulled, both_axes, split_axis=0, concat_axis=0, tiled=True)
             )
     scores = jnp.stack(scores, axis=1)
+    pulled, scores, returned[0] = lax.optimization_barrier((pulled, scores, returned[0]))
     last_returned, scores_flat = exchange([pulled, widen(scores, feat_width)], dev_count, 1)
     returned.append(last_returned)
     scores_flat = scores_flat[:, :slot_cap]

time: 295 us -> 289 us (0.980)
  Pallas kernels: 160 us -> 127 us
  waiting for transfers between devices: 0.01 us -> 29.7 us
  starting transfers between devices: 24.6 us -> 19.2 us
  local copies, waits for them, and re-layouts: 48.7 us -> 51.9 us
    pallas_call x2, Pallas kernels: 160 us -> 127 us  [exchange(): pl.pallas_call(functools.partial(exchange_kernel, dev_count, count), out_...]
    all_to_all x1, waiting for transfers between devices: 0.01 us -> 17.7 us  [local(): lax.all_to_all(pulled, both_axes, split_axis=0, concat_axis=0, tiled=True)]
    all_to_all x1, waiting for transfers between devices: 0.01 us -> 12 us  [local(): lax.all_to_all(outgoing[:, slot], both_axes, split_axis=0, concat_axis=0,...]
    all_to_all x1, starting transfers between devices: 15.6 us -> 11.9 us  [local(): lax.all_to_all(outgoing[:, slot], both_axes, split_axis=0, concat_axis=0,...]
    squeeze x0 -> x1, local copies, waits for them, and re-layouts: none -> 3.3 us  [local(): outgoing[:, slot]]
  transfers between devices with their start and end apart: 2 -> 2, of which waited for: 0 -> 2; matrix products, arithmetic and copies ran while one was open for 30% -> 26% of each run, Pallas kernels for 55% -> 0%
where the time goes in v9:
time: 289 us; the launch traced here: 287 us
  Pallas kernels  127 us (44%)
  local copies, waits for them, and re-layouts  51.9 us (18%)
  matrix products  46.5 us (16%)
  waiting for transfers between devices  29.7 us (10%)
  starting transfers between devices  19.2 us (7%)
  other arithmetic  11.1 us (4%)
    pallas_call x2, Pallas kernels, exchange(): pl.pallas_call(functools.partial(exchange_kernel, dev_count, count), out_...  127 us
    dot_general x8, matrix products, score_block(): jnp.einsum('bqe,bpe->bqp', query_block, passage_block, preferred_element_...  33.2 us
    gather x8, local copies, waits for them, and re-layouts, score_block(): passage_block = jnp.take(passage_unit, tag_block, axis=0)  24.1 us
    all_to_all x1, waiting for transfers between devices, local(): lax.all_to_all(pulled, both_axes, split_axis=0, concat_axis=0, tiled=True)  17.7 us
    dot_general x8, matrix products, score_block(): jnp.einsum('bqp,bpe->bqe', attention, passage_block, preferred_element_ty...  12.9 us
    all_to_all x1, waiting for transfers between devices, local(): lax.all_to_all(outgoing[:, slot], both_axes, split_axis=0, concat_axis=0,...  12 us
    all_to_all x1, starting transfers between devices, local(): lax.all_to_all(outgoing[:, slot], both_axes, split_axis=0, concat_axis=0,...  11.9 us
    all_to_all x1, starting transfers between devices, local(): lax.all_to_all(pulled, both_axes, split_axis=0, concat_axis=0, tiled=True)  7.3 us
  transfers between devices with their start and end apart: 2, of which 2 were waited for; matrix products, arithmetic and copies ran while one was open for 26% of the time, Pallas kernels for 0%

profile of v9, /device:TPU:8, one launch (start us, length us, event | category | flops | bytes accessed | tf_op | source)
XLA Modules:
  0.0 286.9 jit_solution(410327362120527276)
XLA Ops:
  6.8 3.4 %gather_fusion.3 = bf16[512,32,128]{2,1,0:T(8,128)(2,1)} fusion(bf16[8,32,128]{2,1,0:T(8,128)(2,1)S(1)} %fusion.39, s32[1024]{0:T(1024)S(1)} %pad_clamp_fusion.5), kind=kCustom, calls=%fused_computation.5 | custom fusion | bytes 8390656 | tf_op jit(solution)/shard_map/jit(_take)/gather | solution.py:112
  10.3 2.6 copy_select_fusion
  15.5 3.3 %gather_fusion.4 = s32[512]{0:T(512)S(1)} fusion(s32[128]{0:T(128)S(1)} %get-tuple-element.136, s32[1024]{0:T(1024)S(1)} %pad_clamp_fusion.4), kind=kCustom, calls=%fused_computation.6 | custom fusion | bytes 6144 | tf_op jit(solution)/shard_map/jit(_take)/gather | solution.py:113
  19.7 66.7 %shard_map.59 = (bf16[256,32,128]{2,1,0:T(8,128)(2,1)}, f32[256,128]{1,0:T(8,128)}) custom-call(bf16[256,32,128]{2,1,0:T(8,128)(2,1)} %slice_bitcast_fusion.refs_0_, f32[256,128]{1,0:T(8,128)} %pad_convert_fusion.refs_1_), custom_call_target="tpu_custom_call" | custom-call | tf_op jit(solution)/shard_map/pallas_call | solution.py:75
  86.4 3.3 %slice_bitcast_fusion.1 = bf16[256,32,128]{2,1,0:T(8,128)(2,1)} fusion(bf16[256,2,32,128]{3,2,0,1:T(8,128)(2,1)} %copy-done.3), kind=kLoop, calls=%fused_computation.62 | loop fusion | bytes 4194304 | tf_op jit(solution)/shard_map/squeeze | solution.py:147
  89.7 11.9 %all-to-all-start = ((bf16[256,32,128]{2,1,0:T(8,128)(2,1)}), bf16[256,32,128]{2,1,0:T(8,128)(2,1)}, u32[]{:S(2)}, u32[]{:S(2)}) async-start(bf16[256,32,128]{2,1,0:T(8,128)(2,1)} %slice_bitcast_fusion.1), calls=%async_computation | async-start | bytes 4194304 | tf_op jit(solution)/shard_map/all_to_all | solution.py:146
  105.1 37.2 %while.25 = (s32[]{:T(128)}, bf16[4,64,32,128]{3,2,1,0:T(8,128)(2,1)}, f32[4,64]{1,0:T(4,128)S(1)}, bf16[4,64,32,128]{3,2,1,0:T(8,128)(2,1)}, s32[4,64]{1,0:T(4,...) while((s32[]{:T(128)}, bf16[4,64,32,128]{3,2,1,0:T(8,128)(2,1)}, ...), condition=%wide.region_11.13_spmd, body=%wide.region_8.12_spmd.sunk | while | flops 275516736 | bytes 38828104 | solution.py:150
  105.1 3.0 %gather_fusion.1 = bf16[64,256,128]{2,1,0:T(8,128)(2,1)} fusion(bf16[16,256,128]{2,1,0:T(8,128)(2,1)S(1)} %get-tuple-element.272, s32[1024]{0:T(1024)S(1)} %pad_clamp_fusion.10), kind=kCustom, calls=%fused_computation.2.clone.clone.1 | custom fusion | bytes 8388864 | tf_op jit(solution)/shard_map/while/body/eval_jaxpr/jit(_take)/gather | solution.py:124
  108.1 4.2 %fusion.62 = (f32[64,32]{1,0:T(8,128)S(1)}, f32[64,32,256]{2,1,0:T(8,128)S(1)}) fusion(bf16[64,256,128]{2,1,0:T(8,128)(2,1)} %gather_fusion.1, pred[64]{0:T(512)(128)(4,1)S(1)} %get-tuple-element.224, bf16[4,64,32,128]{3,2,1,0:T(8,128)(2,1)} %get-tuple-element.270, s32[]{:T(128)S(6)} %copy.38), kind=kOutput, calls=%fused_computation.35.clone.1 | convolution fusion | flops 137361408 | bytes 6824004 | tf_op jit(solution)/shard_map/while/body/eval_jaxpr/bqe,bpe->bqp/dot_general | solution.py:126
  112.3 1.9 fusion.63
  114.4 3.0 %gather_fusion.1 = bf16[64,256,128]{2,1,0:T(8,128)(2,1)} fusion(bf16[16,256,128]{2,1,0:T(8,128)(2,1)S(1)} %get-tuple-element.272, s32[1024]{0:T(1024)S(1)} %pad_clamp_fusion.10), kind=kCustom, calls=%fused_computation.2.clone.clone.1 | custom fusion | bytes 8388864 | tf_op jit(solution)/shard_map/while/body/eval_jaxpr/jit(_take)/gather | solution.py:124
  117.4 4.2 %fusion.62 = (f32[64,32]{1,0:T(8,128)S(1)}, f32[64,32,256]{2,1,0:T(8,128)S(1)}) fusion(bf16[64,256,128]{2,1,0:T(8,128)(2,1)} %gather_fusion.1, pred[64]{0:T(512)(128)(4,1)S(1)} %get-tuple-element.224, bf16[4,64,32,128]{3,2,1,0:T(8,128)(2,1)} %get-tuple-element.270, s32[]{:T(128)S(6)} %copy.38), kind=kOutput, calls=%fused_computation.35.clone.1 | convolution fusion | flops 137361408 | bytes 6824004 | tf_op jit(solution)/shard_map/while/body/eval_jaxpr/bqe,bpe->bqp/dot_general | solution.py:126
  123.7 3.0 %gather_fusion.1 = bf16[64,256,128]{2,1,0:T(8,128)(2,1)} fusion(bf16[16,256,128]{2,1,0:T(8,128)(2,1)S(1)} %get-tuple-element.272, s32[1024]{0:T(1024)S(1)} %pad_clamp_fusion.10), kind=kCustom, calls=%fused_computation.2.clone.clone.1 | custom fusion | bytes 8388864 | tf_op jit(solution)/shard_map/while/body/eval_jaxpr/jit(_take)/gather | solution.py:124
  126.7 4.2 %fusion.62 = (f32[64,32]{1,0:T(8,128)S(1)}, f32[64,32,256]{2,1,0:T(8,128)S(1)}) fusion(bf16[64,256,128]{2,1,0:T(8,128)(2,1)} %gather_fusion.1, pred[64]{0:T(512)(128)(4,1)S(1)} %get-tuple-element.224, bf16[4,64,32,128]{3,2,1,0:T(8,128)(2,1)} %get-tuple-element.270, s32[]{:T(128)S(6)} %copy.38), kind=kOutput, calls=%fused_computation.35.clone.1 | convolution fusion | flops 137361408 | bytes 6824004 | tf_op jit(solution)/shard_map/while/body/eval_jaxpr/bqe,bpe->bqp/dot_general | solution.py:126
  133.0 3.0 %gather_fusion.1 = bf16[64,256,128]{2,1,0:T(8,128)(2,1)} fusion(bf16[16,256,128]{2,1,0:T(8,128)(2,1)S(1)} %get-tuple-element.272, s32[1024]{0:T(1024)S(1)} %pad_clamp_fusion.10), kind=kCustom, calls=%fused_computation.2.clone.clone.1 | custom fusion | bytes 8388864 | tf_op jit(solution)/shard_map/while/body/eval_jaxpr/jit(_take)/gather | solution.py:124
  136.0 4.2 %fusion.62 = (f32[64,32]{1,0:T(8,128)S(1)}, f32[64,32,256]{2,1,0:T(8,128)S(1)}) fusion(bf16[64,256,128]{2,1,0:T(8,128)(2,1)} %gather_fusion.1, pred[64]{0:T(512)(128)(4,1)S(1)} %get-tuple-element.224, bf16[4,64,32,128]{3,2,1,0:T(8,128)(2,1)} %get-tuple-element.270, s32[]{:T(128)S(6)} %copy.38), kind=kOutput, calls=%fused_computation.35.clone.1 | convolution fusion | flops 137361408 | bytes 6824004 | tf_op jit(solution)/shard_map/while/body/eval_jaxpr/bqe,bpe->bqp/dot_general | solution.py:126
  140.2 1.9 fusion.63
  142.4 12.0 %all-to-all-done = bf16[256,32,128]{2,1,0:T(8,128)(2,1)} async-done(((bf16[256,32,128]{2,1,0:T(8,128)(2,1)}), bf16[256,32,128]{2,1,0:T(8,128)(2,1)}, u32[]{:S(2)}, u32[]{:S(2)}) %all-to-all-start) | async-done | bytes 2097184 | tf_op jit(solution)/shard_map/all_to_all | solution.py:146
  154.4 7.3 %all-to-all-start.1 = ((bf16[256,32,128]{2,1,0:T(8,128)(2,1)}), bf16[256,32,128]{2,1,0:T(8,128)(2,1)}, u32[]{:S(2)}, u32[]{:S(2)}) async-start(bf16[256,32,128]{2,1,0:T(8,128)(2,1)} %bitcast.18), calls=%async_computation.1 | async-start | bytes 4194304 | tf_op jit(solution)/shard_map/all_to_all | solution.py:161
  162.0 34.7 %while.24 = (s32[]{:T(128)}, bf16[4,64,32,128]{3,2,1,0:T(8,128)(2,1)S(1)}, f32[4,64]{1,0:T(4,128)S(1)}, bf16[4,64,32,128]{3,2,1,0:T(8,128)(2,1)}, s32[4,64]{1,0:...) while((s32[]{:T(128)}, bf16[4,64,32,128]{3,2,1,0:T(8,128)(2,1)S(1)}, ...), condition=%wide.region_7.9_spmd, body=%wide.region_4.8_spmd.sunk | while | flops 275516736 | bytes 38853128 | solution.py:150
  162.1 3.0 %gather_fusion = bf16[64,256,128]{2,1,0:T(8,128)(2,1)} fusion(bf16[16,256,128]{2,1,0:T(8,128)(2,1)S(1)} %get-tuple-element.248, s32[1024]{0:T(1024)S(1)} %pad_clamp_fusion.9), kind=kCustom, calls=%fused_computation.clone.clone.1 | custom fusion | bytes 8388864 | tf_op jit(solution)/shard_map/while/body/eval_jaxpr/jit(_take)/gather | solution.py:124
  165.1 4.2 %fusion.60 = (f32[64,32]{1,0:T(8,128)S(1)}, f32[64,32,256]{2,1,0:T(8,128)S(1)}) fusion(bf16[64,256,128]{2,1,0:T(8,128)(2,1)} %gather_fusion, pred[64]{0:T(512)(128)(4,1)S(1)} %get-tuple-element.214, bf16[4,64,32,128]{3,2,1,0:T(8,128)(2,1)} %get-tuple-element.246, s32[]{:T(128)S(6)} %copy.29), kind=kOutput, calls=%fused_computation.12.clone.1 | convolution fusion | flops 137361408 | bytes 6824004 | tf_op jit(solution)/shard_map/while/body/eval_jaxpr/bqe,bpe->bqp/dot_general | solution.py:126
  170.7 3.0 %gather_fusion = bf16[64,256,128]{2,1,0:T(8,128)(2,1)} fusion(bf16[16,256,128]{2,1,0:T(8,128)(2,1)S(1)} %get-tuple-element.248, s32[1024]{0:T(1024)S(1)} %pad_clamp_fusion.9), kind=kCustom, calls=%fused_computation.clone.clone.1 | custom fusion | bytes 8388864 | tf_op jit(solution)/shard_map/while/body/eval_jaxpr/jit(_take)/gather | solution.py:124
  173.7 4.2 %fusion.60 = (f32[64,32]{1,0:T(8,128)S(1)}, f32[64,32,256]{2,1,0:T(8,128)S(1)}) fusion(bf16[64,256,128]{2,1,0:T(8,128)(2,1)} %gather_fusion, pred[64]{0:T(512)(128)(4,1)S(1)} %get-tuple-element.214, bf16[4,64,32,128]{3,2,1,0:T(8,128)(2,1)} %get-tuple-element.246, s32[]{:T(128)S(6)} %copy.29), kind=kOutput, calls=%fused_computation.12.clone.1 | convolution fusion | flops 137361408 | bytes 6824004 | tf_op jit(solution)/shard_map/while/body/eval_jaxpr/bqe,bpe->bqp/dot_general | solution.py:126
  179.4 3.0 %gather_fusion = bf16[64,256,128]{2,1,0:T(8,128)(2,1)} fusion(bf16[16,256,128]{2,1,0:T(8,128)(2,1)S(1)} %get-tuple-element.248, s32[1024]{0:T(1024)S(1)} %pad_clamp_fusion.9), kind=kCustom, calls=%fused_computation.clone.clone.1 | custom fusion | bytes 8388864 | tf_op jit(solution)/shard_map/while/body/eval_jaxpr/jit(_take)/gather | solution.py:124
  182.4 4.2 %fusion.60 = (f32[64,32]{1,0:T(8,128)S(1)}, f32[64,32,256]{2,1,0:T(8,128)S(1)}) fusion(bf16[64,256,128]{2,1,0:T(8,128)(2,1)} %gather_fusion, pred[64]{0:T(512)(128)(4,1)S(1)} %get-tuple-element.214, bf16[4,64,32,128]{3,2,1,0:T(8,128)(2,1)} %get-tuple-element.246, s32[]{:T(128)S(6)} %copy.29), kind=kOutput, calls=%fused_computation.12.clone.1 | convolution fusion | flops 137361408 | bytes 6824004 | tf_op jit(solution)/shard_map/while/body/eval_jaxpr/bqe,bpe->bqp/dot_general | solution.py:126
  188.1 3.0 %gather_fusion = bf16[64,256,128]{2,1,0:T(8,128)(2,1)} fusion(bf16[16,256,128]{2,1,0:T(8,128)(2,1)S(1)} %get-tuple-element.248, s32[1024]{0:T(1024)S(1)} %pad_clamp_fusion.9), kind=kCustom, calls=%fused_computation.clone.clone.1 | custom fusion | bytes 8388864 | tf_op jit(solution)/shard_map/while/body/eval_jaxpr/jit(_take)/gather | solution.py:124
  191.1 4.2 %fusion.60 = (f32[64,32]{1,0:T(8,128)S(1)}, f32[64,32,256]{2,1,0:T(8,128)S(1)}) fusion(bf16[64,256,128]{2,1,0:T(8,128)(2,1)} %gather_fusion, pred[64]{0:T(512)(128)(4,1)S(1)} %get-tuple-element.214, bf16[4,64,32,128]{3,2,1,0:T(8,128)(2,1)} %get-tuple-element.246, s32[]{:T(128)S(6)} %copy.29), kind=kOutput, calls=%fused_computation.12.clone.1 | convolution fusion | flops 137361408 | bytes 6824004 | tf_op jit(solution)/shard_map/while/body/eval_jaxpr/bqe,bpe->bqp/dot_general | solution.py:126
  196.8 17.7 %all-to-all-done.1 = bf16[256,32,128]{2,1,0:T(8,128)(2,1)} async-done(((bf16[256,32,128]{2,1,0:T(8,128)(2,1)}), bf16[256,32,128]{2,1,0:T(8,128)(2,1)}, u32[]{:S(2)}, u32[]{:S(2)}) %all-to-all-start.1) | async-done | bytes 2097184 | tf_op jit(solution)/shard_map/all_to_all | solution.py:161
  215.3 60.6 %shard_map.60 = (bf16[256,32,128]{2,1,0:T(8,128)(2,1)}, f32[256,128]{1,0:T(8,128)}) custom-call(bf16[256,32,128]{2,1,0:T(8,128)(2,1)S(1)} %bitcast.72, f32[256,128]{1,0:T(8,128)} %pad.11.refs_1_), custom_call_target="tpu_custom_call" | custom-call | tf_op jit(solution)/shard_map/pallas_call | solution.py:75
  279.2 2.4 gather_fusion.7
  281.6 2.4 gather_fusion.6
  (122 shorter events, 30.9 us)
Async XLA Ops:
  0.6 1.6 copy-start
  12.8 2.6 copy-start.3
  89.7 12.0 %copy-start.6 = (f32[256,128]{1,0:T(8,128)S(1)}, f32[256,128]{1,0:T(8,128)}, u32[]{:S(2)}) copy-start(f32[256,128]{1,0:T(8,128)} %get-tuple-element.83) | copy-start | bytes 393220
  89.7 12.4 %copy-start.4 = (bf16[16,256,128]{2,1,0:T(8,128)(2,1)S(1)}, bf16[16,256,128]{2,1,0:T(8,128)(2,1)}, u32[]{:S(2)}) copy-start(bf16[16,256,128]{2,1,0:T(8,128)(2,1)} %param.13) | copy-start | bytes 3145732
  89.7 64.7 %all-to-all-start = ((bf16[256,32,128]{2,1,0:T(8,128)(2,1)}), bf16[256,32,128]{2,1,0:T(8,128)(2,1)}, u32[]{:S(2)}, u32[]{:S(2)}) async-start(bf16[256,32,128]{2,1,0:T(8,128)(2,1)} %slice_bitcast_fusion.1), calls=%async_computation | async-start | bytes 4194304 | tf_op jit(solution)/shard_map/all_to_all | solution.py:146
  108.1 4.2 %copy-start.1 = (bf16[64,256,128]{2,1,0:T(8,128)(2,1)S(1)}, bf16[64,256,128]{2,1,0:T(8,128)(2,1)}, u32[]{:S(2)}) copy-start(bf16[64,256,128]{2,1,0:T(8,128)(2,1)} %gather_fusion.1) | copy-start | bytes 12582916 | tf_op jit(solution)/shard_map/while
  117.4 4.2 %copy-start.1 = (bf16[64,256,128]{2,1,0:T(8,128)(2,1)S(1)}, bf16[64,256,128]{2,1,0:T(8,128)(2,1)}, u32[]{:S(2)}) copy-start(bf16[64,256,128]{2,1,0:T(8,128)(2,1)} %gather_fusion.1) | copy-start | bytes 12582916 | tf_op jit(solution)/shard_map/while
  126.7 4.2 %copy-start.1 = (bf16[64,256,128]{2,1,0:T(8,128)(2,1)S(1)}, bf16[64,256,128]{2,1,0:T(8,128)(2,1)}, u32[]{:S(2)}) copy-start(bf16[64,256,128]{2,1,0:T(8,128)(2,1)} %gather_fusion.1) | copy-start | bytes 12582916 | tf_op jit(solution)/shard_map/while
  136.0 4.2 %copy-start.1 = (bf16[64,256,128]{2,1,0:T(8,128)(2,1)S(1)}, bf16[64,256,128]{2,1,0:T(8,128)(2,1)}, u32[]{:S(2)}) copy-start(bf16[64,256,128]{2,1,0:T(8,128)(2,1)} %gather_fusion.1) | copy-start | bytes 12582916 | tf_op jit(solution)/shard_map/while
  154.4 60.1 %all-to-all-start.1 = ((bf16[256,32,128]{2,1,0:T(8,128)(2,1)}), bf16[256,32,128]{2,1,0:T(8,128)(2,1)}, u32[]{:S(2)}, u32[]{:S(2)}) async-start(bf16[256,32,128]{2,1,0:T(8,128)(2,1)} %bitcast.18), calls=%async_computation.1 | async-start | bytes 4194304 | tf_op jit(solution)/shard_map/all_to_all | solution.py:161
  165.1 4.2 %copy-start.2 = (bf16[64,256,128]{2,1,0:T(8,128)(2,1)S(1)}, bf16[64,256,128]{2,1,0:T(8,128)(2,1)}, u32[]{:S(2)}) copy-start(bf16[64,256,128]{2,1,0:T(8,128)(2,1)} %gather_fusion) | copy-start | bytes 12582916 | tf_op jit(solution)/shard_map/while
  173.7 4.2 %copy-start.2 = (bf16[64,256,128]{2,1,0:T(8,128)(2,1)S(1)}, bf16[64,256,128]{2,1,0:T(8,128)(2,1)}, u32[]{:S(2)}) copy-start(bf16[64,256,128]{2,1,0:T(8,128)(2,1)} %gather_fusion) | copy-start | bytes 12582916 | tf_op jit(solution)/shard_map/while
  182.4 4.2 %copy-start.2 = (bf16[64,256,128]{2,1,0:T(8,128)(2,1)S(1)}, bf16[64,256,128]{2,1,0:T(8,128)(2,1)}, u32[]{:S(2)}) copy-start(bf16[64,256,128]{2,1,0:T(8,128)(2,1)} %gather_fusion) | copy-start | bytes 12582916 | tf_op jit(solution)/shard_map/while
  191.1 4.2 %copy-start.2 = (bf16[64,256,128]{2,1,0:T(8,128)(2,1)S(1)}, bf16[64,256,128]{2,1,0:T(8,128)(2,1)}, u32[]{:S(2)}) copy-start(bf16[64,256,128]{2,1,0:T(8,128)(2,1)} %gather_fusion) | copy-start | bytes 12582916 | tf_op jit(solution)/shard_map/while
  196.7 81.6 %copy-start.7 = (s32[8,16]{1,0:T(8,128)S(1)}, s32[8,16]{1,0:T(8,128)}, u32[]{:S(2)}) copy-start(s32[8,16]{1,0:T(8,128)} %param.14) | copy-start | bytes 1540
  283.9 1.1 copy-start.5

commit v10 on v9

--- a/solution.py
+++ b/solution.py
@@ -27,7 +27,9 @@
     me = lax.axis_index("group") * dev_count + lax.axis_index("dev")
 
     def peer_id(step):
-        peer = lax.rem(me + step, total)
+        reach = lax.div(step + 1, 2)
+        offset = jnp.where(lax.rem(step, 2) == 1, reach, total - reach)
+        peer = lax.rem(me + offset, total)
         return peer, (lax.div(peer, dev_count), lax.rem(peer, dev_count))
 
     barrier = pltpu.get_barrier_semaphore()

time: 289 us -> 295 us (1.021)
  Pallas kernels: 127 us -> 134 us
    pallas_call x2, Pallas kernels: 127 us -> 134 us  [exchange(): pl.pallas_call(functools.partial(exchange_kernel, dev_count, count), out_...]
where the time goes in v10:
time: 295 us; the launch traced here: 293 us
  Pallas kernels  134 us (45%)
  local copies, waits for them, and re-layouts  51.9 us (18%)
  matrix products  46.5 us (16%)
  waiting for transfers between devices  29.7 us (10%)
  starting transfers between devices  18.8 us (6%)
  other arithmetic  11.1 us (4%)
    pallas_call x2, Pallas kernels, exchange(): pl.pallas_call(functools.partial(exchange_kernel, dev_count, count), out_...  134 us
    dot_general x8, matrix products, score_block(): jnp.einsum('bqe,bpe->bqp', query_block, passage_block, preferred_element_...  33.2 us
    gather x8, local copies, waits for them, and re-layouts, score_block(): passage_block = jnp.take(passage_unit, tag_block, axis=0)  24.1 us
    all_to_all x1, waiting for transfers between devices, local(): lax.all_to_all(pulled, both_axes, split_axis=0, concat_axis=0, tiled=True)  17.7 us
    dot_general x8, matrix products, score_block(): jnp.einsum('bqp,bpe->bqe', attention, passage_block, preferred_element_ty...  12.9 us
    all_to_all x1, waiting for transfers between devices, local(): lax.all_to_all(outgoing[:, slot], both_axes, split_axis=0, concat_axis=0,...  12 us
    all_to_all x1, starting transfers between devices, local(): lax.all_to_all(outgoing[:, slot], both_axes, split_axis=0, concat_axis=0,...  11.5 us
    all_to_all x1, starting transfers between devices, local(): lax.all_to_all(pulled, both_axes, split_axis=0, concat_axis=0, tiled=True)  7.3 us
  transfers between devices with their start and end apart: 2, of which 2 were waited for; matrix products, arithmetic and copies ran while one was open for 26% of the time, Pallas kernels for 0%

profile of v10, /device:TPU:8, one launch (start us, length us, event | category | flops | bytes accessed | tf_op | source)
XLA Modules:
  0.0 293.1 jit_solution(18277535093349255535)
XLA Ops:
  6.8 3.4 %gather_fusion.3 = bf16[512,32,128]{2,1,0:T(8,128)(2,1)} fusion(bf16[8,32,128]{2,1,0:T(8,128)(2,1)S(1)} %fusion.39, s32[1024]{0:T(1024)S(1)} %pad_clamp_fusion.5), kind=kCustom, calls=%fused_computation.5 | custom fusion | bytes 8390656 | tf_op jit(solution)/shard_map/jit(_take)/gather | solution.py:114
  10.3 2.6 copy_select_fusion
  15.5 3.3 %gather_fusion.4 = s32[512]{0:T(512)S(1)} fusion(s32[128]{0:T(128)S(1)} %get-tuple-element.136, s32[1024]{0:T(1024)S(1)} %pad_clamp_fusion.4), kind=kCustom, calls=%fused_computation.6 | custom fusion | bytes 6144 | tf_op jit(solution)/shard_map/jit(_take)/gather | solution.py:115
  19.7 69.2 %shard_map.59 = (bf16[256,32,128]{2,1,0:T(8,128)(2,1)}, f32[256,128]{1,0:T(8,128)}) custom-call(bf16[256,32,128]{2,1,0:T(8,128)(2,1)} %slice_bitcast_fusion.refs_0_, f32[256,128]{1,0:T(8,128)} %pad_convert_fusion.refs_1_), custom_call_target="tpu_custom_call" | custom-call | tf_op jit(solution)/shard_map/pallas_call | solution.py:77
  88.9 3.3 %slice_bitcast_fusion.1 = bf16[256,32,128]{2,1,0:T(8,128)(2,1)} fusion(bf16[256,2,32,128]{3,2,0,1:T(8,128)(2,1)} %copy-done.3), kind=kLoop, calls=%fused_computation.62 | loop fusion | bytes 4194304 | tf_op jit(solution)/shard_map/squeeze | solution.py:149
  92.2 11.5 %all-to-all-start = ((bf16[256,32,128]{2,1,0:T(8,128)(2,1)}), bf16[256,32,128]{2,1,0:T(8,128)(2,1)}, u32[]{:S(2)}, u32[]{:S(2)}) async-start(bf16[256,32,128]{2,1,0:T(8,128)(2,1)} %slice_bitcast_fusion.1), calls=%async_computation | async-start | bytes 4194304 | tf_op jit(solution)/shard_map/all_to_all | solution.py:148
  107.2 37.2 %while.25 = (s32[]{:T(128)}, bf16[4,64,32,128]{3,2,1,0:T(8,128)(2,1)}, f32[4,64]{1,0:T(4,128)S(1)}, bf16[4,64,32,128]{3,2,1,0:T(8,128)(2,1)}, s32[4,64]{1,0:T(4,...) while((s32[]{:T(128)}, bf16[4,64,32,128]{3,2,1,0:T(8,128)(2,1)}, ...), condition=%wide.region_11.13_spmd, body=%wide.region_8.12_spmd.sunk | while | flops 275516736 | bytes 38828104 | solution.py:152
  107.2 3.0 %gather_fusion.1 = bf16[64,256,128]{2,1,0:T(8,128)(2,1)} fusion(bf16[16,256,128]{2,1,0:T(8,128)(2,1)S(1)} %get-tuple-element.272, s32[1024]{0:T(1024)S(1)} %pad_clamp_fusion.10), kind=kCustom, calls=%fused_computation.2.clone.clone.1 | custom fusion | bytes 8388864 | tf_op jit(solution)/shard_map/while/body/eval_jaxpr/jit(_take)/gather | solution.py:126
  110.3 4.2 %fusion.62 = (f32[64,32]{1,0:T(8,128)S(1)}, f32[64,32,256]{2,1,0:T(8,128)S(1)}) fusion(bf16[64,256,128]{2,1,0:T(8,128)(2,1)} %gather_fusion.1, pred[64]{0:T(512)(128)(4,1)S(1)} %get-tuple-element.224, bf16[4,64,32,128]{3,2,1,0:T(8,128)(2,1)} %get-tuple-element.270, s32[]{:T(128)S(6)} %copy.38), kind=kOutput, calls=%fused_computation.35.clone.1 | convolution fusion | flops 137361408 | bytes 6824004 | tf_op jit(solution)/shard_map/while/body/eval_jaxpr/bqe,bpe->bqp/dot_general | solution.py:128
  114.4 1.9 fusion.63
  116.5 3.0 %gather_fusion.1 = bf16[64,256,128]{2,1,0:T(8,128)(2,1)} fusion(bf16[16,256,128]{2,1,0:T(8,128)(2,1)S(1)} %get-tuple-element.272, s32[1024]{0:T(1024)S(1)} %pad_clamp_fusion.10), kind=kCustom, calls=%fused_computation.2.clone.clone.1 | custom fusion | bytes 8388864 | tf_op jit(solution)/shard_map/while/body/eval_jaxpr/jit(_take)/gather | solution.py:126
  119.6 4.2 %fusion.62 = (f32[64,32]{1,0:T(8,128)S(1)}, f32[64,32,256]{2,1,0:T(8,128)S(1)}) fusion(bf16[64,256,128]{2,1,0:T(8,128)(2,1)} %gather_fusion.1, pred[64]{0:T(512)(128)(4,1)S(1)} %get-tuple-element.224, bf16[4,64,32,128]{3,2,1,0:T(8,128)(2,1)} %get-tuple-element.270, s32[]{:T(128)S(6)} %copy.38), kind=kOutput, calls=%fused_computation.35.clone.1 | convolution fusion | flops 137361408 | bytes 6824004 | tf_op jit(solution)/shard_map/while/body/eval_jaxpr/bqe,bpe->bqp/dot_general | solution.py:128
  125.8 3.0 %gather_fusion.1 = bf16[64,256,128]{2,1,0:T(8,128)(2,1)} fusion(bf16[16,256,128]{2,1,0:T(8,128)(2,1)S(1)} %get-tuple-element.272, s32[1024]{0:T(1024)S(1)} %pad_clamp_fusion.10), kind=kCustom, calls=%fused_computation.2.clone.clone.1 | custom fusion | bytes 8388864 | tf_op jit(solution)/shard_map/while/body/eval_jaxpr/jit(_take)/gather | solution.py:126
  128.8 4.2 %fusion.62 = (f32[64,32]{1,0:T(8,128)S(1)}, f32[64,32,256]{2,1,0:T(8,128)S(1)}) fusion(bf16[64,256,128]{2,1,0:T(8,128)(2,1)} %gather_fusion.1, pred[64]{0:T(512)(128)(4,1)S(1)} %get-tuple-element.224, bf16[4,64,32,128]{3,2,1,0:T(8,128)(2,1)} %get-tuple-element.270, s32[]{:T(128)S(6)} %copy.38), kind=kOutput, calls=%fused_computation.35.clone.1 | convolution fusion | flops 137361408 | bytes 6824004 | tf_op jit(solution)/shard_map/while/body/eval_jaxpr/bqe,bpe->bqp/dot_general | solution.py:128
  135.1 3.0 %gather_fusion.1 = bf16[64,256,128]{2,1,0:T(8,128)(2,1)} fusion(bf16[16,256,128]{2,1,0:T(8,128)(2,1)S(1)} %get-tuple-element.272, s32[1024]{0:T(1024)S(1)} %pad_clamp_fusion.10), kind=kCustom, calls=%fused_computation.2.clone.clone.1 | custom fusion | bytes 8388864 | tf_op jit(solution)/shard_map/while/body/eval_jaxpr/jit(_take)/gather | solution.py:126
  138.1 4.2 %fusion.62 = (f32[64,32]{1,0:T(8,128)S(1)}, f32[64,32,256]{2,1,0:T(8,128)S(1)}) fusion(bf16[64,256,128]{2,1,0:T(8,128)(2,1)} %gather_fusion.1, pred[64]{0:T(512)(128)(4,1)S(1)} %get-tuple-element.224, bf16[4,64,32,128]{3,2,1,0:T(8,128)(2,1)} %get-tuple-element.270, s32[]{:T(128)S(6)} %copy.38), kind=kOutput, calls=%fused_computation.35.clone.1 | convolution fusion | flops 137361408 | bytes 6824004 | tf_op jit(solution)/shard_map/while/body/eval_jaxpr/bqe,bpe->bqp/dot_general | solution.py:128
  142.3 1.9 fusion.63
  144.5 12.0 %all-to-all-done = bf16[256,32,128]{2,1,0:T(8,128)(2,1)} async-done(((bf16[256,32,128]{2,1,0:T(8,128)(2,1)}), bf16[256,32,128]{2,1,0:T(8,128)(2,1)}, u32[]{:S(2)}, u32[]{:S(2)}) %all-to-all-start) | async-done | bytes 2097184 | tf_op jit(solution)/shard_map/all_to_all | solution.py:148
  156.5 7.3 %all-to-all-start.1 = ((bf16[256,32,128]{2,1,0:T(8,128)(2,1)}), bf16[256,32,128]{2,1,0:T(8,128)(2,1)}, u32[]{:S(2)}, u32[]{:S(2)}) async-start(bf16[256,32,128]{2,1,0:T(8,128)(2,1)} %bitcast.18), calls=%async_computation.1 | async-start | bytes 4194304 | tf_op jit(solution)/shard_map/all_to_all | solution.py:163
  164.1 34.7 %while.24 = (s32[]{:T(128)}, bf16[4,64,32,128]{3,2,1,0:T(8,128)(2,1)S(1)}, f32[4,64]{1,0:T(4,128)S(1)}, bf16[4,64,32,128]{3,2,1,0:T(8,128)(2,1)}, s32[4,64]{1,0:...) while((s32[]{:T(128)}, bf16[4,64,32,128]{3,2,1,0:T(8,128)(2,1)S(1)}, ...), condition=%wide.region_7.9_spmd, body=%wide.region_4.8_spmd.sunk | while | flops 275516736 | bytes 38853128 | solution.py:152
  164.2 3.0 %gather_fusion = bf16[64,256,128]{2,1,0:T(8,128)(2,1)} fusion(bf16[16,256,128]{2,1,0:T(8,128)(2,1)S(1)} %get-tuple-element.248, s32[1024]{0:T(1024)S(1)} %pad_clamp_fusion.9), kind=kCustom, calls=%fused_computation.clone.clone.1 | custom fusion | bytes 8388864 | tf_op jit(solution)/shard_map/while/body/eval_jaxpr/jit(_take)/gather | solution.py:126
  167.2 4.2 %fusion.60 = (f32[64,32]{1,0:T(8,128)S(1)}, f32[64,32,256]{2,1,0:T(8,128)S(1)}) fusion(bf16[64,256,128]{2,1,0:T(8,128)(2,1)} %gather_fusion, pred[64]{0:T(512)(128)(4,1)S(1)} %get-tuple-element.214, bf16[4,64,32,128]{3,2,1,0:T(8,128)(2,1)} %get-tuple-element.246, s32[]{:T(128)S(6)} %copy.29), kind=kOutput, calls=%fused_computation.12.clone.1 | convolution fusion | flops 137361408 | bytes 6824004 | tf_op jit(solution)/shard_map/while/body/eval_jaxpr/bqe,bpe->bqp/dot_general | solution.py:128
  172.8 3.0 %gather_fusion = bf16[64,256,128]{2,1,0:T(8,128)(2,1)} fusion(bf16[16,256,128]{2,1,0:T(8,128)(2,1)S(1)} %get-tuple-element.248, s32[1024]{0:T(1024)S(1)} %pad_clamp_fusion.9), kind=kCustom, calls=%fused_computation.clone.clone.1 | custom fusion | bytes 8388864 | tf_op jit(solution)/shard_map/while/body/eval_jaxpr/jit(_take)/gather | solution.py:126
  175.9 4.2 %fusion.60 = (f32[64,32]{1,0:T(8,128)S(1)}, f32[64,32,256]{2,1,0:T(8,128)S(1)}) fusion(bf16[64,256,128]{2,1,0:T(8,128)(2,1)} %gather_fusion, pred[64]{0:T(512)(128)(4,1)S(1)} %get-tuple-element.214, bf16[4,64,32,128]{3,2,1,0:T(8,128)(2,1)} %get-tuple-element.246, s32[]{:T(128)S(6)} %copy.29), kind=kOutput, calls=%fused_computation.12.clone.1 | convolution fusion | flops 137361408 | bytes 6824004 | tf_op jit(solution)/shard_map/while/body/eval_jaxpr/bqe,bpe->bqp/dot_general | solution.py:128
  181.5 3.0 %gather_fusion = bf16[64,256,128]{2,1,0:T(8,128)(2,1)} fusion(bf16[16,256,128]{2,1,0:T(8,128)(2,1)S(1)} %get-tuple-element.248, s32[1024]{0:T(1024)S(1)} %pad_clamp_fusion.9), kind=kCustom, calls=%fused_computation.clone.clone.1 | custom fusion | bytes 8388864 | tf_op jit(solution)/shard_map/while/body/eval_jaxpr/jit(_take)/gather | solution.py:126
  184.5 4.2 %fusion.60 = (f32[64,32]{1,0:T(8,128)S(1)}, f32[64,32,256]{2,1,0:T(8,128)S(1)}) fusion(bf16[64,256,128]{2,1,0:T(8,128)(2,1)} %gather_fusion, pred[64]{0:T(512)(128)(4,1)S(1)} %get-tuple-element.214, bf16[4,64,32,128]{3,2,1,0:T(8,128)(2,1)} %get-tuple-element.246, s32[]{:T(128)S(6)} %copy.29), kind=kOutput, calls=%fused_computation.12.clone.1 | convolution fusion | flops 137361408 | bytes 6824004 | tf_op jit(solution)/shard_map/while/body/eval_jaxpr/bqe,bpe->bqp/dot_general | solution.py:128
  190.2 3.0 %gather_fusion = bf16[64,256,128]{2,1,0:T(8,128)(2,1)} fusion(bf16[16,256,128]{2,1,0:T(8,128)(2,1)S(1)} %get-tuple-element.248, s32[1024]{0:T(1024)S(1)} %pad_clamp_fusion.9), kind=kCustom, calls=%fused_computation.clone.clone.1 | custom fusion | bytes 8388864 | tf_op jit(solution)/shard_map/while/body/eval_jaxpr/jit(_take)/gather | solution.py:126
  193.2 4.2 %fusion.60 = (f32[64,32]{1,0:T(8,128)S(1)}, f32[64,32,256]{2,1,0:T(8,128)S(1)}) fusion(bf16[64,256,128]{2,1,0:T(8,128)(2,1)} %gather_fusion, pred[64]{0:T(512)(128)(4,1)S(1)} %get-tuple-element.214, bf16[4,64,32,128]{3,2,1,0:T(8,128)(2,1)} %get-tuple-element.246, s32[]{:T(128)S(6)} %copy.29), kind=kOutput, calls=%fused_computation.12.clone.1 | convolution fusion | flops 137361408 | bytes 6824004 | tf_op jit(solution)/shard_map/while/body/eval_jaxpr/bqe,bpe->bqp/dot_general | solution.py:128
  198.9 17.7 %all-to-all-done.1 = bf16[256,32,128]{2,1,0:T(8,128)(2,1)} async-done(((bf16[256,32,128]{2,1,0:T(8,128)(2,1)}), bf16[256,32,128]{2,1,0:T(8,128)(2,1)}, u32[]{:S(2)}, u32[]{:S(2)}) %all-to-all-start.1) | async-done | bytes 2097184 | tf_op jit(solution)/shard_map/all_to_all | solution.py:163
  217.4 64.8 %shard_map.60 = (bf16[256,32,128]{2,1,0:T(8,128)(2,1)}, f32[256,128]{1,0:T(8,128)}) custom-call(bf16[256,32,128]{2,1,0:T(8,128)(2,1)S(1)} %bitcast.72, f32[256,128]{1,0:T(8,128)} %pad.11.refs_1_), custom_call_target="tpu_custom_call" | custom-call | tf_op jit(solution)/shard_map/pallas_call | solution.py:77
  285.4 2.4 gather_fusion.7
  287.8 2.3 gather_fusion.6
  (122 shorter events, 30.9 us)
Async XLA Ops:
  0.6 1.6 copy-start
  12.8 2.6 copy-start.3
  92.2 11.7 %copy-start.6 = (f32[256,128]{1,0:T(8,128)S(1)}, f32[256,128]{1,0:T(8,128)}, u32[]{:S(2)}) copy-start(f32[256,128]{1,0:T(8,128)} %get-tuple-element.83) | copy-start | bytes 393220
  92.2 12.0 %copy-start.4 = (bf16[16,256,128]{2,1,0:T(8,128)(2,1)S(1)}, bf16[16,256,128]{2,1,0:T(8,128)(2,1)}, u32[]{:S(2)}) copy-start(bf16[16,256,128]{2,1,0:T(8,128)(2,1)} %param.13) | copy-start | bytes 3145732
  92.2 64.3 %all-to-all-start = ((bf16[256,32,128]{2,1,0:T(8,128)(2,1)}), bf16[256,32,128]{2,1,0:T(8,128)(2,1)}, u32[]{:S(2)}, u32[]{:S(2)}) async-start(bf16[256,32,128]{2,1,0:T(8,128)(2,1)} %slice_bitcast_fusion.1), calls=%async_computation | async-start | bytes 4194304 | tf_op jit(solution)/shard_map/all_to_all | solution.py:148
  110.2 4.2 %copy-start.1 = (bf16[64,256,128]{2,1,0:T(8,128)(2,1)S(1)}, bf16[64,256,128]{2,1,0:T(8,128)(2,1)}, u32[]{:S(2)}) copy-start(bf16[64,256,128]{2,1,0:T(8,128)(2,1)} %gather_fusion.1) | copy-start | bytes 12582916 | tf_op jit(solution)/shard_map/while
  119.6 4.2 %copy-start.1 = (bf16[64,256,128]{2,1,0:T(8,128)(2,1)S(1)}, bf16[64,256,128]{2,1,0:T(8,128)(2,1)}, u32[]{:S(2)}) copy-start(bf16[64,256,128]{2,1,0:T(8,128)(2,1)} %gather_fusion.1) | copy-start | bytes 12582916 | tf_op jit(solution)/shard_map/while
  128.8 4.2 %copy-start.1 = (bf16[64,256,128]{2,1,0:T(8,128)(2,1)S(1)}, bf16[64,256,128]{2,1,0:T(8,128)(2,1)}, u32[]{:S(2)}) copy-start(bf16[64,256,128]{2,1,0:T(8,128)(2,1)} %gather_fusion.1) | copy-start | bytes 12582916 | tf_op jit(solution)/shard_map/while
  138.1 4.2 %copy-start.1 = (bf16[64,256,128]{2,1,0:T(8,128)(2,1)S(1)}, bf16[64,256,128]{2,1,0:T(8,128)(2,1)}, u32[]{:S(2)}) copy-start(bf16[64,256,128]{2,1,0:T(8,128)(2,1)} %gather_fusion.1) | copy-start | bytes 12582916 | tf_op jit(solution)/shard_map/while
  156.5 60.1 %all-to-all-start.1 = ((bf16[256,32,128]{2,1,0:T(8,128)(2,1)}), bf16[256,32,128]{2,1,0:T(8,128)(2,1)}, u32[]{:S(2)}, u32[]{:S(2)}) async-start(bf16[256,32,128]{2,1,0:T(8,128)(2,1)} %bitcast.18), calls=%async_computation.1 | async-start | bytes 4194304 | tf_op jit(solution)/shard_map/all_to_all | solution.py:163
  167.2 4.2 %copy-start.2 = (bf16[64,256,128]{2,1,0:T(8,128)(2,1)S(1)}, bf16[64,256,128]{2,1,0:T(8,128)(2,1)}, u32[]{:S(2)}) copy-start(bf16[64,256,128]{2,1,0:T(8,128)(2,1)} %gather_fusion) | copy-start | bytes 12582916 | tf_op jit(solution)/shard_map/while
  175.9 4.2 %copy-start.2 = (bf16[64,256,128]{2,1,0:T(8,128)(2,1)S(1)}, bf16[64,256,128]{2,1,0:T(8,128)(2,1)}, u32[]{:S(2)}) copy-start(bf16[64,256,128]{2,1,0:T(8,128)(2,1)} %gather_fusion) | copy-start | bytes 12582916 | tf_op jit(solution)/shard_map/while
  184.5 4.2 %copy-start.2 = (bf16[64,256,128]{2,1,0:T(8,128)(2,1)S(1)}, bf16[64,256,128]{2,1,0:T(8,128)(2,1)}, u32[]{:S(2)}) copy-start(bf16[64,256,128]{2,1,0:T(8,128)(2,1)} %gather_fusion) | copy-start | bytes 12582916 | tf_op jit(solution)/shard_map/while
  193.2 4.2 %copy-start.2 = (bf16[64,256,128]{2,1,0:T(8,128)(2,1)S(1)}, bf16[64,256,128]{2,1,0:T(8,128)(2,1)}, u32[]{:S(2)}) copy-start(bf16[64,256,128]{2,1,0:T(8,128)(2,1)} %gather_fusion) | copy-start | bytes 12582916 | tf_op jit(solution)/shard_map/while
  198.8 85.8 %copy-start.7 = (s32[8,16]{1,0:T(8,128)S(1)}, s32[8,16]{1,0:T(8,128)}, u32[]{:S(2)}) copy-start(s32[8,16]{1,0:T(8,128)} %param.14) | copy-start | bytes 1540
  290.2 1.1 copy-start.5

commit v11 on v7

--- a/solution.py
+++ b/solution.py
@@ -104,17 +104,16 @@
     before = jnp.sum(same_target & earlier, axis=1)
     slot_index = target * slot_cap + before
     pair_of_slot = jnp.zeros((slot_total,), jnp.int32).at[slot_index].set(positions)
-    outgoing = jnp.take(query_send, pair_of_slot // list_len, axis=0)
-    labels = jnp.take(local_row, pair_of_slot, axis=0).astype(jnp.bfloat16)
+    slot_owner = (pair_of_slot // list_len).reshape(device_total, slot_cap)
+    labels = jnp.take(local_row, pair_of_slot, axis=0, mode="clip").astype(jnp.bfloat16)
     both_axes = ("group", "dev")
-    outgoing = outgoing.reshape(device_total, slot_cap, query_len, feat_width)
     labels = labels.reshape(device_total, slot_cap)
     tags = exchange(widen(labels, feat_width), dev_count, 0)[:, :slot_cap].astype(jnp.int32)
     block_rows = 64
 
     def score_block(inputs):
         query_block, tag_block = inputs
-        passage_block = jnp.take(passage_unit, tag_block, axis=0)
+        passage_block = jnp.take(passage_unit, tag_block, axis=0, mode="clip")
         logits = (
             jnp.einsum(
                 "bqe,bpe->bqp", query_block, passage_block, preferred_element_type=jnp.float32
@@ -133,9 +132,8 @@
     returned = []
     scores = []
     for slot in range(slot_cap):
-        arrived = lax.all_to_all(
-            outgoing[:, slot], both_axes, split_axis=0, concat_axis=0, tiled=True
-        )
+        outgoing = jnp.take(query_send, slot_owner[:, slot], axis=0, mode="clip")
+        arrived = lax.all_to_all(outgoing, both_axes, split_axis=0, concat_axis=0, tiled=True)
         blocks = device_total // block_rows
         pulled, score = lax.map(
             score_block,
@@ -150,13 +148,13 @@
     scores = jnp.stack(scores, axis=1)
     scores, returned[-1] = lax.optimization_barrier((scores, returned[-1]))
     scores_flat = exchange(widen(scores, feat_width), dev_count, 1)[:, :slot_cap]
-    pair_score = jnp.take(scores_flat.reshape(slot_total), slot_index, axis=0).reshape(
+    pair_score = jnp.take(scores_flat.reshape(slot_total), slot_index, axis=0, mode="clip").reshape(
         query_count, list_len
     )
-    pair_pulled = jnp.take(returned[0], target, axis=0)
+    pair_pulled = jnp.take(returned[0], target, axis=0, mode="clip")
     for slot in range(1, slot_cap):
         pair_pulled = jnp.where(
-            (before == slot)[:, None, None], jnp.take(returned[slot], target, axis=0), pair_pulled
+            (before == slot)[:, None, None], jnp.take(returned[slot], target, axis=0, mode="clip"), pair_pulled
         )
     pair_pulled = pair_pulled.reshape(query_count, list_len, query_len, feat_width)
     exp_scores = jnp.exp(pair_score)

time: 288 us -> 288 us (level)
  matrix products: 49 us -> 46.1 us
  transfers between devices with their start and end apart: 4 -> 4, of which waited for: 2 -> 2; matrix products, arithmetic and copies ran while one was open for 31% -> 32% of each run, Pallas kernels for 38% -> 38%
where the time goes in v11:
time: 288 us; the launch traced here: 285 us
  Pallas kernels  110 us (38%)
  local copies, waits for them, and re-layouts  49.1 us (17%)
  matrix products  46.1 us (16%)
  starting transfers between devices  34.7 us (12%)
  waiting for transfers between devices  31.9 us (11%)
  other arithmetic  12.3 us (4%)
    pallas_call x2, Pallas kernels, exchange(): pl.pallas_call(functools.partial(exchange_kernel, dev_count), out_shape=j...  110 us
    dot_general x8, matrix products, score_block(): jnp.einsum('bqe,bpe->bqp', query_block, passage_block, preferred_element_...  32.3 us
    gather x8, local copies, waits for them, and re-layouts, score_block(): passage_block = jnp.take(passage_unit, tag_block, axis=0, mode='clip')  24.1 us
    all_to_all x2, starting transfers between devices, local(): lax.all_to_all(outgoing, both_axes, split_axis=0, concat_axis=0, tiled=True)  21.1 us
    all_to_all x2, waiting for transfers between devices, local(): lax.all_to_all(outgoing, both_axes, split_axis=0, concat_axis=0, tiled=True)  16.1 us
    all_to_all x2, waiting for transfers between devices, local(): lax.all_to_all(pulled, both_axes, split_axis=0, concat_axis=0, tiled=True)  15.8 us
    all_to_all x2, starting transfers between devices, local(): lax.all_to_all(pulled, both_axes, split_axis=0, concat_axis=0, tiled=True)  13.6 us
    dot_general x8, matrix products, score_block(): jnp.einsum('bqp,bpe->bqe', attention, passage_block, preferred_element_ty...  13.4 us
  transfers between devices with their start and end apart: 4, of which 2 were waited for; matrix products, arithmetic and copies ran while one was open for 32% of the time, Pallas kernels for 38%

profile of v11, /device:TPU:8, one launch (start us, length us, event | category | flops | bytes accessed | tf_op | source)
XLA Modules:
  0.0 284.9 jit_solution(8276942834177626002)
XLA Ops:
  6.9 2.2 gather_fusion.5
  9.1 14.6 %all-to-all-start.1 = ((bf16[256,32,128]{2,1,0:T(8,128)(2,1)}), bf16[256,32,128]{2,1,0:T(8,128)(2,1)S(1)}, u32[]{:S(2)}, u32[]{:S(2)}) async-start(bf16[256,32,128]{2,1,0:T(8,128)(2,1)} %gather_fusion.5), calls=%async_computation.1 | async-start | bytes 4194304 | tf_op jit(solution)/shard_map/all_to_all | solution.py:136
  23.7 3.3 %gather_fusion.4 = s32[512]{0:T(512)S(1)} fusion(s32[128]{0:T(128)S(1)} %get-tuple-element.106, s32[1024]{0:T(1024)S(1)} %pad_clamp_fusion.5), kind=kCustom, calls=%fused_computation.4 | custom fusion | bytes 6144 | tf_op jit(solution)/shard_map/jit(_take)/gather | solution.py:108
  28.0 53.3 %shard_map.59 = f32[256,128]{1,0:T(8,128)} custom-call(f32[256,128]{1,0:T(8,128)} %pad_convert_fusion.rows_ref), custom_call_target="tpu_custom_call" | custom-call | tf_op jit(solution)/shard_map/pallas_call | solution.py:67
  82.5 2.2 gather_fusion.3
  84.8 1.8 fusion.23
  89.7 6.5 %all-to-all-start = ((bf16[256,32,128]{2,1,0:T(8,128)(2,1)}), bf16[256,32,128]{2,1,0:T(8,128)(2,1)S(1)}, u32[]{:S(2)}, u32[]{:S(2)}) async-start(bf16[256,32,128]{2,1,0:T(8,128)(2,1)} %gather_fusion.3), calls=%async_computation | async-start | bytes 4194304 | tf_op jit(solution)/shard_map/all_to_all | solution.py:136
  98.0 36.0 %while.25 = (s32[]{:T(128)}, bf16[4,64,32,128]{3,2,1,0:T(8,128)(2,1)}, f32[4,64]{1,0:T(4,128)S(1)}, bf16[4,64,32,128]{3,2,1,0:T(8,128)(2,1)}, s32[4,64]{1,0:T(4,...) while((s32[]{:T(128)}, bf16[4,64,32,128]{3,2,1,0:T(8,128)(2,1)}, ...), condition=%wide.region_11.12_spmd, body=%wide.region_8.11_spmd.sunk | while | flops 271322048 | bytes 38828920 | solution.py:138
  98.0 3.0 %gather_fusion.1 = bf16[64,256,128]{2,1,0:T(8,128)(2,1)} fusion(bf16[16,256,128]{2,1,0:T(8,128)(2,1)S(1)} %get-tuple-element.215, s32[1024]{0:T(1024)S(1)} %pad_clamp_fusion.11), kind=kCustom, calls=%fused_computation.1.clone.1 | custom fusion | bytes 8388864 | tf_op jit(solution)/shard_map/while/body/eval_jaxpr/jit(_take)/gather | solution.py:116
  101.0 4.1 %fusion.67 = (f32[64,32]{1,0:T(8,128)S(1)}, f32[64,32,256]{2,1,0:T(8,128)S(1)}) fusion(bf16[64,256,128]{2,1,0:T(8,128)(2,1)} %gather_fusion.1, bf16[4,64,32,128]{3,2,1,0:T(8,128)(2,1)} %get-tuple-element.213, s32[]{:T(128)} %get-tuple-element.202), kind=kOutput, calls=%fused_computation.29.clone.1 | convolution fusion | flops 135264256 | bytes 6824448 | tf_op jit(solution)/shard_map/while/body/eval_jaxpr/bqe,bpe->bqp/dot_general | solution.py:118
  107.0 3.0 %gather_fusion.1 = bf16[64,256,128]{2,1,0:T(8,128)(2,1)} fusion(bf16[16,256,128]{2,1,0:T(8,128)(2,1)S(1)} %get-tuple-element.215, s32[1024]{0:T(1024)S(1)} %pad_clamp_fusion.11), kind=kCustom, calls=%fused_computation.1.clone.1 | custom fusion | bytes 8388864 | tf_op jit(solution)/shard_map/while/body/eval_jaxpr/jit(_take)/gather | solution.py:116
  110.0 4.1 %fusion.67 = (f32[64,32]{1,0:T(8,128)S(1)}, f32[64,32,256]{2,1,0:T(8,128)S(1)}) fusion(bf16[64,256,128]{2,1,0:T(8,128)(2,1)} %gather_fusion.1, bf16[4,64,32,128]{3,2,1,0:T(8,128)(2,1)} %get-tuple-element.213, s32[]{:T(128)} %get-tuple-element.202), kind=kOutput, calls=%fused_computation.29.clone.1 | convolution fusion | flops 135264256 | bytes 6824448 | tf_op jit(solution)/shard_map/while/body/eval_jaxpr/bqe,bpe->bqp/dot_general | solution.py:118
  116.0 3.0 %gather_fusion.1 = bf16[64,256,128]{2,1,0:T(8,128)(2,1)} fusion(bf16[16,256,128]{2,1,0:T(8,128)(2,1)S(1)} %get-tuple-element.215, s32[1024]{0:T(1024)S(1)} %pad_clamp_fusion.11), kind=kCustom, calls=%fused_computation.1.clone.1 | custom fusion | bytes 8388864 | tf_op jit(solution)/shard_map/while/body/eval_jaxpr/jit(_take)/gather | solution.py:116
  119.1 4.1 %fusion.67 = (f32[64,32]{1,0:T(8,128)S(1)}, f32[64,32,256]{2,1,0:T(8,128)S(1)}) fusion(bf16[64,256,128]{2,1,0:T(8,128)(2,1)} %gather_fusion.1, bf16[4,64,32,128]{3,2,1,0:T(8,128)(2,1)} %get-tuple-element.213, s32[]{:T(128)} %get-tuple-element.202), kind=kOutput, calls=%fused_computation.29.clone.1 | convolution fusion | flops 135264256 | bytes 6824448 | tf_op jit(solution)/shard_map/while/body/eval_jaxpr/bqe,bpe->bqp/dot_general | solution.py:118
  125.0 3.0 %gather_fusion.1 = bf16[64,256,128]{2,1,0:T(8,128)(2,1)} fusion(bf16[16,256,128]{2,1,0:T(8,128)(2,1)S(1)} %get-tuple-element.215, s32[1024]{0:T(1024)S(1)} %pad_clamp_fusion.11), kind=kCustom, calls=%fused_computation.1.clone.1 | custom fusion | bytes 8388864 | tf_op jit(solution)/shard_map/while/body/eval_jaxpr/jit(_take)/gather | solution.py:116
  128.0 4.1 %fusion.67 = (f32[64,32]{1,0:T(8,128)S(1)}, f32[64,32,256]{2,1,0:T(8,128)S(1)}) fusion(bf16[64,256,128]{2,1,0:T(8,128)(2,1)} %gather_fusion.1, bf16[4,64,32,128]{3,2,1,0:T(8,128)(2,1)} %get-tuple-element.213, s32[]{:T(128)} %get-tuple-element.202), kind=kOutput, calls=%fused_computation.29.clone.1 | convolution fusion | flops 135264256 | bytes 6824448 | tf_op jit(solution)/shard_map/while/body/eval_jaxpr/bqe,bpe->bqp/dot_general | solution.py:118
  134.0 16.1 %all-to-all-done = bf16[256,32,128]{2,1,0:T(8,128)(2,1)S(1)} async-done(((bf16[256,32,128]{2,1,0:T(8,128)(2,1)}), bf16[256,32,128]{2,1,0:T(8,128)(2,1)S(1)}, u32[]{:S(2)}, u32[]{:S(2)}) %all-to-all-start) | async-done | bytes 2097184 | tf_op jit(solution)/shard_map/all_to_all | solution.py:136
  150.0 7.3 %all-to-all-start.2 = ((bf16[256,32,128]{2,1,0:T(8,128)(2,1)}), bf16[256,32,128]{2,1,0:T(8,128)(2,1)}, u32[]{:S(2)}, u32[]{:S(2)}) async-start(bf16[256,32,128]{2,1,0:T(8,128)(2,1)} %bitcast.86), calls=%async_computation.2 | async-start | bytes 4194304 | tf_op jit(solution)/shard_map/all_to_all | solution.py:146
  159.0 35.3 %while.24 = (s32[]{:T(128)}, bf16[4,64,32,128]{3,2,1,0:T(8,128)(2,1)}, f32[4,64]{1,0:T(4,128)S(1)}, bf16[4,64,32,128]{3,2,1,0:T(8,128)(2,1)S(1)}, s32[4,64]{1,0:...) while((s32[]{:T(128)}, bf16[4,64,32,128]{3,2,1,0:T(8,128)(2,1)}, ...), condition=%wide.region_7.8_spmd, body=%wide.region_4.7_spmd.sunk | while | flops 271322048 | bytes 38828412 | solution.py:138
  159.0 3.0 %gather_fusion = bf16[64,256,128]{2,1,0:T(8,128)(2,1)} fusion(bf16[16,256,128]{2,1,0:T(8,128)(2,1)S(1)} %get-tuple-element.239, s32[1024]{0:T(1024)S(1)} %pad_clamp_fusion.10), kind=kCustom, calls=%fused_computation.clone.1 | custom fusion | bytes 8388864 | tf_op jit(solution)/shard_map/while/body/eval_jaxpr/jit(_take)/gather | solution.py:116
  162.0 4.0 %fusion.62 = (f32[64,32]{1,0:T(8,128)S(1)}, f32[64,32,256]{2,1,0:T(8,128)S(1)}) fusion(bf16[64,256,128]{2,1,0:T(8,128)(2,1)} %gather_fusion, bf16[4,64,32,128]{3,2,1,0:T(8,128)(2,1)S(1)} %get-tuple-element.237, s32[]{:T(128)} %get-tuple-element.226), kind=kOutput, calls=%fused_computation.12.clone.1 | convolution fusion | flops 135264256 | bytes 6823940 | tf_op jit(solution)/shard_map/while/body/eval_jaxpr/bqe,bpe->bqp/dot_general | solution.py:118
  167.8 3.0 %gather_fusion = bf16[64,256,128]{2,1,0:T(8,128)(2,1)} fusion(bf16[16,256,128]{2,1,0:T(8,128)(2,1)S(1)} %get-tuple-element.239, s32[1024]{0:T(1024)S(1)} %pad_clamp_fusion.10), kind=kCustom, calls=%fused_computation.clone.1 | custom fusion | bytes 8388864 | tf_op jit(solution)/shard_map/while/body/eval_jaxpr/jit(_take)/gather | solution.py:116
  170.8 4.0 %fusion.62 = (f32[64,32]{1,0:T(8,128)S(1)}, f32[64,32,256]{2,1,0:T(8,128)S(1)}) fusion(bf16[64,256,128]{2,1,0:T(8,128)(2,1)} %gather_fusion, bf16[4,64,32,128]{3,2,1,0:T(8,128)(2,1)S(1)} %get-tuple-element.237, s32[]{:T(128)} %get-tuple-element.226), kind=kOutput, calls=%fused_computation.12.clone.1 | convolution fusion | flops 135264256 | bytes 6823940 | tf_op jit(solution)/shard_map/while/body/eval_jaxpr/bqe,bpe->bqp/dot_general | solution.py:118
  176.7 3.0 %gather_fusion = bf16[64,256,128]{2,1,0:T(8,128)(2,1)} fusion(bf16[16,256,128]{2,1,0:T(8,128)(2,1)S(1)} %get-tuple-element.239, s32[1024]{0:T(1024)S(1)} %pad_clamp_fusion.10), kind=kCustom, calls=%fused_computation.clone.1 | custom fusion | bytes 8388864 | tf_op jit(solution)/shard_map/while/body/eval_jaxpr/jit(_take)/gather | solution.py:116
  179.7 4.0 %fusion.62 = (f32[64,32]{1,0:T(8,128)S(1)}, f32[64,32,256]{2,1,0:T(8,128)S(1)}) fusion(bf16[64,256,128]{2,1,0:T(8,128)(2,1)} %gather_fusion, bf16[4,64,32,128]{3,2,1,0:T(8,128)(2,1)S(1)} %get-tuple-element.237, s32[]{:T(128)} %get-tuple-element.226), kind=kOutput, calls=%fused_computation.12.clone.1 | convolution fusion | flops 135264256 | bytes 6823940 | tf_op jit(solution)/shard_map/while/body/eval_jaxpr/bqe,bpe->bqp/dot_general | solution.py:118
  185.5 3.0 %gather_fusion = bf16[64,256,128]{2,1,0:T(8,128)(2,1)} fusion(bf16[16,256,128]{2,1,0:T(8,128)(2,1)S(1)} %get-tuple-element.239, s32[1024]{0:T(1024)S(1)} %pad_clamp_fusion.10), kind=kCustom, calls=%fused_computation.clone.1 | custom fusion | bytes 8388864 | tf_op jit(solution)/shard_map/while/body/eval_jaxpr/jit(_take)/gather | solution.py:116
  188.5 4.0 %fusion.62 = (f32[64,32]{1,0:T(8,128)S(1)}, f32[64,32,256]{2,1,0:T(8,128)S(1)}) fusion(bf16[64,256,128]{2,1,0:T(8,128)(2,1)} %gather_fusion, bf16[4,64,32,128]{3,2,1,0:T(8,128)(2,1)S(1)} %get-tuple-element.237, s32[]{:T(128)} %get-tuple-element.226), kind=kOutput, calls=%fused_computation.12.clone.1 | convolution fusion | flops 135264256 | bytes 6823940 | tf_op jit(solution)/shard_map/while/body/eval_jaxpr/bqe,bpe->bqp/dot_general | solution.py:118
  194.3 15.8 %all-to-all-done.2 = bf16[256,32,128]{2,1,0:T(8,128)(2,1)} async-done(((bf16[256,32,128]{2,1,0:T(8,128)(2,1)}), bf16[256,32,128]{2,1,0:T(8,128)(2,1)}, u32[]{:S(2)}, u32[]{:S(2)}) %all-to-all-start.2) | async-done | bytes 2097184 | tf_op jit(solution)/shard_map/all_to_all | solution.py:146
  210.1 6.3 %all-to-all-start.3 = ((bf16[256,32,128]{2,1,0:T(8,128)(2,1)}), bf16[256,32,128]{2,1,0:T(8,128)(2,1)S(1)}, u32[]{:S(2)}, u32[]{:S(2)}) async-start(bf16[256,32,128]{2,1,0:T(8,128)(2,1)} %bitcast.85), calls=%async_computation.3 | async-start | bytes 4194304 | tf_op jit(solution)/shard_map/all_to_all | solution.py:146
  217.5 56.4 %shard_map.60 = f32[256,128]{1,0:T(8,128)} custom-call(f32[256,128]{1,0:T(8,128)} %pad.11.rows_ref), custom_call_target="tpu_custom_call" | custom-call | tf_op jit(solution)/shard_map/pallas_call | solution.py:67
  276.3 2.4 gather_fusion.7
  282.6 1.8 fusion.27
  (118 shorter events, 37.4 us)
Async XLA Ops:
  0.6 1.6 copy-start
  9.1 79.3 %all-to-all-start.1 = ((bf16[256,32,128]{2,1,0:T(8,128)(2,1)}), bf16[256,32,128]{2,1,0:T(8,128)(2,1)S(1)}, u32[]{:S(2)}, u32[]{:S(2)}) async-start(bf16[256,32,128]{2,1,0:T(8,128)(2,1)} %gather_fusion.5), calls=%async_computation.1 | async-start | bytes 4194304 | tf_op jit(solution)/shard_map/all_to_all | solution.py:136
  88.4 1.3 copy-start.3
  89.7 60.3 %all-to-all-start = ((bf16[256,32,128]{2,1,0:T(8,128)(2,1)}), bf16[256,32,128]{2,1,0:T(8,128)(2,1)S(1)}, u32[]{:S(2)}, u32[]{:S(2)}) async-start(bf16[256,32,128]{2,1,0:T(8,128)(2,1)} %gather_fusion.3), calls=%async_computation | async-start | bytes 4194304 | tf_op jit(solution)/shard_map/all_to_all | solution.py:136
  101.0 4.1 %copy-start.1 = (bf16[64,256,128]{2,1,0:T(8,128)(2,1)S(1)}, bf16[64,256,128]{2,1,0:T(8,128)(2,1)}, u32[]{:S(2)}) copy-start(bf16[64,256,128]{2,1,0:T(8,128)(2,1)} %gather_fusion.1) | copy-start | bytes 12582916 | tf_op jit(solution)/shard_map/while
  110.0 4.1 %copy-start.1 = (bf16[64,256,128]{2,1,0:T(8,128)(2,1)S(1)}, bf16[64,256,128]{2,1,0:T(8,128)(2,1)}, u32[]{:S(2)}) copy-start(bf16[64,256,128]{2,1,0:T(8,128)(2,1)} %gather_fusion.1) | copy-start | bytes 12582916 | tf_op jit(solution)/shard_map/while
  119.1 4.1 %copy-start.1 = (bf16[64,256,128]{2,1,0:T(8,128)(2,1)S(1)}, bf16[64,256,128]{2,1,0:T(8,128)(2,1)}, u32[]{:S(2)}) copy-start(bf16[64,256,128]{2,1,0:T(8,128)(2,1)} %gather_fusion.1) | copy-start | bytes 12582916 | tf_op jit(solution)/shard_map/while
  128.0 4.1 %copy-start.1 = (bf16[64,256,128]{2,1,0:T(8,128)(2,1)S(1)}, bf16[64,256,128]{2,1,0:T(8,128)(2,1)}, u32[]{:S(2)}) copy-start(bf16[64,256,128]{2,1,0:T(8,128)(2,1)} %gather_fusion.1) | copy-start | bytes 12582916 | tf_op jit(solution)/shard_map/while
  150.0 60.1 %all-to-all-start.2 = ((bf16[256,32,128]{2,1,0:T(8,128)(2,1)}), bf16[256,32,128]{2,1,0:T(8,128)(2,1)}, u32[]{:S(2)}, u32[]{:S(2)}) async-start(bf16[256,32,128]{2,1,0:T(8,128)(2,1)} %bitcast.86), calls=%async_computation.2 | async-start | bytes 4194304 | tf_op jit(solution)/shard_map/all_to_all | solution.py:146
  162.0 4.0 %copy-start.2 = (bf16[64,256,128]{2,1,0:T(8,128)(2,1)S(1)}, bf16[64,256,128]{2,1,0:T(8,128)(2,1)}, u32[]{:S(2)}) copy-start(bf16[64,256,128]{2,1,0:T(8,128)(2,1)} %gather_fusion) | copy-start | bytes 12582916 | tf_op jit(solution)/shard_map/while
  170.8 4.0 %copy-start.2 = (bf16[64,256,128]{2,1,0:T(8,128)(2,1)S(1)}, bf16[64,256,128]{2,1,0:T(8,128)(2,1)}, u32[]{:S(2)}) copy-start(bf16[64,256,128]{2,1,0:T(8,128)(2,1)} %gather_fusion) | copy-start | bytes 12582916 | tf_op jit(solution)/shard_map/while
  179.7 4.0 %copy-start.2 = (bf16[64,256,128]{2,1,0:T(8,128)(2,1)S(1)}, bf16[64,256,128]{2,1,0:T(8,128)(2,1)}, u32[]{:S(2)}) copy-start(bf16[64,256,128]{2,1,0:T(8,128)(2,1)} %gather_fusion) | copy-start | bytes 12582916 | tf_op jit(solution)/shard_map/while
  188.5 4.0 %copy-start.2 = (bf16[64,256,128]{2,1,0:T(8,128)(2,1)S(1)}, bf16[64,256,128]{2,1,0:T(8,128)(2,1)}, u32[]{:S(2)}) copy-start(bf16[64,256,128]{2,1,0:T(8,128)(2,1)} %gather_fusion) | copy-start | bytes 12582916 | tf_op jit(solution)/shard_map/while
  210.1 68.9 %all-to-all-start.3 = ((bf16[256,32,128]{2,1,0:T(8,128)(2,1)}), bf16[256,32,128]{2,1,0:T(8,128)(2,1)S(1)}, u32[]{:S(2)}, u32[]{:S(2)}) async-start(bf16[256,32,128]{2,1,0:T(8,128)(2,1)} %bitcast.85), calls=%async_computation.3 | async-start | bytes 4194304 | tf_op jit(solution)/shard_map/all_to_all | solution.py:146
  280.7 1.9 copy-start.4

commit v12 on v11

--- a/solution.py
+++ b/solution.py
@@ -131,6 +131,7 @@
 
     returned = []
     scores = []
+    pulled_parts = []
     for slot in range(slot_cap):
         outgoing = jnp.take(query_send, slot_owner[:, slot], axis=0, mode="clip")
         arrived = lax.all_to_all(outgoing, both_axes, split_axis=0, concat_axis=0, tiled=True)
@@ -142,27 +143,36 @@
                 tags[:, slot].reshape(blocks, block_rows),
             ),
         )
-        pulled = pulled.reshape(device_total, query_len, feat_width)
-        returned.append(lax.all_to_all(pulled, both_axes, split_axis=0, concat_axis=0, tiled=True))
+        pulled_parts.append(pulled.reshape(device_total, query_len, feat_width))
         scores.append(score.reshape(device_total))
+        if slot < slot_cap - 1:
+            returned.append(
+                lax.all_to_all(
+                    pulled_parts[-1], both_axes, split_axis=0, concat_axis=0, tiled=True
+                )
+            )
+    returned.append(
+        lax.all_to_all(pulled_parts[-1], both_axes, split_axis=0, concat_axis=0, tiled=True)
+    )
     scores = jnp.stack(scores, axis=1)
-    scores, returned[-1] = lax.optimization_barrier((scores, returned[-1]))
     scores_flat = exchange(widen(scores, feat_width), dev_count, 1)[:, :slot_cap]
     pair_score = jnp.take(scores_flat.reshape(slot_total), slot_index, axis=0, mode="clip").reshape(
         query_count, list_len
     )
-    pair_pulled = jnp.take(returned[0], target, axis=0, mode="clip")
-    for slot in range(1, slot_cap):
-        pair_pulled = jnp.where(
-            (before == slot)[:, None, None], jnp.take(returned[slot], target, axis=0, mode="clip"), pair_pulled
-        )
-    pair_pulled = pair_pulled.reshape(query_count, list_len, query_len, feat_width)
     exp_scores = jnp.exp(pair_score)
     total = jnp.sum(exp_scores, axis=-1, keepdims=True)
     loss = jnp.log(total[:, 0]) - pair_score[:, 0]
     first = (jnp.arange(list_len) == 0).astype(jnp.float32)
     coeff = exp_scores / total - first[None, :]
-    unit_grad = jnp.einsum("bk,bkqe->bqe", coeff, pair_pulled.astype(jnp.float32))
+    slot_of_pair = before.reshape(query_count, list_len)
+    unit_grad = None
+    for slot in range(slot_cap):
+        part = jnp.take(returned[slot], target, axis=0, mode="clip").reshape(
+            query_count, list_len, query_len, feat_width
+        )
+        weight = jnp.where(slot_of_pair == slot, coeff, 0.0)
+        term = jnp.einsum("bk,bkqe->bqe", weight, part.astype(jnp.float32))
+        unit_grad = term if unit_grad is None else unit_grad + term
     along = jnp.sum(query_unit * unit_grad, axis=-1, keepdims=True)
     query_grad = (unit_grad - query_unit * along) * query_scale
     return (loss, query_grad)

time: 288 us -> 286 us (level)
  transfers between devices with their start and end apart: 4 -> 4, of which waited for: 2 -> 2; matrix products, arithmetic and copies ran while one was open for 32% -> 33% of each run, Pallas kernels for 38% -> 39%
where the time goes in v12:
time: 286 us; the launch traced here: 283 us
  Pallas kernels  110 us (38%)
  local copies, waits for them, and re-layouts  48.3 us (17%)
  matrix products  46.5 us (16%)
  starting transfers between devices  34.7 us (12%)
  waiting for transfers between devices  31.9 us (11%)
  other arithmetic  10.9 us (4%)
    pallas_call x2, Pallas kernels, exchange(): pl.pallas_call(functools.partial(exchange_kernel, dev_count), out_shape=j...  110 us
    dot_general x8, matrix products, score_block(): jnp.einsum('bqe,bpe->bqp', query_block, passage_block, preferred_element_...  32.3 us
    gather x8, local copies, waits for them, and re-layouts, score_block(): passage_block = jnp.take(passage_unit, tag_block, axis=0, mode='clip')  24.1 us
    all_to_all x2, starting transfers between devices, local(): lax.all_to_all(outgoing, both_axes, split_axis=0, concat_axis=0, tiled=True)  21.1 us
    all_to_all x2, waiting for transfers between devices, local(): lax.all_to_all(outgoing, both_axes, split_axis=0, concat_axis=0, tiled=True)  16 us
    all_to_all x2, waiting for transfers between devices, local(): lax.all_to_all(pulled_parts[-1], both_axes, split_axis=0, concat_axis=0,...  15.8 us
    all_to_all x2, starting transfers between devices, local(): lax.all_to_all(pulled_parts[-1], both_axes, split_axis=0, concat_axis=0,...  13.6 us
    dot_general x8, matrix products, score_block(): jnp.einsum('bqp,bpe->bqe', attention, passage_block, preferred_element_ty...  13.4 us
  transfers between devices with their start and end apart: 4, of which 2 were waited for; matrix products, arithmetic and copies ran while one was open for 33% of the time, Pallas kernels for 39%

profile of v12, /device:TPU:8, one launch (start us, length us, event | category | flops | bytes accessed | tf_op | source)
XLA Modules:
  0.0 283.0 jit_solution(3124064224844875862)
XLA Ops:
  6.9 2.2 gather_fusion.5
  9.1 14.6 %all-to-all-start.1 = ((bf16[256,32,128]{2,1,0:T(8,128)(2,1)}), bf16[256,32,128]{2,1,0:T(8,128)(2,1)S(1)}, u32[]{:S(2)}, u32[]{:S(2)}) async-start(bf16[256,32,128]{2,1,0:T(8,128)(2,1)} %gather_fusion.5), calls=%async_computation.1 | async-start | bytes 4194304 | tf_op jit(solution)/shard_map/all_to_all | solution.py:137
  23.8 3.3 %gather_fusion.4 = s32[512]{0:T(512)S(1)} fusion(s32[128]{0:T(128)S(1)} %get-tuple-element.102, s32[1024]{0:T(1024)S(1)} %pad_clamp_fusion.5), kind=kCustom, calls=%fused_computation.4 | custom fusion | bytes 6144 | tf_op jit(solution)/shard_map/jit(_take)/gather | solution.py:108
  28.0 53.3 %shard_map.59 = f32[256,128]{1,0:T(8,128)} custom-call(f32[256,128]{1,0:T(8,128)} %pad_convert_fusion.rows_ref), custom_call_target="tpu_custom_call" | custom-call | tf_op jit(solution)/shard_map/pallas_call | solution.py:67
  82.5 2.2 gather_fusion.3
  84.8 1.8 fusion.23
  89.7 6.5 %all-to-all-start = ((bf16[256,32,128]{2,1,0:T(8,128)(2,1)}), bf16[256,32,128]{2,1,0:T(8,128)(2,1)S(1)}, u32[]{:S(2)}, u32[]{:S(2)}) async-start(bf16[256,32,128]{2,1,0:T(8,128)(2,1)} %gather_fusion.3), calls=%async_computation | async-start | bytes 4194304 | tf_op jit(solution)/shard_map/all_to_all | solution.py:137
  98.0 36.0 %while.25 = (s32[]{:T(128)}, bf16[4,64,32,128]{3,2,1,0:T(8,128)(2,1)}, f32[4,64]{1,0:T(4,128)S(1)}, bf16[4,64,32,128]{3,2,1,0:T(8,128)(2,1)}, s32[4,64]{1,0:T(4,...) while((s32[]{:T(128)}, bf16[4,64,32,128]{3,2,1,0:T(8,128)(2,1)}, ...), condition=%wide.region_11.12_spmd, body=%wide.region_8.11_spmd.sunk | while | flops 271322048 | bytes 38828920 | solution.py:139
  98.0 3.0 %gather_fusion.1 = bf16[64,256,128]{2,1,0:T(8,128)(2,1)} fusion(bf16[16,256,128]{2,1,0:T(8,128)(2,1)S(1)} %get-tuple-element.215, s32[1024]{0:T(1024)S(1)} %pad_clamp_fusion.11), kind=kCustom, calls=%fused_computation.1.clone.1 | custom fusion | bytes 8388864 | tf_op jit(solution)/shard_map/while/body/eval_jaxpr/jit(_take)/gather | solution.py:116
  101.0 4.1 %fusion.71 = (f32[64,32]{1,0:T(8,128)S(1)}, f32[64,32,256]{2,1,0:T(8,128)S(1)}) fusion(bf16[64,256,128]{2,1,0:T(8,128)(2,1)} %gather_fusion.1, bf16[4,64,32,128]{3,2,1,0:T(8,128)(2,1)} %get-tuple-element.213, s32[]{:T(128)} %get-tuple-element.202), kind=kOutput, calls=%fused_computation.29.clone.1 | convolution fusion | flops 135264256 | bytes 6824448 | tf_op jit(solution)/shard_map/while/body/eval_jaxpr/bqe,bpe->bqp/dot_general | solution.py:118
  107.0 3.0 %gather_fusion.1 = bf16[64,256,128]{2,1,0:T(8,128)(2,1)} fusion(bf16[16,256,128]{2,1,0:T(8,128)(2,1)S(1)} %get-tuple-element.215, s32[1024]{0:T(1024)S(1)} %pad_clamp_fusion.11), kind=kCustom, calls=%fused_computation.1.clone.1 | custom fusion | bytes 8388864 | tf_op jit(solution)/shard_map/while/body/eval_jaxpr/jit(_take)/gather | solution.py:116
  110.0 4.1 %fusion.71 = (f32[64,32]{1,0:T(8,128)S(1)}, f32[64,32,256]{2,1,0:T(8,128)S(1)}) fusion(bf16[64,256,128]{2,1,0:T(8,128)(2,1)} %gather_fusion.1, bf16[4,64,32,128]{3,2,1,0:T(8,128)(2,1)} %get-tuple-element.213, s32[]{:T(128)} %get-tuple-element.202), kind=kOutput, calls=%fused_computation.29.clone.1 | convolution fusion | flops 135264256 | bytes 6824448 | tf_op jit(solution)/shard_map/while/body/eval_jaxpr/bqe,bpe->bqp/dot_general | solution.py:118
  116.1 3.0 %gather_fusion.1 = bf16[64,256,128]{2,1,0:T(8,128)(2,1)} fusion(bf16[16,256,128]{2,1,0:T(8,128)(2,1)S(1)} %get-tuple-element.215, s32[1024]{0:T(1024)S(1)} %pad_clamp_fusion.11), kind=kCustom, calls=%fused_computation.1.clone.1 | custom fusion | bytes 8388864 | tf_op jit(solution)/shard_map/while/body/eval_jaxpr/jit(_take)/gather | solution.py:116
  119.1 4.1 %fusion.71 = (f32[64,32]{1,0:T(8,128)S(1)}, f32[64,32,256]{2,1,0:T(8,128)S(1)}) fusion(bf16[64,256,128]{2,1,0:T(8,128)(2,1)} %gather_fusion.1, bf16[4,64,32,128]{3,2,1,0:T(8,128)(2,1)} %get-tuple-element.213, s32[]{:T(128)} %get-tuple-element.202), kind=kOutput, calls=%fused_computation.29.clone.1 | convolution fusion | flops 135264256 | bytes 6824448 | tf_op jit(solution)/shard_map/while/body/eval_jaxpr/bqe,bpe->bqp/dot_general | solution.py:118
  125.0 3.0 %gather_fusion.1 = bf16[64,256,128]{2,1,0:T(8,128)(2,1)} fusion(bf16[16,256,128]{2,1,0:T(8,128)(2,1)S(1)} %get-tuple-element.215, s32[1024]{0:T(1024)S(1)} %pad_clamp_fusion.11), kind=kCustom, calls=%fused_computation.1.clone.1 | custom fusion | bytes 8388864 | tf_op jit(solution)/shard_map/while/body/eval_jaxpr/jit(_take)/gather | solution.py:116
  128.0 4.1 %fusion.71 = (f32[64,32]{1,0:T(8,128)S(1)}, f32[64,32,256]{2,1,0:T(8,128)S(1)}) fusion(bf16[64,256,128]{2,1,0:T(8,128)(2,1)} %gather_fusion.1, bf16[4,64,32,128]{3,2,1,0:T(8,128)(2,1)} %get-tuple-element.213, s32[]{:T(128)} %get-tuple-element.202), kind=kOutput, calls=%fused_computation.29.clone.1 | convolution fusion | flops 135264256 | bytes 6824448 | tf_op jit(solution)/shard_map/while/body/eval_jaxpr/bqe,bpe->bqp/dot_general | solution.py:118
  134.0 16.0 %all-to-all-done = bf16[256,32,128]{2,1,0:T(8,128)(2,1)S(1)} async-done(((bf16[256,32,128]{2,1,0:T(8,128)(2,1)}), bf16[256,32,128]{2,1,0:T(8,128)(2,1)S(1)}, u32[]{:S(2)}, u32[]{:S(2)}) %all-to-all-start) | async-done | bytes 2097184 | tf_op jit(solution)/shard_map/all_to_all | solution.py:137
  150.0 7.3 %all-to-all-start.3 = ((bf16[256,32,128]{2,1,0:T(8,128)(2,1)}), bf16[256,32,128]{2,1,0:T(8,128)(2,1)}, u32[]{:S(2)}, u32[]{:S(2)}) async-start(bf16[256,32,128]{2,1,0:T(8,128)(2,1)} %bitcast.92), calls=%async_computation.3 | async-start | bytes 4194304 | tf_op jit(solution)/shard_map/all_to_all | solution.py:155
  159.0 35.3 %while.24 = (s32[]{:T(128)}, bf16[4,64,32,128]{3,2,1,0:T(8,128)(2,1)}, f32[4,64]{1,0:T(4,128)S(1)}, bf16[4,64,32,128]{3,2,1,0:T(8,128)(2,1)S(1)}, s32[4,64]{1,0:...) while((s32[]{:T(128)}, bf16[4,64,32,128]{3,2,1,0:T(8,128)(2,1)}, ...), condition=%wide.region_7.8_spmd, body=%wide.region_4.7_spmd.sunk | while | flops 271322048 | bytes 38828412 | solution.py:139
  159.0 3.0 %gather_fusion = bf16[64,256,128]{2,1,0:T(8,128)(2,1)} fusion(bf16[16,256,128]{2,1,0:T(8,128)(2,1)S(1)} %get-tuple-element.239, s32[1024]{0:T(1024)S(1)} %pad_clamp_fusion.10), kind=kCustom, calls=%fused_computation.clone.1 | custom fusion | bytes 8388864 | tf_op jit(solution)/shard_map/while/body/eval_jaxpr/jit(_take)/gather | solution.py:116
  162.0 4.0 %fusion.66 = (f32[64,32]{1,0:T(8,128)S(1)}, f32[64,32,256]{2,1,0:T(8,128)S(1)}) fusion(bf16[64,256,128]{2,1,0:T(8,128)(2,1)} %gather_fusion, bf16[4,64,32,128]{3,2,1,0:T(8,128)(2,1)S(1)} %get-tuple-element.237, s32[]{:T(128)} %get-tuple-element.226), kind=kOutput, calls=%fused_computation.12.clone.1 | convolution fusion | flops 135264256 | bytes 6823940 | tf_op jit(solution)/shard_map/while/body/eval_jaxpr/bqe,bpe->bqp/dot_general | solution.py:118
  167.8 3.0 %gather_fusion = bf16[64,256,128]{2,1,0:T(8,128)(2,1)} fusion(bf16[16,256,128]{2,1,0:T(8,128)(2,1)S(1)} %get-tuple-element.239, s32[1024]{0:T(1024)S(1)} %pad_clamp_fusion.10), kind=kCustom, calls=%fused_computation.clone.1 | custom fusion | bytes 8388864 | tf_op jit(solution)/shard_map/while/body/eval_jaxpr/jit(_take)/gather | solution.py:116
  170.9 4.0 %fusion.66 = (f32[64,32]{1,0:T(8,128)S(1)}, f32[64,32,256]{2,1,0:T(8,128)S(1)}) fusion(bf16[64,256,128]{2,1,0:T(8,128)(2,1)} %gather_fusion, bf16[4,64,32,128]{3,2,1,0:T(8,128)(2,1)S(1)} %get-tuple-element.237, s32[]{:T(128)} %get-tuple-element.226), kind=kOutput, calls=%fused_computation.12.clone.1 | convolution fusion | flops 135264256 | bytes 6823940 | tf_op jit(solution)/shard_map/while/body/eval_jaxpr/bqe,bpe->bqp/dot_general | solution.py:118
  176.7 3.0 %gather_fusion = bf16[64,256,128]{2,1,0:T(8,128)(2,1)} fusion(bf16[16,256,128]{2,1,0:T(8,128)(2,1)S(1)} %get-tuple-element.239, s32[1024]{0:T(1024)S(1)} %pad_clamp_fusion.10), kind=kCustom, calls=%fused_computation.clone.1 | custom fusion | bytes 8388864 | tf_op jit(solution)/shard_map/while/body/eval_jaxpr/jit(_take)/gather | solution.py:116
  179.7 4.0 %fusion.66 = (f32[64,32]{1,0:T(8,128)S(1)}, f32[64,32,256]{2,1,0:T(8,128)S(1)}) fusion(bf16[64,256,128]{2,1,0:T(8,128)(2,1)} %gather_fusion, bf16[4,64,32,128]{3,2,1,0:T(8,128)(2,1)S(1)} %get-tuple-element.237, s32[]{:T(128)} %get-tuple-element.226), kind=kOutput, calls=%fused_computation.12.clone.1 | convolution fusion | flops 135264256 | bytes 6823940 | tf_op jit(solution)/shard_map/while/body/eval_jaxpr/bqe,bpe->bqp/dot_general | solution.py:118
  185.5 3.0 %gather_fusion = bf16[64,256,128]{2,1,0:T(8,128)(2,1)} fusion(bf16[16,256,128]{2,1,0:T(8,128)(2,1)S(1)} %get-tuple-element.239, s32[1024]{0:T(1024)S(1)} %pad_clamp_fusion.10), kind=kCustom, calls=%fused_computation.clone.1 | custom fusion | bytes 8388864 | tf_op jit(solution)/shard_map/while/body/eval_jaxpr/jit(_take)/gather | solution.py:116
  188.5 4.0 %fusion.66 = (f32[64,32]{1,0:T(8,128)S(1)}, f32[64,32,256]{2,1,0:T(8,128)S(1)}) fusion(bf16[64,256,128]{2,1,0:T(8,128)(2,1)} %gather_fusion, bf16[4,64,32,128]{3,2,1,0:T(8,128)(2,1)S(1)} %get-tuple-element.237, s32[]{:T(128)} %get-tuple-element.226), kind=kOutput, calls=%fused_computation.12.clone.1 | convolution fusion | flops 135264256 | bytes 6823940 | tf_op jit(solution)/shard_map/while/body/eval_jaxpr/bqe,bpe->bqp/dot_general | solution.py:118
  194.3 15.8 %all-to-all-done.3 = bf16[256,32,128]{2,1,0:T(8,128)(2,1)} async-done(((bf16[256,32,128]{2,1,0:T(8,128)(2,1)}), bf16[256,32,128]{2,1,0:T(8,128)(2,1)}, u32[]{:S(2)}, u32[]{:S(2)}) %all-to-all-start.3) | async-done | bytes 2097184 | tf_op jit(solution)/shard_map/all_to_all | solution.py:155
  210.1 6.3 %all-to-all-start.2 = ((bf16[256,32,128]{2,1,0:T(8,128)(2,1)}), bf16[256,32,128]{2,1,0:T(8,128)(2,1)S(1)}, u32[]{:S(2)}, u32[]{:S(2)}) async-start(bf16[256,32,128]{2,1,0:T(8,128)(2,1)} %bitcast.91), calls=%async_computation.2 | async-start | bytes 4194304 | tf_op jit(solution)/shard_map/all_to_all | solution.py:150
  217.6 56.3 %shard_map.60 = f32[256,128]{1,0:T(8,128)} custom-call(f32[256,128]{1,0:T(8,128)} %pad.11.rows_ref), custom_call_target="tpu_custom_call" | custom-call | tf_op jit(solution)/shard_map/pallas_call | solution.py:67
  277.2 2.4 gather_fusion.8
  281.1 1.8 fusion.27
  (119 shorter events, 35.5 us)
Async XLA Ops:
  0.6 1.6 copy-start
  9.1 79.3 %all-to-all-start.1 = ((bf16[256,32,128]{2,1,0:T(8,128)(2,1)}), bf16[256,32,128]{2,1,0:T(8,128)(2,1)S(1)}, u32[]{:S(2)}, u32[]{:S(2)}) async-start(bf16[256,32,128]{2,1,0:T(8,128)(2,1)} %gather_fusion.5), calls=%async_computation.1 | async-start | bytes 4194304 | tf_op jit(solution)/shard_map/all_to_all | solution.py:137
  88.4 1.3 copy-start.3
  89.7 60.3 %all-to-all-start = ((bf16[256,32,128]{2,1,0:T(8,128)(2,1)}), bf16[256,32,128]{2,1,0:T(8,128)(2,1)S(1)}, u32[]{:S(2)}, u32[]{:S(2)}) async-start(bf16[256,32,128]{2,1,0:T(8,128)(2,1)} %gather_fusion.3), calls=%async_computation | async-start | bytes 4194304 | tf_op jit(solution)/shard_map/all_to_all | solution.py:137
  101.0 4.1 %copy-start.1 = (bf16[64,256,128]{2,1,0:T(8,128)(2,1)S(1)}, bf16[64,256,128]{2,1,0:T(8,128)(2,1)}, u32[]{:S(2)}) copy-start(bf16[64,256,128]{2,1,0:T(8,128)(2,1)} %gather_fusion.1) | copy-start | bytes 12582916 | tf_op jit(solution)/shard_map/while
  110.0 4.1 %copy-start.1 = (bf16[64,256,128]{2,1,0:T(8,128)(2,1)S(1)}, bf16[64,256,128]{2,1,0:T(8,128)(2,1)}, u32[]{:S(2)}) copy-start(bf16[64,256,128]{2,1,0:T(8,128)(2,1)} %gather_fusion.1) | copy-start | bytes 12582916 | tf_op jit(solution)/shard_map/while
  119.1 4.1 %copy-start.1 = (bf16[64,256,128]{2,1,0:T(8,128)(2,1)S(1)}, bf16[64,256,128]{2,1,0:T(8,128)(2,1)}, u32[]{:S(2)}) copy-start(bf16[64,256,128]{2,1,0:T(8,128)(2,1)} %gather_fusion.1) | copy-start | bytes 12582916 | tf_op jit(solution)/shard_map/while
  128.0 4.1 %copy-start.1 = (bf16[64,256,128]{2,1,0:T(8,128)(2,1)S(1)}, bf16[64,256,128]{2,1,0:T(8,128)(2,1)}, u32[]{:S(2)}) copy-start(bf16[64,256,128]{2,1,0:T(8,128)(2,1)} %gather_fusion.1) | copy-start | bytes 12582916 | tf_op jit(solution)/shard_map/while
  150.0 60.1 %all-to-all-start.3 = ((bf16[256,32,128]{2,1,0:T(8,128)(2,1)}), bf16[256,32,128]{2,1,0:T(8,128)(2,1)}, u32[]{:S(2)}, u32[]{:S(2)}) async-start(bf16[256,32,128]{2,1,0:T(8,128)(2,1)} %bitcast.92), calls=%async_computation.3 | async-start | bytes 4194304 | tf_op jit(solution)/shard_map/all_to_all | solution.py:155
  162.0 4.0 %copy-start.2 = (bf16[64,256,128]{2,1,0:T(8,128)(2,1)S(1)}, bf16[64,256,128]{2,1,0:T(8,128)(2,1)}, u32[]{:S(2)}) copy-start(bf16[64,256,128]{2,1,0:T(8,128)(2,1)} %gather_fusion) | copy-start | bytes 12582916 | tf_op jit(solution)/shard_map/while
  170.8 4.0 %copy-start.2 = (bf16[64,256,128]{2,1,0:T(8,128)(2,1)S(1)}, bf16[64,256,128]{2,1,0:T(8,128)(2,1)}, u32[]{:S(2)}) copy-start(bf16[64,256,128]{2,1,0:T(8,128)(2,1)} %gather_fusion) | copy-start | bytes 12582916 | tf_op jit(solution)/shard_map/while
  179.7 4.0 %copy-start.2 = (bf16[64,256,128]{2,1,0:T(8,128)(2,1)S(1)}, bf16[64,256,128]{2,1,0:T(8,128)(2,1)}, u32[]{:S(2)}) copy-start(bf16[64,256,128]{2,1,0:T(8,128)(2,1)} %gather_fusion) | copy-start | bytes 12582916 | tf_op jit(solution)/shard_map/while
  188.5 4.0 %copy-start.2 = (bf16[64,256,128]{2,1,0:T(8,128)(2,1)S(1)}, bf16[64,256,128]{2,1,0:T(8,128)(2,1)}, u32[]{:S(2)}) copy-start(bf16[64,256,128]{2,1,0:T(8,128)(2,1)} %gather_fusion) | copy-start | bytes 12582916 | tf_op jit(solution)/shard_map/while
  210.1 69.8 %all-to-all-start.2 = ((bf16[256,32,128]{2,1,0:T(8,128)(2,1)}), bf16[256,32,128]{2,1,0:T(8,128)(2,1)S(1)}, u32[]{:S(2)}, u32[]{:S(2)}) async-start(bf16[256,32,128]{2,1,0:T(8,128)(2,1)} %bitcast.91), calls=%async_computation.2 | async-start | bytes 4194304 | tf_op jit(solution)/shard_map/all_to_all | solution.py:150
  279.5 1.6 copy-start.4

commit v13 on v12

--- a/solution.py
+++ b/solution.py
@@ -155,6 +155,8 @@
         lax.all_to_all(pulled_parts[-1], both_axes, split_axis=0, concat_axis=0, tiled=True)
     )
     scores = jnp.stack(scores, axis=1)
+    first_part = jnp.take(returned[0], target, axis=0, mode="clip")
+    scores, first_part = lax.optimization_barrier((scores, first_part))
     scores_flat = exchange(widen(scores, feat_width), dev_count, 1)[:, :slot_cap]
     pair_score = jnp.take(scores_flat.reshape(slot_total), slot_index, axis=0, mode="clip").reshape(
         query_count, list_len
@@ -167,9 +169,11 @@
     slot_of_pair = before.reshape(query_count, list_len)
     unit_grad = None
     for slot in range(slot_cap):
-        part = jnp.take(returned[slot], target, axis=0, mode="clip").reshape(
-            query_count, list_len, query_len, feat_width
-        )
+        if slot == 0:
+            part = first_part
+        else:
+            part = jnp.take(returned[slot], target, axis=0, mode="clip")
+        part = part.reshape(query_count, list_len, query_len, feat_width)
         weight = jnp.where(slot_of_pair == slot, coeff, 0.0)
         term = jnp.einsum("bk,bkqe->bqe", weight, part.astype(jnp.float32))
         unit_grad = term if unit_grad is None else unit_grad + term

time: 286 us -> 285 us (level)
  Pallas kernels: 110 us -> 107 us
  transfers between devices with their start and end apart: 4 -> 4, of which waited for: 2 -> 2; matrix products, arithmetic and copies ran while one was open for 33% -> 33% of each run, Pallas kernels for 39% -> 38%
where the time goes in v13:
time: 285 us; the launch traced here: 283 us
  Pallas kernels  107 us (38%)
  local copies, waits for them, and re-layouts  49.2 us (17%)
  matrix products  47.7 us (17%)
  starting transfers between devices  34.7 us (12%)
  waiting for transfers between devices  31.9 us (11%)
  other arithmetic  10.9 us (4%)
    pallas_call x2, Pallas kernels, exchange(): pl.pallas_call(functools.partial(exchange_kernel, dev_count), out_shape=j...  107 us
    dot_general x8, matrix products, score_block(): jnp.einsum('bqe,bpe->bqp', query_block, passage_block, preferred_element_...  32.3 us
    gather x8, local copies, waits for them, and re-layouts, score_block(): passage_block = jnp.take(passage_unit, tag_block, axis=0, mode='clip')  24.1 us
    all_to_all x2, starting transfers between devices, local(): lax.all_to_all(outgoing, both_axes, split_axis=0, concat_axis=0, tiled=True)  21.1 us
    all_to_all x2, waiting for transfers between devices, local(): lax.all_to_all(outgoing, both_axes, split_axis=0, concat_axis=0, tiled=True)  16.1 us
    all_to_all x2, waiting for transfers between devices, local(): lax.all_to_all(pulled_parts[-1], both_axes, split_axis=0, concat_axis=0,...  15.8 us
    all_to_all x2, starting transfers between devices, local(): lax.all_to_all(pulled_parts[-1], both_axes, split_axis=0, concat_axis=0,...  13.6 us
    dot_general x8, matrix products, score_block(): jnp.einsum('bqp,bpe->bqe', attention, passage_block, preferred_element_ty...  13.4 us
  transfers between devices with their start and end apart: 4, of which 2 were waited for; matrix products, arithmetic and copies ran while one was open for 33% of the time, Pallas kernels for 38%

profile of v13, /device:TPU:8, one launch (start us, length us, event | category | flops | bytes accessed | tf_op | source)
XLA Modules:
  0.0 282.7 jit_solution(18218484891175851729)
XLA Ops:
  6.9 2.2 gather_fusion.3
  9.1 14.6 %all-to-all-start = ((bf16[256,32,128]{2,1,0:T(8,128)(2,1)}), bf16[256,32,128]{2,1,0:T(8,128)(2,1)S(1)}, u32[]{:S(2)}, u32[]{:S(2)}) async-start(bf16[256,32,128]{2,1,0:T(8,128)(2,1)} %gather_fusion.3), calls=%async_computation | async-start | bytes 4194304 | tf_op jit(solution)/shard_map/all_to_all | solution.py:137
  23.7 3.3 %gather_fusion.4 = s32[512]{0:T(512)S(1)} fusion(s32[128]{0:T(128)S(1)} %get-tuple-element.106, s32[1024]{0:T(1024)S(1)} %pad_clamp_fusion.5), kind=kCustom, calls=%fused_computation.4 | custom fusion | bytes 6144 | tf_op jit(solution)/shard_map/jit(_take)/gather | solution.py:108
  28.0 53.3 %shard_map.59 = f32[256,128]{1,0:T(8,128)} custom-call(f32[256,128]{1,0:T(8,128)} %pad_convert_fusion.rows_ref), custom_call_target="tpu_custom_call" | custom-call | tf_op jit(solution)/shard_map/pallas_call | solution.py:67
  82.5 2.2 gather_fusion.5
  84.8 1.8 fusion.23
  89.7 6.5 %all-to-all-start.1 = ((bf16[256,32,128]{2,1,0:T(8,128)(2,1)}), bf16[256,32,128]{2,1,0:T(8,128)(2,1)S(1)}, u32[]{:S(2)}, u32[]{:S(2)}) async-start(bf16[256,32,128]{2,1,0:T(8,128)(2,1)} %gather_fusion.5), calls=%async_computation.1 | async-start | bytes 4194304 | tf_op jit(solution)/shard_map/all_to_all | solution.py:137
  97.9 36.0 %while.24 = (s32[]{:T(128)}, bf16[4,64,32,128]{3,2,1,0:T(8,128)(2,1)}, f32[4,64]{1,0:T(4,128)S(1)}, bf16[4,64,32,128]{3,2,1,0:T(8,128)(2,1)}, s32[4,64]{1,0:T(4,...) while((s32[]{:T(128)}, bf16[4,64,32,128]{3,2,1,0:T(8,128)(2,1)}, ...), condition=%wide.region_7.8_spmd, body=%wide.region_4.7_spmd.sunk | while | flops 271322048 | bytes 38828920 | solution.py:139
  98.0 3.0 %gather_fusion = bf16[64,256,128]{2,1,0:T(8,128)(2,1)} fusion(bf16[16,256,128]{2,1,0:T(8,128)(2,1)S(1)} %get-tuple-element.243, s32[1024]{0:T(1024)S(1)} %pad_clamp_fusion.10), kind=kCustom, calls=%fused_computation.clone.1 | custom fusion | bytes 8388864 | tf_op jit(solution)/shard_map/while/body/eval_jaxpr/jit(_take)/gather | solution.py:116
  101.0 4.1 %fusion.66 = (f32[64,32]{1,0:T(8,128)S(1)}, f32[64,32,256]{2,1,0:T(8,128)S(1)}) fusion(bf16[64,256,128]{2,1,0:T(8,128)(2,1)} %gather_fusion, bf16[4,64,32,128]{3,2,1,0:T(8,128)(2,1)} %get-tuple-element.241, s32[]{:T(128)} %get-tuple-element.230), kind=kOutput, calls=%fused_computation.12.clone.1 | convolution fusion | flops 135264256 | bytes 6824448 | tf_op jit(solution)/shard_map/while/body/eval_jaxpr/bqe,bpe->bqp/dot_general | solution.py:118
  107.0 3.0 %gather_fusion = bf16[64,256,128]{2,1,0:T(8,128)(2,1)} fusion(bf16[16,256,128]{2,1,0:T(8,128)(2,1)S(1)} %get-tuple-element.243, s32[1024]{0:T(1024)S(1)} %pad_clamp_fusion.10), kind=kCustom, calls=%fused_computation.clone.1 | custom fusion | bytes 8388864 | tf_op jit(solution)/shard_map/while/body/eval_jaxpr/jit(_take)/gather | solution.py:116
  110.0 4.1 %fusion.66 = (f32[64,32]{1,0:T(8,128)S(1)}, f32[64,32,256]{2,1,0:T(8,128)S(1)}) fusion(bf16[64,256,128]{2,1,0:T(8,128)(2,1)} %gather_fusion, bf16[4,64,32,128]{3,2,1,0:T(8,128)(2,1)} %get-tuple-element.241, s32[]{:T(128)} %get-tuple-element.230), kind=kOutput, calls=%fused_computation.12.clone.1 | convolution fusion | flops 135264256 | bytes 6824448 | tf_op jit(solution)/shard_map/while/body/eval_jaxpr/bqe,bpe->bqp/dot_general | solution.py:118
  116.0 3.0 %gather_fusion = bf16[64,256,128]{2,1,0:T(8,128)(2,1)} fusion(bf16[16,256,128]{2,1,0:T(8,128)(2,1)S(1)} %get-tuple-element.243, s32[1024]{0:T(1024)S(1)} %pad_clamp_fusion.10), kind=kCustom, calls=%fused_computation.clone.1 | custom fusion | bytes 8388864 | tf_op jit(solution)/shard_map/while/body/eval_jaxpr/jit(_take)/gather | solution.py:116
  119.1 4.1 %fusion.66 = (f32[64,32]{1,0:T(8,128)S(1)}, f32[64,32,256]{2,1,0:T(8,128)S(1)}) fusion(bf16[64,256,128]{2,1,0:T(8,128)(2,1)} %gather_fusion, bf16[4,64,32,128]{3,2,1,0:T(8,128)(2,1)} %get-tuple-element.241, s32[]{:T(128)} %get-tuple-element.230), kind=kOutput, calls=%fused_computation.12.clone.1 | convolution fusion | flops 135264256 | bytes 6824448 | tf_op jit(solution)/shard_map/while/body/eval_jaxpr/bqe,bpe->bqp/dot_general | solution.py:118
  125.0 3.0 %gather_fusion = bf16[64,256,128]{2,1,0:T(8,128)(2,1)} fusion(bf16[16,256,128]{2,1,0:T(8,128)(2,1)S(1)} %get-tuple-element.243, s32[1024]{0:T(1024)S(1)} %pad_clamp_fusion.10), kind=kCustom, calls=%fused_computation.clone.1 | custom fusion | bytes 8388864 | tf_op jit(solution)/shard_map/while/body/eval_jaxpr/jit(_take)/gather | solution.py:116
  128.0 4.1 %fusion.66 = (f32[64,32]{1,0:T(8,128)S(1)}, f32[64,32,256]{2,1,0:T(8,128)S(1)}) fusion(bf16[64,256,128]{2,1,0:T(8,128)(2,1)} %gather_fusion, bf16[4,64,32,128]{3,2,1,0:T(8,128)(2,1)} %get-tuple-element.241, s32[]{:T(128)} %get-tuple-element.230), kind=kOutput, calls=%fused_computation.12.clone.1 | convolution fusion | flops 135264256 | bytes 6824448 | tf_op jit(solution)/shard_map/while/body/eval_jaxpr/bqe,bpe->bqp/dot_general | solution.py:118
  134.0 16.0 %all-to-all-done.1 = bf16[256,32,128]{2,1,0:T(8,128)(2,1)S(1)} async-done(((bf16[256,32,128]{2,1,0:T(8,128)(2,1)}), bf16[256,32,128]{2,1,0:T(8,128)(2,1)S(1)}, u32[]{:S(2)}, u32[]{:S(2)}) %all-to-all-start.1) | async-done | bytes 2097184 | tf_op jit(solution)/shard_map/all_to_all | solution.py:137
  150.0 7.3 %all-to-all-start.2 = ((bf16[256,32,128]{2,1,0:T(8,128)(2,1)}), bf16[256,32,128]{2,1,0:T(8,128)(2,1)}, u32[]{:S(2)}, u32[]{:S(2)}) async-start(bf16[256,32,128]{2,1,0:T(8,128)(2,1)} %bitcast.92), calls=%async_computation.2 | async-start | bytes 4194304 | tf_op jit(solution)/shard_map/all_to_all | solution.py:150
  159.0 35.3 %while.25 = (s32[]{:T(128)}, bf16[4,64,32,128]{3,2,1,0:T(8,128)(2,1)}, f32[4,64]{1,0:T(4,128)S(1)}, bf16[4,64,32,128]{3,2,1,0:T(8,128)(2,1)S(1)}, s32[4,64]{1,0:...) while((s32[]{:T(128)}, bf16[4,64,32,128]{3,2,1,0:T(8,128)(2,1)}, ...), condition=%wide.region_11.12_spmd, body=%wide.region_8.11_spmd.sunk | while | flops 271322048 | bytes 38828412 | solution.py:139
  159.0 3.0 %gather_fusion.1 = bf16[64,256,128]{2,1,0:T(8,128)(2,1)} fusion(bf16[16,256,128]{2,1,0:T(8,128)(2,1)S(1)} %get-tuple-element.219, s32[1024]{0:T(1024)S(1)} %pad_clamp_fusion.11), kind=kCustom, calls=%fused_computation.1.clone.1 | custom fusion | bytes 8388864 | tf_op jit(solution)/shard_map/while/body/eval_jaxpr/jit(_take)/gather | solution.py:116
  162.0 4.0 %fusion.71 = (f32[64,32]{1,0:T(8,128)S(1)}, f32[64,32,256]{2,1,0:T(8,128)S(1)}) fusion(bf16[64,256,128]{2,1,0:T(8,128)(2,1)} %gather_fusion.1, bf16[4,64,32,128]{3,2,1,0:T(8,128)(2,1)S(1)} %get-tuple-element.217, s32[]{:T(128)} %get-tuple-element.206), kind=kOutput, calls=%fused_computation.29.clone.1 | convolution fusion | flops 135264256 | bytes 6823940 | tf_op jit(solution)/shard_map/while/body/eval_jaxpr/bqe,bpe->bqp/dot_general | solution.py:118
  167.8 3.0 %gather_fusion.1 = bf16[64,256,128]{2,1,0:T(8,128)(2,1)} fusion(bf16[16,256,128]{2,1,0:T(8,128)(2,1)S(1)} %get-tuple-element.219, s32[1024]{0:T(1024)S(1)} %pad_clamp_fusion.11), kind=kCustom, calls=%fused_computation.1.clone.1 | custom fusion | bytes 8388864 | tf_op jit(solution)/shard_map/while/body/eval_jaxpr/jit(_take)/gather | solution.py:116
  170.8 4.0 %fusion.71 = (f32[64,32]{1,0:T(8,128)S(1)}, f32[64,32,256]{2,1,0:T(8,128)S(1)}) fusion(bf16[64,256,128]{2,1,0:T(8,128)(2,1)} %gather_fusion.1, bf16[4,64,32,128]{3,2,1,0:T(8,128)(2,1)S(1)} %get-tuple-element.217, s32[]{:T(128)} %get-tuple-element.206), kind=kOutput, calls=%fused_computation.29.clone.1 | convolution fusion | flops 135264256 | bytes 6823940 | tf_op jit(solution)/shard_map/while/body/eval_jaxpr/bqe,bpe->bqp/dot_general | solution.py:118
  176.7 3.0 %gather_fusion.1 = bf16[64,256,128]{2,1,0:T(8,128)(2,1)} fusion(bf16[16,256,128]{2,1,0:T(8,128)(2,1)S(1)} %get-tuple-element.219, s32[1024]{0:T(1024)S(1)} %pad_clamp_fusion.11), kind=kCustom, calls=%fused_computation.1.clone.1 | custom fusion | bytes 8388864 | tf_op jit(solution)/shard_map/while/body/eval_jaxpr/jit(_take)/gather | solution.py:116
  179.7 4.0 %fusion.71 = (f32[64,32]{1,0:T(8,128)S(1)}, f32[64,32,256]{2,1,0:T(8,128)S(1)}) fusion(bf16[64,256,128]{2,1,0:T(8,128)(2,1)} %gather_fusion.1, bf16[4,64,32,128]{3,2,1,0:T(8,128)(2,1)S(1)} %get-tuple-element.217, s32[]{:T(128)} %get-tuple-element.206), kind=kOutput, calls=%fused_computation.29.clone.1 | convolution fusion | flops 135264256 | bytes 6823940 | tf_op jit(solution)/shard_map/while/body/eval_jaxpr/bqe,bpe->bqp/dot_general | solution.py:118
  185.5 3.0 %gather_fusion.1 = bf16[64,256,128]{2,1,0:T(8,128)(2,1)} fusion(bf16[16,256,128]{2,1,0:T(8,128)(2,1)S(1)} %get-tuple-element.219, s32[1024]{0:T(1024)S(1)} %pad_clamp_fusion.11), kind=kCustom, calls=%fused_computation.1.clone.1 | custom fusion | bytes 8388864 | tf_op jit(solution)/shard_map/while/body/eval_jaxpr/jit(_take)/gather | solution.py:116
  188.5 4.0 %fusion.71 = (f32[64,32]{1,0:T(8,128)S(1)}, f32[64,32,256]{2,1,0:T(8,128)S(1)}) fusion(bf16[64,256,128]{2,1,0:T(8,128)(2,1)} %gather_fusion.1, bf16[4,64,32,128]{3,2,1,0:T(8,128)(2,1)S(1)} %get-tuple-element.217, s32[]{:T(128)} %get-tuple-element.206), kind=kOutput, calls=%fused_computation.29.clone.1 | convolution fusion | flops 135264256 | bytes 6823940 | tf_op jit(solution)/shard_map/while/body/eval_jaxpr/bqe,bpe->bqp/dot_general | solution.py:118
  194.3 15.8 %all-to-all-done.2 = bf16[256,32,128]{2,1,0:T(8,128)(2,1)} async-done(((bf16[256,32,128]{2,1,0:T(8,128)(2,1)}), bf16[256,32,128]{2,1,0:T(8,128)(2,1)}, u32[]{:S(2)}, u32[]{:S(2)}) %all-to-all-start.2) | async-done | bytes 2097184 | tf_op jit(solution)/shard_map/all_to_all | solution.py:150
  210.1 6.3 %all-to-all-start.3 = ((bf16[256,32,128]{2,1,0:T(8,128)(2,1)}), bf16[256,32,128]{2,1,0:T(8,128)(2,1)S(1)}, u32[]{:S(2)}, u32[]{:S(2)}) async-start(bf16[256,32,128]{2,1,0:T(8,128)(2,1)} %bitcast.91), calls=%async_computation.3 | async-start | bytes 4194304 | tf_op jit(solution)/shard_map/all_to_all | solution.py:155
  216.8 2.3 gather_fusion.6
  220.0 53.9 %shard_map.60 = f32[256,128]{1,0:T(8,128)} custom-call(f32[256,128]{1,0:T(8,128)} %pad.11.rows_ref), custom_call_target="tpu_custom_call" | custom-call | tf_op jit(solution)/shard_map/pallas_call | solution.py:67
  280.9 1.8 fusion.27
  (119 shorter events, 37.6 us)
Async XLA Ops:
  0.6 1.6 copy-start
  9.1 79.3 %all-to-all-start = ((bf16[256,32,128]{2,1,0:T(8,128)(2,1)}), bf16[256,32,128]{2,1,0:T(8,128)(2,1)S(1)}, u32[]{:S(2)}, u32[]{:S(2)}) async-start(bf16[256,32,128]{2,1,0:T(8,128)(2,1)} %gather_fusion.3), calls=%async_computation | async-start | bytes 4194304 | tf_op jit(solution)/shard_map/all_to_all | solution.py:137
  88.4 1.3 copy-start.3
  89.7 60.3 %all-to-all-start.1 = ((bf16[256,32,128]{2,1,0:T(8,128)(2,1)}), bf16[256,32,128]{2,1,0:T(8,128)(2,1)S(1)}, u32[]{:S(2)}, u32[]{:S(2)}) async-start(bf16[256,32,128]{2,1,0:T(8,128)(2,1)} %gather_fusion.5), calls=%async_computation.1 | async-start | bytes 4194304 | tf_op jit(solution)/shard_map/all_to_all | solution.py:137
  101.0 4.1 %copy-start.1 = (bf16[64,256,128]{2,1,0:T(8,128)(2,1)S(1)}, bf16[64,256,128]{2,1,0:T(8,128)(2,1)}, u32[]{:S(2)}) copy-start(bf16[64,256,128]{2,1,0:T(8,128)(2,1)} %gather_fusion) | copy-start | bytes 12582916 | tf_op jit(solution)/shard_map/while
  110.0 4.1 %copy-start.1 = (bf16[64,256,128]{2,1,0:T(8,128)(2,1)S(1)}, bf16[64,256,128]{2,1,0:T(8,128)(2,1)}, u32[]{:S(2)}) copy-start(bf16[64,256,128]{2,1,0:T(8,128)(2,1)} %gather_fusion) | copy-start | bytes 12582916 | tf_op jit(solution)/shard_map/while
  119.1 4.1 %copy-start.1 = (bf16[64,256,128]{2,1,0:T(8,128)(2,1)S(1)}, bf16[64,256,128]{2,1,0:T(8,128)(2,1)}, u32[]{:S(2)}) copy-start(bf16[64,256,128]{2,1,0:T(8,128)(2,1)} %gather_fusion) | copy-start | bytes 12582916 | tf_op jit(solution)/shard_map/while
  128.0 4.1 %copy-start.1 = (bf16[64,256,128]{2,1,0:T(8,128)(2,1)S(1)}, bf16[64,256,128]{2,1,0:T(8,128)(2,1)}, u32[]{:S(2)}) copy-start(bf16[64,256,128]{2,1,0:T(8,128)(2,1)} %gather_fusion) | copy-start | bytes 12582916 | tf_op jit(solution)/shard_map/while
  150.0 60.1 %all-to-all-start.2 = ((bf16[256,32,128]{2,1,0:T(8,128)(2,1)}), bf16[256,32,128]{2,1,0:T(8,128)(2,1)}, u32[]{:S(2)}, u32[]{:S(2)}) async-start(bf16[256,32,128]{2,1,0:T(8,128)(2,1)} %bitcast.92), calls=%async_computation.2 | async-start | bytes 4194304 | tf_op jit(solution)/shard_map/all_to_all | solution.py:150
  162.0 4.0 %copy-start.2 = (bf16[64,256,128]{2,1,0:T(8,128)(2,1)S(1)}, bf16[64,256,128]{2,1,0:T(8,128)(2,1)}, u32[]{:S(2)}) copy-start(bf16[64,256,128]{2,1,0:T(8,128)(2,1)} %gather_fusion.1) | copy-start | bytes 12582916 | tf_op jit(solution)/shard_map/while
  170.8 4.0 %copy-start.2 = (bf16[64,256,128]{2,1,0:T(8,128)(2,1)S(1)}, bf16[64,256,128]{2,1,0:T(8,128)(2,1)}, u32[]{:S(2)}) copy-start(bf16[64,256,128]{2,1,0:T(8,128)(2,1)} %gather_fusion.1) | copy-start | bytes 12582916 | tf_op jit(solution)/shard_map/while
  179.7 4.0 %copy-start.2 = (bf16[64,256,128]{2,1,0:T(8,128)(2,1)S(1)}, bf16[64,256,128]{2,1,0:T(8,128)(2,1)}, u32[]{:S(2)}) copy-start(bf16[64,256,128]{2,1,0:T(8,128)(2,1)} %gather_fusion.1) | copy-start | bytes 12582916 | tf_op jit(solution)/shard_map/while
  188.5 4.0 %copy-start.2 = (bf16[64,256,128]{2,1,0:T(8,128)(2,1)S(1)}, bf16[64,256,128]{2,1,0:T(8,128)(2,1)}, u32[]{:S(2)}) copy-start(bf16[64,256,128]{2,1,0:T(8,128)(2,1)} %gather_fusion.1) | copy-start | bytes 12582916 | tf_op jit(solution)/shard_map/while
  210.1 67.0 %all-to-all-start.3 = ((bf16[256,32,128]{2,1,0:T(8,128)(2,1)}), bf16[256,32,128]{2,1,0:T(8,128)(2,1)S(1)}, u32[]{:S(2)}, u32[]{:S(2)}) async-start(bf16[256,32,128]{2,1,0:T(8,128)(2,1)} %bitcast.91), calls=%async_computation.3 | async-start | bytes 4194304 | tf_op jit(solution)/shard_map/all_to_all | solution.py:155
  277.2 3.7 %copy-start.4 = (bf16[8,32,128]{2,1,0:T(8,128)(2,1)S(1)}, bf16[8,32,128]{2,1,0:T(8,128)(2,1)}, u32[]{:S(2)}) copy-start(bf16[8,32,128]{2,1,0:T(8,128)(2,1)} %param.8) | copy-start | bytes 196612

commit v14 on v12

--- a/solution.py
+++ b/solution.py
@@ -165,13 +165,18 @@
     first = (jnp.arange(list_len) == 0).astype(jnp.float32)
     coeff = exp_scores / total - first[None, :]
     slot_of_pair = before.reshape(query_count, list_len)
+    holder = target.reshape(query_count, list_len)
+    holder_hit = holder[:, :, None] == jnp.arange(device_total)[None, None, :]
     unit_grad = None
     for slot in range(slot_cap):
-        part = jnp.take(returned[slot], target, axis=0, mode="clip").reshape(
-            query_count, list_len, query_len, feat_width
-        )
         weight = jnp.where(slot_of_pair == slot, coeff, 0.0)
-        term = jnp.einsum("bk,bkqe->bqe", weight, part.astype(jnp.float32))
+        weight = jnp.sum(jnp.where(holder_hit, weight[:, :, None], 0.0), axis=1)
+        term = jnp.dot(
+            weight,
+            returned[slot].reshape(device_total, query_len * feat_width).astype(jnp.float32),
+            precision=lax.Precision.HIGHEST,
+            preferred_element_type=jnp.float32,
+        ).reshape(query_count, query_len, feat_width)
         unit_grad = term if unit_grad is None else unit_grad + term
     along = jnp.sum(query_unit * unit_grad, axis=-1, keepdims=True)
     query_grad = (unit_grad - query_unit * along) * query_scale

time: 286 us -> 299 us (1.045)
  matrix products: 46.5 us -> 52.3 us
  local copies, waits for them, and re-layouts: 48.3 us -> 53 us
  other arithmetic: 10.9 us -> 14 us
    all_to_all x0 -> x2, local copies, waits for them, and re-layouts: none -> 7.05 us  [local(): lax.all_to_all(pulled_parts[-1], both_axes, split_axis=0, concat_axis=0,...]
    dot_general x2, matrix products: 0.81 us -> 6.65 us  [local(): jnp.dot(weight, returned[slot].reshape(device_total, query_len * feat_wid...]
    gather x2 -> x0, local copies, waits for them, and re-layouts: 3.11 us -> none  [local(): jnp.take(returned[slot], target, axis=0, mode='clip')]
  transfers between devices with their start and end apart: 4 -> 4, of which waited for: 2 -> 2; matrix products, arithmetic and copies ran while one was open for 33% -> 33% of each run, Pallas kernels for 39% -> 37%
where the time goes in v14:
time: 299 us; the launch traced here: 297 us
  Pallas kernels  109 us (36%)
  local copies, waits for them, and re-layouts  53 us (18%)
  matrix products  52.3 us (17%)
  starting transfers between devices  34.7 us (12%)
  waiting for transfers between devices  31.9 us (11%)
  other arithmetic  14 us (5%)
    pallas_call x2, Pallas kernels, exchange(): pl.pallas_call(functools.partial(exchange_kernel, dev_count), out_shape=j...  109 us
    dot_general x8, matrix products, score_block(): jnp.einsum('bqe,bpe->bqp', query_block, passage_block, preferred_element_...  32.3 us
    gather x8, local copies, waits for them, and re-layouts, score_block(): passage_block = jnp.take(passage_unit, tag_block, axis=0, mode='clip')  24.1 us
    all_to_all x2, starting transfers between devices, local(): lax.all_to_all(outgoing, both_axes, split_axis=0, concat_axis=0, tiled=True)  21.1 us
    all_to_all x2, waiting for transfers between devices, local(): lax.all_to_all(outgoing, both_axes, split_axis=0, concat_axis=0, tiled=True)  16.1 us
    all_to_all x2, waiting for transfers between devices, local(): lax.all_to_all(pulled_parts[-1], both_axes, split_axis=0, concat_axis=0,...  15.8 us
    all_to_all x2, starting transfers between devices, local(): lax.all_to_all(pulled_parts[-1], both_axes, split_axis=0, concat_axis=0,...  13.6 us
    dot_general x8, matrix products, score_block(): jnp.einsum('bqp,bpe->bqe', attention, passage_block, preferred_element_ty...  13.4 us
  transfers between devices with their start and end apart: 4, of which 2 were waited for; matrix products, arithmetic and copies ran while one was open for 33% of the time, Pallas kernels for 37%

profile of v14, /device:TPU:8, one launch (start us, length us, event | category | flops | bytes accessed | tf_op | source)
XLA Modules:
  0.0 296.5 jit_solution(4760145090322499951)
XLA Ops:
  9.1 14.6 %all-to-all-start.1 = ((bf16[256,32,128]{2,1,0:T(8,128)(2,1)}), bf16[256,32,128]{2,1,0:T(8,128)(2,1)S(1)}, u32[]{:S(2)}, u32[]{:S(2)}) async-start(bf16[256,32,128]{2,1,0:T(8,128)(2,1)} %gather_fusion.5), calls=%async_computation.1 | async-start | bytes 4194304 | tf_op jit(solution)/shard_map/all_to_all | solution.py:137
  23.8 3.3 %gather_fusion.4 = s32[512]{0:T(512)S(1)} fusion(s32[128]{0:T(128)S(1)} %get-tuple-element.122, s32[1024]{0:T(1024)S(1)} %pad_clamp_fusion.4), kind=kCustom, calls=%fused_computation.4 | custom fusion | bytes 6144 | tf_op jit(solution)/shard_map/jit(_take)/gather | solution.py:108
  28.0 53.3 %shard_map.59 = f32[256,128]{1,0:T(8,128)} custom-call(f32[256,128]{1,0:T(8,128)} %pad_convert_fusion.rows_ref), custom_call_target="tpu_custom_call" | custom-call | tf_op jit(solution)/shard_map/pallas_call | solution.py:67
  89.8 6.5 %all-to-all-start = ((bf16[256,32,128]{2,1,0:T(8,128)(2,1)}), bf16[256,32,128]{2,1,0:T(8,128)(2,1)S(1)}, u32[]{:S(2)}, u32[]{:S(2)}) async-start(bf16[256,32,128]{2,1,0:T(8,128)(2,1)} %gather_fusion.3), calls=%async_computation | async-start | bytes 4194304 | tf_op jit(solution)/shard_map/all_to_all | solution.py:137
  98.0 36.0 %while.25 = (s32[]{:T(128)}, bf16[4,64,32,128]{3,2,1,0:T(8,128)(2,1)}, f32[4,64]{1,0:T(4,128)S(1)}, bf16[4,64,32,128]{3,2,1,0:T(8,128)(2,1)}, s32[4,64]{1,0:T(4,...) while((s32[]{:T(128)}, bf16[4,64,32,128]{3,2,1,0:T(8,128)(2,1)}, ...), condition=%wide.region_11.12_spmd, body=%wide.region_8.11_spmd.sunk | while | flops 271322048 | bytes 38828920 | solution.py:139
  98.0 3.0 %gather_fusion.1 = bf16[64,256,128]{2,1,0:T(8,128)(2,1)} fusion(bf16[16,256,128]{2,1,0:T(8,128)(2,1)S(1)} %get-tuple-element.237, s32[1024]{0:T(1024)S(1)} %pad_clamp_fusion.10), kind=kCustom, calls=%fused_computation.1.clone.1 | custom fusion | bytes 8388864 | tf_op jit(solution)/shard_map/while/body/eval_jaxpr/jit(_take)/gather | solution.py:116
  101.0 4.1 %fusion.75 = (f32[64,32]{1,0:T(8,128)S(1)}, f32[64,32,256]{2,1,0:T(8,128)S(1)}) fusion(bf16[64,256,128]{2,1,0:T(8,128)(2,1)} %gather_fusion.1, bf16[4,64,32,128]{3,2,1,0:T(8,128)(2,1)} %get-tuple-element.235, s32[]{:T(128)} %get-tuple-element.224), kind=kOutput, calls=%fused_computation.27.clone.1 | convolution fusion | flops 135264256 | bytes 6824448 | tf_op jit(solution)/shard_map/while/body/eval_jaxpr/bqe,bpe->bqp/dot_general | solution.py:118
  107.0 3.0 %gather_fusion.1 = bf16[64,256,128]{2,1,0:T(8,128)(2,1)} fusion(bf16[16,256,128]{2,1,0:T(8,128)(2,1)S(1)} %get-tuple-element.237, s32[1024]{0:T(1024)S(1)} %pad_clamp_fusion.10), kind=kCustom, calls=%fused_computation.1.clone.1 | custom fusion | bytes 8388864 | tf_op jit(solution)/shard_map/while/body/eval_jaxpr/jit(_take)/gather | solution.py:116
  110.0 4.1 %fusion.75 = (f32[64,32]{1,0:T(8,128)S(1)}, f32[64,32,256]{2,1,0:T(8,128)S(1)}) fusion(bf16[64,256,128]{2,1,0:T(8,128)(2,1)} %gather_fusion.1, bf16[4,64,32,128]{3,2,1,0:T(8,128)(2,1)} %get-tuple-element.235, s32[]{:T(128)} %get-tuple-element.224), kind=kOutput, calls=%fused_computation.27.clone.1 | convolution fusion | flops 135264256 | bytes 6824448 | tf_op jit(solution)/shard_map/while/body/eval_jaxpr/bqe,bpe->bqp/dot_general | solution.py:118
  116.1 3.0 %gather_fusion.1 = bf16[64,256,128]{2,1,0:T(8,128)(2,1)} fusion(bf16[16,256,128]{2,1,0:T(8,128)(2,1)S(1)} %get-tuple-element.237, s32[1024]{0:T(1024)S(1)} %pad_clamp_fusion.10), kind=kCustom, calls=%fused_computation.1.clone.1 | custom fusion | bytes 8388864 | tf_op jit(solution)/shard_map/while/body/eval_jaxpr/jit(_take)/gather | solution.py:116
  119.1 4.1 %fusion.75 = (f32[64,32]{1,0:T(8,128)S(1)}, f32[64,32,256]{2,1,0:T(8,128)S(1)}) fusion(bf16[64,256,128]{2,1,0:T(8,128)(2,1)} %gather_fusion.1, bf16[4,64,32,128]{3,2,1,0:T(8,128)(2,1)} %get-tuple-element.235, s32[]{:T(128)} %get-tuple-element.224), kind=kOutput, calls=%fused_computation.27.clone.1 | convolution fusion | flops 135264256 | bytes 6824448 | tf_op jit(solution)/shard_map/while/body/eval_jaxpr/bqe,bpe->bqp/dot_general | solution.py:118
  125.0 3.0 %gather_fusion.1 = bf16[64,256,128]{2,1,0:T(8,128)(2,1)} fusion(bf16[16,256,128]{2,1,0:T(8,128)(2,1)S(1)} %get-tuple-element.237, s32[1024]{0:T(1024)S(1)} %pad_clamp_fusion.10), kind=kCustom, calls=%fused_computation.1.clone.1 | custom fusion | bytes 8388864 | tf_op jit(solution)/shard_map/while/body/eval_jaxpr/jit(_take)/gather | solution.py:116
  128.1 4.1 %fusion.75 = (f32[64,32]{1,0:T(8,128)S(1)}, f32[64,32,256]{2,1,0:T(8,128)S(1)}) fusion(bf16[64,256,128]{2,1,0:T(8,128)(2,1)} %gather_fusion.1, bf16[4,64,32,128]{3,2,1,0:T(8,128)(2,1)} %get-tuple-element.235, s32[]{:T(128)} %get-tuple-element.224), kind=kOutput, calls=%fused_computation.27.clone.1 | convolution fusion | flops 135264256 | bytes 6824448 | tf_op jit(solution)/shard_map/while/body/eval_jaxpr/bqe,bpe->bqp/dot_general | solution.py:118
  134.0 16.1 %all-to-all-done = bf16[256,32,128]{2,1,0:T(8,128)(2,1)S(1)} async-done(((bf16[256,32,128]{2,1,0:T(8,128)(2,1)}), bf16[256,32,128]{2,1,0:T(8,128)(2,1)S(1)}, u32[]{:S(2)}, u32[]{:S(2)}) %all-to-all-start) | async-done | bytes 2097184 | tf_op jit(solution)/shard_map/all_to_all | solution.py:137
  150.0 7.3 %all-to-all-start.3 = ((bf16[256,32,128]{2,1,0:T(8,128)(2,1)}), bf16[256,32,128]{2,1,0:T(8,128)(2,1)}, u32[]{:S(2)}, u32[]{:S(2)}) async-start(bf16[256,32,128]{2,1,0:T(8,128)(2,1)} %bitcast.95), calls=%async_computation.3 | async-start | bytes 4194304 | tf_op jit(solution)/shard_map/all_to_all | solution.py:155
  159.0 35.3 %while.24 = (s32[]{:T(128)}, bf16[4,64,32,128]{3,2,1,0:T(8,128)(2,1)}, f32[4,64]{1,0:T(4,128)S(1)}, bf16[4,64,32,128]{3,2,1,0:T(8,128)(2,1)S(1)}, s32[4,64]{1,0:...) while((s32[]{:T(128)}, bf16[4,64,32,128]{3,2,1,0:T(8,128)(2,1)}, ...), condition=%wide.region_7.8_spmd, body=%wide.region_4.7_spmd.sunk | while | flops 271322048 | bytes 38828412 | solution.py:139
  159.0 3.0 %gather_fusion = bf16[64,256,128]{2,1,0:T(8,128)(2,1)} fusion(bf16[16,256,128]{2,1,0:T(8,128)(2,1)S(1)} %get-tuple-element.261, s32[1024]{0:T(1024)S(1)} %pad_clamp_fusion.9), kind=kCustom, calls=%fused_computation.clone.1 | custom fusion | bytes 8388864 | tf_op jit(solution)/shard_map/while/body/eval_jaxpr/jit(_take)/gather | solution.py:116
  162.0 4.0 %fusion.70 = (f32[64,32]{1,0:T(8,128)S(1)}, f32[64,32,256]{2,1,0:T(8,128)S(1)}) fusion(bf16[64,256,128]{2,1,0:T(8,128)(2,1)} %gather_fusion, bf16[4,64,32,128]{3,2,1,0:T(8,128)(2,1)S(1)} %get-tuple-element.259, s32[]{:T(128)} %get-tuple-element.248), kind=kOutput, calls=%fused_computation.10.clone.1 | convolution fusion | flops 135264256 | bytes 6823940 | tf_op jit(solution)/shard_map/while/body/eval_jaxpr/bqe,bpe->bqp/dot_general | solution.py:118
  167.9 3.0 %gather_fusion = bf16[64,256,128]{2,1,0:T(8,128)(2,1)} fusion(bf16[16,256,128]{2,1,0:T(8,128)(2,1)S(1)} %get-tuple-element.261, s32[1024]{0:T(1024)S(1)} %pad_clamp_fusion.9), kind=kCustom, calls=%fused_computation.clone.1 | custom fusion | bytes 8388864 | tf_op jit(solution)/shard_map/while/body/eval_jaxpr/jit(_take)/gather | solution.py:116
  170.9 4.0 %fusion.70 = (f32[64,32]{1,0:T(8,128)S(1)}, f32[64,32,256]{2,1,0:T(8,128)S(1)}) fusion(bf16[64,256,128]{2,1,0:T(8,128)(2,1)} %gather_fusion, bf16[4,64,32,128]{3,2,1,0:T(8,128)(2,1)S(1)} %get-tuple-element.259, s32[]{:T(128)} %get-tuple-element.248), kind=kOutput, calls=%fused_computation.10.clone.1 | convolution fusion | flops 135264256 | bytes 6823940 | tf_op jit(solution)/shard_map/while/body/eval_jaxpr/bqe,bpe->bqp/dot_general | solution.py:118
  176.7 3.0 %gather_fusion = bf16[64,256,128]{2,1,0:T(8,128)(2,1)} fusion(bf16[16,256,128]{2,1,0:T(8,128)(2,1)S(1)} %get-tuple-element.261, s32[1024]{0:T(1024)S(1)} %pad_clamp_fusion.9), kind=kCustom, calls=%fused_computation.clone.1 | custom fusion | bytes 8388864 | tf_op jit(solution)/shard_map/while/body/eval_jaxpr/jit(_take)/gather | solution.py:116
  179.7 4.0 %fusion.70 = (f32[64,32]{1,0:T(8,128)S(1)}, f32[64,32,256]{2,1,0:T(8,128)S(1)}) fusion(bf16[64,256,128]{2,1,0:T(8,128)(2,1)} %gather_fusion, bf16[4,64,32,128]{3,2,1,0:T(8,128)(2,1)S(1)} %get-tuple-element.259, s32[]{:T(128)} %get-tuple-element.248), kind=kOutput, calls=%fused_computation.10.clone.1 | convolution fusion | flops 135264256 | bytes 6823940 | tf_op jit(solution)/shard_map/while/body/eval_jaxpr/bqe,bpe->bqp/dot_general | solution.py:118
  185.5 3.0 %gather_fusion = bf16[64,256,128]{2,1,0:T(8,128)(2,1)} fusion(bf16[16,256,128]{2,1,0:T(8,128)(2,1)S(1)} %get-tuple-element.261, s32[1024]{0:T(1024)S(1)} %pad_clamp_fusion.9), kind=kCustom, calls=%fused_computation.clone.1 | custom fusion | bytes 8388864 | tf_op jit(solution)/shard_map/while/body/eval_jaxpr/jit(_take)/gather | solution.py:116
  188.5 4.0 %fusion.70 = (f32[64,32]{1,0:T(8,128)S(1)}, f32[64,32,256]{2,1,0:T(8,128)S(1)}) fusion(bf16[64,256,128]{2,1,0:T(8,128)(2,1)} %gather_fusion, bf16[4,64,32,128]{3,2,1,0:T(8,128)(2,1)S(1)} %get-tuple-element.259, s32[]{:T(128)} %get-tuple-element.248), kind=kOutput, calls=%fused_computation.10.clone.1 | convolution fusion | flops 135264256 | bytes 6823940 | tf_op jit(solution)/shard_map/while/body/eval_jaxpr/bqe,bpe->bqp/dot_general | solution.py:118
  194.3 15.8 %all-to-all-done.3 = bf16[256,32,128]{2,1,0:T(8,128)(2,1)} async-done(((bf16[256,32,128]{2,1,0:T(8,128)(2,1)}), bf16[256,32,128]{2,1,0:T(8,128)(2,1)}, u32[]{:S(2)}, u32[]{:S(2)}) %all-to-all-start.3) | async-done | bytes 2097184 | tf_op jit(solution)/shard_map/all_to_all | solution.py:155
  210.1 6.3 %all-to-all-start.2 = ((bf16[256,32,128]{2,1,0:T(8,128)(2,1)}), bf16[256,32,128]{2,1,0:T(8,128)(2,1)S(1)}, u32[]{:S(2)}, u32[]{:S(2)}) async-start(bf16[256,32,128]{2,1,0:T(8,128)(2,1)} %bitcast.94), calls=%async_computation.2 | async-start | bytes 4194304 | tf_op jit(solution)/shard_map/all_to_all | solution.py:150
  217.7 56.2 %shard_map.60 = f32[256,128]{1,0:T(8,128)} custom-call(f32[256,128]{1,0:T(8,128)} %pad.11.rows_ref), custom_call_target="tpu_custom_call" | custom-call | tf_op jit(solution)/shard_map/pallas_call | solution.py:67
  277.3 4.3 %copy.32 = bf16[256,32,128]{0,2,1:T(8,128)(2,1)} copy(bf16[256,32,128]{2,1,0:T(8,128)(2,1)} %all-to-all-done.3) | data formatting | bytes 4194304 | tf_op jit(solution)/shard_map/all_to_all | solution.py:155
  281.6 3.3 %fusion.25 = f32[8,32,128]{2,0,1:T(8,128)S(1)} fusion(bf16[256,32,128]{0,2,1:T(8,128)(2,1)} %copy.32, f32[8,256]{1,0:T(8,128)S(1)} %get-tuple-element.97), kind=kOutput, calls=%fused_computation.47 | convolution fusion | flops 100663296 | bytes 2236416 | tf_op jit(solution)/shard_map/dot_general | solution.py:174
  284.9 2.8 copy.31
  287.7 3.3 %fusion.32 = f32[8,32,128]{2,0,1:T(8,128)S(1)} fusion(f32[8,32,128]{2,0,1:T(8,128)S(1)} %fusion.25, bf16[256,32,128]{0,2,1:T(8,128)(2,1)} %copy.31, f32[8,256]{1,0:T(8,128)S(1)} %get-tuple-element.96), kind=kOutput, calls=%fused_computation.54 | convolution fusion | flops 100696064 | bytes 2367488 | tf_op jit(solution)/shard_map/dot_general | solution.py:174
  291.1 4.8 %fusion.31 = f32[8,32,128]{2,0,1:T(8,128)S(1)} fusion(f32[8,32,128]{2,0,1:T(8,128)S(1)} %fusion.32, f32[8,32]{0,1:T(8,128)S(1)} %add_rsqrt_fusion.1, bf16[8,32,128]{2,1,0:T(8,128)(2,1)S(1)} %copy-done.4), kind=kOutput, calls=%fused_computation.53 | output fusion | flops 262527 | bytes 328704 | tf_op jit(solution)/shard_map/mul | solution.py:182
  (124 shorter events, 41.1 us)
Async XLA Ops:
  0.6 1.6 copy-start
  9.1 79.3 %all-to-all-start.1 = ((bf16[256,32,128]{2,1,0:T(8,128)(2,1)}), bf16[256,32,128]{2,1,0:T(8,128)(2,1)S(1)}, u32[]{:S(2)}, u32[]{:S(2)}) async-start(bf16[256,32,128]{2,1,0:T(8,128)(2,1)} %gather_fusion.5), calls=%async_computation.1 | async-start | bytes 4194304 | tf_op jit(solution)/shard_map/all_to_all | solution.py:137
  88.4 1.3 copy-start.3
  89.8 60.3 %all-to-all-start = ((bf16[256,32,128]{2,1,0:T(8,128)(2,1)}), bf16[256,32,128]{2,1,0:T(8,128)(2,1)S(1)}, u32[]{:S(2)}, u32[]{:S(2)}) async-start(bf16[256,32,128]{2,1,0:T(8,128)(2,1)} %gather_fusion.3), calls=%async_computation | async-start | bytes 4194304 | tf_op jit(solution)/shard_map/all_to_all | solution.py:137
  101.0 4.1 %copy-start.1 = (bf16[64,256,128]{2,1,0:T(8,128)(2,1)S(1)}, bf16[64,256,128]{2,1,0:T(8,128)(2,1)}, u32[]{:S(2)}) copy-start(bf16[64,256,128]{2,1,0:T(8,128)(2,1)} %gather_fusion.1) | copy-start | bytes 12582916 | tf_op jit(solution)/shard_map/while
  110.0 4.1 %copy-start.1 = (bf16[64,256,128]{2,1,0:T(8,128)(2,1)S(1)}, bf16[64,256,128]{2,1,0:T(8,128)(2,1)}, u32[]{:S(2)}) copy-start(bf16[64,256,128]{2,1,0:T(8,128)(2,1)} %gather_fusion.1) | copy-start | bytes 12582916 | tf_op jit(solution)/shard_map/while
  119.1 4.1 %copy-start.1 = (bf16[64,256,128]{2,1,0:T(8,128)(2,1)S(1)}, bf16[64,256,128]{2,1,0:T(8,128)(2,1)}, u32[]{:S(2)}) copy-start(bf16[64,256,128]{2,1,0:T(8,128)(2,1)} %gather_fusion.1) | copy-start | bytes 12582916 | tf_op jit(solution)/shard_map/while
  128.1 4.1 %copy-start.1 = (bf16[64,256,128]{2,1,0:T(8,128)(2,1)S(1)}, bf16[64,256,128]{2,1,0:T(8,128)(2,1)}, u32[]{:S(2)}) copy-start(bf16[64,256,128]{2,1,0:T(8,128)(2,1)} %gather_fusion.1) | copy-start | bytes 12582916 | tf_op jit(solution)/shard_map/while
  150.0 60.1 %all-to-all-start.3 = ((bf16[256,32,128]{2,1,0:T(8,128)(2,1)}), bf16[256,32,128]{2,1,0:T(8,128)(2,1)}, u32[]{:S(2)}, u32[]{:S(2)}) async-start(bf16[256,32,128]{2,1,0:T(8,128)(2,1)} %bitcast.95), calls=%async_computation.3 | async-start | bytes 4194304 | tf_op jit(solution)/shard_map/all_to_all | solution.py:155
  162.0 4.0 %copy-start.2 = (bf16[64,256,128]{2,1,0:T(8,128)(2,1)S(1)}, bf16[64,256,128]{2,1,0:T(8,128)(2,1)}, u32[]{:S(2)}) copy-start(bf16[64,256,128]{2,1,0:T(8,128)(2,1)} %gather_fusion) | copy-start | bytes 12582916 | tf_op jit(solution)/shard_map/while
  170.9 4.0 %copy-start.2 = (bf16[64,256,128]{2,1,0:T(8,128)(2,1)S(1)}, bf16[64,256,128]{2,1,0:T(8,128)(2,1)}, u32[]{:S(2)}) copy-start(bf16[64,256,128]{2,1,0:T(8,128)(2,1)} %gather_fusion) | copy-start | bytes 12582916 | tf_op jit(solution)/shard_map/while
  179.7 4.0 %copy-start.2 = (bf16[64,256,128]{2,1,0:T(8,128)(2,1)S(1)}, bf16[64,256,128]{2,1,0:T(8,128)(2,1)}, u32[]{:S(2)}) copy-start(bf16[64,256,128]{2,1,0:T(8,128)(2,1)} %gather_fusion) | copy-start | bytes 12582916 | tf_op jit(solution)/shard_map/while
  188.5 4.0 %copy-start.2 = (bf16[64,256,128]{2,1,0:T(8,128)(2,1)S(1)}, bf16[64,256,128]{2,1,0:T(8,128)(2,1)}, u32[]{:S(2)}) copy-start(bf16[64,256,128]{2,1,0:T(8,128)(2,1)} %gather_fusion) | copy-start | bytes 12582916 | tf_op jit(solution)/shard_map/while
  210.1 6.6 %copy-start.5 = (s32[8,16]{1,0:T(8,128)S(1)}, s32[8,16]{1,0:T(8,128)}, u32[]{:S(2)}) copy-start(s32[8,16]{1,0:T(8,128)} %param.10) | copy-start | bytes 1540
  210.1 74.8 %all-to-all-start.2 = ((bf16[256,32,128]{2,1,0:T(8,128)(2,1)}), bf16[256,32,128]{2,1,0:T(8,128)(2,1)S(1)}, u32[]{:S(2)}, u32[]{:S(2)}) async-start(bf16[256,32,128]{2,1,0:T(8,128)(2,1)} %bitcast.94), calls=%async_computation.2 | async-start | bytes 4194304 | tf_op jit(solution)/shard_map/all_to_all | solution.py:150
  287.7 3.3 %copy-start.4 = (bf16[8,32,128]{2,1,0:T(8,128)(2,1)S(1)}, bf16[8,32,128]{2,1,0:T(8,128)(2,1)}, u32[]{:S(2)}) copy-start(bf16[8,32,128]{2,1,0:T(8,128)(2,1)} %param.8) | copy-start | bytes 196612

commit v15 on v12

--- a/solution.py
+++ b/solution.py
@@ -109,6 +109,7 @@
     both_axes = ("group", "dev")
     labels = labels.reshape(device_total, slot_cap)
     tags = exchange(widen(labels, feat_width), dev_count, 0)[:, :slot_cap].astype(jnp.int32)
+    tags, query_send = lax.optimization_barrier((tags, query_send))
     block_rows = 64
 
     def score_block(inputs):

time: 286 us -> 300 us (1.049)
  waiting for transfers between devices: 31.9 us -> 79.3 us
  Pallas kernels: 110 us -> 78.1 us
  starting transfers between devices: 34.7 us -> 30.3 us
    all_to_all x2, waiting for transfers between devices: 16 us -> 63.5 us  [local(): lax.all_to_all(outgoing, both_axes, split_axis=0, concat_axis=0, tiled=True)]
    pallas_call x2, Pallas kernels: 110 us -> 78.1 us  [exchange(): pl.pallas_call(functools.partial(exchange_kernel, dev_count), out_shape=j...]
    all_to_all x2, starting transfers between devices: 21.1 us -> 16.7 us  [local(): lax.all_to_all(outgoing, both_axes, split_axis=0, concat_axis=0, tiled=True)]
  transfers between devices with their start and end apart: 4 -> 4, of which waited for: 2 -> 3; matrix products, arithmetic and copies ran while one was open for 33% -> 30% of each run, Pallas kernels for 39% -> 19%
where the time goes in v15:
time: 300 us; the launch traced here: 297 us
  waiting for transfers between devices  79.3 us (26%)
  Pallas kernels  78.1 us (26%)
  local copies, waits for them, and re-layouts  50.1 us (17%)
  matrix products  48.9 us (16%)
  starting transfers between devices  30.3 us (10%)
  other arithmetic  9.19 us (3%)
    pallas_call x2, Pallas kernels, exchange(): pl.pallas_call(functools.partial(exchange_kernel, dev_count), out_shape=j...  78.1 us
    all_to_all x2, waiting for transfers between devices, local(): lax.all_to_all(outgoing, both_axes, split_axis=0, concat_axis=0, tiled=True)  63.5 us
    dot_general x8, matrix products, score_block(): jnp.einsum('bqe,bpe->bqp', query_block, passage_block, preferred_element_...  32.3 us
    gather x8, local copies, waits for them, and re-layouts, score_block(): passage_block = jnp.take(passage_unit, tag_block, axis=0, mode='clip')  24.1 us
    all_to_all x2, starting transfers between devices, local(): lax.all_to_all(outgoing, both_axes, split_axis=0, concat_axis=0, tiled=True)  16.7 us
    all_to_all x2, waiting for transfers between devices, local(): lax.all_to_all(pulled_parts[-1], both_axes, split_axis=0, concat_axis=0,...  15.9 us
    all_to_all x2, starting transfers between devices, local(): lax.all_to_all(pulled_parts[-1], both_axes, split_axis=0, concat_axis=0,...  13.6 us
    dot_general x8, matrix products, score_block(): jnp.einsum('bqp,bpe->bqe', attention, passage_block, preferred_element_ty...  13.4 us
  transfers between devices with their start and end apart: 4, of which 3 were waited for; matrix products, arithmetic and copies ran while one was open for 30% of the time, Pallas kernels for 19%

profile of v15, /device:TPU:8, one launch (start us, length us, event | category | flops | bytes accessed | tf_op | source)
XLA Modules:
  0.0 297.1 jit_solution(12431611624337198158)
XLA Ops:
  4.7 3.3 %gather_fusion.3 = s32[512]{0:T(512)S(1)} fusion(s32[128]{0:T(128)S(1)} %and_select_fusion.3, s32[1024]{0:T(1024)S(1)} %pad_clamp_fusion.6), kind=kCustom, calls=%fused_computation.3 | custom fusion | bytes 6144 | tf_op jit(solution)/shard_map/jit(_take)/gather | solution.py:108
  8.9 21.8 %shard_map.59 = f32[256,128]{1,0:T(8,128)} custom-call(f32[256,128]{1,0:T(8,128)} %pad_convert_fusion.rows_ref), custom_call_target="tpu_custom_call" | custom-call | tf_op jit(solution)/shard_map/pallas_call | solution.py:67
  32.2 2.2 gather_fusion.5
  34.4 10.4 %all-to-all-start.1 = ((bf16[256,32,128]{2,1,0:T(8,128)(2,1)}), bf16[256,32,128]{2,1,0:T(8,128)(2,1)S(1)}, u32[]{:S(2)}, u32[]{:S(2)}) async-start(bf16[256,32,128]{2,1,0:T(8,128)(2,1)} %gather_fusion.5), calls=%async_computation.1 | async-start | bytes 4194304 | tf_op jit(solution)/shard_map/all_to_all | solution.py:138
  44.9 2.2 gather_fusion.4
  47.4 1.8 fusion.23
  51.0 47.5 %all-to-all-done.1 = bf16[256,32,128]{2,1,0:T(8,128)(2,1)S(1)} async-done(((bf16[256,32,128]{2,1,0:T(8,128)(2,1)}), bf16[256,32,128]{2,1,0:T(8,128)(2,1)S(1)}, u32[]{:S(2)}, u32[]{:S(2)}) %all-to-all-start.1) | async-done | bytes 2097184 | tf_op jit(solution)/shard_map/all_to_all | solution.py:138
  99.9 6.3 %all-to-all-start = ((bf16[256,32,128]{2,1,0:T(8,128)(2,1)}), bf16[256,32,128]{2,1,0:T(8,128)(2,1)S(1)}, u32[]{:S(2)}, u32[]{:S(2)}) async-start(bf16[256,32,128]{2,1,0:T(8,128)(2,1)} %gather_fusion.4), calls=%async_computation | async-start | bytes 4194304 | tf_op jit(solution)/shard_map/all_to_all | solution.py:138
  107.9 36.0 %while.25 = (s32[]{:T(128)}, bf16[4,64,32,128]{3,2,1,0:T(8,128)(2,1)}, f32[4,64]{1,0:T(4,128)S(1)}, bf16[4,64,32,128]{3,2,1,0:T(8,128)(2,1)}, s32[4,64]{1,0:T(4,...) while((s32[]{:T(128)}, bf16[4,64,32,128]{3,2,1,0:T(8,128)(2,1)}, ...), condition=%wide.region_11.12_spmd, body=%wide.region_8.11_spmd.sunk | while | flops 271322048 | bytes 38828920 | solution.py:140
  107.9 3.0 %gather_fusion.1 = bf16[64,256,128]{2,1,0:T(8,128)(2,1)} fusion(bf16[16,256,128]{2,1,0:T(8,128)(2,1)S(1)} %get-tuple-element.219, s32[1024]{0:T(1024)S(1)} %pad_clamp_fusion.11), kind=kCustom, calls=%fused_computation.1.clone.1 | custom fusion | bytes 8388864 | tf_op jit(solution)/shard_map/while/body/eval_jaxpr/jit(_take)/gather | solution.py:117
  110.9 4.1 %fusion.71 = (f32[64,32]{1,0:T(8,128)S(1)}, f32[64,32,256]{2,1,0:T(8,128)S(1)}) fusion(bf16[64,256,128]{2,1,0:T(8,128)(2,1)} %gather_fusion.1, bf16[4,64,32,128]{3,2,1,0:T(8,128)(2,1)} %get-tuple-element.217, s32[]{:T(128)} %get-tuple-element.206), kind=kOutput, calls=%fused_computation.29.clone.1 | convolution fusion | flops 135264256 | bytes 6824448 | tf_op jit(solution)/shard_map/while/body/eval_jaxpr/bqe,bpe->bqp/dot_general | solution.py:119
  117.0 3.0 %gather_fusion.1 = bf16[64,256,128]{2,1,0:T(8,128)(2,1)} fusion(bf16[16,256,128]{2,1,0:T(8,128)(2,1)S(1)} %get-tuple-element.219, s32[1024]{0:T(1024)S(1)} %pad_clamp_fusion.11), kind=kCustom, calls=%fused_computation.1.clone.1 | custom fusion | bytes 8388864 | tf_op jit(solution)/shard_map/while/body/eval_jaxpr/jit(_take)/gather | solution.py:117
  120.0 4.1 %fusion.71 = (f32[64,32]{1,0:T(8,128)S(1)}, f32[64,32,256]{2,1,0:T(8,128)S(1)}) fusion(bf16[64,256,128]{2,1,0:T(8,128)(2,1)} %gather_fusion.1, bf16[4,64,32,128]{3,2,1,0:T(8,128)(2,1)} %get-tuple-element.217, s32[]{:T(128)} %get-tuple-element.206), kind=kOutput, calls=%fused_computation.29.clone.1 | convolution fusion | flops 135264256 | bytes 6824448 | tf_op jit(solution)/shard_map/while/body/eval_jaxpr/bqe,bpe->bqp/dot_general | solution.py:119
  126.0 3.0 %gather_fusion.1 = bf16[64,256,128]{2,1,0:T(8,128)(2,1)} fusion(bf16[16,256,128]{2,1,0:T(8,128)(2,1)S(1)} %get-tuple-element.219, s32[1024]{0:T(1024)S(1)} %pad_clamp_fusion.11), kind=kCustom, calls=%fused_computation.1.clone.1 | custom fusion | bytes 8388864 | tf_op jit(solution)/shard_map/while/body/eval_jaxpr/jit(_take)/gather | solution.py:117
  129.0 4.1 %fusion.71 = (f32[64,32]{1,0:T(8,128)S(1)}, f32[64,32,256]{2,1,0:T(8,128)S(1)}) fusion(bf16[64,256,128]{2,1,0:T(8,128)(2,1)} %gather_fusion.1, bf16[4,64,32,128]{3,2,1,0:T(8,128)(2,1)} %get-tuple-element.217, s32[]{:T(128)} %get-tuple-element.206), kind=kOutput, calls=%fused_computation.29.clone.1 | convolution fusion | flops 135264256 | bytes 6824448 | tf_op jit(solution)/shard_map/while/body/eval_jaxpr/bqe,bpe->bqp/dot_general | solution.py:119
  135.0 3.0 %gather_fusion.1 = bf16[64,256,128]{2,1,0:T(8,128)(2,1)} fusion(bf16[16,256,128]{2,1,0:T(8,128)(2,1)S(1)} %get-tuple-element.219, s32[1024]{0:T(1024)S(1)} %pad_clamp_fusion.11), kind=kCustom, calls=%fused_computation.1.clone.1 | custom fusion | bytes 8388864 | tf_op jit(solution)/shard_map/while/body/eval_jaxpr/jit(_take)/gather | solution.py:117
  138.0 4.1 %fusion.71 = (f32[64,32]{1,0:T(8,128)S(1)}, f32[64,32,256]{2,1,0:T(8,128)S(1)}) fusion(bf16[64,256,128]{2,1,0:T(8,128)(2,1)} %gather_fusion.1, bf16[4,64,32,128]{3,2,1,0:T(8,128)(2,1)} %get-tuple-element.217, s32[]{:T(128)} %get-tuple-element.206), kind=kOutput, calls=%fused_computation.29.clone.1 | convolution fusion | flops 135264256 | bytes 6824448 | tf_op jit(solution)/shard_map/while/body/eval_jaxpr/bqe,bpe->bqp/dot_general | solution.py:119
  143.9 16.0 %all-to-all-done = bf16[256,32,128]{2,1,0:T(8,128)(2,1)S(1)} async-done(((bf16[256,32,128]{2,1,0:T(8,128)(2,1)}), bf16[256,32,128]{2,1,0:T(8,128)(2,1)S(1)}, u32[]{:S(2)}, u32[]{:S(2)}) %all-to-all-start) | async-done | bytes 2097184 | tf_op jit(solution)/shard_map/all_to_all | solution.py:138
  159.9 7.3 %all-to-all-start.3 = ((bf16[256,32,128]{2,1,0:T(8,128)(2,1)}), bf16[256,32,128]{2,1,0:T(8,128)(2,1)}, u32[]{:S(2)}, u32[]{:S(2)}) async-start(bf16[256,32,128]{2,1,0:T(8,128)(2,1)} %bitcast.92), calls=%async_computation.3 | async-start | bytes 4194304 | tf_op jit(solution)/shard_map/all_to_all | solution.py:156
  168.9 35.3 %while.24 = (s32[]{:T(128)}, bf16[4,64,32,128]{3,2,1,0:T(8,128)(2,1)}, f32[4,64]{1,0:T(4,128)S(1)}, bf16[4,64,32,128]{3,2,1,0:T(8,128)(2,1)S(1)}, s32[4,64]{1,0:...) while((s32[]{:T(128)}, bf16[4,64,32,128]{3,2,1,0:T(8,128)(2,1)}, ...), condition=%wide.region_7.8_spmd, body=%wide.region_4.7_spmd.sunk | while | flops 271322048 | bytes 38828412 | solution.py:140
  168.9 3.0 %gather_fusion = bf16[64,256,128]{2,1,0:T(8,128)(2,1)} fusion(bf16[16,256,128]{2,1,0:T(8,128)(2,1)S(1)} %get-tuple-element.243, s32[1024]{0:T(1024)S(1)} %pad_clamp_fusion.10), kind=kCustom, calls=%fused_computation.clone.1 | custom fusion | bytes 8388864 | tf_op jit(solution)/shard_map/while/body/eval_jaxpr/jit(_take)/gather | solution.py:117
  171.9 4.0 %fusion.66 = (f32[64,32]{1,0:T(8,128)S(1)}, f32[64,32,256]{2,1,0:T(8,128)S(1)}) fusion(bf16[64,256,128]{2,1,0:T(8,128)(2,1)} %gather_fusion, bf16[4,64,32,128]{3,2,1,0:T(8,128)(2,1)S(1)} %get-tuple-element.241, s32[]{:T(128)} %get-tuple-element.230), kind=kOutput, calls=%fused_computation.12.clone.1 | convolution fusion | flops 135264256 | bytes 6823940 | tf_op jit(solution)/shard_map/while/body/eval_jaxpr/bqe,bpe->bqp/dot_general | solution.py:119
  177.7 3.0 %gather_fusion = bf16[64,256,128]{2,1,0:T(8,128)(2,1)} fusion(bf16[16,256,128]{2,1,0:T(8,128)(2,1)S(1)} %get-tuple-element.243, s32[1024]{0:T(1024)S(1)} %pad_clamp_fusion.10), kind=kCustom, calls=%fused_computation.clone.1 | custom fusion | bytes 8388864 | tf_op jit(solution)/shard_map/while/body/eval_jaxpr/jit(_take)/gather | solution.py:117
  180.7 4.0 %fusion.66 = (f32[64,32]{1,0:T(8,128)S(1)}, f32[64,32,256]{2,1,0:T(8,128)S(1)}) fusion(bf16[64,256,128]{2,1,0:T(8,128)(2,1)} %gather_fusion, bf16[4,64,32,128]{3,2,1,0:T(8,128)(2,1)S(1)} %get-tuple-element.241, s32[]{:T(128)} %get-tuple-element.230), kind=kOutput, calls=%fused_computation.12.clone.1 | convolution fusion | flops 135264256 | bytes 6823940 | tf_op jit(solution)/shard_map/while/body/eval_jaxpr/bqe,bpe->bqp/dot_general | solution.py:119
  186.6 3.0 %gather_fusion = bf16[64,256,128]{2,1,0:T(8,128)(2,1)} fusion(bf16[16,256,128]{2,1,0:T(8,128)(2,1)S(1)} %get-tuple-element.243, s32[1024]{0:T(1024)S(1)} %pad_clamp_fusion.10), kind=kCustom, calls=%fused_computation.clone.1 | custom fusion | bytes 8388864 | tf_op jit(solution)/shard_map/while/body/eval_jaxpr/jit(_take)/gather | solution.py:117
  189.6 4.0 %fusion.66 = (f32[64,32]{1,0:T(8,128)S(1)}, f32[64,32,256]{2,1,0:T(8,128)S(1)}) fusion(bf16[64,256,128]{2,1,0:T(8,128)(2,1)} %gather_fusion, bf16[4,64,32,128]{3,2,1,0:T(8,128)(2,1)S(1)} %get-tuple-element.241, s32[]{:T(128)} %get-tuple-element.230), kind=kOutput, calls=%fused_computation.12.clone.1 | convolution fusion | flops 135264256 | bytes 6823940 | tf_op jit(solution)/shard_map/while/body/eval_jaxpr/bqe,bpe->bqp/dot_general | solution.py:119
  195.4 3.0 %gather_fusion = bf16[64,256,128]{2,1,0:T(8,128)(2,1)} fusion(bf16[16,256,128]{2,1,0:T(8,128)(2,1)S(1)} %get-tuple-element.243, s32[1024]{0:T(1024)S(1)} %pad_clamp_fusion.10), kind=kCustom, calls=%fused_computation.clone.1 | custom fusion | bytes 8388864 | tf_op jit(solution)/shard_map/while/body/eval_jaxpr/jit(_take)/gather | solution.py:117
  198.4 4.0 %fusion.66 = (f32[64,32]{1,0:T(8,128)S(1)}, f32[64,32,256]{2,1,0:T(8,128)S(1)}) fusion(bf16[64,256,128]{2,1,0:T(8,128)(2,1)} %gather_fusion, bf16[4,64,32,128]{3,2,1,0:T(8,128)(2,1)S(1)} %get-tuple-element.241, s32[]{:T(128)} %get-tuple-element.230), kind=kOutput, calls=%fused_computation.12.clone.1 | convolution fusion | flops 135264256 | bytes 6823940 | tf_op jit(solution)/shard_map/while/body/eval_jaxpr/bqe,bpe->bqp/dot_general | solution.py:119
  204.2 15.8 %all-to-all-done.3 = bf16[256,32,128]{2,1,0:T(8,128)(2,1)} async-done(((bf16[256,32,128]{2,1,0:T(8,128)(2,1)}), bf16[256,32,128]{2,1,0:T(8,128)(2,1)}, u32[]{:S(2)}, u32[]{:S(2)}) %all-to-all-start.3) | async-done | bytes 2097184 | tf_op jit(solution)/shard_map/all_to_all | solution.py:156
  220.0 6.3 %all-to-all-start.2 = ((bf16[256,32,128]{2,1,0:T(8,128)(2,1)}), bf16[256,32,128]{2,1,0:T(8,128)(2,1)S(1)}, u32[]{:S(2)}, u32[]{:S(2)}) async-start(bf16[256,32,128]{2,1,0:T(8,128)(2,1)} %bitcast.91), calls=%async_computation.2 | async-start | bytes 4194304 | tf_op jit(solution)/shard_map/all_to_all | solution.py:151
  227.5 56.3 %shard_map.60 = f32[256,128]{1,0:T(8,128)} custom-call(f32[256,128]{1,0:T(8,128)} %pad.11.rows_ref), custom_call_target="tpu_custom_call" | custom-call | tf_op jit(solution)/shard_map/pallas_call | solution.py:67
  287.1 3.3 %gather_fusion.8 = bf16[128,32,128]{2,1,0:T(8,128)(2,1)} fusion(bf16[256,32,128]{2,1,0:T(8,128)(2,1)} %all-to-all-done.3, s32[1024]{0:T(1024)S(1)} %pad_clamp_fusion.2), kind=kCustom, calls=%fused_computation.8 | custom fusion | bytes 2097664 | tf_op jit(solution)/shard_map/jit(_take)/gather | solution.py:171
  (119 shorter events, 39.0 us)
Async XLA Ops:
  0.6 1.6 copy-start
  0.6 31.0 %copy-start.4 = (bf16[8,32,128]{2,1,0:T(8,128)(2,1)S(1)}, bf16[8,32,128]{2,1,0:T(8,128)(2,1)}, u32[]{:S(2)}) copy-start(bf16[8,32,128]{2,1,0:T(8,128)(2,1)} %param.8) | copy-start | bytes 196612
  34.4 64.1 %all-to-all-start.1 = ((bf16[256,32,128]{2,1,0:T(8,128)(2,1)}), bf16[256,32,128]{2,1,0:T(8,128)(2,1)S(1)}, u32[]{:S(2)}, u32[]{:S(2)}) async-start(bf16[256,32,128]{2,1,0:T(8,128)(2,1)} %gather_fusion.5), calls=%async_computation.1 | async-start | bytes 4194304 | tf_op jit(solution)/shard_map/all_to_all | solution.py:138
  98.6 1.3 copy-start.3
  99.9 60.0 %all-to-all-start = ((bf16[256,32,128]{2,1,0:T(8,128)(2,1)}), bf16[256,32,128]{2,1,0:T(8,128)(2,1)S(1)}, u32[]{:S(2)}, u32[]{:S(2)}) async-start(bf16[256,32,128]{2,1,0:T(8,128)(2,1)} %gather_fusion.4), calls=%async_computation | async-start | bytes 4194304 | tf_op jit(solution)/shard_map/all_to_all | solution.py:138
  110.9 4.1 %copy-start.1 = (bf16[64,256,128]{2,1,0:T(8,128)(2,1)S(1)}, bf16[64,256,128]{2,1,0:T(8,128)(2,1)}, u32[]{:S(2)}) copy-start(bf16[64,256,128]{2,1,0:T(8,128)(2,1)} %gather_fusion.1) | copy-start | bytes 12582916 | tf_op jit(solution)/shard_map/while
  120.0 4.1 %copy-start.1 = (bf16[64,256,128]{2,1,0:T(8,128)(2,1)S(1)}, bf16[64,256,128]{2,1,0:T(8,128)(2,1)}, u32[]{:S(2)}) copy-start(bf16[64,256,128]{2,1,0:T(8,128)(2,1)} %gather_fusion.1) | copy-start | bytes 12582916 | tf_op jit(solution)/shard_map/while
  129.0 4.1 %copy-start.1 = (bf16[64,256,128]{2,1,0:T(8,128)(2,1)S(1)}, bf16[64,256,128]{2,1,0:T(8,128)(2,1)}, u32[]{:S(2)}) copy-start(bf16[64,256,128]{2,1,0:T(8,128)(2,1)} %gather_fusion.1) | copy-start | bytes 12582916 | tf_op jit(solution)/shard_map/while
  138.0 4.1 %copy-start.1 = (bf16[64,256,128]{2,1,0:T(8,128)(2,1)S(1)}, bf16[64,256,128]{2,1,0:T(8,128)(2,1)}, u32[]{:S(2)}) copy-start(bf16[64,256,128]{2,1,0:T(8,128)(2,1)} %gather_fusion.1) | copy-start | bytes 12582916 | tf_op jit(solution)/shard_map/while
  159.9 60.1 %all-to-all-start.3 = ((bf16[256,32,128]{2,1,0:T(8,128)(2,1)}), bf16[256,32,128]{2,1,0:T(8,128)(2,1)}, u32[]{:S(2)}, u32[]{:S(2)}) async-start(bf16[256,32,128]{2,1,0:T(8,128)(2,1)} %bitcast.92), calls=%async_computation.3 | async-start | bytes 4194304 | tf_op jit(solution)/shard_map/all_to_all | solution.py:156
  171.9 4.0 %copy-start.2 = (bf16[64,256,128]{2,1,0:T(8,128)(2,1)S(1)}, bf16[64,256,128]{2,1,0:T(8,128)(2,1)}, u32[]{:S(2)}) copy-start(bf16[64,256,128]{2,1,0:T(8,128)(2,1)} %gather_fusion) | copy-start | bytes 12582916 | tf_op jit(solution)/shard_map/while
  180.7 4.0 %copy-start.2 = (bf16[64,256,128]{2,1,0:T(8,128)(2,1)S(1)}, bf16[64,256,128]{2,1,0:T(8,128)(2,1)}, u32[]{:S(2)}) copy-start(bf16[64,256,128]{2,1,0:T(8,128)(2,1)} %gather_fusion) | copy-start | bytes 12582916 | tf_op jit(solution)/shard_map/while
  189.6 4.0 %copy-start.2 = (bf16[64,256,128]{2,1,0:T(8,128)(2,1)S(1)}, bf16[64,256,128]{2,1,0:T(8,128)(2,1)}, u32[]{:S(2)}) copy-start(bf16[64,256,128]{2,1,0:T(8,128)(2,1)} %gather_fusion) | copy-start | bytes 12582916 | tf_op jit(solution)/shard_map/while
  198.4 4.0 %copy-start.2 = (bf16[64,256,128]{2,1,0:T(8,128)(2,1)S(1)}, bf16[64,256,128]{2,1,0:T(8,128)(2,1)}, u32[]{:S(2)}) copy-start(bf16[64,256,128]{2,1,0:T(8,128)(2,1)} %gather_fusion) | copy-start | bytes 12582916 | tf_op jit(solution)/shard_map/while
  220.0 72.0 %all-to-all-start.2 = ((bf16[256,32,128]{2,1,0:T(8,128)(2,1)}), bf16[256,32,128]{2,1,0:T(8,128)(2,1)S(1)}, u32[]{:S(2)}, u32[]{:S(2)}) async-start(bf16[256,32,128]{2,1,0:T(8,128)(2,1)} %bitcast.91), calls=%async_computation.2 | async-start | bytes 4194304 | tf_op jit(solution)/shard_map/all_to_all | solution.py:151

commit v16 on v12

--- a/solution.py
+++ b/solution.py
@@ -156,9 +156,12 @@
     )
     scores = jnp.stack(scores, axis=1)
     scores_flat = exchange(widen(scores, feat_width), dev_count, 1)[:, :slot_cap]
-    pair_score = jnp.take(scores_flat.reshape(slot_total), slot_index, axis=0, mode="clip").reshape(
-        query_count, list_len
-    )
+    pair_score = jnp.take(scores_flat[:, 0], target, axis=0, mode="clip")
+    for slot in range(1, slot_cap):
+        pair_score = jnp.where(
+            before == slot, jnp.take(scores_flat[:, slot], target, axis=0, mode="clip"), pair_score
+        )
+    pair_score = pair_score.reshape(query_count, list_len)
     exp_scores = jnp.exp(pair_score)
     total = jnp.sum(exp_scores, axis=-1, keepdims=True)
     loss = jnp.log(total[:, 0]) - pair_score[:, 0]

time: 286 us -> 287 us (level)
  no operation moved by 1% of the time
where the time goes in v16:
time: 287 us; the launch traced here: 284 us
  Pallas kernels  110 us (38%)
  local copies, waits for them, and re-layouts  49.8 us (17%)
  matrix products  46.5 us (16%)
  starting transfers between devices  34.7 us (12%)
  waiting for transfers between devices  31.9 us (11%)
  other arithmetic  10.9 us (4%)
    pallas_call x2, Pallas kernels, exchange(): pl.pallas_call(functools.partial(exchange_kernel, dev_count), out_shape=j...  110 us
    dot_general x8, matrix products, score_block(): jnp.einsum('bqe,bpe->bqp', query_block, passage_block, preferred_element_...  32.3 us
    gather x8, local copies, waits for them, and re-layouts, score_block(): passage_block = jnp.take(passage_unit, tag_block, axis=0, mode='clip')  24.1 us
    all_to_all x2, starting transfers between devices, local(): lax.all_to_all(outgoing, both_axes, split_axis=0, concat_axis=0, tiled=True)  21.1 us
    all_to_all x2, waiting for transfers between devices, local(): lax.all_to_all(outgoing, both_axes, split_axis=0, concat_axis=0, tiled=True)  16.1 us
    all_to_all x2, waiting for transfers between devices, local(): lax.all_to_all(pulled_parts[-1], both_axes, split_axis=0, concat_axis=0,...  15.8 us
    all_to_all x2, starting transfers between devices, local(): lax.all_to_all(pulled_parts[-1], both_axes, split_axis=0, concat_axis=0,...  13.6 us
    dot_general x8, matrix products, score_block(): jnp.einsum('bqp,bpe->bqe', attention, passage_block, preferred_element_ty...  13.4 us
  transfers between devices with their start and end apart: 4, of which 2 were waited for; matrix products, arithmetic and copies ran while one was open for 33% of the time, Pallas kernels for 39%

profile of v16, /device:TPU:8, one launch (start us, length us, event | category | flops | bytes accessed | tf_op | source)
XLA Modules:
  0.0 284.4 jit_solution(1537204224522453189)
XLA Ops:
  6.9 2.2 gather_fusion.5
  9.1 14.6 %all-to-all-start.1 = ((bf16[256,32,128]{2,1,0:T(8,128)(2,1)}), bf16[256,32,128]{2,1,0:T(8,128)(2,1)S(1)}, u32[]{:S(2)}, u32[]{:S(2)}) async-start(bf16[256,32,128]{2,1,0:T(8,128)(2,1)} %gather_fusion.5), calls=%async_computation.1 | async-start | bytes 4194304 | tf_op jit(solution)/shard_map/all_to_all | solution.py:137
  23.7 3.3 %gather_fusion.4 = s32[512]{0:T(512)S(1)} fusion(s32[128]{0:T(128)S(1)} %get-tuple-element.104, s32[1024]{0:T(1024)S(1)} %pad_clamp_fusion.4), kind=kCustom, calls=%fused_computation.4 | custom fusion | bytes 6144 | tf_op jit(solution)/shard_map/jit(_take)/gather | solution.py:108
  27.9 53.3 %shard_map.59 = f32[256,128]{1,0:T(8,128)} custom-call(f32[256,128]{1,0:T(8,128)} %pad_convert_fusion.rows_ref), custom_call_target="tpu_custom_call" | custom-call | tf_op jit(solution)/shard_map/pallas_call | solution.py:67
  82.5 2.2 gather_fusion.3
  84.7 1.8 fusion.23
  89.7 6.5 %all-to-all-start = ((bf16[256,32,128]{2,1,0:T(8,128)(2,1)}), bf16[256,32,128]{2,1,0:T(8,128)(2,1)S(1)}, u32[]{:S(2)}, u32[]{:S(2)}) async-start(bf16[256,32,128]{2,1,0:T(8,128)(2,1)} %gather_fusion.3), calls=%async_computation | async-start | bytes 4194304 | tf_op jit(solution)/shard_map/all_to_all | solution.py:137
  97.9 36.0 %while.25 = (s32[]{:T(128)}, bf16[4,64,32,128]{3,2,1,0:T(8,128)(2,1)}, f32[4,64]{1,0:T(4,128)S(1)}, bf16[4,64,32,128]{3,2,1,0:T(8,128)(2,1)}, s32[4,64]{1,0:T(4,...) while((s32[]{:T(128)}, bf16[4,64,32,128]{3,2,1,0:T(8,128)(2,1)}, ...), condition=%wide.region_11.12_spmd, body=%wide.region_8.11_spmd.sunk | while | flops 271322048 | bytes 38828920 | solution.py:139
  98.0 3.0 %gather_fusion.1 = bf16[64,256,128]{2,1,0:T(8,128)(2,1)} fusion(bf16[16,256,128]{2,1,0:T(8,128)(2,1)S(1)} %get-tuple-element.219, s32[1024]{0:T(1024)S(1)} %pad_clamp_fusion.10), kind=kCustom, calls=%fused_computation.1.clone.1 | custom fusion | bytes 8388864 | tf_op jit(solution)/shard_map/while/body/eval_jaxpr/jit(_take)/gather | solution.py:116
  101.0 4.1 %fusion.70 = (f32[64,32]{1,0:T(8,128)S(1)}, f32[64,32,256]{2,1,0:T(8,128)S(1)}) fusion(bf16[64,256,128]{2,1,0:T(8,128)(2,1)} %gather_fusion.1, bf16[4,64,32,128]{3,2,1,0:T(8,128)(2,1)} %get-tuple-element.217, s32[]{:T(128)} %get-tuple-element.206), kind=kOutput, calls=%fused_computation.30.clone.1 | convolution fusion | flops 135264256 | bytes 6824448 | tf_op jit(solution)/shard_map/while/body/eval_jaxpr/bqe,bpe->bqp/dot_general | solution.py:118
  107.0 3.0 %gather_fusion.1 = bf16[64,256,128]{2,1,0:T(8,128)(2,1)} fusion(bf16[16,256,128]{2,1,0:T(8,128)(2,1)S(1)} %get-tuple-element.219, s32[1024]{0:T(1024)S(1)} %pad_clamp_fusion.10), kind=kCustom, calls=%fused_computation.1.clone.1 | custom fusion | bytes 8388864 | tf_op jit(solution)/shard_map/while/body/eval_jaxpr/jit(_take)/gather | solution.py:116
  110.0 4.1 %fusion.70 = (f32[64,32]{1,0:T(8,128)S(1)}, f32[64,32,256]{2,1,0:T(8,128)S(1)}) fusion(bf16[64,256,128]{2,1,0:T(8,128)(2,1)} %gather_fusion.1, bf16[4,64,32,128]{3,2,1,0:T(8,128)(2,1)} %get-tuple-element.217, s32[]{:T(128)} %get-tuple-element.206), kind=kOutput, calls=%fused_computation.30.clone.1 | convolution fusion | flops 135264256 | bytes 6824448 | tf_op jit(solution)/shard_map/while/body/eval_jaxpr/bqe,bpe->bqp/dot_general | solution.py:118
  116.0 3.0 %gather_fusion.1 = bf16[64,256,128]{2,1,0:T(8,128)(2,1)} fusion(bf16[16,256,128]{2,1,0:T(8,128)(2,1)S(1)} %get-tuple-element.219, s32[1024]{0:T(1024)S(1)} %pad_clamp_fusion.10), kind=kCustom, calls=%fused_computation.1.clone.1 | custom fusion | bytes 8388864 | tf_op jit(solution)/shard_map/while/body/eval_jaxpr/jit(_take)/gather | solution.py:116
  119.1 4.1 %fusion.70 = (f32[64,32]{1,0:T(8,128)S(1)}, f32[64,32,256]{2,1,0:T(8,128)S(1)}) fusion(bf16[64,256,128]{2,1,0:T(8,128)(2,1)} %gather_fusion.1, bf16[4,64,32,128]{3,2,1,0:T(8,128)(2,1)} %get-tuple-element.217, s32[]{:T(128)} %get-tuple-element.206), kind=kOutput, calls=%fused_computation.30.clone.1 | convolution fusion | flops 135264256 | bytes 6824448 | tf_op jit(solution)/shard_map/while/body/eval_jaxpr/bqe,bpe->bqp/dot_general | solution.py:118
  125.0 3.0 %gather_fusion.1 = bf16[64,256,128]{2,1,0:T(8,128)(2,1)} fusion(bf16[16,256,128]{2,1,0:T(8,128)(2,1)S(1)} %get-tuple-element.219, s32[1024]{0:T(1024)S(1)} %pad_clamp_fusion.10), kind=kCustom, calls=%fused_computation.1.clone.1 | custom fusion | bytes 8388864 | tf_op jit(solution)/shard_map/while/body/eval_jaxpr/jit(_take)/gather | solution.py:116
  128.0 4.1 %fusion.70 = (f32[64,32]{1,0:T(8,128)S(1)}, f32[64,32,256]{2,1,0:T(8,128)S(1)}) fusion(bf16[64,256,128]{2,1,0:T(8,128)(2,1)} %gather_fusion.1, bf16[4,64,32,128]{3,2,1,0:T(8,128)(2,1)} %get-tuple-element.217, s32[]{:T(128)} %get-tuple-element.206), kind=kOutput, calls=%fused_computation.30.clone.1 | convolution fusion | flops 135264256 | bytes 6824448 | tf_op jit(solution)/shard_map/while/body/eval_jaxpr/bqe,bpe->bqp/dot_general | solution.py:118
  134.0 16.1 %all-to-all-done = bf16[256,32,128]{2,1,0:T(8,128)(2,1)S(1)} async-done(((bf16[256,32,128]{2,1,0:T(8,128)(2,1)}), bf16[256,32,128]{2,1,0:T(8,128)(2,1)S(1)}, u32[]{:S(2)}, u32[]{:S(2)}) %all-to-all-start) | async-done | bytes 2097184 | tf_op jit(solution)/shard_map/all_to_all | solution.py:137
  150.0 7.3 %all-to-all-start.3 = ((bf16[256,32,128]{2,1,0:T(8,128)(2,1)}), bf16[256,32,128]{2,1,0:T(8,128)(2,1)}, u32[]{:S(2)}, u32[]{:S(2)}) async-start(bf16[256,32,128]{2,1,0:T(8,128)(2,1)} %bitcast.87), calls=%async_computation.3 | async-start | bytes 4194304 | tf_op jit(solution)/shard_map/all_to_all | solution.py:155
  159.0 35.3 %while.24 = (s32[]{:T(128)}, bf16[4,64,32,128]{3,2,1,0:T(8,128)(2,1)}, f32[4,64]{1,0:T(4,128)S(1)}, bf16[4,64,32,128]{3,2,1,0:T(8,128)(2,1)S(1)}, s32[4,64]{1,0:...) while((s32[]{:T(128)}, bf16[4,64,32,128]{3,2,1,0:T(8,128)(2,1)}, ...), condition=%wide.region_7.8_spmd, body=%wide.region_4.7_spmd.sunk | while | flops 271322048 | bytes 38828412 | solution.py:139
  159.0 3.0 %gather_fusion = bf16[64,256,128]{2,1,0:T(8,128)(2,1)} fusion(bf16[16,256,128]{2,1,0:T(8,128)(2,1)S(1)} %get-tuple-element.243, s32[1024]{0:T(1024)S(1)} %pad_clamp_fusion.9), kind=kCustom, calls=%fused_computation.clone.1 | custom fusion | bytes 8388864 | tf_op jit(solution)/shard_map/while/body/eval_jaxpr/jit(_take)/gather | solution.py:116
  162.0 4.0 %fusion.65 = (f32[64,32]{1,0:T(8,128)S(1)}, f32[64,32,256]{2,1,0:T(8,128)S(1)}) fusion(bf16[64,256,128]{2,1,0:T(8,128)(2,1)} %gather_fusion, bf16[4,64,32,128]{3,2,1,0:T(8,128)(2,1)S(1)} %get-tuple-element.241, s32[]{:T(128)} %get-tuple-element.230), kind=kOutput, calls=%fused_computation.13.clone.1 | convolution fusion | flops 135264256 | bytes 6823940 | tf_op jit(solution)/shard_map/while/body/eval_jaxpr/bqe,bpe->bqp/dot_general | solution.py:118
  167.8 3.0 %gather_fusion = bf16[64,256,128]{2,1,0:T(8,128)(2,1)} fusion(bf16[16,256,128]{2,1,0:T(8,128)(2,1)S(1)} %get-tuple-element.243, s32[1024]{0:T(1024)S(1)} %pad_clamp_fusion.9), kind=kCustom, calls=%fused_computation.clone.1 | custom fusion | bytes 8388864 | tf_op jit(solution)/shard_map/while/body/eval_jaxpr/jit(_take)/gather | solution.py:116
  170.8 4.0 %fusion.65 = (f32[64,32]{1,0:T(8,128)S(1)}, f32[64,32,256]{2,1,0:T(8,128)S(1)}) fusion(bf16[64,256,128]{2,1,0:T(8,128)(2,1)} %gather_fusion, bf16[4,64,32,128]{3,2,1,0:T(8,128)(2,1)S(1)} %get-tuple-element.241, s32[]{:T(128)} %get-tuple-element.230), kind=kOutput, calls=%fused_computation.13.clone.1 | convolution fusion | flops 135264256 | bytes 6823940 | tf_op jit(solution)/shard_map/while/body/eval_jaxpr/bqe,bpe->bqp/dot_general | solution.py:118
  176.7 3.0 %gather_fusion = bf16[64,256,128]{2,1,0:T(8,128)(2,1)} fusion(bf16[16,256,128]{2,1,0:T(8,128)(2,1)S(1)} %get-tuple-element.243, s32[1024]{0:T(1024)S(1)} %pad_clamp_fusion.9), kind=kCustom, calls=%fused_computation.clone.1 | custom fusion | bytes 8388864 | tf_op jit(solution)/shard_map/while/body/eval_jaxpr/jit(_take)/gather | solution.py:116
  179.7 4.0 %fusion.65 = (f32[64,32]{1,0:T(8,128)S(1)}, f32[64,32,256]{2,1,0:T(8,128)S(1)}) fusion(bf16[64,256,128]{2,1,0:T(8,128)(2,1)} %gather_fusion, bf16[4,64,32,128]{3,2,1,0:T(8,128)(2,1)S(1)} %get-tuple-element.241, s32[]{:T(128)} %get-tuple-element.230), kind=kOutput, calls=%fused_computation.13.clone.1 | convolution fusion | flops 135264256 | bytes 6823940 | tf_op jit(solution)/shard_map/while/body/eval_jaxpr/bqe,bpe->bqp/dot_general | solution.py:118
  185.5 3.0 %gather_fusion = bf16[64,256,128]{2,1,0:T(8,128)(2,1)} fusion(bf16[16,256,128]{2,1,0:T(8,128)(2,1)S(1)} %get-tuple-element.243, s32[1024]{0:T(1024)S(1)} %pad_clamp_fusion.9), kind=kCustom, calls=%fused_computation.clone.1 | custom fusion | bytes 8388864 | tf_op jit(solution)/shard_map/while/body/eval_jaxpr/jit(_take)/gather | solution.py:116
  188.5 4.0 %fusion.65 = (f32[64,32]{1,0:T(8,128)S(1)}, f32[64,32,256]{2,1,0:T(8,128)S(1)}) fusion(bf16[64,256,128]{2,1,0:T(8,128)(2,1)} %gather_fusion, bf16[4,64,32,128]{3,2,1,0:T(8,128)(2,1)S(1)} %get-tuple-element.241, s32[]{:T(128)} %get-tuple-element.230), kind=kOutput, calls=%fused_computation.13.clone.1 | convolution fusion | flops 135264256 | bytes 6823940 | tf_op jit(solution)/shard_map/while/body/eval_jaxpr/bqe,bpe->bqp/dot_general | solution.py:118
  194.3 15.8 %all-to-all-done.3 = bf16[256,32,128]{2,1,0:T(8,128)(2,1)} async-done(((bf16[256,32,128]{2,1,0:T(8,128)(2,1)}), bf16[256,32,128]{2,1,0:T(8,128)(2,1)}, u32[]{:S(2)}, u32[]{:S(2)}) %all-to-all-start.3) | async-done | bytes 2097184 | tf_op jit(solution)/shard_map/all_to_all | solution.py:155
  210.1 6.3 %all-to-all-start.2 = ((bf16[256,32,128]{2,1,0:T(8,128)(2,1)}), bf16[256,32,128]{2,1,0:T(8,128)(2,1)S(1)}, u32[]{:S(2)}, u32[]{:S(2)}) async-start(bf16[256,32,128]{2,1,0:T(8,128)(2,1)} %bitcast.86), calls=%async_computation.2 | async-start | bytes 4194304 | tf_op jit(solution)/shard_map/all_to_all | solution.py:150
  217.6 56.3 %shard_map.60 = f32[256,128]{1,0:T(8,128)} custom-call(f32[256,128]{1,0:T(8,128)} %pad.11.rows_ref), custom_call_target="tpu_custom_call" | custom-call | tf_op jit(solution)/shard_map/pallas_call | solution.py:67
  278.6 2.4 gather_fusion.9
  282.6 1.8 fusion.27
  (119 shorter events, 37.0 us)
Async XLA Ops:
  0.6 1.6 copy-start
  9.1 79.3 %all-to-all-start.1 = ((bf16[256,32,128]{2,1,0:T(8,128)(2,1)}), bf16[256,32,128]{2,1,0:T(8,128)(2,1)S(1)}, u32[]{:S(2)}, u32[]{:S(2)}) async-start(bf16[256,32,128]{2,1,0:T(8,128)(2,1)} %gather_fusion.5), calls=%async_computation.1 | async-start | bytes 4194304 | tf_op jit(solution)/shard_map/all_to_all | solution.py:137
  88.4 1.3 copy-start.3
  89.7 60.3 %all-to-all-start = ((bf16[256,32,128]{2,1,0:T(8,128)(2,1)}), bf16[256,32,128]{2,1,0:T(8,128)(2,1)S(1)}, u32[]{:S(2)}, u32[]{:S(2)}) async-start(bf16[256,32,128]{2,1,0:T(8,128)(2,1)} %gather_fusion.3), calls=%async_computation | async-start | bytes 4194304 | tf_op jit(solution)/shard_map/all_to_all | solution.py:137
  101.0 4.1 %copy-start.1 = (bf16[64,256,128]{2,1,0:T(8,128)(2,1)S(1)}, bf16[64,256,128]{2,1,0:T(8,128)(2,1)}, u32[]{:S(2)}) copy-start(bf16[64,256,128]{2,1,0:T(8,128)(2,1)} %gather_fusion.1) | copy-start | bytes 12582916 | tf_op jit(solution)/shard_map/while
  110.0 4.1 %copy-start.1 = (bf16[64,256,128]{2,1,0:T(8,128)(2,1)S(1)}, bf16[64,256,128]{2,1,0:T(8,128)(2,1)}, u32[]{:S(2)}) copy-start(bf16[64,256,128]{2,1,0:T(8,128)(2,1)} %gather_fusion.1) | copy-start | bytes 12582916 | tf_op jit(solution)/shard_map/while
  119.0 4.1 %copy-start.1 = (bf16[64,256,128]{2,1,0:T(8,128)(2,1)S(1)}, bf16[64,256,128]{2,1,0:T(8,128)(2,1)}, u32[]{:S(2)}) copy-start(bf16[64,256,128]{2,1,0:T(8,128)(2,1)} %gather_fusion.1) | copy-start | bytes 12582916 | tf_op jit(solution)/shard_map/while
  128.0 4.1 %copy-start.1 = (bf16[64,256,128]{2,1,0:T(8,128)(2,1)S(1)}, bf16[64,256,128]{2,1,0:T(8,128)(2,1)}, u32[]{:S(2)}) copy-start(bf16[64,256,128]{2,1,0:T(8,128)(2,1)} %gather_fusion.1) | copy-start | bytes 12582916 | tf_op jit(solution)/shard_map/while
  150.0 60.1 %all-to-all-start.3 = ((bf16[256,32,128]{2,1,0:T(8,128)(2,1)}), bf16[256,32,128]{2,1,0:T(8,128)(2,1)}, u32[]{:S(2)}, u32[]{:S(2)}) async-start(bf16[256,32,128]{2,1,0:T(8,128)(2,1)} %bitcast.87), calls=%async_computation.3 | async-start | bytes 4194304 | tf_op jit(solution)/shard_map/all_to_all | solution.py:155
  162.0 4.0 %copy-start.2 = (bf16[64,256,128]{2,1,0:T(8,128)(2,1)S(1)}, bf16[64,256,128]{2,1,0:T(8,128)(2,1)}, u32[]{:S(2)}) copy-start(bf16[64,256,128]{2,1,0:T(8,128)(2,1)} %gather_fusion) | copy-start | bytes 12582916 | tf_op jit(solution)/shard_map/while
  170.8 4.0 %copy-start.2 = (bf16[64,256,128]{2,1,0:T(8,128)(2,1)S(1)}, bf16[64,256,128]{2,1,0:T(8,128)(2,1)}, u32[]{:S(2)}) copy-start(bf16[64,256,128]{2,1,0:T(8,128)(2,1)} %gather_fusion) | copy-start | bytes 12582916 | tf_op jit(solution)/shard_map/while
  179.7 4.0 %copy-start.2 = (bf16[64,256,128]{2,1,0:T(8,128)(2,1)S(1)}, bf16[64,256,128]{2,1,0:T(8,128)(2,1)}, u32[]{:S(2)}) copy-start(bf16[64,256,128]{2,1,0:T(8,128)(2,1)} %gather_fusion) | copy-start | bytes 12582916 | tf_op jit(solution)/shard_map/while
  188.5 4.0 %copy-start.2 = (bf16[64,256,128]{2,1,0:T(8,128)(2,1)S(1)}, bf16[64,256,128]{2,1,0:T(8,128)(2,1)}, u32[]{:S(2)}) copy-start(bf16[64,256,128]{2,1,0:T(8,128)(2,1)} %gather_fusion) | copy-start | bytes 12582916 | tf_op jit(solution)/shard_map/while
  210.1 71.3 %all-to-all-start.2 = ((bf16[256,32,128]{2,1,0:T(8,128)(2,1)}), bf16[256,32,128]{2,1,0:T(8,128)(2,1)S(1)}, u32[]{:S(2)}, u32[]{:S(2)}) async-start(bf16[256,32,128]{2,1,0:T(8,128)(2,1)} %bitcast.86), calls=%async_computation.2 | async-start | bytes 4194304 | tf_op jit(solution)/shard_map/all_to_all | solution.py:150
  281.0 1.6 copy-start.4

commit v17 on v12

--- a/solution.py
+++ b/solution.py
@@ -108,7 +108,7 @@
     labels = jnp.take(local_row, pair_of_slot, axis=0, mode="clip").astype(jnp.bfloat16)
     both_axes = ("group", "dev")
     labels = labels.reshape(device_total, slot_cap)
-    tags = exchange(widen(labels, feat_width), dev_count, 0)[:, :slot_cap].astype(jnp.int32)
+    tags = exchange(labels.astype(jnp.float32), dev_count, 0).astype(jnp.int32)
     block_rows = 64
 
     def score_block(inputs):
@@ -155,7 +155,7 @@
         lax.all_to_all(pulled_parts[-1], both_axes, split_axis=0, concat_axis=0, tiled=True)
     )
     scores = jnp.stack(scores, axis=1)
-    scores_flat = exchange(widen(scores, feat_width), dev_count, 1)[:, :slot_cap]
+    scores_flat = exchange(scores, dev_count, 1)
     pair_score = jnp.take(scores_flat.reshape(slot_total), slot_index, axis=0, mode="clip").reshape(
         query_count, list_len
     )

time: 286 us -> 286 us (level)
  no operation moved by 1% of the time
where the time goes in v17:
time: 286 us; the launch traced here: 283 us
  Pallas kernels  110 us (38%)
  local copies, waits for them, and re-layouts  48.9 us (17%)
  matrix products  46.5 us (16%)
  starting transfers between devices  34.7 us (12%)
  waiting for transfers between devices  31.9 us (11%)
  other arithmetic  10.2 us (4%)
    pallas_call x2, Pallas kernels, exchange(): pl.pallas_call(functools.partial(exchange_kernel, dev_count), out_shape=j...  110 us
    dot_general x8, matrix products, score_block(): jnp.einsum('bqe,bpe->bqp', query_block, passage_block, preferred_element_...  32.3 us
    gather x8, local copies, waits for them, and re-layouts, score_block(): passage_block = jnp.take(passage_unit, tag_block, axis=0, mode='clip')  24.1 us
    all_to_all x2, starting transfers between devices, local(): lax.all_to_all(outgoing, both_axes, split_axis=0, concat_axis=0, tiled=True)  21.1 us
    all_to_all x2, waiting for transfers between devices, local(): lax.all_to_all(outgoing, both_axes, split_axis=0, concat_axis=0, tiled=True)  16.1 us
    all_to_all x2, waiting for transfers between devices, local(): lax.all_to_all(pulled_parts[-1], both_axes, split_axis=0, concat_axis=0,...  15.8 us
    all_to_all x2, starting transfers between devices, local(): lax.all_to_all(pulled_parts[-1], both_axes, split_axis=0, concat_axis=0,...  13.6 us
    dot_general x8, matrix products, score_block(): jnp.einsum('bqp,bpe->bqe', attention, passage_block, preferred_element_ty...  13.4 us
  transfers between devices with their start and end apart: 4, of which 2 were waited for; matrix products, arithmetic and copies ran while one was open for 33% of the time, Pallas kernels for 39%

profile of v17, /device:TPU:8, one launch (start us, length us, event | category | flops | bytes accessed | tf_op | source)
XLA Modules:
  0.0 283.0 jit_solution(12073276321390048075)
XLA Ops:
  6.9 2.2 gather_fusion.5
  9.1 14.6 %all-to-all-start.1 = ((bf16[256,32,128]{2,1,0:T(8,128)(2,1)}), bf16[256,32,128]{2,1,0:T(8,128)(2,1)S(1)}, u32[]{:S(2)}, u32[]{:S(2)}) async-start(bf16[256,32,128]{2,1,0:T(8,128)(2,1)} %gather_fusion.5), calls=%async_computation.1 | async-start | bytes 4194304 | tf_op jit(solution)/shard_map/all_to_all | solution.py:137
  23.7 3.3 %gather_fusion.4 = s32[512]{0:T(512)S(1)} fusion(s32[128]{0:T(128)S(1)} %get-tuple-element.102, s32[1024]{0:T(1024)S(1)} %pad_clamp_fusion.5), kind=kCustom, calls=%fused_computation.4 | custom fusion | bytes 6144 | tf_op jit(solution)/shard_map/jit(_take)/gather | solution.py:108
  27.9 53.3 %shard_map.59 = f32[256,2]{1,0:T(8,128)} custom-call(f32[256,2]{1,0:T(8,128)} %reshape.273.rows_ref), custom_call_target="tpu_custom_call" | custom-call | tf_op jit(solution)/shard_map/pallas_call | solution.py:67
  82.5 2.2 gather_fusion.3
  84.8 1.8 fusion.23
  89.7 6.5 %all-to-all-start = ((bf16[256,32,128]{2,1,0:T(8,128)(2,1)}), bf16[256,32,128]{2,1,0:T(8,128)(2,1)S(1)}, u32[]{:S(2)}, u32[]{:S(2)}) async-start(bf16[256,32,128]{2,1,0:T(8,128)(2,1)} %gather_fusion.3), calls=%async_computation | async-start | bytes 4194304 | tf_op jit(solution)/shard_map/all_to_all | solution.py:137
  98.0 36.0 %while.25 = (s32[]{:T(128)}, bf16[4,64,32,128]{3,2,1,0:T(8,128)(2,1)}, f32[4,64]{1,0:T(4,128)S(1)}, bf16[4,64,32,128]{3,2,1,0:T(8,128)(2,1)}, s32[4,64]{1,0:T(4,...) while((s32[]{:T(128)}, bf16[4,64,32,128]{3,2,1,0:T(8,128)(2,1)}, ...), condition=%wide.region_11.12_spmd, body=%wide.region_8.11_spmd.sunk | while | flops 271322048 | bytes 38828920 | solution.py:139
  98.0 3.0 %gather_fusion.1 = bf16[64,256,128]{2,1,0:T(8,128)(2,1)} fusion(bf16[16,256,128]{2,1,0:T(8,128)(2,1)S(1)} %get-tuple-element.215, s32[1024]{0:T(1024)S(1)} %pad_clamp_fusion.11), kind=kCustom, calls=%fused_computation.1.clone.1 | custom fusion | bytes 8388864 | tf_op jit(solution)/shard_map/while/body/eval_jaxpr/jit(_take)/gather | solution.py:116
  101.0 4.1 %fusion.71 = (f32[64,32]{1,0:T(8,128)S(1)}, f32[64,32,256]{2,1,0:T(8,128)S(1)}) fusion(bf16[64,256,128]{2,1,0:T(8,128)(2,1)} %gather_fusion.1, bf16[4,64,32,128]{3,2,1,0:T(8,128)(2,1)} %get-tuple-element.213, s32[]{:T(128)} %get-tuple-element.202), kind=kOutput, calls=%fused_computation.29.clone.1 | convolution fusion | flops 135264256 | bytes 6824448 | tf_op jit(solution)/shard_map/while/body/eval_jaxpr/bqe,bpe->bqp/dot_general | solution.py:118
  107.0 3.0 %gather_fusion.1 = bf16[64,256,128]{2,1,0:T(8,128)(2,1)} fusion(bf16[16,256,128]{2,1,0:T(8,128)(2,1)S(1)} %get-tuple-element.215, s32[1024]{0:T(1024)S(1)} %pad_clamp_fusion.11), kind=kCustom, calls=%fused_computation.1.clone.1 | custom fusion | bytes 8388864 | tf_op jit(solution)/shard_map/while/body/eval_jaxpr/jit(_take)/gather | solution.py:116
  110.0 4.1 %fusion.71 = (f32[64,32]{1,0:T(8,128)S(1)}, f32[64,32,256]{2,1,0:T(8,128)S(1)}) fusion(bf16[64,256,128]{2,1,0:T(8,128)(2,1)} %gather_fusion.1, bf16[4,64,32,128]{3,2,1,0:T(8,128)(2,1)} %get-tuple-element.213, s32[]{:T(128)} %get-tuple-element.202), kind=kOutput, calls=%fused_computation.29.clone.1 | convolution fusion | flops 135264256 | bytes 6824448 | tf_op jit(solution)/shard_map/while/body/eval_jaxpr/bqe,bpe->bqp/dot_general | solution.py:118
  116.0 3.0 %gather_fusion.1 = bf16[64,256,128]{2,1,0:T(8,128)(2,1)} fusion(bf16[16,256,128]{2,1,0:T(8,128)(2,1)S(1)} %get-tuple-element.215, s32[1024]{0:T(1024)S(1)} %pad_clamp_fusion.11), kind=kCustom, calls=%fused_computation.1.clone.1 | custom fusion | bytes 8388864 | tf_op jit(solution)/shard_map/while/body/eval_jaxpr/jit(_take)/gather | solution.py:116
  119.1 4.1 %fusion.71 = (f32[64,32]{1,0:T(8,128)S(1)}, f32[64,32,256]{2,1,0:T(8,128)S(1)}) fusion(bf16[64,256,128]{2,1,0:T(8,128)(2,1)} %gather_fusion.1, bf16[4,64,32,128]{3,2,1,0:T(8,128)(2,1)} %get-tuple-element.213, s32[]{:T(128)} %get-tuple-element.202), kind=kOutput, calls=%fused_computation.29.clone.1 | convolution fusion | flops 135264256 | bytes 6824448 | tf_op jit(solution)/shard_map/while/body/eval_jaxpr/bqe,bpe->bqp/dot_general | solution.py:118
  125.0 3.0 %gather_fusion.1 = bf16[64,256,128]{2,1,0:T(8,128)(2,1)} fusion(bf16[16,256,128]{2,1,0:T(8,128)(2,1)S(1)} %get-tuple-element.215, s32[1024]{0:T(1024)S(1)} %pad_clamp_fusion.11), kind=kCustom, calls=%fused_computation.1.clone.1 | custom fusion | bytes 8388864 | tf_op jit(solution)/shard_map/while/body/eval_jaxpr/jit(_take)/gather | solution.py:116
  128.0 4.1 %fusion.71 = (f32[64,32]{1,0:T(8,128)S(1)}, f32[64,32,256]{2,1,0:T(8,128)S(1)}) fusion(bf16[64,256,128]{2,1,0:T(8,128)(2,1)} %gather_fusion.1, bf16[4,64,32,128]{3,2,1,0:T(8,128)(2,1)} %get-tuple-element.213, s32[]{:T(128)} %get-tuple-element.202), kind=kOutput, calls=%fused_computation.29.clone.1 | convolution fusion | flops 135264256 | bytes 6824448 | tf_op jit(solution)/shard_map/while/body/eval_jaxpr/bqe,bpe->bqp/dot_general | solution.py:118
  134.0 16.1 %all-to-all-done = bf16[256,32,128]{2,1,0:T(8,128)(2,1)S(1)} async-done(((bf16[256,32,128]{2,1,0:T(8,128)(2,1)}), bf16[256,32,128]{2,1,0:T(8,128)(2,1)S(1)}, u32[]{:S(2)}, u32[]{:S(2)}) %all-to-all-start) | async-done | bytes 2097184 | tf_op jit(solution)/shard_map/all_to_all | solution.py:137
  150.0 7.3 %all-to-all-start.3 = ((bf16[256,32,128]{2,1,0:T(8,128)(2,1)}), bf16[256,32,128]{2,1,0:T(8,128)(2,1)}, u32[]{:S(2)}, u32[]{:S(2)}) async-start(bf16[256,32,128]{2,1,0:T(8,128)(2,1)} %bitcast.91), calls=%async_computation.3 | async-start | bytes 4194304 | tf_op jit(solution)/shard_map/all_to_all | solution.py:155
  159.0 35.3 %while.24 = (s32[]{:T(128)}, bf16[4,64,32,128]{3,2,1,0:T(8,128)(2,1)}, f32[4,64]{1,0:T(4,128)S(1)}, bf16[4,64,32,128]{3,2,1,0:T(8,128)(2,1)S(1)}, s32[4,64]{1,0:...) while((s32[]{:T(128)}, bf16[4,64,32,128]{3,2,1,0:T(8,128)(2,1)}, ...), condition=%wide.region_7.8_spmd, body=%wide.region_4.7_spmd.sunk | while | flops 271322048 | bytes 38828412 | solution.py:139
  159.0 3.0 %gather_fusion = bf16[64,256,128]{2,1,0:T(8,128)(2,1)} fusion(bf16[16,256,128]{2,1,0:T(8,128)(2,1)S(1)} %get-tuple-element.239, s32[1024]{0:T(1024)S(1)} %pad_clamp_fusion.10), kind=kCustom, calls=%fused_computation.clone.1 | custom fusion | bytes 8388864 | tf_op jit(solution)/shard_map/while/body/eval_jaxpr/jit(_take)/gather | solution.py:116
  162.0 4.0 %fusion.66 = (f32[64,32]{1,0:T(8,128)S(1)}, f32[64,32,256]{2,1,0:T(8,128)S(1)}) fusion(bf16[64,256,128]{2,1,0:T(8,128)(2,1)} %gather_fusion, bf16[4,64,32,128]{3,2,1,0:T(8,128)(2,1)S(1)} %get-tuple-element.237, s32[]{:T(128)} %get-tuple-element.226), kind=kOutput, calls=%fused_computation.12.clone.1 | convolution fusion | flops 135264256 | bytes 6823940 | tf_op jit(solution)/shard_map/while/body/eval_jaxpr/bqe,bpe->bqp/dot_general | solution.py:118
  167.8 3.0 %gather_fusion = bf16[64,256,128]{2,1,0:T(8,128)(2,1)} fusion(bf16[16,256,128]{2,1,0:T(8,128)(2,1)S(1)} %get-tuple-element.239, s32[1024]{0:T(1024)S(1)} %pad_clamp_fusion.10), kind=kCustom, calls=%fused_computation.clone.1 | custom fusion | bytes 8388864 | tf_op jit(solution)/shard_map/while/body/eval_jaxpr/jit(_take)/gather | solution.py:116
  170.8 4.0 %fusion.66 = (f32[64,32]{1,0:T(8,128)S(1)}, f32[64,32,256]{2,1,0:T(8,128)S(1)}) fusion(bf16[64,256,128]{2,1,0:T(8,128)(2,1)} %gather_fusion, bf16[4,64,32,128]{3,2,1,0:T(8,128)(2,1)S(1)} %get-tuple-element.237, s32[]{:T(128)} %get-tuple-element.226), kind=kOutput, calls=%fused_computation.12.clone.1 | convolution fusion | flops 135264256 | bytes 6823940 | tf_op jit(solution)/shard_map/while/body/eval_jaxpr/bqe,bpe->bqp/dot_general | solution.py:118
  176.7 3.0 %gather_fusion = bf16[64,256,128]{2,1,0:T(8,128)(2,1)} fusion(bf16[16,256,128]{2,1,0:T(8,128)(2,1)S(1)} %get-tuple-element.239, s32[1024]{0:T(1024)S(1)} %pad_clamp_fusion.10), kind=kCustom, calls=%fused_computation.clone.1 | custom fusion | bytes 8388864 | tf_op jit(solution)/shard_map/while/body/eval_jaxpr/jit(_take)/gather | solution.py:116
  179.7 4.0 %fusion.66 = (f32[64,32]{1,0:T(8,128)S(1)}, f32[64,32,256]{2,1,0:T(8,128)S(1)}) fusion(bf16[64,256,128]{2,1,0:T(8,128)(2,1)} %gather_fusion, bf16[4,64,32,128]{3,2,1,0:T(8,128)(2,1)S(1)} %get-tuple-element.237, s32[]{:T(128)} %get-tuple-element.226), kind=kOutput, calls=%fused_computation.12.clone.1 | convolution fusion | flops 135264256 | bytes 6823940 | tf_op jit(solution)/shard_map/while/body/eval_jaxpr/bqe,bpe->bqp/dot_general | solution.py:118
  185.5 3.0 %gather_fusion = bf16[64,256,128]{2,1,0:T(8,128)(2,1)} fusion(bf16[16,256,128]{2,1,0:T(8,128)(2,1)S(1)} %get-tuple-element.239, s32[1024]{0:T(1024)S(1)} %pad_clamp_fusion.10), kind=kCustom, calls=%fused_computation.clone.1 | custom fusion | bytes 8388864 | tf_op jit(solution)/shard_map/while/body/eval_jaxpr/jit(_take)/gather | solution.py:116
  188.5 4.0 %fusion.66 = (f32[64,32]{1,0:T(8,128)S(1)}, f32[64,32,256]{2,1,0:T(8,128)S(1)}) fusion(bf16[64,256,128]{2,1,0:T(8,128)(2,1)} %gather_fusion, bf16[4,64,32,128]{3,2,1,0:T(8,128)(2,1)S(1)} %get-tuple-element.237, s32[]{:T(128)} %get-tuple-element.226), kind=kOutput, calls=%fused_computation.12.clone.1 | convolution fusion | flops 135264256 | bytes 6823940 | tf_op jit(solution)/shard_map/while/body/eval_jaxpr/bqe,bpe->bqp/dot_general | solution.py:118
  194.3 15.8 %all-to-all-done.3 = bf16[256,32,128]{2,1,0:T(8,128)(2,1)} async-done(((bf16[256,32,128]{2,1,0:T(8,128)(2,1)}), bf16[256,32,128]{2,1,0:T(8,128)(2,1)}, u32[]{:S(2)}, u32[]{:S(2)}) %all-to-all-start.3) | async-done | bytes 2097184 | tf_op jit(solution)/shard_map/all_to_all | solution.py:155
  210.1 6.3 %all-to-all-start.2 = ((bf16[256,32,128]{2,1,0:T(8,128)(2,1)}), bf16[256,32,128]{2,1,0:T(8,128)(2,1)S(1)}, u32[]{:S(2)}, u32[]{:S(2)}) async-start(bf16[256,32,128]{2,1,0:T(8,128)(2,1)} %bitcast.90), calls=%async_computation.2 | async-start | bytes 4194304 | tf_op jit(solution)/shard_map/all_to_all | solution.py:150
  217.6 56.3 %shard_map.60 = f32[256,2]{1,0:T(8,128)} custom-call(f32[256,2]{1,0:T(8,128)} %copy.9.rows_ref), custom_call_target="tpu_custom_call" | custom-call | tf_op jit(solution)/shard_map/pallas_call | solution.py:67
  277.2 2.4 gather_fusion.8
  281.1 1.8 fusion.27
  (117 shorter events, 35.4 us)
Async XLA Ops:
  0.6 1.6 copy-start
  9.1 79.3 %all-to-all-start.1 = ((bf16[256,32,128]{2,1,0:T(8,128)(2,1)}), bf16[256,32,128]{2,1,0:T(8,128)(2,1)S(1)}, u32[]{:S(2)}, u32[]{:S(2)}) async-start(bf16[256,32,128]{2,1,0:T(8,128)(2,1)} %gather_fusion.5), calls=%async_computation.1 | async-start | bytes 4194304 | tf_op jit(solution)/shard_map/all_to_all | solution.py:137
  88.4 1.3 copy-start.3
  89.7 60.3 %all-to-all-start = ((bf16[256,32,128]{2,1,0:T(8,128)(2,1)}), bf16[256,32,128]{2,1,0:T(8,128)(2,1)S(1)}, u32[]{:S(2)}, u32[]{:S(2)}) async-start(bf16[256,32,128]{2,1,0:T(8,128)(2,1)} %gather_fusion.3), calls=%async_computation | async-start | bytes 4194304 | tf_op jit(solution)/shard_map/all_to_all | solution.py:137
  101.0 4.1 %copy-start.1 = (bf16[64,256,128]{2,1,0:T(8,128)(2,1)S(1)}, bf16[64,256,128]{2,1,0:T(8,128)(2,1)}, u32[]{:S(2)}) copy-start(bf16[64,256,128]{2,1,0:T(8,128)(2,1)} %gather_fusion.1) | copy-start | bytes 12582916 | tf_op jit(solution)/shard_map/while
  110.0 4.1 %copy-start.1 = (bf16[64,256,128]{2,1,0:T(8,128)(2,1)S(1)}, bf16[64,256,128]{2,1,0:T(8,128)(2,1)}, u32[]{:S(2)}) copy-start(bf16[64,256,128]{2,1,0:T(8,128)(2,1)} %gather_fusion.1) | copy-start | bytes 12582916 | tf_op jit(solution)/shard_map/while
  119.1 4.1 %copy-start.1 = (bf16[64,256,128]{2,1,0:T(8,128)(2,1)S(1)}, bf16[64,256,128]{2,1,0:T(8,128)(2,1)}, u32[]{:S(2)}) copy-start(bf16[64,256,128]{2,1,0:T(8,128)(2,1)} %gather_fusion.1) | copy-start | bytes 12582916 | tf_op jit(solution)/shard_map/while
  128.0 4.1 %copy-start.1 = (bf16[64,256,128]{2,1,0:T(8,128)(2,1)S(1)}, bf16[64,256,128]{2,1,0:T(8,128)(2,1)}, u32[]{:S(2)}) copy-start(bf16[64,256,128]{2,1,0:T(8,128)(2,1)} %gather_fusion.1) | copy-start | bytes 12582916 | tf_op jit(solution)/shard_map/while
  150.0 60.1 %all-to-all-start.3 = ((bf16[256,32,128]{2,1,0:T(8,128)(2,1)}), bf16[256,32,128]{2,1,0:T(8,128)(2,1)}, u32[]{:S(2)}, u32[]{:S(2)}) async-start(bf16[256,32,128]{2,1,0:T(8,128)(2,1)} %bitcast.91), calls=%async_computation.3 | async-start | bytes 4194304 | tf_op jit(solution)/shard_map/all_to_all | solution.py:155
  162.0 4.0 %copy-start.2 = (bf16[64,256,128]{2,1,0:T(8,128)(2,1)S(1)}, bf16[64,256,128]{2,1,0:T(8,128)(2,1)}, u32[]{:S(2)}) copy-start(bf16[64,256,128]{2,1,0:T(8,128)(2,1)} %gather_fusion) | copy-start | bytes 12582916 | tf_op jit(solution)/shard_map/while
  170.8 4.0 %copy-start.2 = (bf16[64,256,128]{2,1,0:T(8,128)(2,1)S(1)}, bf16[64,256,128]{2,1,0:T(8,128)(2,1)}, u32[]{:S(2)}) copy-start(bf16[64,256,128]{2,1,0:T(8,128)(2,1)} %gather_fusion) | copy-start | bytes 12582916 | tf_op jit(solution)/shard_map/while
  179.7 4.0 %copy-start.2 = (bf16[64,256,128]{2,1,0:T(8,128)(2,1)S(1)}, bf16[64,256,128]{2,1,0:T(8,128)(2,1)}, u32[]{:S(2)}) copy-start(bf16[64,256,128]{2,1,0:T(8,128)(2,1)} %gather_fusion) | copy-start | bytes 12582916 | tf_op jit(solution)/shard_map/while
  188.5 4.0 %copy-start.2 = (bf16[64,256,128]{2,1,0:T(8,128)(2,1)S(1)}, bf16[64,256,128]{2,1,0:T(8,128)(2,1)}, u32[]{:S(2)}) copy-start(bf16[64,256,128]{2,1,0:T(8,128)(2,1)} %gather_fusion) | copy-start | bytes 12582916 | tf_op jit(solution)/shard_map/while
  210.1 69.8 %all-to-all-start.2 = ((bf16[256,32,128]{2,1,0:T(8,128)(2,1)}), bf16[256,32,128]{2,1,0:T(8,128)(2,1)S(1)}, u32[]{:S(2)}, u32[]{:S(2)}) async-start(bf16[256,32,128]{2,1,0:T(8,128)(2,1)} %bitcast.90), calls=%async_computation.2 | async-start | bytes 4194304 | tf_op jit(solution)/shard_map/all_to_all | solution.py:150
  279.5 1.6 copy-start.4
